TPU v7x, 32 devices: a whole 2x2x4 slice. The times are simulated.
32 devices in a mesh: row: 8 (over z, core), col: 4 (over y, x).
Axes of the slice: x: 2, y: 2, z: 4, core: 2. Of those that a mesh axis runs over, the one named last changes fastest.
Arguments:
- intensity: float32 [1024, 1024], P('row', 'col'), may hold values from 0 to 1
- start_block: float32 [16, 1024, 1024], P(None, 'row', 'col'), may hold values from -60 to 60
- old_direction: float32 [16, 1024, 1024], P(None, 'row', 'col'), may hold values from -60 to 60
Outputs:
- new_block: float32 [16, 1024, 1024], P(None, 'row', 'col')
- new_direction: float32 [16, 1024, 1024], P(None, 'row', 'col')
- ritz_values: float32 [16], replicated
All inputs are finite; a program needn't handle non-finite values.
Results may differ from a plain program's by a relative error of at most 0.0003.
Values sent between devices are 32-bit elements; how exact they have to be, the bound alone decides.
No kernel may reach another device: no remote copies, remote signals or barrier semaphores. Data moves between devices by JAX's collectives and lax.ppermute only.
A program may use at most 128 MiB of HBM per device.

v0:
```python
import math

import jax
import jax.numpy as jnp
from jax import lax
from jax.sharding import PartitionSpec as P

SWEEPS = 8


beta_value = 4.0
spatial_rate = 0.25
shift_numerator = 16.0
ritz_offset = 1.5
highest = lax.Precision.HIGHEST


def extended(block, sides, width):
    for axis, dim in sides:
        count = lax.axis_size(axis)
        forward = [(i, i + 1) for i in range(count - 1)]
        backward = [(target, source) for source, target in forward]
        low = lax.ppermute(
            lax.slice_in_dim(block, block.shape[dim] - width, None, axis=dim), axis, forward
        )
        high = lax.ppermute(lax.slice_in_dim(block, 0, width, axis=dim), axis, backward)
        block = jnp.concatenate([low, block, high], axis=dim)
    return block


def offset_list():
    return [(row_step, col_step) for row_step in range(-2, 3) for col_step in range(-2, 3)]


def lower_factor(matrix):
    order_size = matrix.shape[0]
    positions = jnp.arange(order_size, dtype=jnp.int32)

    def one_column(turn_index, factor):
        column = lax.dynamic_slice_in_dim(matrix, turn_index, 1, 1)[:, 0]
        factor_row = lax.dynamic_slice_in_dim(factor, turn_index, 1, 0)[0]
        column = column - jnp.dot(factor, factor_row, precision=highest)
        pivot_value = jnp.sqrt(lax.dynamic_slice_in_dim(column, turn_index, 1, 0)[0])
        column = jnp.where(positions >= turn_index, column / pivot_value, 0.0)
        return lax.dynamic_update_slice_in_dim(factor, column[:, None], turn_index, 1)

    return lax.fori_loop(0, order_size, one_column, jnp.zeros(matrix.shape, jnp.float32))


def lower_solve(factor, target):
    order_size = factor.shape[0]

    def lower_one_row(turn_index, solved):
        factor_row = lax.dynamic_slice_in_dim(factor, turn_index, 1, 0)[0]
        pivot_value = lax.dynamic_slice_in_dim(factor_row, turn_index, 1, 0)[0]
        target_row = lax.dynamic_slice_in_dim(target, turn_index, 1, 0)[0]
        entry_value = (target_row - jnp.dot(factor_row, solved, precision=highest)) / pivot_value
        return lax.dynamic_update_slice_in_dim(solved, entry_value[None], turn_index, 0)

    return lax.fori_loop(0, order_size, lower_one_row, jnp.zeros(target.shape, jnp.float32))


def upper_solve(factor, target):
    order_size = factor.shape[0]

    def upper_one_row(step_count, solved):
        turn_index = order_size - 1 - step_count
        column = lax.dynamic_slice_in_dim(factor, turn_index, 1, 1)[:, 0]
        pivot_value = lax.dynamic_slice_in_dim(column, turn_index, 1, 0)[0]
        target_row = lax.dynamic_slice_in_dim(target, turn_index, 1, 0)[0]
        entry_value = (target_row - jnp.dot(column, solved, precision=highest)) / pivot_value
        return lax.dynamic_update_slice_in_dim(solved, entry_value[None], turn_index, 0)

    return lax.fori_loop(0, order_size, upper_one_row, jnp.zeros(target.shape, jnp.float32))


def cosine_table(freq_index, pos_index, length):
    angle_units = (2 * pos_index[None, :] + 1) * freq_index[:, None] % (4 * length)
    angle = angle_units.astype(jnp.float32) * (math.pi / (2 * length))
    norming = jnp.where(freq_index == 0, math.sqrt(0.5), 1.0).astype(jnp.float32) * math.sqrt(
        2.0 / length
    )
    return jnp.cos(angle) * norming[:, None]


def cosine_pass(values, axis_dim, inverse):
    length = values.shape[axis_dim]
    block_len = math.gcd(length, 512)
    all_index = jnp.arange(length, dtype=jnp.int32)
    result = jnp.zeros(values.shape, jnp.float32)

    def one_block(turn_index, result):
        block_start = turn_index * block_len
        block_index = block_start + jnp.arange(block_len, dtype=jnp.int32)
        if inverse:
            cos_table = cosine_table(all_index, block_index, length)
            if axis_dim == 1:
                block_out = jnp.einsum("kn,vkc->vnc", cos_table, values, precision=highest)
            else:
                block_out = jnp.einsum("vrk,kn->vrn", values, cos_table, precision=highest)
        else:
            cos_table = cosine_table(block_index, all_index, length)
            if axis_dim == 1:
                block_out = jnp.einsum("kn,vnc->vkc", cos_table, values, precision=highest)
            else:
                block_out = jnp.einsum("vrn,kn->vrk", values, cos_table, precision=highest)
        return lax.dynamic_update_slice_in_dim(result, block_out, block_start, axis_dim)

    return lax.fori_loop(0, length // block_len, one_block, result)


def laplace_values(index, length):
    sine_part = jnp.sin(math.pi / (2 * length) * index.astype(jnp.float32))
    return 4.0 * sine_part * sine_part


def apply_graph(weights, padded, height, breadth):
    result = jnp.zeros((padded.shape[0], height, breadth), jnp.float32)
    for weight_map, (row_step, col_step) in zip(weights, offset_list()):
        result = (
            result
            + weight_map[None]
            * padded[:, 2 + row_step : 2 + row_step + height, 2 + col_step : 2 + col_step + breadth]
        )
    return result


def rayleigh_ritz(big_a, big_b, pixel_total):
    basis_size = big_a.shape[0]
    fields = basis_size // 3
    scaling = 1.0 / jnp.sqrt(jnp.diagonal(big_b) + 1e-06)
    norm_a = scaling[:, None] * (0.5 * (big_a + big_a.T)) * scaling[None, :]
    norm_b = scaling[:, None] * (0.5 * (big_b + big_b.T)) * scaling[None, :]
    factor_low = lower_factor(norm_b)
    left_solve = lower_solve(factor_low, norm_a)
    reduced = lower_solve(factor_low, left_solve.T).T
    reduced = 0.5 * (reduced + reduced.T) + ritz_offset * jnp.eye(basis_size, dtype=jnp.float32)
    basis_q = jnp.eye(basis_size, fields, dtype=jnp.float32)
    for sweep in range(SWEEPS):
        images_q = jnp.dot(reduced, basis_q, precision=highest)
        upper_u = lower_factor(jnp.dot(images_q.T, images_q, precision=highest))
        basis_q = lower_solve(upper_u, images_q.T).T
    ritz_values = jnp.sum(basis_q * jnp.dot(reduced, basis_q, precision=highest), 0) - ritz_offset
    coeffs = math.sqrt(pixel_total) * scaling[:, None] * upper_solve(factor_low, basis_q)
    return (ritz_values, coeffs)


def local(intensity, start_block, old_direction):
    fields, height, breadth = start_block.shape
    grid_rows = height * lax.axis_size("row")
    grid_cols = breadth * lax.axis_size("col")
    spectral_shift = shift_numerator / (grid_rows * grid_cols)
    row_first = lax.axis_index("row") * height
    col_first = lax.axis_index("col") * breadth
    padded_image = extended(intensity, (("row", 0), ("col", 1)), 2)
    row_global = row_first - 2 + jnp.arange(height + 4, dtype=jnp.int32)
    col_global = col_first - 2 + jnp.arange(breadth + 4, dtype=jnp.int32)
    row_inside = (row_global >= 0) & (row_global < grid_rows)
    col_inside = (col_global >= 0) & (col_global < grid_cols)
    inside = (row_inside[:, None] & col_inside[None, :]).astype(jnp.float32)
    center = padded_image[2 : 2 + height, 2 : 2 + breadth]
    weights = []
    for row_step, col_step in offset_list():
        shifted = padded_image[
            2 + row_step : 2 + row_step + height, 2 + col_step : 2 + col_step + breadth
        ]
        inside_part = inside[
            2 + row_step : 2 + row_step + height, 2 + col_step : 2 + col_step + breadth
        ]
        contrast = center - shifted
        weights.append(
            inside_part
            * jnp.exp(
                -beta_value * contrast * contrast
                - spatial_rate * (row_step * row_step + col_step * col_step)
            )
        )
    degree = weights[0]
    for weight_map in weights[1:]:
        degree = degree + weight_map
    both_fields = jnp.concatenate([start_block, old_direction], 0)
    padded_both = extended(both_fields, (("row", 1), ("col", 2)), 2)
    graph_both = apply_graph(weights, padded_both, height, breadth)
    degree_flat = degree.reshape(1, -1)
    x_flat = start_block.reshape(fields, -1)
    p_flat = old_direction.reshape(fields, -1)
    gx_flat = graph_both[:fields].reshape(fields, -1)
    gp_flat = graph_both[fields:].reshape(fields, -1)
    affinity_x, gram_x = lax.psum(
        (
            jnp.dot(x_flat, gx_flat.T, precision=highest),
            jnp.dot(x_flat * degree_flat, x_flat.T, precision=highest),
        ),
        ("row", "col"),
    )
    factor = lower_factor(gram_x)
    rayleigh = upper_solve(factor, lower_solve(factor, affinity_x))
    residual = (gx_flat - jnp.dot(rayleigh.T, x_flat * degree_flat, precision=highest)).reshape(
        fields, height, breadth
    )
    gathered = lax.all_to_all(residual, "row", split_axis=0, concat_axis=1, tiled=True)
    spectrum = cosine_pass(gathered, 1, False)
    items = lax.all_to_all(spectrum, "col", split_axis=1, concat_axis=2, tiled=True)
    forward = cosine_pass(items, 2, False)
    row_index = lax.axis_index("col") * items.shape[1] + jnp.arange(items.shape[1], dtype=jnp.int32)
    col_index = jnp.arange(items.shape[2], dtype=jnp.int32)
    divisor = (
        laplace_values(row_index, grid_rows)[:, None]
        + laplace_values(col_index, grid_cols)[None, :]
        + spectral_shift
    )
    solved = cosine_pass(forward / divisor[None], 2, True)
    returned = lax.all_to_all(solved, "col", split_axis=2, concat_axis=1, tiled=True)
    precond = lax.all_to_all(
        cosine_pass(returned, 1, True), "row", split_axis=1, concat_axis=0, tiled=True
    )
    padded_h = extended(precond, (("row", 1), ("col", 2)), 2)
    graph_h = apply_graph(weights, padded_h, height, breadth)
    h_flat = precond.reshape(fields, -1)
    gh_flat = graph_h.reshape(fields, -1)
    basis_all = jnp.concatenate([x_flat, h_flat, p_flat], 0)
    graph_all = jnp.concatenate([gx_flat, gh_flat, gp_flat], 0)
    big_a, big_b = lax.psum(
        (
            jnp.dot(basis_all, graph_all.T, precision=highest),
            jnp.dot(basis_all * degree_flat, basis_all.T, precision=highest),
        ),
        ("row", "col"),
    )
    ritz_values, coeffs = rayleigh_ritz(big_a, big_b, grid_rows * grid_cols)
    new_block = jnp.dot(coeffs.T, basis_all, precision=highest).reshape(fields, height, breadth)
    new_direction = jnp.dot(coeffs[fields:].T, basis_all[fields:], precision=highest).reshape(
        fields, height, breadth
    )
    return (new_block, new_direction, ritz_values)


def solution(mesh):
    return jax.shard_map(
        local,
        mesh=mesh,
        in_specs=(P("row", "col"), P(None, "row", "col"), P(None, "row", "col")),
        out_specs=(P(None, "row", "col"), P(None, "row", "col"), P()),
        check_vma=False,
    )
```

profile of v0, /device:TPU:0, one launch (start us, length us, event | category | flops | bytes accessed | tf_op | source)
XLA Modules:
  0.0 1377.3 jit_solution(7252420978095683549)
XLA Ops:
  11.8 5.2 collective-permute-start.3
  53.7 6.3 fusion.376
  68.7 9.5 maximum_maximum_fusion
  78.3 56.4 %fusion.275 = f32[32,128,256]{2,0,1:T(8,128)} fusion(f32[32,128,256]{2,0,1:T(8,128)} %copy-done.2, f32[32,2,256]{2,0,1:T(8,128)S(1)} %collective-permute-done.4, f32[32,2,256]{2,0,1:T(8,128)S(1)} %collective-permute-done.3, f32[32,132,258]{2,0,1:T(8,128)} %get-tuple-element.3403, f32[32,132,258]{2,0,1:T(8,128)} %get-tuple-element.3402, ...), kind=kLoop, calls=%fused_computation.357 | loop fusion | flops 55574528 | bytes 95682560 | tf_op jit(solution)/shard_map/add | solution.py:121
  141.8 42.9 %all-reduce.1 = (f32[16,16]{0,1:T(8,128)S(1)}, f32[16,16]{1,0:T(8,128)S(1)}) all-reduce(f32[16,16]{0,1:T(8,128)S(1)} %fusion.371, f32[16,16]{1,0:T(8,128)S(1)} %fusion.376), channel_id=1, replica_groups=mesh['row'=8,'col'=4] {'row','col'}, use_global_device_ids=true, to_apply=%region_3.4 | all-reduce | flops 512 | bytes 4096 | tf_op jit(solution)/shard_map/psum | solution.py:189
  184.8 25.8 %while.427 = (s32[]{:T(128)}, f32[16,16]{1,0:T(8,128)S(1)}, f32[16,16]{0,1:T(8,128)S(1)}, s32[]{:T(128)}, s32[]{:T(128)}) while((s32[]{:T(128)}, f32[16,16]{1,0:T(8,128)S(1)}, f32[16,16]{0,1:T(8,128)S(1)}, s32[]{:T(128)}, s32[]{:T(128)}) %tuple.943), condition=%wide.region_2.3_spmd.clone, body=%wide.region_1.0_spmd.clone.sunk | while | flops 3138 | bytes 10781 | solution.py:47
  210.7 22.5 %while.414 = (s32[]{:T(128)}, f32[16,16]{1,0:T(8,128)S(1)}, f32[16,16]{1,0:T(8,128)S(1)}, f32[16,16]{1,0:T(8,128)S(1)}, s32[]{:T(128)}, /*index=5*/s32[]{:T(128)}, s32[]{:T(128)}) while((s32[]{:T(128)}, f32[16,16]{1,0:T(8,128)S(1)}, f32[16,16]{1,0:T(8,128)S(1)}, f32[16,16]{1,0:T(8,128)S(1)}, s32[]{:T(128)}, /*index=5*/s32[]{:T(128)}, ...), condition=%wide.region_5.6_spmd, body=%wide.region_4.5_spmd.sunk | while | flops 3107 | bytes 11053 | solution.py:60
  233.3 22.7 %while.415 = (s32[]{:T(128)}, f32[16,16]{1,0:T(8,128)S(1)}, f32[16,16]{1,0:T(8,128)S(1)}, f32[16,16]{0,1:T(8,128)S(1)}, s32[]{:T(128)}, /*index=5*/s32[]{:T(128)}, s32[]{:T(128)}, s32[]{:T(128)}) while((s32[]{:T(128)}, f32[16,16]{1,0:T(8,128)S(1)}, f32[16,16]{1,0:T(8,128)S(1)}, f32[16,16]{0,1:T(8,128)S(1)}, s32[]{:T(128)}, ...), condition=%wide.region_7.8_spmd, body=%wide.region_6.7_spmd.sunk | while | flops 3111 | bytes 10599 | solution.py:74
  265.9 49.1 %all-to-all-done = f32[16,128,256]{2,1,0:T(8,128)S(1)} async-done(((f32[16,128,256]{2,1,0:T(8,128)}), f32[16,128,256]{2,1,0:T(8,128)S(1)}, u32[]{:S(2)}, u32[]{:S(2)}) %all-to-all-start) | async-done | bytes 2097184 | tf_op jit(solution)/shard_map/all_to_all | solution.py:201
  317.0 27.5 %while.428 = (s32[]{:T(128)}, f32[2,1024,256]{2,0,1:T(2,128)S(1)}, f32[2,1024,256]{2,1,0:T(8,128)}, s32[]{:T(128)}, s32[]{:T(128)}, /*index=5*/s32[]{:T(128)}, s32[]{:T(128)}) while((s32[]{:T(128)}, f32[2,1024,256]{2,0,1:T(2,128)S(1)}, f32[2,1024,256]{2,1,0:T(8,128)}, s32[]{:T(128)}, s32[]{:T(128)}, /*index=5*/s32[]{:T(128)}, ...), condition=%wide.region_9.10_spmd.clone, body=%wide.region_8.9_spmd.clone.sunk | while | flops 3229094400 | bytes 5259399 | solution.py:109
  317.1 12.8 fusion.724
  330.8 12.8 fusion.724
  351.1 24.4 %all-to-all-done.1 = f32[2,1024,256]{2,0,1:T(2,128)S(1)} async-done(((f32[2,1024,256]{2,0,1:T(2,128)}), f32[2,1024,256]{2,0,1:T(2,128)S(1)}, u32[]{:S(2)}, u32[]{:S(2)}) %all-to-all-start.1) | async-done | bytes 2097184 | tf_op jit(solution)/shard_map/all_to_all | solution.py:203
  383.1 28.8 %while.429 = (s32[]{:T(128)}, f32[2,256,1024]{2,1,0:T(8,128)}, f32[2,256,1024]{2,1,0:T(8,128)}, s32[]{:T(128)}, s32[]{:T(128)}, /*index=5*/s32[]{:T(128)}, s32[]{:T(128)}) while((s32[]{:T(128)}, f32[2,256,1024]{2,1,0:T(8,128)}, f32[2,256,1024]{2,1,0:T(8,128)}, s32[]{:T(128)}, s32[]{:T(128)}, /*index=5*/s32[]{:T(128)}, ...), condition=%wide.region_11.12_spmd.clone, body=%wide.region_10.11_spmd.clone.sunk | while | flops 3229094400 | bytes 7356551 | solution.py:109
  383.5 12.8 fusion.728
  397.7 12.8 fusion.728
  415.8 27.7 %while.439 = (s32[]{:T(128)}, f32[2,256,1024]{1,0,2:T(2,128)S(1)}, f32[2,256,1024]{2,1,0:T(8,128)}, s32[]{:T(128)}, s32[]{:T(128)}, /*index=5*/s32[]{:T(128)}, s32[]{:T(128)}) while((s32[]{:T(128)}, f32[2,256,1024]{1,0,2:T(2,128)S(1)}, f32[2,256,1024]{2,1,0:T(8,128)}, s32[]{:T(128)}, s32[]{:T(128)}, ...), condition=%wide.region_13.14_spmd.clone.clone, body=%wide.region_12.13_spmd.clone.clone.sunk | while | flops 3229094400 | bytes 5255299 | solution.py:109
  416.0 12.8 fusion.767
  429.7 12.8 fusion.767
  448.4 24.3 %all-to-all-done.2 = f32[2,256,1024]{1,0,2:T(2,128)S(1)} async-done(((f32[2,256,1024]{1,0,2:T(2,128)}), f32[2,256,1024]{1,0,2:T(2,128)S(1)}, u32[]{:S(2)}, u32[]{:S(2)}) %all-to-all-start.2) | async-done | bytes 2097184 | tf_op jit(solution)/shard_map/all_to_all | solution.py:213
  475.5 27.7 %while.440 = (s32[]{:T(128)}, f32[2,1024,256]{2,0,1:T(2,128)S(1)}, f32[2,1024,256]{2,1,0:T(8,128)}, s32[]{:T(128)}, s32[]{:T(128)}, /*index=5*/s32[]{:T(128)}, s32[]{:T(128)}) while((s32[]{:T(128)}, f32[2,1024,256]{2,0,1:T(2,128)S(1)}, f32[2,1024,256]{2,1,0:T(8,128)}, s32[]{:T(128)}, s32[]{:T(128)}, ...), condition=%wide.region_15.16_spmd.clone.clone, body=%wide.region_14.15_spmd.clone.clone.sunk | while | flops 3229094400 | bytes 5255299 | solution.py:109
  475.8 12.8 fusion.770
  489.5 12.8 fusion.770
  515.8 42.3 %all-to-all-done.3 = f32[2,1024,256]{2,0,1:T(2,128)} async-done(((f32[2,1024,256]{2,0,1:T(2,128)}), f32[2,1024,256]{2,0,1:T(2,128)}, u32[]{:S(2)}, u32[]{:S(2)}) %all-to-all-start.3) | async-done | bytes 2097184 | tf_op jit(solution)/shard_map/all_to_all | solution.py:214
  579.0 8.4 fusion.258
  590.7 40.9 %fusion.305 = f32[128,2,8,256]{3,2,1,0:T(8,128)} fusion(f32[16,132,256]{2,0,1:T(8,128)} %copy-done.15, f32[16,132,2]{2,0,1:T(8,128)} %copy.245, f32[16,132,2]{2,0,1:T(8,128)S(1)} %copy.243, f32[16,130,256]{2,0,1:T(8,128)} %copy-done.14, f32[16,130,256]{2,0,1:T(8,128)} %copy-done.16, f32[128,256]{1,0:T(8,128)} %get-tuple-element.3401, ...), kind=kLoop, calls=%fused_computation.409 | loop fusion | flops 36175872 | bytes 18056192
  634.4 7.9 fusion.260
  642.4 42.6 %all-reduce = (f32[48,48]{0,1:T(8,128)S(1)}, f32[48,48]{1,0:T(8,128)S(1)}) all-reduce(f32[48,48]{0,1:T(8,128)S(1)} %fusion.260, f32[48,48]{1,0:T(8,128)S(1)} %fusion.258), channel_id=1, replica_groups=mesh['row'=8,'col'=4] {'row','col'}, use_global_device_ids=true, to_apply=%region_19.20 | all-reduce | flops 4608 | bytes 36864 | tf_op jit(solution)/shard_map/psum | solution.py:223
  686.3 83.9 %while.430 = (s32[]{:T(128)}, f32[48,48]{1,0:T(8,128)S(1)}, f32[48,48]{0,1:T(8,128)S(1)}, s32[]{:T(128)}, s32[]{:T(128)}) while((s32[]{:T(128)}, f32[48,48]{1,0:T(8,128)S(1)}, f32[48,48]{0,1:T(8,128)S(1)}, s32[]{:T(128)}, s32[]{:T(128)}) %tuple.964), condition=%wide.region_18.19_spmd.clone, body=%wide.region_17.18_spmd.clone.sunk | while | flops 27842 | bytes 28061 | solution.py:47
  770.2 67.8 %while.416 = (s32[]{:T(128)}, f32[48,48]{1,0:T(8,128)S(1)}, f32[48,48]{1,0:T(8,128)S(1)}, f32[48,48]{1,0:T(8,128)S(1)}, s32[]{:T(128)}, /*index=5*/s32[]{:T(128)}, s32[]{:T(128)}) while((s32[]{:T(128)}, f32[48,48]{1,0:T(8,128)S(1)}, f32[48,48]{1,0:T(8,128)S(1)}, f32[48,48]{1,0:T(8,128)S(1)}, s32[]{:T(128)}, /*index=5*/s32[]{:T(128)}, ...), condition=%wide.region_21.22_spmd, body=%wide.region_20.21_spmd.sunk | while | flops 27747 | bytes 27821 | solution.py:60
  838.1 67.8 %while.417 = (s32[]{:T(128)}, f32[48,48]{1,0:T(8,128)S(1)}, f32[48,48]{1,0:T(8,128)S(1)}, f32[48,48]{1,0:T(8,128)S(1)}, s32[]{:T(128)}, /*index=5*/s32[]{:T(128)}, s32[]{:T(128)}) while((s32[]{:T(128)}, f32[48,48]{1,0:T(8,128)S(1)}, f32[48,48]{1,0:T(8,128)S(1)}, f32[48,48]{1,0:T(8,128)S(1)}, s32[]{:T(128)}, /*index=5*/s32[]{:T(128)}, ...), condition=%wide.region_23.24_spmd, body=%wide.region_22.23_spmd.sunk | while | flops 27747 | bytes 27821 | solution.py:60
  906.3 25.8 %while.431 = (s32[]{:T(128)}, f32[16,16]{1,0:T(8,128)S(1)}, f32[16,16]{0,1:T(8,128)S(1)}, s32[]{:T(128)}, s32[]{:T(128)}) while((s32[]{:T(128)}, f32[16,16]{1,0:T(8,128)S(1)}, f32[16,16]{0,1:T(8,128)S(1)}, s32[]{:T(128)}, s32[]{:T(128)}) %tuple.973), condition=%wide.region_25.26_spmd.clone, body=%wide.region_24.25_spmd.clone.sunk | while | flops 3138 | bytes 10781 | solution.py:47
  932.1 22.5 %while.418 = (s32[]{:T(128)}, f32[16,48]{1,0:T(8,128)S(1)}, f32[16,48]{1,0:T(8,128)S(1)}, f32[16,16]{1,0:T(8,128)S(1)}, s32[]{:T(128)}, /*index=5*/s32[]{:T(128)}, s32[]{:T(128)}) while((s32[]{:T(128)}, f32[16,48]{1,0:T(8,128)S(1)}, f32[16,48]{1,0:T(8,128)S(1)}, f32[16,16]{1,0:T(8,128)S(1)}, s32[]{:T(128)}, /*index=5*/s32[]{:T(128)}, ...), condition=%wide.region_27.28_spmd, body=%wide.region_26.27_spmd.sunk | while | flops 9315 | bytes 11437 | solution.py:60
  955.0 25.8 %while.432 = (s32[]{:T(128)}, f32[16,16]{1,0:T(8,128)S(1)}, f32[16,16]{0,1:T(8,128)S(1)}, s32[]{:T(128)}, s32[]{:T(128)}) while((s32[]{:T(128)}, f32[16,16]{1,0:T(8,128)S(1)}, f32[16,16]{0,1:T(8,128)S(1)}, s32[]{:T(128)}, s32[]{:T(128)}) %tuple.979), condition=%wide.region_29.30_spmd.clone, body=%wide.region_28.29_spmd.clone.sunk | while | flops 3138 | bytes 10781 | solution.py:47
  980.8 22.5 %while.419 = (s32[]{:T(128)}, f32[16,48]{1,0:T(8,128)S(1)}, f32[16,48]{1,0:T(8,128)S(1)}, f32[16,16]{1,0:T(8,128)S(1)}, s32[]{:T(128)}, /*index=5*/s32[]{:T(128)}, s32[]{:T(128)}) while((s32[]{:T(128)}, f32[16,48]{1,0:T(8,128)S(1)}, f32[16,48]{1,0:T(8,128)S(1)}, f32[16,16]{1,0:T(8,128)S(1)}, s32[]{:T(128)}, /*index=5*/s32[]{:T(128)}, ...), condition=%wide.region_31.32_spmd, body=%wide.region_30.31_spmd.sunk | while | flops 9315 | bytes 11437 | solution.py:60
  1003.6 25.8 %while.433 = (s32[]{:T(128)}, f32[16,16]{1,0:T(8,128)S(1)}, f32[16,16]{0,1:T(8,128)S(1)}, s32[]{:T(128)}, s32[]{:T(128)}) while((s32[]{:T(128)}, f32[16,16]{1,0:T(8,128)S(1)}, f32[16,16]{0,1:T(8,128)S(1)}, s32[]{:T(128)}, s32[]{:T(128)}) %tuple.985), condition=%wide.region_33.34_spmd.clone, body=%wide.region_32.33_spmd.clone.sunk | while | flops 3138 | bytes 10781 | solution.py:47
  1029.4 22.5 %while.420 = (s32[]{:T(128)}, f32[16,48]{1,0:T(8,128)S(1)}, f32[16,48]{1,0:T(8,128)S(1)}, f32[16,16]{1,0:T(8,128)S(1)}, s32[]{:T(128)}, /*index=5*/s32[]{:T(128)}, s32[]{:T(128)}) while((s32[]{:T(128)}, f32[16,48]{1,0:T(8,128)S(1)}, f32[16,48]{1,0:T(8,128)S(1)}, f32[16,16]{1,0:T(8,128)S(1)}, s32[]{:T(128)}, /*index=5*/s32[]{:T(128)}, ...), condition=%wide.region_35.36_spmd, body=%wide.region_34.35_spmd.sunk | while | flops 9315 | bytes 11437 | solution.py:60
  1052.3 25.8 %while.434 = (s32[]{:T(128)}, f32[16,16]{1,0:T(8,128)S(1)}, f32[16,16]{0,1:T(8,128)S(1)}, s32[]{:T(128)}, s32[]{:T(128)}) while((s32[]{:T(128)}, f32[16,16]{1,0:T(8,128)S(1)}, f32[16,16]{0,1:T(8,128)S(1)}, s32[]{:T(128)}, s32[]{:T(128)}) %tuple.991), condition=%wide.region_37.38_spmd.clone, body=%wide.region_36.37_spmd.clone.sunk | while | flops 3138 | bytes 10781 | solution.py:47
  1078.0 22.5 %while.421 = (s32[]{:T(128)}, f32[16,48]{1,0:T(8,128)S(1)}, f32[16,48]{1,0:T(8,128)S(1)}, f32[16,16]{1,0:T(8,128)S(1)}, s32[]{:T(128)}, /*index=5*/s32[]{:T(128)}, s32[]{:T(128)}) while((s32[]{:T(128)}, f32[16,48]{1,0:T(8,128)S(1)}, f32[16,48]{1,0:T(8,128)S(1)}, f32[16,16]{1,0:T(8,128)S(1)}, s32[]{:T(128)}, /*index=5*/s32[]{:T(128)}, ...), condition=%wide.region_39.40_spmd, body=%wide.region_38.39_spmd.sunk | while | flops 9315 | bytes 11437 | solution.py:60
  1100.9 25.8 %while.435 = (s32[]{:T(128)}, f32[16,16]{1,0:T(8,128)S(1)}, f32[16,16]{0,1:T(8,128)S(1)}, s32[]{:T(128)}, s32[]{:T(128)}) while((s32[]{:T(128)}, f32[16,16]{1,0:T(8,128)S(1)}, f32[16,16]{0,1:T(8,128)S(1)}, s32[]{:T(128)}, s32[]{:T(128)}) %tuple.997), condition=%wide.region_41.42_spmd.clone, body=%wide.region_40.41_spmd.clone.sunk | while | flops 3138 | bytes 10781 | solution.py:47
  1126.7 22.5 %while.422 = (s32[]{:T(128)}, f32[16,48]{1,0:T(8,128)S(1)}, f32[16,48]{1,0:T(8,128)S(1)}, f32[16,16]{1,0:T(8,128)S(1)}, s32[]{:T(128)}, /*index=5*/s32[]{:T(128)}, s32[]{:T(128)}) while((s32[]{:T(128)}, f32[16,48]{1,0:T(8,128)S(1)}, f32[16,48]{1,0:T(8,128)S(1)}, f32[16,16]{1,0:T(8,128)S(1)}, s32[]{:T(128)}, /*index=5*/s32[]{:T(128)}, ...), condition=%wide.region_43.44_spmd, body=%wide.region_42.43_spmd.sunk | while | flops 9315 | bytes 11437 | solution.py:60
  1149.5 25.8 %while.436 = (s32[]{:T(128)}, f32[16,16]{1,0:T(8,128)S(1)}, f32[16,16]{0,1:T(8,128)S(1)}, s32[]{:T(128)}, s32[]{:T(128)}) while((s32[]{:T(128)}, f32[16,16]{1,0:T(8,128)S(1)}, f32[16,16]{0,1:T(8,128)S(1)}, s32[]{:T(128)}, s32[]{:T(128)}) %tuple.1003), condition=%wide.region_45.46_spmd.clone, body=%wide.region_44.45_spmd.clone.sunk | while | flops 3138 | bytes 10781 | solution.py:47
  1175.3 22.5 %while.423 = (s32[]{:T(128)}, f32[16,48]{1,0:T(8,128)S(1)}, f32[16,48]{1,0:T(8,128)S(1)}, f32[16,16]{1,0:T(8,128)S(1)}, s32[]{:T(128)}, /*index=5*/s32[]{:T(128)}, s32[]{:T(128)}) while((s32[]{:T(128)}, f32[16,48]{1,0:T(8,128)S(1)}, f32[16,48]{1,0:T(8,128)S(1)}, f32[16,16]{1,0:T(8,128)S(1)}, s32[]{:T(128)}, /*index=5*/s32[]{:T(128)}, ...), condition=%wide.region_47.48_spmd, body=%wide.region_46.47_spmd.sunk | while | flops 9315 | bytes 11437 | solution.py:60
  1198.2 25.8 %while.437 = (s32[]{:T(128)}, f32[16,16]{1,0:T(8,128)S(1)}, f32[16,16]{0,1:T(8,128)S(1)}, s32[]{:T(128)}, s32[]{:T(128)}) while((s32[]{:T(128)}, f32[16,16]{1,0:T(8,128)S(1)}, f32[16,16]{0,1:T(8,128)S(1)}, s32[]{:T(128)}, s32[]{:T(128)}) %tuple.1009), condition=%wide.region_49.50_spmd.clone, body=%wide.region_48.49_spmd.clone.sunk | while | flops 3138 | bytes 10781 | solution.py:47
  1223.9 22.5 %while.424 = (s32[]{:T(128)}, f32[16,48]{1,0:T(8,128)S(1)}, f32[16,48]{1,0:T(8,128)S(1)}, f32[16,16]{1,0:T(8,128)S(1)}, s32[]{:T(128)}, /*index=5*/s32[]{:T(128)}, s32[]{:T(128)}) while((s32[]{:T(128)}, f32[16,48]{1,0:T(8,128)S(1)}, f32[16,48]{1,0:T(8,128)S(1)}, f32[16,16]{1,0:T(8,128)S(1)}, s32[]{:T(128)}, /*index=5*/s32[]{:T(128)}, ...), condition=%wide.region_51.52_spmd, body=%wide.region_50.51_spmd.sunk | while | flops 9315 | bytes 11437 | solution.py:60
  1246.8 25.8 %while.438 = (s32[]{:T(128)}, f32[16,16]{1,0:T(8,128)S(1)}, f32[16,16]{0,1:T(8,128)S(1)}, s32[]{:T(128)}, s32[]{:T(128)}) while((s32[]{:T(128)}, f32[16,16]{1,0:T(8,128)S(1)}, f32[16,16]{0,1:T(8,128)S(1)}, s32[]{:T(128)}, s32[]{:T(128)}) %tuple.1015), condition=%wide.region_53.54_spmd.clone, body=%wide.region_52.53_spmd.clone.sunk | while | flops 3138 | bytes 10781 | solution.py:47
  1272.6 22.5 %while.425 = (s32[]{:T(128)}, f32[16,48]{1,0:T(8,128)S(1)}, f32[16,48]{1,0:T(8,128)S(1)}, f32[16,16]{1,0:T(8,128)S(1)}, s32[]{:T(128)}, /*index=5*/s32[]{:T(128)}, s32[]{:T(128)}) while((s32[]{:T(128)}, f32[16,48]{1,0:T(8,128)S(1)}, f32[16,48]{1,0:T(8,128)S(1)}, f32[16,16]{1,0:T(8,128)S(1)}, s32[]{:T(128)}, /*index=5*/s32[]{:T(128)}, ...), condition=%wide.region_55.56_spmd, body=%wide.region_54.55_spmd.sunk | while | flops 9315 | bytes 11437 | solution.py:60
  1295.5 68.1 %while.426 = (s32[]{:T(128)}, f32[48,16]{1,0:T(8,128)S(1)}, f32[48,16]{1,0:T(8,128)S(1)}, f32[48,48]{0,1:T(8,128)S(1)}, s32[]{:T(128)}, /*index=5*/s32[]{:T(128)}, s32[]{:T(128)}, s32[]{:T(128)}) while((s32[]{:T(128)}, f32[48,16]{1,0:T(8,128)S(1)}, f32[48,16]{1,0:T(8,128)S(1)}, f32[48,48]{0,1:T(8,128)S(1)}, s32[]{:T(128)}, ...), condition=%wide.region_57.58_spmd, body=%wide.region_56.57_spmd.sunk | while | flops 9255 | bytes 26983 | solution.py:74
  (2127 shorter events, 770.1 us)
Async XLA Ops:
  1.4 19.7 %collective-permute-start = (f32[2,256]{1,0:T(2,128)S(1)}, f32[2,256]{1,0:T(2,128)S(1)}, u32[]{:S(2)}, u32[]{:S(2)}) collective-permute-start(f32[2,256]{1,0:T(2,128)S(1)} %get-tuple-element.3421), channel_id=1, source_target_pairs={{0,4},{4,8},{8,12},{12,16},{16,20},{20,24},{24,28},{1,5},{5,9},{9,... | collective-permute-start | bytes 6152 | tf_op jit(solution)/shard_map/ppermute | solution.py:23
  3.7 4.3 copy-start.17
  3.7 17.4 %collective-permute-start.1 = (f32[2,256]{1,0:T(2,128)S(1)}, f32[2,256]{1,0:T(2,128)S(1)}, u32[]{:S(2)}, u32[]{:S(2)}) collective-permute-start(f32[2,256]{1,0:T(2,128)S(1)} %get-tuple-element.3422), channel_id=1, source_target_pairs={{4,0},{8,4},{12,8},{16,12},{20,16},{24,20},{28,24},{5,1},{9,5},{13... | collective-permute-start | bytes 6152 | tf_op jit(solution)/shard_map/ppermute | solution.py:26
  8.0 10.5 copy-start.24
  8.0 10.5 copy-start.1
  9.2 1.9 copy-start.2
  11.8 24.4 %collective-permute-start.3 = (f32[32,2,256]{2,0,1:T(8,128)}, f32[32,2,256]{2,0,1:T(8,128)S(1)}, u32[]{:S(2)}, u32[]{:S(2)}) collective-permute-start(f32[32,2,256]{2,0,1:T(8,128)} %get-tuple-element.3408), channel_id=1, source_target_pairs={{0,4},{4,8},{8,12},{12,16},{16,20},{20,24},{24,28},{1,5},{5,9},{9,... | collective-permute-start | bytes 196616 | tf_op jit(solution)/shard_map/ppermute | solution.py:23
  17.1 19.2 %collective-permute-start.4 = (f32[32,2,256]{2,0,1:T(8,128)}, f32[32,2,256]{2,0,1:T(8,128)S(1)}, u32[]{:S(2)}, u32[]{:S(2)}) collective-permute-start(f32[32,2,256]{2,0,1:T(8,128)} %get-tuple-element.3409), channel_id=1, source_target_pairs={{4,0},{8,4},{12,8},{16,12},{20,16},{24,20},{28,24},{5,1},{9,5},{13... | collective-permute-start | bytes 196616 | tf_op jit(solution)/shard_map/ppermute | solution.py:26
  21.2 5.3 collective-permute-start.2
  24.6 6.2 collective-permute-start.6
  25.9 5.0 copy-start.36
  34.7 43.6 %copy-start.25 = (f32[128,256]{1,0:T(8,128)}, f32[128,256]{1,0:T(8,128)S(1)}, u32[]{:S(2)}) copy-start(f32[128,256]{1,0:T(8,128)S(1)} %get-tuple-element.3379) | copy-start | bytes 393220
  34.7 43.6 %copy-start.26 = (f32[128,256]{1,0:T(8,128)}, f32[128,256]{1,0:T(8,128)S(1)}, u32[]{:S(2)}) copy-start(f32[128,256]{1,0:T(8,128)S(1)} %get-tuple-element.3380) | copy-start | bytes 393220
  34.7 43.6 %copy-start.27 = (f32[128,256]{1,0:T(8,128)}, f32[128,256]{1,0:T(8,128)S(1)}, u32[]{:S(2)}) copy-start(f32[128,256]{1,0:T(8,128)S(1)} %get-tuple-element.3381) | copy-start | bytes 393220
  34.7 43.6 %copy-start.28 = (f32[128,256]{1,0:T(8,128)}, f32[128,256]{1,0:T(8,128)S(1)}, u32[]{:S(2)}) copy-start(f32[128,256]{1,0:T(8,128)S(1)} %get-tuple-element.3382) | copy-start | bytes 393220
  34.7 43.6 %copy-start.29 = (f32[128,256]{1,0:T(8,128)}, f32[128,256]{1,0:T(8,128)S(1)}, u32[]{:S(2)}) copy-start(f32[128,256]{1,0:T(8,128)S(1)} %get-tuple-element.3383) | copy-start | bytes 393220
  34.7 3.2 copy-start.3
  44.6 16.1 %collective-permute-start.5 = (f32[32,132,2]{1,0,2:T(8,128)S(1)}, f32[32,132,2]{1,0,2:T(8,128)S(1)}, u32[]{:S(2)}, u32[]{:S(2)}) collective-permute-start(f32[32,132,2]{1,0,2:T(8,128)S(1)} %copy.222), channel_id=1, source_target_pairs={{0,1},{1,2},{2,3},{4,5},{5,6},{6,7},{8,9},{9,10},{10,11},{12,13},{... | collective-permute-start | bytes 101384 | tf_op jit(solution)/shard_map/ppermute | solution.py:23
  52.1 7.9 copy-start.35
  52.1 12.2 collective-permute-start.7
  68.7 9.6 copy-start.30
  68.7 9.6 copy-start.31
  134.7 5.2 copy-start.6
  255.9 2.4 copy-start.10
  255.9 2.3 copy-start.32
  256.1 4.2 copy-start.12
  262.2 52.7 %all-to-all-start = ((f32[16,128,256]{2,1,0:T(8,128)}), f32[16,128,256]{2,1,0:T(8,128)S(1)}, u32[]{:S(2)}, u32[]{:S(2)}) async-start(f32[16,128,256]{2,1,0:T(8,128)} %bitcast.831), calls=%async_computation | async-start | bytes 4194304 | tf_op jit(solution)/shard_map/all_to_all | solution.py:201
  345.9 29.6 %all-to-all-start.1 = ((f32[2,1024,256]{2,0,1:T(2,128)}), f32[2,1024,256]{2,0,1:T(2,128)S(1)}, u32[]{:S(2)}, u32[]{:S(2)}) async-start(f32[2,1024,256]{2,0,1:T(2,128)} %copy-done.19), calls=%async_computation.1 | async-start | bytes 4194304 | tf_op jit(solution)/shard_map/all_to_all | solution.py:203
  444.8 27.9 %all-to-all-start.2 = ((f32[2,256,1024]{1,0,2:T(2,128)}), f32[2,256,1024]{1,0,2:T(2,128)S(1)}, u32[]{:S(2)}, u32[]{:S(2)}) async-start(f32[2,256,1024]{1,0,2:T(2,128)} %copy-done.20), calls=%async_computation.2 | async-start | bytes 4194304 | tf_op jit(solution)/shard_map/all_to_all | solution.py:213
  504.6 4.9 copy-start.18
  504.6 53.6 %all-to-all-start.3 = ((f32[2,1024,256]{2,0,1:T(2,128)}), f32[2,1024,256]{2,0,1:T(2,128)}, u32[]{:S(2)}, u32[]{:S(2)}) async-start(f32[2,1024,256]{2,0,1:T(2,128)} %copy-done.21), calls=%async_computation.3 | async-start | bytes 4194304 | tf_op jit(solution)/shard_map/all_to_all | solution.py:214
  509.5 2.6 copy-start.11
  512.0 2.3 copy-start.22
  514.4 49.9 %slice-start = ((s8[6291456]{0:T(1024)(128)(4,1)}), s8[2097152]{0:T(1024)(128)(4,1)S(1)}, s32[]{:S(2)}) async-start(s8[6291456]{0:T(1024)(128)(4,1)} %bitcast.810), calls=%async_computation.4 | async-start | bytes 4194304
  558.1 6.2 slice-start.1
  560.1 6.7 copy-start.4
  560.2 6.6 collective-permute-start.8
  561.7 7.6 collective-permute-start.9
  564.3 2.3 copy-start.7
  566.8 2.6 copy-start
  570.8 2.1 copy-start.15
  572.8 6.2 copy-start.33
  573.5 13.9 %collective-permute-start.10 = (f32[16,132,2]{1,0,2:T(8,128)S(1)}, f32[16,132,2]{1,0,2:T(8,128)S(1)}, u32[]{:S(2)}, u32[]{:S(2)}) collective-permute-start(f32[16,132,2]{1,0,2:T(8,128)S(1)} %copy.242), channel_id=1, source_target_pairs={{0,1},{1,2},{2,3},{4,5},{5,6},{6,7},{8,9},{9,10},{10,11},{12,13},{... | collective-permute-start | bytes 50696 | tf_op jit(solution)/shard_map/ppermute | solution.py:23
  577.5 10.7 collective-permute-start.11
  587.4 3.3 copy-start.5
  631.6 2.2 copy-start.13
  631.6 2.8 copy-start.23
  838.1 525.6 %copy-start.8 = (f32[2,8,128,256]{3,1,2,0:T(8,128)S(1)}, f32[2,8,128,256]{3,1,2,0:T(8,128)}, u32[]{:S(2)}) copy-start(f32[2,8,128,256]{3,1,2,0:T(8,128)} %copy.290) | copy-start | bytes 6291460
  (7 other events, 9.6 us)
where the time goes:
time: 1390 us; the launch traced here: 1380 us
  local copies, waits for them, and re-layouts  432 us (31%)
  matrix products  407 us (29%)
  waiting for transfers between devices  145 us (10%)
  loops' own time  143 us (10%)
  other arithmetic  118 us (8%)
  blocking collectives  85.6 us (6%)
  starting transfers between devices  45.6 us (3%)
    dot_general x240, matrix products, lower_one_row(): jnp.dot(factor_row, solved, precision=highest)  187 us
    dynamic_slice x240, local copies, waits for them, and re-layouts, lower_one_row(): pivot_value = lax.dynamic_slice_in_dim(factor_row, turn_index, 1, 0)[0]  141 us
    another operation x10, loops' own time, lower_factor(): lax.fori_loop(0, order_size, one_column, jnp.zeros(matrix.shape, jnp.floa...  136 us
    dynamic_slice x192, local copies, waits for them, and re-layouts, one_column(): lax.dynamic_slice_in_dim(column, turn_index, 1, 0)[0]  116 us
    add x1, other arithmetic, apply_graph(): result + weight_map[None] * padded[:, 2 + row_step:2 + row_step + height,...  56.4 us
    dot_general x64, matrix products, upper_one_row(): jnp.dot(column, solved, precision=highest)  50 us
    all_to_all x1, waiting for transfers between devices, local(): lax.all_to_all(residual, 'row', split_axis=0, concat_axis=1, tiled=True)  49.1 us
    psum x1, blocking collectives, local(): lax.psum((jnp.dot(x_flat, gx_flat.T, precision=highest), jnp.dot(x_flat *...  42.9 us
  transfers between devices with their start and end apart: 16, of which 6 were waited for; matrix products, arithmetic and copies ran while one was open for 3% of the time, Pallas kernels for 0%

commit v1 on v0

v1 whole, which is shorter than its diff:
```python
import functools
import math

import jax
import jax.numpy as jnp
import numpy as np
from jax import lax
from jax.experimental import pallas as pl
from jax.experimental.pallas import tpu as pltpu
from jax.sharding import PartitionSpec as P

SWEEPS = 8
beta_value = 4.0
spatial_rate = 0.25
shift_numerator = 16.0
ritz_offset = 1.5
highest = lax.Precision.HIGHEST
f32 = jnp.float32
bf16 = jnp.bfloat16
BOTH = ("row", "col")
LANES = 128
OFFSETS = [(a, b) for a in range(-2, 3) for b in range(-2, 3)]
VMEM_BYTES = 50 * 2**20


def params():
    return pltpu.CompilerParams(vmem_limit_bytes=VMEM_BYTES)


def cost(flops, nbytes):
    return pl.CostEstimate(flops=int(flops), bytes_accessed=int(nbytes), transcendentals=0)


@functools.lru_cache(None)
def cosine_tables(length):
    k = np.arange(length)[:, None]
    n = np.arange(length)[None, :]
    table = np.cos(np.pi * ((2 * n + 1) * k % (4 * length)) / (2 * length)) * np.sqrt(2.0 / length)
    table[0] *= np.sqrt(0.5)
    high = table.astype(jnp.bfloat16)
    low = (table - high.astype(np.float64)).astype(jnp.bfloat16)
    return high, low


def ratio_sinh(a, b):
    return np.exp(a - b) * (1 - np.exp(-2 * a)) / (1 - np.exp(-2 * b))


@functools.lru_cache(None)
def row_tables(strips, depth, cols):
    rows = strips * depth
    lam = 4 * np.sin(np.pi * np.arange(cols) / (2 * cols)) ** 2
    mu = lam + shift_numerator / (rows * cols)
    excess = np.zeros((depth, cols))
    excess[0] = mu
    for r in range(1, depth):
        last = r == depth - 1
        prev = excess[r - 1]
        excess[r] = mu + prev / (1 + prev) - (1.0 if last else 0.0) + (0.0 if last else 0.0)
        if last:
            excess[r] = mu + prev / (1 + prev)
    eps = excess / (1 + excess)
    last_inv = 1.0 / (mu + eps[depth - 2])
    theta = 2 * np.arcsinh(np.sqrt(mu) / 2)
    levels = strips.bit_length() - 1
    gain, cross = [], []
    top = np.zeros((strips, levels, cols))
    bot = np.zeros((strips, levels, cols))
    for level in range(levels):
        m = 1 << level
        n = m * depth
        half = np.sinh(theta / 2)
        b = n * theta
        a = (n - 0.5) * theta
        end_end = np.exp(a - b) * (1 + np.exp(-2 * a)) / (1 - np.exp(-2 * b)) / (2 * half)
        first_last = 2 * np.cosh(theta / 2) * np.exp(-b) / (1 - np.exp(-2 * b)) / (2 * half)
        gain.append(1 / (1 + 2 * end_end))
        cross.append(first_last)
        rho = [ratio_sinh(p * depth * theta, b) for p in range(m + 1)]
        for s in range(strips):
            p = s % m
            if (s >> level) & 1:
                top[s, level], bot[s, level] = rho[m - p], rho[m - 1 - p]
            else:
                top[s, level], bot[s, level] = rho[p], rho[p + 1]
    cast = lambda x: np.asarray(x, np.float32)
    return cast(eps), cast(last_inv[None]), cast(gain), cast(cross), cast(top), cast(bot)


def split(x):
    high = x.astype(bf16)
    return high, (x - high.astype(f32)).astype(bf16)


def weights_kernel(index_ref, image_ref, w_ref, deg_ref):
    depth, cols = deg_ref.shape
    total_rows = index_ref[1]
    center = image_ref[2 : 2 + depth, :]
    row = lax.broadcasted_iota(jnp.int32, (depth, cols), 0) + index_ref[0] * depth
    col = lax.broadcasted_iota(jnp.int32, (depth, cols), 1)
    degree = jnp.zeros((depth, cols), f32)
    for b in range(-2, 3):
        moved = pltpu.roll(center, b % cols, 1) if b else center
        col_ok = (col - b >= 0) & (col - b < cols)
        total = None
        for a in range(-2, 3):
            if a == 0 and b == 0:
                weight = jnp.ones((depth, cols), f32)
            else:
                contrast = moved - image_ref[2 + a : 2 + a + depth, :]
                ok = col_ok & (row + a >= 0) & (row + a < total_rows)
                weight = jnp.where(
                    ok,
                    jnp.exp(-beta_value * contrast * contrast - spatial_rate * (a * a + b * b)),
                    0.0,
                )
            w_ref[OFFSETS.index((a, b))] = weight
            total = weight if total is None else total + weight
        degree = degree + (pltpu.roll(total, (-b) % cols, 1) if b else total)
    deg_ref[...] = degree


def make_weights(strip_index, image, depth, total_rows):
    cols = image.shape[1]
    index = jnp.stack([strip_index, jnp.int32(total_rows)]).astype(jnp.int32)
    return pl.pallas_call(
        weights_kernel,
        out_shape=(
            jax.ShapeDtypeStruct((25, depth, cols), f32),
            jax.ShapeDtypeStruct((depth, cols), f32),
        ),
        in_specs=[
            pl.BlockSpec(memory_space=pltpu.SMEM),
            pl.BlockSpec(memory_space=pltpu.VMEM),
        ],
        out_specs=(pl.BlockSpec(memory_space=pltpu.VMEM),) * 2,
        compiler_params=params(),
        cost_estimate=cost(60 * depth * cols * 25, 25 * depth * cols * 4),
        name="weights",
    )(index, image)


def graph_kernel(order, keep, lane_shift, v_ref, top_ref, bot_ref, w_ref, deg_ref, *rest):
    others, rest = rest[: len(order) - 1], rest[len(order) - 1 :]
    if keep:
        g_ref, gram_ref, pad_ref, acc_ref = rest
    else:
        gram_ref, pad_ref, acc_ref = rest
    chunks, depth, fields, width = v_ref.shape
    cols = chunks * width
    for c in range(chunks):
        lanes = slice(c * width, (c + 1) * width)
        pad_ref[0:2, :, lanes] = top_ref[c]
        pad_ref[2 : 2 + depth, :, lanes] = v_ref[c]
        pad_ref[2 + depth : 4 + depth, :, lanes] = bot_ref[c]
    parts = len(order)

    def one_row(r, acc):
        result = None
        for b in range(-2, 3):
            total = None
            for a in range(-2, 3):
                value = pad_ref[r + 2 + a]
                if a or b:
                    value = w_ref[OFFSETS.index((a, b)), pl.ds(r, 1), :] * value
                total = value if total is None else total + value
            if b:
                total = pltpu.roll(total, (-b) % cols, 1)
            result = total if result is None else result + total
        if keep:
            g_ref[r] = result
        own = pad_ref[r + 2]
        weighted = deg_ref[pl.ds(r, 1), :] * own
        left, position = [], 0
        for which in order:
            if which == "v":
                left.append(split(own))
            else:
                ref = others[position]
                position += 1
                left.append(split(jnp.concatenate([ref[c, r] for c in range(chunks)], 1)))
        left = jnp.concatenate([p[0] for p in left] + [p[1] for p in left], 0)
        graph_pair, degree_pair = split(result), split(weighted)
        right = jnp.concatenate(
            [graph_pair[0], degree_pair[0], graph_pair[1], degree_pair[1]], 0
        )
        return acc + lax.dot_general(
            left, right, (((1,), (1,)), ((), ())), preferred_element_type=f32
        )

    acc = lax.fori_loop(0, depth, one_row, jnp.zeros((2 * parts * fields, 4 * fields), f32))
    half = parts * fields
    acc_ref[...] = jnp.zeros(acc_ref.shape, f32)
    acc_ref[:, 0 : 4 * fields] = acc[:half] + acc[half:]
    both = acc_ref[...]
    both = both + pltpu.roll(both, LANES - 2 * fields, 1)
    lane = lax.broadcasted_iota(jnp.int32, both.shape, 1)
    both = jnp.where(lane < 2 * fields, both, 0.0)
    if lane_shift:
        both = pltpu.roll(both, lane_shift, 1)
    gram_ref[...] = both


def apply_graph(order, keep, lane_shift, v, top, bot, w, deg, *others):
    chunks, depth, fields, width = v.shape
    cols = chunks * width
    parts = len(order)
    out_shape = (jax.ShapeDtypeStruct((parts * fields, LANES), f32),)
    if keep:
        out_shape = (jax.ShapeDtypeStruct((depth, fields, cols), f32),) + out_shape
    return pl.pallas_call(
        functools.partial(graph_kernel, order, keep, lane_shift),
        out_shape=out_shape,
        in_specs=[pl.BlockSpec(memory_space=pltpu.VMEM)] * (5 + len(others)),
        out_specs=(pl.BlockSpec(memory_space=pltpu.VMEM),) * len(out_shape),
        scratch_shapes=[
            pltpu.VMEM((depth + 4, fields, cols), f32),
            pltpu.VMEM((parts * fields, LANES), f32),
        ],
        compiler_params=params(),
        cost_estimate=cost(50 * fields * depth * cols * 4, 4 * cols * depth * (25 + 3 * fields)),
        name="graph_" + "".join(order),
    )(v, top, bot, w, deg, *others)


def forward_kernel(scaled, x_ref, *rest):
    if scaled:
        deg_ref, high_ref, low_ref, out_ref = rest
        chunks, depth, fields, width = x_ref.shape
    else:
        high_ref, low_ref, out_ref = rest
        depth, fields, _ = x_ref.shape
    cols = high_ref.shape[0]
    block = 8
    contract = (((1,), (1,)), ((), ()))

    def one_block(i, _):
        start = i * block
        if scaled:
            value = jnp.concatenate([x_ref[c, pl.ds(start, block)] for c in range(chunks)], 2)
            value = value * deg_ref[pl.ds(start, block), :][:, None, :]
        else:
            value = x_ref[pl.ds(start, block)]
        high, low = split(value.reshape(block * fields, cols))
        result = lax.dot_general(high, high_ref[...], contract, preferred_element_type=f32)
        result += lax.dot_general(high, low_ref[...], contract, preferred_element_type=f32)
        result += lax.dot_general(low, high_ref[...], contract, preferred_element_type=f32)
        out_ref[pl.ds(start, block)] = result.reshape(block, fields, cols)
        return 0

    lax.fori_loop(0, depth // block, one_block, 0)


def cosine_forward(x, deg, high, low, depth, fields):
    cols = high.shape[0]
    args = (x,) + ((deg,) if deg is not None else ()) + (high, low)
    return pl.pallas_call(
        functools.partial(forward_kernel, deg is not None),
        out_shape=jax.ShapeDtypeStruct((depth, fields, cols), f32),
        in_specs=[pl.BlockSpec(memory_space=pltpu.VMEM)] * len(args),
        out_specs=pl.BlockSpec(memory_space=pltpu.VMEM),
        compiler_params=params(),
        cost_estimate=cost(6 * depth * fields * cols * cols, 4 * cols * (2 * depth * fields + cols)),
        name="cosine_forward",
    )(*args)


def solve_kernel(gram_ref, fg_ref, fd_ref, eps_ref, last_ref, f_ref, ends_ref):
    depth, fields, cols = fg_ref.shape
    gram = gram_ref[...]
    affinity = pltpu.roll(gram, LANES - 4 * fields, 1)[:, :fields]
    mass = pltpu.roll(gram, LANES - 5 * fields, 1)[:, :fields]
    row = lax.broadcasted_iota(jnp.int32, (fields, fields), 0)
    for k in range(fields):
        inverse = 1.0 / mass[k : k + 1, k : k + 1]
        column = mass[:, k : k + 1]
        mass_row = mass[k : k + 1, :] * inverse
        affinity_row = affinity[k : k + 1, :] * inverse
        affinity = jnp.where(row == k, affinity_row, affinity - column * affinity_row)
        mass = jnp.where(row == k, mass_row, mass - column * mass_row)
    rayleigh_t = affinity.T

    def one_row(r, carry):
        value = fg_ref[r] - jnp.dot(
            rayleigh_t, fd_ref[r], precision=highest, preferred_element_type=f32
        )
        f_ref[r] = value
        keep = eps_ref[pl.ds(jnp.maximum(r - 1, 0), 1), :]
        return value + (carry - keep * carry)

    down = lax.fori_loop(0, depth, one_row, jnp.zeros((fields, cols), f32))

    def back_row(i, carry):
        r = depth - 1 - i
        keep = eps_ref[pl.ds(jnp.maximum(i - 1, 0), 1), :]
        return f_ref[r] + (carry - keep * carry)

    up = lax.fori_loop(0, depth, back_row, jnp.zeros((fields, cols), f32))
    last = last_ref[...]
    ends_ref[0] = up * last
    ends_ref[1] = down * last


def row_solve(gram, fg, fd, eps, last):
    depth, fields, cols = fg.shape
    return pl.pallas_call(
        solve_kernel,
        out_shape=(
            jax.ShapeDtypeStruct((depth, fields, cols), f32),
            jax.ShapeDtypeStruct((2, fields, cols), f32),
        ),
        in_specs=[pl.BlockSpec(memory_space=pltpu.VMEM)] * 5,
        out_specs=(pl.BlockSpec(memory_space=pltpu.VMEM),) * 2,
        compiler_params=params(),
        cost_estimate=cost(200 * depth * fields * cols, 4 * 3 * depth * fields * cols),
        name="row_solve",
    )(gram, fg, fd, eps, last)


def inverse_kernel(levels, *refs):
    g_refs = refs[:levels]
    f_ref, top_ref, bot_ref, eps_ref, last_ref, high_ref, low_ref, out_ref, u_ref = refs[levels:]
    depth, fields, cols = f_ref.shape
    chunks, _, _, width = out_ref.shape
    flux_top = jnp.zeros((fields, cols), f32)
    flux_bot = jnp.zeros((fields, cols), f32)
    for level in range(levels):
        g = g_refs[level][...]
        flux_top = flux_top + g * top_ref[level : level + 1, :]
        flux_bot = flux_bot - g * bot_ref[level : level + 1, :]

    u_ref[0] = f_ref[0] + flux_top

    def down_row(r, carry):
        keep = eps_ref[pl.ds(r - 1, 1), :]
        value = f_ref[r] + (carry - keep * carry)
        u_ref[r] = value
        return value

    value = lax.fori_loop(1, depth, down_row, u_ref[0])
    value = (value + flux_bot) * last_ref[...]
    u_ref[depth - 1] = value

    def up_row(i, carry):
        r = depth - 2 - i
        keep = eps_ref[pl.ds(r, 1), :]
        total = u_ref[r] + carry
        total = total - keep * total
        u_ref[r] = total
        return total

    lax.fori_loop(0, depth - 1, up_row, value)
    block = 8

    def one_block(i, _):
        start = i * block
        high, low = split(u_ref[pl.ds(start, block)].reshape(block * fields, cols))
        result = jnp.dot(high, high_ref[...], preferred_element_type=f32)
        result += jnp.dot(high, low_ref[...], preferred_element_type=f32)
        result += jnp.dot(low, high_ref[...], preferred_element_type=f32)
        result = result.reshape(block, fields, cols)
        for c in range(chunks):
            out_ref[c, pl.ds(start, block)] = result[:, :, c * width : (c + 1) * width]
        return 0

    lax.fori_loop(0, depth // block, one_block, 0)


def row_inverse(gs, f, top, bot, eps, last, high, low, chunks):
    depth, fields, cols = f.shape
    return pl.pallas_call(
        functools.partial(inverse_kernel, len(gs)),
        out_shape=jax.ShapeDtypeStruct((chunks, depth, fields, cols // chunks), f32),
        in_specs=[pl.BlockSpec(memory_space=pltpu.VMEM)] * (len(gs) + 7),
        out_specs=pl.BlockSpec(memory_space=pltpu.VMEM),
        scratch_shapes=[pltpu.VMEM((depth, fields, cols), f32)],
        compiler_params=params(),
        cost_estimate=cost(6 * depth * fields * cols * cols, 4 * cols * (2 * depth * fields + cols)),
        name="row_inverse",
    )(*gs, f, top, bot, eps, last, high, low)


def hdot(a, b, contract):
    return lax.dot_general(
        a, b, ((contract[0], contract[1]), ((), ())), precision=highest, preferred_element_type=f32
    )


def cholesky_apply(matrix, target):
    size = matrix.shape[0]
    step = 8
    mats = [matrix[i : i + step] for i in range(0, size, step)]
    tars = [target[i : i + step] for i in range(0, size, step)]
    local_row = lax.broadcasted_iota(jnp.int32, (step, 1), 0)
    for k in range(size):
        own, inner = divmod(k, step)
        pivot_row = mats[own][inner : inner + 1, :]
        target_row = tars[own][inner : inner + 1, :]
        inverse = 1.0 / pivot_row[:, k : k + 1]
        for i in range(own, size // step):
            factor = mats[i][:, k : k + 1] * inverse
            if i == own:
                factor = jnp.where(local_row > inner, factor, 0.0)
            mats[i] = mats[i] - factor * pivot_row
            tars[i] = tars[i] - factor * target_row
    matrix = jnp.concatenate(mats, 0)
    target = jnp.concatenate(tars, 0)
    row = lax.broadcasted_iota(jnp.int32, matrix.shape, 0)
    col = lax.broadcasted_iota(jnp.int32, matrix.shape, 1)
    pivots = jnp.sum(jnp.where(row == col, matrix, 0.0), 1, keepdims=True)
    return target * (1.0 / jnp.sqrt(pivots))


def ritz_kernel(fields, pixel_total, first_ref, second_ref, ritz_ref, coeff_ref):
    size = 3 * fields
    gram = second_ref[...]
    first = first_ref[...]
    row = lax.broadcasted_iota(jnp.int32, (LANES, size), 0)
    col = lax.broadcasted_iota(jnp.int32, (LANES, size), 1)
    place_a = jnp.zeros((LANES, size), jnp.bool_)
    place_b = jnp.zeros((LANES, size), jnp.bool_)
    for group, target in ((4, 0), (0, 1), (2, 2)):
        inside = (col >= target * fields) & (col < (target + 1) * fields)
        place_a = place_a | (inside & (row - group * fields == col - target * fields))
        place_b = place_b | (inside & (row - (group + 1) * fields == col - target * fields))
    place_a = place_a.astype(f32)
    place_b = place_b.astype(f32)
    srow = lax.broadcasted_iota(jnp.int32, (size, size), 0)
    scol = lax.broadcasted_iota(jnp.int32, (size, size), 1)
    same = srow // fields == scol // fields
    eye = (srow == scol).astype(f32)

    def assemble(place):
        part = hdot(gram, place, ((1,), (0,)))
        top = hdot(first, place, ((1,), (0,)))
        part = jnp.concatenate([part[:fields] + top, part[fields:]], 0)
        both = part + part.T
        return jnp.where(same, 0.5 * both, both)

    big_a = assemble(place_a)
    big_b = assemble(place_b)
    diagonal = big_b * eye
    scale_col = 1.0 / jnp.sqrt(jnp.sum(diagonal, 1, keepdims=True) + 1e-6)
    scale_row = 1.0 / jnp.sqrt(jnp.sum(diagonal, 0, keepdims=True) + 1e-6)
    norm_a = scale_col * big_a * scale_row
    norm_b = scale_col * big_b * scale_row
    inverse = cholesky_apply(norm_b, eye)
    reduced = hdot(hdot(inverse, norm_a, ((1,), (0,))), inverse, ((1,), (1,)))
    reduced = 0.5 * (reduced + reduced.T) + ritz_offset * eye
    power = hdot(reduced, reduced, ((1,), (0,)))
    power = hdot(power, power, ((1,), (0,)))
    images = power[:fields]
    basis = cholesky_apply(hdot(images, images, ((1,), (1,))), images)
    images = hdot(basis, power, ((1,), (0,)))
    basis = cholesky_apply(hdot(images, images, ((1,), (1,))), images)
    basis = cholesky_apply(hdot(basis, basis, ((1,), (1,))), basis)
    images = hdot(basis, reduced, ((1,), (0,)))
    ritz = jnp.sum(basis * images, 1, keepdims=True) - ritz_offset
    ritz_ref[...] = jnp.broadcast_to(ritz, ritz_ref.shape)
    coeff_ref[...] = math.sqrt(pixel_total) * hdot(basis, inverse, ((1,), (0,))) * scale_row


def ritz_step(first, second, fields, pixel_total):
    return pl.pallas_call(
        functools.partial(ritz_kernel, fields, pixel_total),
        out_shape=(
            jax.ShapeDtypeStruct((fields, LANES), f32),
            jax.ShapeDtypeStruct((fields, 3 * fields), f32),
        ),
        in_specs=[pl.BlockSpec(memory_space=pltpu.VMEM)] * 2,
        out_specs=(pl.BlockSpec(memory_space=pltpu.VMEM),) * 2,
        compiler_params=params(),
        cost_estimate=cost(1 << 25, 1 << 16),
        name="ritz",
    )(first, second)


def combine_kernel(coeff_ref, x_ref, h_ref, p_ref, block_ref, direction_ref):
    rows, fields, _ = x_ref.shape
    high, low = split(coeff_ref[...])
    left = jnp.concatenate([high, high, low], 1)

    def one_row(r, _):
        h_high, h_low = split(h_ref[r])
        p_high, p_low = split(p_ref[r])
        x_high, x_low = split(x_ref[r])
        right = jnp.concatenate(
            [x_high, h_high, p_high, x_low, h_low, p_low, x_high, h_high, p_high], 0
        )
        result = jnp.dot(left, right, preferred_element_type=f32)
        block_ref[r] = result[:fields]
        direction_ref[r] = result[fields:]
        return 0

    lax.fori_loop(0, rows, one_row, 0)


def combine(coeffs, x, h, p):
    rows, fields, width = x.shape
    zero = jnp.zeros((fields, fields), f32)
    both = jnp.concatenate([coeffs, jnp.concatenate([zero, coeffs[:, fields:]], 1)], 0)
    tile = 32
    spec = pl.BlockSpec((tile, fields, width), lambda i: (i, 0, 0))
    return pl.pallas_call(
        combine_kernel,
        grid=(rows // tile,),
        out_shape=(jax.ShapeDtypeStruct((rows, fields, width), f32),) * 2,
        in_specs=[pl.BlockSpec(both.shape, lambda i: (0, 0)), spec, spec, spec],
        out_specs=(spec, spec),
        compiler_params=params(),
        cost_estimate=cost(200 * rows * fields * width, 20 * rows * fields * width),
        name="combine",
    )(both, x, h, p)


def shifted(block, strips):
    down = [(i, i + 1) for i in range(strips - 1)]
    up = [(i + 1, i) for i in range(strips - 1)]
    return down, up


def local(intensity, start_block, old_direction):
    fields, height, width = start_block.shape
    chunks = lax.axis_size("col")
    strips = lax.axis_size("row") * chunks
    depth = height // chunks
    rows, cols = strips * depth, chunks * width
    strip = lax.axis_index("row") * chunks + lax.axis_index("col")
    down, up = shifted(None, strips)
    levels = strips.bit_length() - 1

    eps, last, gain, cross, top_all, bot_all = (
        jnp.asarray(t) for t in row_tables(strips, depth, cols)
    )
    high, low = (jnp.asarray(t) for t in cosine_tables(cols))
    top_mine = lax.dynamic_index_in_dim(top_all, strip, 0, False)
    bot_mine = lax.dynamic_index_in_dim(bot_all, strip, 0, False)

    def to_strips(block):
        return lax.all_to_all(block, "col", 0, 0)

    def total(value):
        for level in range(levels):
            value = value + lax.ppermute(value, BOTH, [(i, i ^ (1 << level)) for i in range(strips)])
        return value

    def halo(block):
        above = lax.ppermute(block[:, depth - 2 :], BOTH, down)
        below = lax.ppermute(block[:, :2], BOTH, up)
        return above, below

    x_rows = jnp.transpose(start_block.reshape(fields, chunks, depth, width), (1, 2, 0, 3))
    p_rows = jnp.transpose(old_direction.reshape(fields, chunks, depth, width), (1, 2, 0, 3))
    image = to_strips(intensity.reshape(chunks, depth, width))
    x_strip = to_strips(x_rows)
    p_strip = to_strips(p_rows)

    image = jnp.transpose(image, (1, 0, 2)).reshape(depth, cols)
    image = jnp.concatenate(
        [lax.ppermute(image[-2:], BOTH, down), image, lax.ppermute(image[:2], BOTH, up)], 0
    )
    w, deg = make_weights(strip, image, depth, rows)

    graph_x, gram_x = apply_graph(("v",), True, 4 * fields, x_strip, *halo(x_strip), w, deg)
    gram_x = total(gram_x)
    spectrum_g = cosine_forward(graph_x, None, high, low, depth, fields)
    spectrum_d = cosine_forward(x_strip, deg, high, low, depth, fields)
    (gram_p,) = apply_graph(
        ("x", "v"), False, 2 * fields, p_strip, *halo(p_strip), w, deg, x_strip
    )
    f, ends = row_solve(gram_x, spectrum_g, spectrum_d, eps, last)

    gs = []
    for level in range(levels):
        theirs = lax.ppermute(ends, BOTH, [(i, i ^ (1 << level)) for i in range(strips)])
        right = ((strip >> level) & 1) == 1
        lower = jnp.where(right, theirs, ends)
        upper = jnp.where(right, ends, theirs)
        g = (lower[1] - upper[0]) * gain[level]
        gs.append(g)
        ends = jnp.stack([lower[0] - g * cross[level], upper[1] + g * cross[level]])

    h_strip = row_inverse(gs, f, top_mine, bot_mine, eps, last, high, low, chunks)
    (gram_h,) = apply_graph(
        ("x", "v", "p"), False, 0, h_strip, *halo(h_strip), w, deg, x_strip, p_strip
    )
    h_block = lax.all_to_all(h_strip, "col", 0, 0).reshape(height, fields, width)
    zero = jnp.zeros((fields, LANES), f32)
    gram = gram_h + jnp.concatenate([gram_p[:fields], zero, gram_p[fields:]], 0)
    ritz, coeffs = ritz_step(gram_x, total(gram), fields, rows * cols)
    new_block, new_direction = combine(
        coeffs,
        x_rows.reshape(height, fields, width),
        h_block,
        p_rows.reshape(height, fields, width),
    )
    return (
        jnp.transpose(new_block, (1, 0, 2)),
        jnp.transpose(new_direction, (1, 0, 2)),
        ritz[:, 0],
    )


def solution(mesh):
    return jax.shard_map(
        local,
        mesh=mesh,
        in_specs=(P("row", "col"), P(None, "row", "col"), P(None, "row", "col")),
        out_specs=(P(None, "row", "col"), P(None, "row", "col"), P()),
        check_vma=False,
    )
```

time: 1390 us -> 287 us (0.21)
  local copies, waits for them, and re-layouts: 432 us -> 21.9 us
  matrix products: 407 us -> 0 us
  loops' own time: 143 us -> 0 us
  other arithmetic: 118 us -> 0.57 us
  Pallas kernels: 0 us -> 117 us
  blocking collectives: 85.6 us -> 0 us
  waiting for transfers between devices: 145 us -> 93.2 us
    dot_general x528 -> x0, matrix products: 407 us -> none  [the longest x240 187 us: lower_one_row(): jnp.dot(factor_row, solved, precision=highest)]
    dynamic_slice x496 -> x0, local copies, waits for them, and re-layouts: 295 us -> none  [the longest x240 141 us: lower_one_row(): pivot_value = lax.dynamic_slice_in_dim(factor_row, turn_index, 1, 0)[0]]
    another operation x27 -> x0, loops' own time: 143 us -> none  [the longest x10 136 us: lower_factor(): lax.fori_loop(0, order_size, one_column, jnp.zeros(matrix.shape, jnp.floa...]
    all_to_all x4, waiting for transfers between devices: 140 us -> 20.5 us  [the longest x3 20.5 us: to_strips(): return lax.all_to_all(block, 'col', 0, 0)]
    pallas_call x0 -> x10, Pallas kernels: none -> 117 us  [the longest x3 42.5 us: apply_graph(): pl.pallas_call(functools.partial(graph_kernel, order, keep, lane_shift),...]
    psum x2 -> x0, blocking collectives: 85.6 us -> none  [the longest x1 42.9 us: local(): lax.psum((jnp.dot(x_flat, gx_flat.T, precision=highest), jnp.dot(x_flat *...]
    ppermute x12 -> x23, waiting for transfers between devices: 4.9 us -> 72.8 us  [the longest x3 23.7 us: halo(): above = lax.ppermute(block[:, depth - 2:], BOTH, down)]
    add x16 -> x12, other arithmetic: 60.3 us -> 0.14 us  [the longest x1 0.07 us: local(): gram = gram_h + jnp.concatenate([gram_p[:fields], zero, gram_p[fields:]], 0)]
  transfers between devices with their start and end apart: 16 -> 27, of which waited for: 6 -> 20; matrix products, arithmetic and copies ran while one was open for 3% -> 3% of each run, Pallas kernels for 0% -> 25%
where the time goes in v1:
time: 287 us; the launch traced here: 286 us
  Pallas kernels  117 us (41%)
  waiting for transfers between devices  93.2 us (32%)
  starting transfers between devices  52.3 us (18%)
  local copies, waits for them, and re-layouts  21.9 us (8%)
    pallas_call x3, Pallas kernels, apply_graph(): pl.pallas_call(functools.partial(graph_kernel, order, keep, lane_shift),...  42.5 us
    ppermute x3, waiting for transfers between devices, halo(): above = lax.ppermute(block[:, depth - 2:], BOTH, down)  23.7 us
    pallas_call x2, Pallas kernels, cosine_forward(): pl.pallas_call(functools.partial(forward_kernel, deg is not None), out_sh...  23.2 us
    ppermute x5, waiting for transfers between devices, local(): lax.ppermute(ends, BOTH, [(i, i ^ 1 << level) for i in range(strips)])  21.7 us
    all_to_all x3, waiting for transfers between devices, to_strips(): return lax.all_to_all(block, 'col', 0, 0)  20.5 us
    unnamed x48, local copies, waits for them, and re-layouts  20.2 us
    pallas_call x1, Pallas kernels, combine(): pl.pallas_call(combine_kernel, grid=(rows // tile,), out_shape=(jax.Shape...  20 us
    ppermute x10, waiting for transfers between devices, total(): lax.ppermute(value, BOTH, [(i, i ^ 1 << level) for i in range(strips)])  18.8 us
  transfers between devices with their start and end apart: 27, of which 20 were waited for; matrix products, arithmetic and copies ran while one was open for 3% of the time, Pallas kernels for 25%

profile of v1, /device:TPU:0, one launch (start us, length us, event | category | flops | bytes accessed | tf_op | source)
XLA Modules:
  0.0 285.8 jit_solution(2401694220205738623)
XLA Ops:
  0.6 5.2 %all-to-all-start.1 = ((f32[4,32,256]{2,1,0:T(8,128)}), f32[4,32,256]{2,1,0:T(8,128)S(1)}, u32[]{:S(2)}, u32[]{:S(2)}) async-start(f32[4,32,256]{2,1,0:T(8,128)} %bitcast.49), calls=%async_computation.1 | async-start | bytes 262144 | tf_op jit(solution)/shard_map/all_to_all | solution.py:540
  5.8 4.1 %copy.35 = f32[16,128,256]{2,0,1:T(8,128)} copy(f32[16,128,256]{2,1,0:T(8,128)} %param.12) | data formatting | bytes 4194304 | tf_op args[1]
  10.8 3.6 %all-to-all-start = ((f32[4,32,16,256]{3,2,1,0:T(8,128)}), f32[4,32,16,256]{3,2,1,0:T(8,128)S(1)}, u32[]{:S(2)}, u32[]{:S(2)}) async-start(f32[4,32,16,256]{3,2,1,0:T(8,128)} %bitcast.41), calls=%async_computation | async-start | bytes 4194304 | tf_op jit(solution)/shard_map/all_to_all | solution.py:540
  14.5 3.9 %collective-permute-start.2 = (f32[2,1024]{1,0:T(2,128)S(1)}, f32[2,1024]{1,0:T(2,128)S(1)}, u32[]{:S(2)}, u32[]{:S(2)}) collective-permute-start(f32[2,1024]{1,0:T(2,128)S(1)} %bitcast.51), channel_id=1, source_target_pairs={{0,1},{1,2},{2,3},{3,4},{4,5},{5,6},{6,7},{7,8},{8,9},{9,10},{10,1... | collective-permute-start | bytes 24584 | tf_op jit(solution)/shard_map/ppermute | solution.py:560
  19.7 19.0 %all-to-all-done.v_ref.x_ref.rest_0_ = f32[4,32,16,256]{3,2,1,0:T(8,128)S(1)} async-done(((f32[4,32,16,256]{3,2,1,0:T(8,128)}), f32[4,32,16,256]{3,2,1,0:T(8,128)S(1)}, u32[]{:S(2)}, u32[]{:S(2)}) %all-to-all-start) | async-done | bytes 2097184 | tf_op jit(solution)/shard_map/all_to_all | solution.py:540
  38.6 3.3 %collective-permute-start = (f32[4,2,16,256]{3,2,1,0:T(8,128)S(1)}, f32[4,2,16,256]{3,2,1,0:T(8,128)S(1)}, u32[]{:S(2)}, u32[]{:S(2)}) collective-permute-start(f32[4,2,16,256]{3,2,1,0:T(8,128)S(1)} %get-tuple-element.41), channel_id=1, source_target_pairs={{0,1},{1,2},{2,3},{3,4},{4,5},{5,6},{6,7},{7,8},{8,9},{9,10},{10,1... | collective-permute-start | bytes 393224 | tf_op jit(solution)/shard_map/ppermute | solution.py:548
  43.4 2.1 weights.1
  45.6 1.7 copy-done
  47.3 1.6 collective-permute-done.1.bot_ref
  48.8 13.4 %graph_v.1 = (f32[32,16,1024]{2,1,0:T(8,128)S(1)}, f32[16,128]{1,0:T(8,128)S(1)}) custom-call(f32[4,32,16,256]{3,2,1,0:T(8,128)} %copy-done.10, f32[4,2,16,256]{3,2,1,0:T(8,128)S(1)} %collective-permute-done.top_ref, f32[4,2,16,256]{3,2,1,0:T(8,128)S(1)} %collective-permute-done.1.bot_ref, f32[25,32,1024]{2,1,0:T(8,128)} %copy-done, ...), custom_call_target="tpu_custom_call" | custom-call | flops 104857600 | bytes 9568256 | tf_op jit(solution)/shard_map/graph_v/pallas_call | solution.py:211
  62.2 1.3 copy-done.9
  63.6 2.3 collective-permute-start.4
  65.9 1.6 collective-permute-done.4
  67.5 1.6 collective-permute-start.5
  69.1 2.0 collective-permute-done.5
  72.4 2.4 collective-permute-start.7
  74.8 11.6 %cosine_forward.3.fd_ref = f32[32,16,1024]{2,1,0:T(8,128)S(1)} custom-call(f32[4,32,16,256]{3,2,1,0:T(8,128)} %copy-done.10, f32[32,1024]{1,0:T(8,128)S(1)} %get-tuple-element.14.deg_ref.rest_0_, bf16[1024,1024]{1,0:T(8,128)(2,1)} %constant.53.clone.rest_0_.rest_1_.refs_10_, bf16[1024,1024]{1,0:T(8,128)(2,1)} %constant.54.clone.rest_1_.rest_2_.refs_11_), custom_call_target="tpu_custom_call" | custom-call | flops 3221225472 | bytes 8388608 | tf_op jit(solution)/shard_map/cosine_forward/pallas_call | solution.py:257
  86.4 1.3 copy-done.4
  87.8 2.6 collective-permute-start.8
  90.4 11.6 %cosine_forward.2.fg_ref = f32[32,16,1024]{2,1,0:T(8,128)S(1)} custom-call(f32[32,16,1024]{2,1,0:T(8,128)} %copy-done.9, bf16[1024,1024]{1,0:T(8,128)(2,1)} %constant.53.clone.rest_0_.rest_1_.refs_10_, bf16[1024,1024]{1,0:T(8,128)(2,1)} %constant.54.clone.rest_1_.rest_2_.refs_11_), custom_call_target="tpu_custom_call" | custom-call | flops 3221225472 | bytes 8388608 | tf_op jit(solution)/shard_map/cosine_forward/pallas_call | solution.py:257
  102.0 1.3 copy-done.5
  103.4 11.0 %row_solve.1 = (f32[32,16,1024]{2,1,0:T(8,128)S(1)}, f32[2,16,1024]{2,1,0:T(8,128)S(1)}) custom-call(f32[16,128]{1,0:T(8,128)S(1)} %add.64.gram_ref.first_ref, f32[32,16,1024]{2,1,0:T(8,128)} %copy-done.5, f32[32,16,1024]{2,1,0:T(8,128)} %copy-done.4, f32[32,1024]{1,0:T(8,128)S(1)} %copy-done.6, f32[1,1024]{1,0:T(1,128)S(1)} %copy-done.7), custom_call_target="tpu_custom_call" | custom-call | flops 104857600 | bytes 6291456 | tf_op jit(solution)/shard_map/row_solve/pallas_call | solution.py:306
  114.3 1.3 copy-done.8
  116.9 3.8 %collective-permute-done.9 = f32[2,16,1024]{2,1,0:T(8,128)S(1)} collective-permute-done((f32[2,16,1024]{2,1,0:T(8,128)S(1)}, f32[2,16,1024]{2,1,0:T(8,128)S(1)}, u32[]{:S(2)}, u32[]{:S(2)}) %collective-permute-start.9) | collective-permute-done | bytes 131104 | tf_op jit(solution)/shard_map/ppermute | solution.py:575
  121.7 4.1 %collective-permute-done.10 = f32[2,16,1024]{2,1,0:T(8,128)S(1)} collective-permute-done((f32[2,16,1024]{2,1,0:T(8,128)S(1)}, f32[2,16,1024]{2,1,0:T(8,128)S(1)}, u32[]{:S(2)}, u32[]{:S(2)}) %collective-permute-start.10) | collective-permute-done | bytes 131104 | tf_op jit(solution)/shard_map/ppermute | solution.py:575
  126.0 2.6 copy.34
  128.6 3.7 %all-to-all-start.2 = ((f32[4,32,16,256]{3,2,1,0:T(8,128)}), f32[4,32,16,256]{3,2,1,0:T(8,128)S(1)}, u32[]{:S(2)}, u32[]{:S(2)}) async-start(f32[4,32,16,256]{3,2,1,0:T(8,128)} %bitcast.43), calls=%async_computation.2 | async-start | bytes 4194304 | tf_op jit(solution)/shard_map/all_to_all | solution.py:540
  133.8 5.4 %collective-permute-done.12 = f32[2,16,1024]{2,1,0:T(8,128)S(1)} collective-permute-done((f32[2,16,1024]{2,1,0:T(8,128)S(1)}, f32[2,16,1024]{2,1,0:T(8,128)S(1)}, u32[]{:S(2)}, u32[]{:S(2)}) %collective-permute-start.12) | collective-permute-done | bytes 131104 | tf_op jit(solution)/shard_map/ppermute | solution.py:575
  139.7 8.3 %collective-permute-done.13 = f32[2,16,1024]{2,1,0:T(8,128)S(1)} collective-permute-done((f32[2,16,1024]{2,1,0:T(8,128)S(1)}, f32[2,16,1024]{2,1,0:T(8,128)S(1)}, u32[]{:S(2)}, u32[]{:S(2)}) %collective-permute-start.13) | collective-permute-done | bytes 131104 | tf_op jit(solution)/shard_map/ppermute | solution.py:575
  148.1 8.0 %row_inverse.1.v_ref = f32[4,32,16,256]{3,2,1,0:T(8,128)S(1)} custom-call(f32[16,1024]{1,0:T(8,128)S(1)} %get-tuple-element.67.refs_0_, f32[16,1024]{1,0:T(8,128)S(1)} %get-tuple-element.66.refs_1_, f32[16,1024]{1,0:T(8,128)S(1)} %get-tuple-element.65.refs_2_, f32[16,1024]{1,0:T(8,128)S(1)} %get-tuple-element.64.refs_3_, f32[16,1024]{1,0:T(8,128)S(1)} %fusion.4.refs_4_, ...), custom_call_target="tpu_custom_call" | custom-call | flops 3221225472 | bytes 8388608 | tf_op jit(solution)/shard_map/row_inverse/pallas_call | solution.py:371
  156.1 1.4 copy-done.2
  158.1 4.5 %all-to-all-start.3 = ((f32[4,32,16,256]{3,2,1,0:T(8,128)}), f32[4,32,16,256]{3,2,1,0:T(8,128)}, u32[]{:S(2)}, u32[]{:S(2)}) async-start(f32[4,32,16,256]{3,2,1,0:T(8,128)} %copy-done.2), calls=%async_computation.3 | async-start | bytes 4194304 | tf_op jit(solution)/shard_map/all_to_all | solution.py:587
  162.6 3.9 %collective-permute-start.16 = (f32[4,2,16,256]{3,2,1,0:T(8,128)S(1)}, f32[4,2,16,256]{3,2,1,0:T(8,128)S(1)}, u32[]{:S(2)}, u32[]{:S(2)}) collective-permute-start(f32[4,2,16,256]{3,2,1,0:T(8,128)S(1)} %get-tuple-element.37), channel_id=1, source_target_pairs={{0,1},{1,2},{2,3},{3,4},{4,5},{5,6},{6,7},{7,8},{8,9},{9,10},{10,1... | collective-permute-start | bytes 393224 | tf_op jit(solution)/shard_map/ppermute | solution.py:548
  167.9 22.7 %collective-permute-done.16.top_ref = f32[4,2,16,256]{3,2,1,0:T(8,128)S(1)} collective-permute-done((f32[4,2,16,256]{3,2,1,0:T(8,128)S(1)}, f32[4,2,16,256]{3,2,1,0:T(8,128)S(1)}, u32[]{:S(2)}, u32[]{:S(2)}) %collective-permute-start.16) | collective-permute-done | bytes 131104 | tf_op jit(solution)/shard_map/ppermute | solution.py:548
  190.5 2.6 collective-permute-done.17.bot_ref
  193.2 13.9 %graph_xv.1 = f32[32,128]{1,0:T(8,128)S(1)} custom-call(f32[4,32,16,256]{3,2,1,0:T(8,128)S(1)} %all-to-all-done.2.rest_1_.v_ref, f32[4,2,16,256]{3,2,1,0:T(8,128)S(1)} %collective-permute-done.16.top_ref, f32[4,2,16,256]{3,2,1,0:T(8,128)S(1)} %collective-permute-done.17.bot_ref, f32[25,32,1024]{2,1,0:T(8,128)} %copy-done, ...), custom_call_target="tpu_custom_call" | custom-call | flops 104857600 | bytes 9568256 | tf_op jit(solution)/shard_map/graph_xv/pallas_call | solution.py:211
  207.1 3.3 %collective-permute-start.14 = (f32[4,2,16,256]{3,2,1,0:T(8,128)S(1)}, f32[4,2,16,256]{3,2,1,0:T(8,128)S(1)}, u32[]{:S(2)}, u32[]{:S(2)}) collective-permute-start(f32[4,2,16,256]{3,2,1,0:T(8,128)S(1)} %get-tuple-element.39), channel_id=1, source_target_pairs={{0,1},{1,2},{2,3},{3,4},{4,5},{5,6},{6,7},{7,8},{8,9},{9,10},{10,1... | collective-permute-start | bytes 393224 | tf_op jit(solution)/shard_map/ppermute | solution.py:548
  210.5 1.5 collective-permute-start.15
  213.0 4.4 %collective-permute-done.15.bot_ref = f32[4,2,16,256]{3,2,1,0:T(8,128)S(1)} collective-permute-done((f32[4,2,16,256]{3,2,1,0:T(8,128)S(1)}, f32[4,2,16,256]{3,2,1,0:T(8,128)S(1)}, u32[]{:S(2)}, u32[]{:S(2)}) %collective-permute-start.15) | collective-permute-done | bytes 131104 | tf_op jit(solution)/shard_map/ppermute | solution.py:549
  217.3 15.2 %graph_xvp.1 = f32[48,128]{1,0:T(8,128)S(1)} custom-call(f32[4,32,16,256]{3,2,1,0:T(8,128)S(1)} %copy-done.3, f32[4,2,16,256]{3,2,1,0:T(8,128)S(1)} %collective-permute-done.14.top_ref, f32[4,2,16,256]{3,2,1,0:T(8,128)S(1)} %collective-permute-done.15.bot_ref, f32[25,32,1024]{2,1,0:T(8,128)} %copy-done, f32[32,1024]{1,0:T(8,128)S(1)} %get-tuple-element.14.deg_ref.rest_0_, ...), custom_call_target="tpu_custom_call" | custom-call | flops 104857600 | bytes 9568256 | tf_op jit(solution)/shard_map/graph_xvp/pallas_call | solution.py:211
  233.6 2.8 collective-permute-done.18
  237.3 3.0 %collective-permute-done.19 = f32[48,128]{1,0:T(8,128)S(1)} collective-permute-done((f32[48,128]{1,0:T(8,128)S(1)}, f32[48,128]{1,0:T(8,128)S(1)}, u32[]{:S(2)}, u32[]{:S(2)}) %collective-permute-start.19) | collective-permute-done | bytes 24608 | tf_op jit(solution)/shard_map/ppermute | solution.py:544
  242.3 3.0 %collective-permute-done.21 = f32[48,128]{1,0:T(8,128)S(1)} collective-permute-done((f32[48,128]{1,0:T(8,128)S(1)}, f32[48,128]{1,0:T(8,128)S(1)}, u32[]{:S(2)}, u32[]{:S(2)}) %collective-permute-start.21) | collective-permute-done | bytes 24608 | tf_op jit(solution)/shard_map/ppermute | solution.py:544
  246.0 4.0 %collective-permute-done.22 = f32[48,128]{1,0:T(8,128)S(1)} collective-permute-done((f32[48,128]{1,0:T(8,128)S(1)}, f32[48,128]{1,0:T(8,128)S(1)}, u32[]{:S(2)}, u32[]{:S(2)}) %collective-permute-start.22) | collective-permute-done | bytes 24608 | tf_op jit(solution)/shard_map/ppermute | solution.py:544
  250.0 9.9 %ritz.1 = (f32[16,128]{1,0:T(8,128)S(1)}, f32[16,48]{1,0:T(8,128)S(1)}) custom-call(f32[16,128]{1,0:T(8,128)S(1)} %add.64.gram_ref.first_ref, f32[48,128]{1,0:T(8,128)S(1)} %add.75.second_ref), custom_call_target="tpu_custom_call" | custom-call | flops 33554432 | bytes 65536 | tf_op jit(solution)/shard_map/ritz/pallas_call | solution.py:464
  260.7 20.0 %combine.1 = (f32[128,16,256]{2,1,0:T(8,128)S(1)}, f32[128,16,256]{2,1,0:T(8,128)}) custom-call(f32[32,48]{1,0:T(8,128)S(1)} %select_maximum_fusion.coeff_ref, f32[128,16,256]{2,1,0:T(8,128)} %bitcast.42, f32[128,16,256]{2,1,0:T(8,128)} %bitcast.18.h_ref, f32[128,16,256]{2,1,0:T(8,128)} %bitcast.44), custom_call_target="tpu_custom_call" | custom-call | flops 104857600 | bytes 10485760 | tf_op jit(solution)/shard_map/combine/pallas_call | solution.py:504
  280.7 2.5 copy.27
  283.3 2.5 copy.28
  (104 shorter events, 17.6 us)
Async XLA Ops:
  0.6 10.2 %all-to-all-start.1 = ((f32[4,32,256]{2,1,0:T(8,128)}), f32[4,32,256]{2,1,0:T(8,128)S(1)}, u32[]{:S(2)}, u32[]{:S(2)}) async-start(f32[4,32,256]{2,1,0:T(8,128)} %bitcast.49), calls=%async_computation.1 | async-start | bytes 262144 | tf_op jit(solution)/shard_map/all_to_all | solution.py:540
  10.8 27.8 %all-to-all-start = ((f32[4,32,16,256]{3,2,1,0:T(8,128)}), f32[4,32,16,256]{3,2,1,0:T(8,128)S(1)}, u32[]{:S(2)}, u32[]{:S(2)}) async-start(f32[4,32,16,256]{3,2,1,0:T(8,128)} %bitcast.41), calls=%async_computation | async-start | bytes 4194304 | tf_op jit(solution)/shard_map/all_to_all | solution.py:540
  14.5 28.9 %collective-permute-start.2 = (f32[2,1024]{1,0:T(2,128)S(1)}, f32[2,1024]{1,0:T(2,128)S(1)}, u32[]{:S(2)}, u32[]{:S(2)}) collective-permute-start(f32[2,1024]{1,0:T(2,128)S(1)} %bitcast.51), channel_id=1, source_target_pairs={{0,1},{1,2},{2,3},{3,4},{4,5},{5,6},{6,7},{7,8},{8,9},{9,10},{10,1... | collective-permute-start | bytes 24584 | tf_op jit(solution)/shard_map/ppermute | solution.py:560
  18.4 25.0 %collective-permute-start.3 = (f32[2,1024]{1,0:T(2,128)S(1)}, f32[2,1024]{1,0:T(2,128)S(1)}, u32[]{:S(2)}, u32[]{:S(2)}) collective-permute-start(f32[2,1024]{1,0:T(2,128)S(1)} %bitcast.50), channel_id=1, source_target_pairs={{1,0},{2,1},{3,2},{4,3},{5,4},{6,5},{7,6},{8,7},{9,8},{10,9},{11,1... | collective-permute-start | bytes 24584 | tf_op jit(solution)/shard_map/ppermute | solution.py:560
  38.6 10.2 %copy-start.10 = (f32[4,32,16,256]{3,2,1,0:T(8,128)}, f32[4,32,16,256]{3,2,1,0:T(8,128)S(1)}, u32[]{:S(2)}) copy-start(f32[4,32,16,256]{3,2,1,0:T(8,128)S(1)} %all-to-all-done.v_ref.x_ref.rest_0_) | copy-start | bytes 6291460
  38.6 8.6 %collective-permute-start = (f32[4,2,16,256]{3,2,1,0:T(8,128)S(1)}, f32[4,2,16,256]{3,2,1,0:T(8,128)S(1)}, u32[]{:S(2)}, u32[]{:S(2)}) collective-permute-start(f32[4,2,16,256]{3,2,1,0:T(8,128)S(1)} %get-tuple-element.41), channel_id=1, source_target_pairs={{0,1},{1,2},{2,3},{3,4},{4,5},{5,6},{6,7},{7,8},{8,9},{9,10},{10,1... | collective-permute-start | bytes 393224 | tf_op jit(solution)/shard_map/ppermute | solution.py:548
  42.0 6.9 %collective-permute-start.1 = (f32[4,2,16,256]{3,2,1,0:T(8,128)S(1)}, f32[4,2,16,256]{3,2,1,0:T(8,128)S(1)}, u32[]{:S(2)}, u32[]{:S(2)}) collective-permute-start(f32[4,2,16,256]{3,2,1,0:T(8,128)S(1)} %get-tuple-element.40), channel_id=1, source_target_pairs={{1,0},{2,1},{3,2},{4,3},{5,4},{6,5},{7,6},{8,7},{9,8},{10,9},{11,1... | collective-permute-start | bytes 393224 | tf_op jit(solution)/shard_map/ppermute | solution.py:549
  45.6 1.7 copy-start
  62.2 1.3 copy-start.9
  63.6 3.9 %collective-permute-start.4 = (f32[16,128]{1,0:T(8,128)S(1)}, f32[16,128]{1,0:T(8,128)S(1)}, u32[]{:S(2)}, u32[]{:S(2)}) collective-permute-start(f32[16,128]{1,0:T(8,128)S(1)} %get-tuple-element.15), channel_id=1, source_target_pairs={{0,1},{1,0},{2,3},{3,2},{4,5},{5,4},{6,7},{7,6},{8,9},{9,8},{10,11... | collective-permute-start | bytes 24584 | tf_op jit(solution)/shard_map/ppermute | solution.py:544
  67.5 3.7 %collective-permute-start.5 = (f32[16,128]{1,0:T(8,128)S(1)}, f32[16,128]{1,0:T(8,128)S(1)}, u32[]{:S(2)}, u32[]{:S(2)}) collective-permute-start(f32[16,128]{1,0:T(8,128)S(1)} %add.60), channel_id=1, source_target_pairs={{0,2},{1,3},{2,0},{3,1},{4,6},{5,7},{6,4},{7,5},{8,10},{9,11},{10,... | collective-permute-start | bytes 24584 | tf_op jit(solution)/shard_map/ppermute | solution.py:544
  71.2 1.2 collective-permute-start.6
  72.4 15.4 %collective-permute-start.7 = (f32[16,128]{1,0:T(8,128)S(1)}, f32[16,128]{1,0:T(8,128)S(1)}, u32[]{:S(2)}, u32[]{:S(2)}) collective-permute-start(f32[16,128]{1,0:T(8,128)S(1)} %add.62), channel_id=1, source_target_pairs={{0,8},{1,9},{2,10},{3,11},{4,12},{5,13},{6,14},{7,15},{8,0},{9,1},... | collective-permute-start | bytes 24584 | tf_op jit(solution)/shard_map/ppermute | solution.py:544
  86.4 1.3 copy-start.4
  87.8 15.5 %collective-permute-start.8 = (f32[16,128]{1,0:T(8,128)S(1)}, f32[16,128]{1,0:T(8,128)S(1)}, u32[]{:S(2)}, u32[]{:S(2)}) collective-permute-start(f32[16,128]{1,0:T(8,128)S(1)} %add.63), channel_id=1, source_target_pairs={{0,16},{1,17},{2,18},{3,19},{4,20},{5,21},{6,22},{7,23},{8,24},{9,... | collective-permute-start | bytes 24584 | tf_op jit(solution)/shard_map/ppermute | solution.py:544
  90.4 12.9 %copy-start.6 = (f32[32,1024]{1,0:T(8,128)S(1)}, f32[32,1024]{1,0:T(8,128)}, u32[]{:S(2)}) copy-start(f32[32,1024]{1,0:T(8,128)} %constant.47.clone.eps_ref.refs_8_) | copy-start | bytes 393220
  90.4 12.9 %copy-start.7 = (f32[1,1024]{1,0:T(1,128)S(1)}, f32[1,1024]{1,0:T(1,128)}, u32[]{:S(2)}) copy-start(f32[1,1024]{1,0:T(1,128)} %constant.48.clone.last_ref.refs_9_) | copy-start | bytes 12292
  101.9 1.3 copy-start.5
  103.3 17.4 %copy-start.15 = (f32[1024]{0:T(1024)S(1)}, f32[1024]{0:T(1024)}, u32[]{:S(2)}) copy-start(f32[1024]{0:T(1024)} %constant.58) | copy-start | bytes 12292
  103.3 17.4 %copy-start.20 = (f32[1024]{0:T(1024)S(1)}, f32[1024]{0:T(1024)}, u32[]{:S(2)}) copy-start(f32[1024]{0:T(1024)} %constant.60) | copy-start | bytes 12292
  103.3 22.5 %copy-start.16 = (f32[1024]{0:T(1024)S(1)}, f32[1024]{0:T(1024)}, u32[]{:S(2)}) copy-start(f32[1024]{0:T(1024)} %constant.62) | copy-start | bytes 12292
  103.3 22.5 %copy-start.19 = (f32[1024]{0:T(1024)S(1)}, f32[1024]{0:T(1024)}, u32[]{:S(2)}) copy-start(f32[1024]{0:T(1024)} %constant.64) | copy-start | bytes 12292
  115.7 10.3 %copy-start.11 = (f32[16,128,256]{2,1,0:T(8,128)S(1)}, f32[16,128,256]{2,1,0:T(8,128)}, u32[]{:S(2)}) copy-start(f32[16,128,256]{2,1,0:T(8,128)} %param.13) | copy-start | bytes 6291460
  115.7 5.0 %collective-permute-start.9 = (f32[2,16,1024]{2,1,0:T(8,128)S(1)}, f32[2,16,1024]{2,1,0:T(8,128)S(1)}, u32[]{:S(2)}, u32[]{:S(2)}) collective-permute-start(f32[2,16,1024]{2,1,0:T(8,128)S(1)} %get-tuple-element.17), channel_id=1, source_target_pairs={{0,1},{1,0},{2,3},{3,2},{4,5},{5,4},{6,7},{7,6},{8,9},{9,8},{10,11... | collective-permute-start | bytes 393224 | tf_op jit(solution)/shard_map/ppermute | solution.py:575
  120.8 5.0 %collective-permute-start.10 = (f32[2,16,1024]{2,1,0:T(8,128)S(1)}, f32[2,16,1024]{2,1,0:T(8,128)S(1)}, u32[]{:S(2)}, u32[]{:S(2)}) collective-permute-start(f32[2,16,1024]{2,1,0:T(8,128)S(1)} %pad_maximum_fusion.2), channel_id=1, source_target_pairs={{0,2},{1,3},{2,0},{3,1},{4,6},{5,7},{6,4},{7,5},{8,10},{9,11},{10,... | collective-permute-start | bytes 393224 | tf_op jit(solution)/shard_map/ppermute | solution.py:575
  125.9 7.2 %collective-permute-start.11 = (f32[2,16,1024]{2,1,0:T(8,128)S(1)}, f32[2,16,1024]{2,1,0:T(8,128)S(1)}, u32[]{:S(2)}, u32[]{:S(2)}) collective-permute-start(f32[2,16,1024]{2,1,0:T(8,128)S(1)} %pad_maximum_fusion.3), channel_id=1, source_target_pairs={{0,4},{1,5},{2,6},{3,7},{4,0},{5,1},{6,2},{7,3},{8,12},{9,13},{10,... | collective-permute-start | bytes 393224 | tf_op jit(solution)/shard_map/ppermute | solution.py:575
  128.6 4.6 %copy-start.13 = (f32[1024]{0:T(1024)S(1)}, f32[1024]{0:T(1024)}, u32[]{:S(2)}) copy-start(f32[1024]{0:T(1024)} %constant.66) | copy-start | bytes 12292
  128.6 4.6 %copy-start.18 = (f32[1024]{0:T(1024)S(1)}, f32[1024]{0:T(1024)}, u32[]{:S(2)}) copy-start(f32[1024]{0:T(1024)} %constant.68) | copy-start | bytes 12292
  128.6 29.5 %all-to-all-start.2 = ((f32[4,32,16,256]{3,2,1,0:T(8,128)}), f32[4,32,16,256]{3,2,1,0:T(8,128)S(1)}, u32[]{:S(2)}, u32[]{:S(2)}) async-start(f32[4,32,16,256]{3,2,1,0:T(8,128)} %bitcast.43), calls=%async_computation.2 | async-start | bytes 4194304 | tf_op jit(solution)/shard_map/all_to_all | solution.py:540
  132.3 6.9 %copy-start.14 = (f32[1024]{0:T(1024)S(1)}, f32[1024]{0:T(1024)}, u32[]{:S(2)}) copy-start(f32[1024]{0:T(1024)} %constant.70) | copy-start | bytes 12292
  132.3 6.9 %copy-start.17 = (f32[1024]{0:T(1024)S(1)}, f32[1024]{0:T(1024)}, u32[]{:S(2)}) copy-start(f32[1024]{0:T(1024)} %constant.72) | copy-start | bytes 12292
  132.3 15.7 %copy-start.21 = (f32[1024]{0:T(1024)S(1)}, f32[1024]{0:T(1024)}, u32[]{:S(2)}) copy-start(f32[1024]{0:T(1024)} %constant.74) | copy-start | bytes 12292
  133.2 6.0 %collective-permute-start.12 = (f32[2,16,1024]{2,1,0:T(8,128)S(1)}, f32[2,16,1024]{2,1,0:T(8,128)S(1)}, u32[]{:S(2)}, u32[]{:S(2)}) collective-permute-start(f32[2,16,1024]{2,1,0:T(8,128)S(1)} %pad_maximum_fusion.4), channel_id=1, source_target_pairs={{0,8},{1,9},{2,10},{3,11},{4,12},{5,13},{6,14},{7,15},{8,0},{9,1},... | collective-permute-start | bytes 393224 | tf_op jit(solution)/shard_map/ppermute | solution.py:575
  139.3 8.8 %collective-permute-start.13 = (f32[2,16,1024]{2,1,0:T(8,128)S(1)}, f32[2,16,1024]{2,1,0:T(8,128)S(1)}, u32[]{:S(2)}, u32[]{:S(2)}) collective-permute-start(f32[2,16,1024]{2,1,0:T(8,128)S(1)} %pad_maximum_fusion), channel_id=1, source_target_pairs={{0,16},{1,17},{2,18},{3,19},{4,20},{5,21},{6,22},{7,23},{8,24},{9,... | collective-permute-start | bytes 393224 | tf_op jit(solution)/shard_map/ppermute | solution.py:575
  156.1 1.4 copy-start.2
  158.1 35.1 %copy-start.1 = (f32[4,32,16,256]{3,2,1,0:T(8,128)}, f32[4,32,16,256]{3,2,1,0:T(8,128)S(1)}, u32[]{:S(2)}) copy-start(f32[4,32,16,256]{3,2,1,0:T(8,128)S(1)} %all-to-all-done.2.rest_1_.v_ref) | copy-start | bytes 6291460
  158.1 102.6 %all-to-all-start.3 = ((f32[4,32,16,256]{3,2,1,0:T(8,128)}), f32[4,32,16,256]{3,2,1,0:T(8,128)}, u32[]{:S(2)}, u32[]{:S(2)}) async-start(f32[4,32,16,256]{3,2,1,0:T(8,128)} %copy-done.2), calls=%async_computation.3 | async-start | bytes 4194304 | tf_op jit(solution)/shard_map/all_to_all | solution.py:587
  162.6 28.0 %collective-permute-start.16 = (f32[4,2,16,256]{3,2,1,0:T(8,128)S(1)}, f32[4,2,16,256]{3,2,1,0:T(8,128)S(1)}, u32[]{:S(2)}, u32[]{:S(2)}) collective-permute-start(f32[4,2,16,256]{3,2,1,0:T(8,128)S(1)} %get-tuple-element.37), channel_id=1, source_target_pairs={{0,1},{1,2},{2,3},{3,4},{4,5},{5,6},{6,7},{7,8},{8,9},{9,10},{10,1... | collective-permute-start | bytes 393224 | tf_op jit(solution)/shard_map/ppermute | solution.py:548
  166.5 26.7 %collective-permute-start.17 = (f32[4,2,16,256]{3,2,1,0:T(8,128)S(1)}, f32[4,2,16,256]{3,2,1,0:T(8,128)S(1)}, u32[]{:S(2)}, u32[]{:S(2)}) collective-permute-start(f32[4,2,16,256]{3,2,1,0:T(8,128)S(1)} %get-tuple-element.36), channel_id=1, source_target_pairs={{1,0},{2,1},{3,2},{4,3},{5,4},{6,5},{7,6},{8,7},{9,8},{10,9},{11,1... | collective-permute-start | bytes 393224 | tf_op jit(solution)/shard_map/ppermute | solution.py:549
  167.9 39.2 %copy-start.3 = (f32[4,32,16,256]{3,2,1,0:T(8,128)S(1)}, f32[4,32,16,256]{3,2,1,0:T(8,128)}, u32[]{:S(2)}) copy-start(f32[4,32,16,256]{3,2,1,0:T(8,128)} %copy-done.2) | copy-start | bytes 6291460
  207.1 5.8 %collective-permute-start.14 = (f32[4,2,16,256]{3,2,1,0:T(8,128)S(1)}, f32[4,2,16,256]{3,2,1,0:T(8,128)S(1)}, u32[]{:S(2)}, u32[]{:S(2)}) collective-permute-start(f32[4,2,16,256]{3,2,1,0:T(8,128)S(1)} %get-tuple-element.39), channel_id=1, source_target_pairs={{0,1},{1,2},{2,3},{3,4},{4,5},{5,6},{6,7},{7,8},{8,9},{9,10},{10,1... | collective-permute-start | bytes 393224 | tf_op jit(solution)/shard_map/ppermute | solution.py:548
  210.5 6.9 %collective-permute-start.15 = (f32[4,2,16,256]{3,2,1,0:T(8,128)S(1)}, f32[4,2,16,256]{3,2,1,0:T(8,128)S(1)}, u32[]{:S(2)}, u32[]{:S(2)}) collective-permute-start(f32[4,2,16,256]{3,2,1,0:T(8,128)S(1)} %get-tuple-element.38), channel_id=1, source_target_pairs={{1,0},{2,1},{3,2},{4,3},{5,4},{6,5},{7,6},{8,7},{9,8},{10,9},{11,1... | collective-permute-start | bytes 393224 | tf_op jit(solution)/shard_map/ppermute | solution.py:549
  232.6 3.8 %collective-permute-start.18 = (f32[48,128]{1,0:T(8,128)S(1)}, f32[48,128]{1,0:T(8,128)S(1)}, u32[]{:S(2)}, u32[]{:S(2)}) collective-permute-start(f32[48,128]{1,0:T(8,128)S(1)} %maximum_add_fusion), channel_id=1, source_target_pairs={{0,1},{1,0},{2,3},{3,2},{4,5},{5,4},{6,7},{7,6},{8,9},{9,8},{10,11... | collective-permute-start | bytes 73736 | tf_op jit(solution)/shard_map/ppermute | solution.py:544
  236.4 3.8 %collective-permute-start.19 = (f32[48,128]{1,0:T(8,128)S(1)}, f32[48,128]{1,0:T(8,128)S(1)}, u32[]{:S(2)}, u32[]{:S(2)}) collective-permute-start(f32[48,128]{1,0:T(8,128)S(1)} %add.71), channel_id=1, source_target_pairs={{0,2},{1,3},{2,0},{3,1},{4,6},{5,7},{6,4},{7,5},{8,10},{9,11},{10,... | collective-permute-start | bytes 73736 | tf_op jit(solution)/shard_map/ppermute | solution.py:544
  240.3 1.2 collective-permute-start.20
  241.5 3.8 %collective-permute-start.21 = (f32[48,128]{1,0:T(8,128)S(1)}, f32[48,128]{1,0:T(8,128)S(1)}, u32[]{:S(2)}, u32[]{:S(2)}) collective-permute-start(f32[48,128]{1,0:T(8,128)S(1)} %add.73), channel_id=1, source_target_pairs={{0,8},{1,9},{2,10},{3,11},{4,12},{5,13},{6,14},{7,15},{8,0},{9,1},... | collective-permute-start | bytes 73736 | tf_op jit(solution)/shard_map/ppermute | solution.py:544
  245.3 4.7 %collective-permute-start.22 = (f32[48,128]{1,0:T(8,128)S(1)}, f32[48,128]{1,0:T(8,128)S(1)}, u32[]{:S(2)}, u32[]{:S(2)}) collective-permute-start(f32[48,128]{1,0:T(8,128)S(1)} %add.74), channel_id=1, source_target_pairs={{0,16},{1,17},{2,18},{3,19},{4,20},{5,21},{6,22},{7,23},{8,24},{9,... | collective-permute-start | bytes 73736 | tf_op jit(solution)/shard_map/ppermute | solution.py:544
  280.7 2.5 copy-start.12
  (1 other events, 1.3 us)

commit v2 on v1

--- a/solution.py
+++ b/solution.py
@@ -19,12 +19,21 @@
 bf16 = jnp.bfloat16
 BOTH = ("row", "col")
 LANES = 128
+UNROLL = 4
 OFFSETS = [(a, b) for a in range(-2, 3) for b in range(-2, 3)]
-VMEM_BYTES = 50 * 2**20
-
-
-def params():
-    return pltpu.CompilerParams(vmem_limit_bytes=VMEM_BYTES)
+
+
+def params(*arrays, extra=4 * 2**20):
+    total = extra
+    for a in arrays:
+        shape = (1, 1) + tuple(a.shape)
+        padded = math.prod(shape[:-2]) * (-(-shape[-2] // 8) * 8) * (-(-shape[-1] // LANES) * LANES)
+        total += padded * a.dtype.itemsize
+    return pltpu.CompilerParams(vmem_limit_bytes=total)
+
+
+def room(*shape):
+    return jax.ShapeDtypeStruct(shape, f32)
 
 
 def cost(flops, nbytes):
@@ -92,6 +101,13 @@
     return high, (x - high.astype(f32)).astype(bf16)
 
 
+def split3(x):
+    high = x.astype(bf16)
+    rest = x - high.astype(f32)
+    middle = rest.astype(bf16)
+    return high, middle, (rest - middle.astype(f32)).astype(bf16)
+
+
 def weights_kernel(index_ref, image_ref, w_ref, deg_ref):
     depth, cols = deg_ref.shape
     total_rows = index_ref[1]
@@ -114,7 +130,7 @@
                     jnp.exp(-beta_value * contrast * contrast - spatial_rate * (a * a + b * b)),
                     0.0,
                 )
-            w_ref[OFFSETS.index((a, b))] = weight
+            w_ref[:, OFFSETS.index((a, b)), :] = weight
             total = weight if total is None else total + weight
         degree = degree + (pltpu.roll(total, (-b) % cols, 1) if b else total)
     deg_ref[...] = degree
@@ -126,7 +142,7 @@
     return pl.pallas_call(
         weights_kernel,
         out_shape=(
-            jax.ShapeDtypeStruct((25, depth, cols), f32),
+            jax.ShapeDtypeStruct((depth, 25, cols), f32),
             jax.ShapeDtypeStruct((depth, cols), f32),
         ),
         in_specs=[
@@ -134,7 +150,7 @@
             pl.BlockSpec(memory_space=pltpu.VMEM),
         ],
         out_specs=(pl.BlockSpec(memory_space=pltpu.VMEM),) * 2,
-        compiler_params=params(),
+        compiler_params=params(image, room(depth, 25, cols), extra=16 * 2**20),
         cost_estimate=cost(60 * depth * cols * 25, 25 * depth * cols * 4),
         name="weights",
     )(index, image)
@@ -143,9 +159,9 @@
 def graph_kernel(order, keep, lane_shift, v_ref, top_ref, bot_ref, w_ref, deg_ref, *rest):
     others, rest = rest[: len(order) - 1], rest[len(order) - 1 :]
     if keep:
-        g_ref, gram_ref, pad_ref, acc_ref = rest
+        g_ref, gram_ref, pad_ref, acc_ref, sum_ref = rest
     else:
-        gram_ref, pad_ref, acc_ref = rest
+        gram_ref, pad_ref, acc_ref, sum_ref = rest
     chunks, depth, fields, width = v_ref.shape
     cols = chunks * width
     for c in range(chunks):
@@ -154,19 +170,25 @@
         pad_ref[2 : 2 + depth, :, lanes] = v_ref[c]
         pad_ref[2 + depth : 4 + depth, :, lanes] = bot_ref[c]
     parts = len(order)
+    groups = fields // 8
 
     def one_row(r, acc):
-        result = None
-        for b in range(-2, 3):
-            total = None
-            for a in range(-2, 3):
-                value = pad_ref[r + 2 + a]
-                if a or b:
-                    value = w_ref[OFFSETS.index((a, b)), pl.ds(r, 1), :] * value
-                total = value if total is None else total + value
-            if b:
-                total = pltpu.roll(total, (-b) % cols, 1)
-            result = total if result is None else result + total
+        for c in range(chunks):
+            lanes = slice(c * width, (c + 1) * width)
+            values = [pad_ref[r + a, :, lanes].reshape(groups, 8, width) for a in range(5)]
+            for b in range(-2, 3):
+                total = None
+                for a in range(-2, 3):
+                    value = values[a + 2]
+                    if a or b:
+                        o = OFFSETS.index((a, b))
+                        weight = w_ref[r, o : o + 1, lanes]
+                        value = weight[None] * value
+                    total = value if total is None else total + value
+                sum_ref[b + 2, :, lanes] = total.reshape(fields, width)
+        result = sum_ref[2]
+        for b in (-2, -1, 1, 2):
+            result = result + pltpu.roll(sum_ref[b + 2], (-b) % cols, 1)
         if keep:
             g_ref[r] = result
         own = pad_ref[r + 2]
@@ -188,7 +210,8 @@
             left, right, (((1,), (1,)), ((), ())), preferred_element_type=f32
         )
 
-    acc = lax.fori_loop(0, depth, one_row, jnp.zeros((2 * parts * fields, 4 * fields), f32))
+    start = jnp.zeros((2 * parts * fields, 4 * fields), f32)
+    acc = lax.fori_loop(0, depth, one_row, start, unroll=UNROLL)
     half = parts * fields
     acc_ref[...] = jnp.zeros(acc_ref.shape, f32)
     acc_ref[:, 0 : 4 * fields] = acc[:half] + acc[half:]
@@ -216,8 +239,9 @@
         scratch_shapes=[
             pltpu.VMEM((depth + 4, fields, cols), f32),
             pltpu.VMEM((parts * fields, LANES), f32),
+            pltpu.VMEM((5, fields, cols), f32),
         ],
-        compiler_params=params(),
+        compiler_params=params(v, w, deg, *others, room(2 * depth + 10, fields, cols)),
         cost_estimate=cost(50 * fields * depth * cols * 4, 4 * cols * depth * (25 + 3 * fields)),
         name="graph_" + "".join(order),
     )(v, top, bot, w, deg, *others)
@@ -231,8 +255,8 @@
         high_ref, low_ref, out_ref = rest
         depth, fields, _ = x_ref.shape
     cols = high_ref.shape[0]
-    block = 8
-    contract = (((1,), (1,)), ((), ()))
+    block = math.gcd(depth, 16)
+    contract = (((1,), (0,)), ((), ()))
 
     def one_block(i, _):
         start = i * block
@@ -259,7 +283,7 @@
         out_shape=jax.ShapeDtypeStruct((depth, fields, cols), f32),
         in_specs=[pl.BlockSpec(memory_space=pltpu.VMEM)] * len(args),
         out_specs=pl.BlockSpec(memory_space=pltpu.VMEM),
-        compiler_params=params(),
+        compiler_params=params(*args, room(depth, fields, cols), extra=12 * 2**20),
         cost_estimate=cost(6 * depth * fields * cols * cols, 4 * cols * (2 * depth * fields + cols)),
         name="cosine_forward",
     )(*args)
@@ -278,24 +302,25 @@
         affinity_row = affinity[k : k + 1, :] * inverse
         affinity = jnp.where(row == k, affinity_row, affinity - column * affinity_row)
         mass = jnp.where(row == k, mass_row, mass - column * mass_row)
-    rayleigh_t = affinity.T
+    ray = split3(affinity.T)
+    left = jnp.concatenate([ray[i] for i in (0, 0, 0, 1, 1, 2)], 1)
 
     def one_row(r, carry):
-        value = fg_ref[r] - jnp.dot(
-            rayleigh_t, fd_ref[r], precision=highest, preferred_element_type=f32
-        )
+        piece = split3(fd_ref[r])
+        right = jnp.concatenate([piece[i] for i in (0, 1, 2, 0, 1, 0)], 0)
+        value = fg_ref[r] - jnp.dot(left, right, preferred_element_type=f32)
         f_ref[r] = value
         keep = eps_ref[pl.ds(jnp.maximum(r - 1, 0), 1), :]
         return value + (carry - keep * carry)
 
-    down = lax.fori_loop(0, depth, one_row, jnp.zeros((fields, cols), f32))
+    down = lax.fori_loop(0, depth, one_row, jnp.zeros((fields, cols), f32), unroll=UNROLL)
 
     def back_row(i, carry):
         r = depth - 1 - i
         keep = eps_ref[pl.ds(jnp.maximum(i - 1, 0), 1), :]
         return f_ref[r] + (carry - keep * carry)
 
-    up = lax.fori_loop(0, depth, back_row, jnp.zeros((fields, cols), f32))
+    up = lax.fori_loop(0, depth, back_row, jnp.zeros((fields, cols), f32), unroll=UNROLL)
     last = last_ref[...]
     ends_ref[0] = up * last
     ends_ref[1] = down * last
@@ -311,7 +336,7 @@
         ),
         in_specs=[pl.BlockSpec(memory_space=pltpu.VMEM)] * 5,
         out_specs=(pl.BlockSpec(memory_space=pltpu.VMEM),) * 2,
-        compiler_params=params(),
+        compiler_params=params(fg, fd, eps, room(depth, fields, cols)),
         cost_estimate=cost(200 * depth * fields * cols, 4 * 3 * depth * fields * cols),
         name="row_solve",
     )(gram, fg, fd, eps, last)
@@ -374,7 +399,7 @@
         in_specs=[pl.BlockSpec(memory_space=pltpu.VMEM)] * (len(gs) + 7),
         out_specs=pl.BlockSpec(memory_space=pltpu.VMEM),
         scratch_shapes=[pltpu.VMEM((depth, fields, cols), f32)],
-        compiler_params=params(),
+        compiler_params=params(*gs, f, high, low, room(2 * depth, fields, cols), extra=12 * 2**20),
         cost_estimate=cost(6 * depth * fields * cols * cols, 4 * cols * (2 * depth * fields + cols)),
         name="row_inverse",
     )(*gs, f, top, bot, eps, last, high, low)
@@ -457,7 +482,7 @@
     images = hdot(basis, reduced, ((1,), (0,)))
     ritz = jnp.sum(basis * images, 1, keepdims=True) - ritz_offset
     ritz_ref[...] = jnp.broadcast_to(ritz, ritz_ref.shape)
-    coeff_ref[...] = math.sqrt(pixel_total) * hdot(basis, inverse, ((1,), (0,))) * scale_row
+    coeff_ref[...] = math.sqrt(pixel_total) * scale_col * hdot(inverse, basis, ((0,), (1,)))
 
 
 def ritz_step(first, second, fields, pixel_total):
@@ -465,7 +490,7 @@
         functools.partial(ritz_kernel, fields, pixel_total),
         out_shape=(
             jax.ShapeDtypeStruct((fields, LANES), f32),
-            jax.ShapeDtypeStruct((fields, 3 * fields), f32),
+            jax.ShapeDtypeStruct((3 * fields, fields), f32),
         ),
         in_specs=[pl.BlockSpec(memory_space=pltpu.VMEM)] * 2,
         out_specs=(pl.BlockSpec(memory_space=pltpu.VMEM),) * 2,
@@ -475,42 +500,64 @@
     )(first, second)
 
 
-def combine_kernel(coeff_ref, x_ref, h_ref, p_ref, block_ref, direction_ref):
-    rows, fields, _ = x_ref.shape
-    high, low = split(coeff_ref[...])
-    left = jnp.concatenate([high, high, low], 1)
-
-    def one_row(r, _):
-        h_high, h_low = split(h_ref[r])
-        p_high, p_low = split(p_ref[r])
-        x_high, x_low = split(x_ref[r])
-        right = jnp.concatenate(
-            [x_high, h_high, p_high, x_low, h_low, p_low, x_high, h_high, p_high], 0
-        )
-        result = jnp.dot(left, right, preferred_element_type=f32)
-        block_ref[r] = result[:fields]
-        direction_ref[r] = result[fields:]
-        return 0
-
-    lax.fori_loop(0, rows, one_row, 0)
+def combine_kernel(tiles, coeff_ref, x_ref, h_ref, p_ref, block_ref, direction_ref, high_ref, low_ref):
+    fields = x_ref.shape[0]
+    width = x_ref.shape[2]
+    group = 8 * fields
+
+    @pl.when(pl.program_id(0) == 0)
+    def _():
+        r = lax.broadcasted_iota(jnp.int32, (group, fields), 0)
+        c = lax.broadcasted_iota(jnp.int32, (group, fields), 1)
+        rows_of = (r // 8 == c).astype(f32)
+        f = lax.broadcasted_iota(jnp.int32, (fields, group), 0)
+        q = lax.broadcasted_iota(jnp.int32, (fields, group), 1)
+        row = lax.broadcasted_iota(jnp.int32, (group, group), 0)
+        col = lax.broadcasted_iota(jnp.int32, (group, group), 1)
+        coeffs = coeff_ref[...]
+        for part in range(3):
+            own = coeffs[part * fields : (part + 1) * fields, :].T
+            if part == 1:
+                cols_of, same = q % fields == f, row % 8 == col // fields
+            else:
+                cols_of, same = q // 8 == f, row % 8 == col % 8
+            wide = hdot(own, cols_of.astype(f32), ((1,), (0,)))
+            wide = jnp.where(same, hdot(rows_of, wide, ((1,), (0,))), 0.0)
+            lanes = slice(part * group, (part + 1) * group)
+            high_ref[:, lanes], low_ref[:, lanes] = split(wide)
+
+    dot = functools.partial(jnp.dot, preferred_element_type=f32)
+    for t in range(tiles):
+        rows = slice(8 * t, 8 * t + 8)
+        x = split(x_ref[:, rows, :].reshape(group, width))
+        h = split(h_ref[rows].reshape(group, width))
+        p = split(p_ref[:, rows, :].reshape(group, width))
+        hp = [jnp.concatenate([h[i], p[i]], 0) for i in range(2)]
+        x_high, x_low = high_ref[:, :group], low_ref[:, :group]
+        hp_high, hp_low = high_ref[:, group:], low_ref[:, group:]
+        direction = dot(hp_high, hp[0]) + dot(hp_low, hp[0]) + dot(hp_high, hp[1])
+        x_left = jnp.concatenate([x_high, x_high, x_low], 1)
+        block = direction + dot(x_left, jnp.concatenate([x[0], x[1], x[0]], 0))
+        block_ref[:, rows, :] = block.reshape(fields, 8, width)
+        direction_ref[:, rows, :] = direction.reshape(fields, 8, width)
 
 
 def combine(coeffs, x, h, p):
-    rows, fields, width = x.shape
-    zero = jnp.zeros((fields, fields), f32)
-    both = jnp.concatenate([coeffs, jnp.concatenate([zero, coeffs[:, fields:]], 1)], 0)
+    fields, rows, width = x.shape
     tile = 32
-    spec = pl.BlockSpec((tile, fields, width), lambda i: (i, 0, 0))
+    spec = pl.BlockSpec((fields, tile, width), lambda i: (0, i, 0))
+    h_spec = pl.BlockSpec((tile, fields, width), lambda i: (i, 0, 0))
     return pl.pallas_call(
-        combine_kernel,
+        functools.partial(combine_kernel, tile // 8),
         grid=(rows // tile,),
-        out_shape=(jax.ShapeDtypeStruct((rows, fields, width), f32),) * 2,
-        in_specs=[pl.BlockSpec(both.shape, lambda i: (0, 0)), spec, spec, spec],
+        out_shape=(jax.ShapeDtypeStruct((fields, rows, width), f32),) * 2,
+        in_specs=[pl.BlockSpec(coeffs.shape, lambda i: (0, 0)), spec, h_spec, spec],
         out_specs=(spec, spec),
-        compiler_params=params(),
+        scratch_shapes=[pltpu.VMEM((8 * fields, 24 * fields), bf16)] * 2,
+        compiler_params=params(room(12 * tile, fields, width)),
         cost_estimate=cost(200 * rows * fields * width, 20 * rows * fields * width),
         name="combine",
-    )(both, x, h, p)
+    )(coeffs, x, h, p)
 
 
 def shifted(block, strips):
@@ -533,6 +580,7 @@
         jnp.asarray(t) for t in row_tables(strips, depth, cols)
     )
     high, low = (jnp.asarray(t) for t in cosine_tables(cols))
+    high_t, low_t = (jnp.asarray(t.T.copy()) for t in cosine_tables(cols))
     top_mine = lax.dynamic_index_in_dim(top_all, strip, 0, False)
     bot_mine = lax.dynamic_index_in_dim(bot_all, strip, 0, False)
 
@@ -540,7 +588,8 @@
         return lax.all_to_all(block, "col", 0, 0)
 
     def total(value):
-        for level in range(levels):
+        first = chunks.bit_length() - 1
+        for level in [*range(first, levels), *range(first)]:
             value = value + lax.ppermute(value, BOTH, [(i, i ^ (1 << level)) for i in range(strips)])
         return value
 
@@ -553,7 +602,6 @@
     p_rows = jnp.transpose(old_direction.reshape(fields, chunks, depth, width), (1, 2, 0, 3))
     image = to_strips(intensity.reshape(chunks, depth, width))
     x_strip = to_strips(x_rows)
-    p_strip = to_strips(p_rows)
 
     image = jnp.transpose(image, (1, 0, 2)).reshape(depth, cols)
     image = jnp.concatenate(
@@ -561,14 +609,19 @@
     )
     w, deg = make_weights(strip, image, depth, rows)
 
-    graph_x, gram_x = apply_graph(("v",), True, 4 * fields, x_strip, *halo(x_strip), w, deg)
+    x_strip, w, p_rows = lax.optimization_barrier((x_strip, w, p_rows))
+    x_halo = halo(x_strip)
+    p_rows, x_halo = lax.optimization_barrier((p_rows, x_halo))
+    p_strip = to_strips(p_rows)
+    graph_x, gram_x = apply_graph(("v",), True, 4 * fields, x_strip, *x_halo, w, deg)
     gram_x = total(gram_x)
-    spectrum_g = cosine_forward(graph_x, None, high, low, depth, fields)
-    spectrum_d = cosine_forward(x_strip, deg, high, low, depth, fields)
+    spectrum_g = cosine_forward(graph_x, None, high_t, low_t, depth, fields)
+    spectrum_d = cosine_forward(x_strip, deg, high_t, low_t, depth, fields)
+    gram_x, p_strip = lax.optimization_barrier((gram_x, p_strip))
+    f, ends = row_solve(gram_x, spectrum_g, spectrum_d, eps, last)
     (gram_p,) = apply_graph(
         ("x", "v"), False, 2 * fields, p_strip, *halo(p_strip), w, deg, x_strip
     )
-    f, ends = row_solve(gram_x, spectrum_g, spectrum_d, eps, last)
 
     gs = []
     for level in range(levels):
@@ -580,25 +633,19 @@
         gs.append(g)
         ends = jnp.stack([lower[0] - g * cross[level], upper[1] + g * cross[level]])
 
+    gs[-1], gram_p = lax.optimization_barrier((gs[-1], gram_p))
     h_strip = row_inverse(gs, f, top_mine, bot_mine, eps, last, high, low, chunks)
+    h_halo = halo(h_strip)
+    h_send, h_halo = lax.optimization_barrier((h_strip, h_halo))
+    h_block = lax.all_to_all(h_send, "col", 0, 0).reshape(height, fields, width)
     (gram_h,) = apply_graph(
-        ("x", "v", "p"), False, 0, h_strip, *halo(h_strip), w, deg, x_strip, p_strip
+        ("x", "v", "p"), False, 0, h_strip, *h_halo, w, deg, x_strip, p_strip
     )
-    h_block = lax.all_to_all(h_strip, "col", 0, 0).reshape(height, fields, width)
     zero = jnp.zeros((fields, LANES), f32)
     gram = gram_h + jnp.concatenate([gram_p[:fields], zero, gram_p[fields:]], 0)
     ritz, coeffs = ritz_step(gram_x, total(gram), fields, rows * cols)
-    new_block, new_direction = combine(
-        coeffs,
-        x_rows.reshape(height, fields, width),
-        h_block,
-        p_rows.reshape(height, fields, width),
-    )
-    return (
-        jnp.transpose(new_block, (1, 0, 2)),
-        jnp.transpose(new_direction, (1, 0, 2)),
-        ritz[:, 0],
-    )
+    new_block, new_direction = combine(coeffs, start_block, h_block, old_direction)
+    return new_block, new_direction, ritz[:, 0]
 
 
 def solution(mesh):

time: 287 us -> 214 us (0.75)
  Pallas kernels: 117 us -> 58.3 us
  waiting for transfers between devices: 93.2 us -> 60.8 us
  local copies, waits for them, and re-layouts: 21.9 us -> 32.1 us
  starting transfers between devices: 52.3 us -> 59.2 us
    ppermute x3, waiting for transfers between devices: 23.7 us -> 3.26 us  [halo(): above = lax.ppermute(block[:, depth - 2:], BOTH, down)]
    all_to_all x3, waiting for transfers between devices: 20.5 us -> 0.9 us  [to_strips(): return lax.all_to_all(block, 'col', 0, 0)]
    pallas_call x3, Pallas kernels: 42.5 us -> 23.5 us  [apply_graph(): pl.pallas_call(functools.partial(graph_kernel, order, keep, lane_shift),...]
    pallas_call x2, Pallas kernels: 23.2 us -> 7.25 us  [cosine_forward(): pl.pallas_call(functools.partial(forward_kernel, deg is not None), out_sh...]
    ppermute x1, waiting for transfers between devices: 0.01 us -> 14.1 us  [local(): lax.ppermute(image[:2], BOTH, up)]
    pallas_call x2, Pallas kernels: 22.1 us -> 8.94 us  [the longest x1 5.84 us: combine(): pl.pallas_call(functools.partial(combine_kernel, tile // 8), grid=(rows /...]
    unnamed x48 -> x60, local copies, waits for them, and re-layouts: 20.2 us -> 28.8 us
    ppermute x5, waiting for transfers between devices: 21.7 us -> 13.1 us  [local(): lax.ppermute(ends, BOTH, [(i, i ^ 1 << level) for i in range(strips)])]
  transfers between devices with their start and end apart: 27 -> 27, of which waited for: 20 -> 19; matrix products, arithmetic and copies ran while one was open for 3% -> 6% of each run, Pallas kernels for 25% -> 21%
where the time goes in v2:
time: 214 us; the launch traced here: 213 us
  waiting for transfers between devices  60.8 us (28%)
  starting transfers between devices  59.2 us (28%)
  Pallas kernels  58.3 us (27%)
  local copies, waits for them, and re-layouts  32.1 us (15%)
    unnamed x60, local copies, waits for them, and re-layouts  28.8 us
    pallas_call x3, Pallas kernels, apply_graph(): pl.pallas_call(functools.partial(graph_kernel, order, keep, lane_shift),...  23.5 us
    ppermute x10, waiting for transfers between devices, total(): lax.ppermute(value, BOTH, [(i, i ^ 1 << level) for i in range(strips)])  17.8 us
    ppermute x1, waiting for transfers between devices, local(): lax.ppermute(image[:2], BOTH, up)  14.1 us
    ppermute x10, starting transfers between devices, total(): lax.ppermute(value, BOTH, [(i, i ^ 1 << level) for i in range(strips)])  13.7 us
    all_to_all x3, starting transfers between devices, to_strips(): return lax.all_to_all(block, 'col', 0, 0)  13.3 us
    ppermute x5, waiting for transfers between devices, local(): lax.ppermute(ends, BOTH, [(i, i ^ 1 << level) for i in range(strips)])  13.1 us
    ppermute x3, waiting for transfers between devices, halo(): below = lax.ppermute(block[:, :2], BOTH, up)  11.7 us
  transfers between devices with their start and end apart: 27, of which 19 were waited for; matrix products, arithmetic and copies ran while one was open for 6% of the time, Pallas kernels for 21%

profile of v2, /device:TPU:0, one launch (start us, length us, event | category | flops | bytes accessed | tf_op | source)
XLA Modules:
  0.0 212.7 jit_solution(18318939202322203564)
XLA Ops:
  0.6 5.2 %all-to-all-start.1 = ((f32[4,32,256]{2,1,0:T(8,128)}), f32[4,32,256]{2,1,0:T(8,128)S(1)}, u32[]{:S(2)}, u32[]{:S(2)}) async-start(f32[4,32,256]{2,1,0:T(8,128)} %bitcast.35), calls=%async_computation.1 | async-start | bytes 262144 | tf_op jit(solution)/shard_map/all_to_all | solution.py:588
  5.8 4.1 %copy.22 = f32[16,128,256]{2,0,1:T(8,128)} copy(f32[16,128,256]{2,1,0:T(8,128)} %x_ref.1) | data formatting | bytes 4194304 | tf_op args[1]
  10.8 3.6 %all-to-all-start = ((f32[4,32,16,256]{3,2,1,0:T(8,128)}), f32[4,32,16,256]{3,2,1,0:T(8,128)S(1)}, u32[]{:S(2)}, u32[]{:S(2)}) async-start(f32[4,32,16,256]{3,2,1,0:T(8,128)} %bitcast.31), calls=%async_computation | async-start | bytes 4194304 | tf_op jit(solution)/shard_map/all_to_all | solution.py:588
  15.8 4.5 %collective-permute-start = (f32[2,1024]{1,0:T(2,128)S(1)}, f32[2,1024]{1,0:T(2,128)S(1)}, u32[]{:S(2)}, u32[]{:S(2)}) collective-permute-start(f32[2,1024]{1,0:T(2,128)S(1)} %bitcast.36), channel_id=1, source_target_pairs={{0,1},{1,2},{2,3},{3,4},{4,5},{5,6},{6,7},{7,8},{8,9},{9,10},{10,1... | collective-permute-start | bytes 24584 | tf_op jit(solution)/shard_map/ppermute | solution.py:608
  20.4 4.2 %copy.24 = f32[16,128,256]{2,0,1:T(8,128)} copy(f32[16,128,256]{2,1,0:T(8,128)} %p_ref.1) | data formatting | bytes 4194304 | tf_op args[2]
  24.6 14.1 %collective-permute-done.1 = f32[2,1024]{1,0:T(2,128)S(1)} collective-permute-done((f32[2,1024]{1,0:T(2,128)S(1)}, f32[2,1024]{1,0:T(2,128)S(1)}, u32[]{:S(2)}, u32[]{:S(2)}) %collective-permute-start.1) | collective-permute-done | bytes 8224 | tf_op jit(solution)/shard_map/ppermute | solution.py:608
  38.7 3.1 %weights.1 = (f32[32,25,1024]{2,1,0:T(8,128)S(1)}, f32[32,1024]{1,0:T(8,128)S(1)}) custom-call(s32[2]{0:T(128)S(1)} %pad_add_fusion.index_ref, f32[36,1024]{1,0:T(8,128)S(1)} %pad_maximum_fusion.1.image_ref), custom_call_target="tpu_custom_call" | custom-call | flops 49152000 | bytes 3276800 | tf_op jit(solution)/shard_map/weights/pallas_call | solution.py:142
  41.8 2.0 copy-done
  43.9 3.3 %collective-permute-start.2 = (f32[4,2,16,256]{3,2,1,0:T(8,128)S(1)}, f32[4,2,16,256]{3,2,1,0:T(8,128)S(1)}, u32[]{:S(2)}, u32[]{:S(2)}) collective-permute-start(f32[4,2,16,256]{3,2,1,0:T(8,128)S(1)} %get-tuple-element.54), channel_id=1, source_target_pairs={{0,1},{1,2},{2,3},{3,4},{4,5},{5,6},{6,7},{7,8},{8,9},{9,10},{10,1... | collective-permute-start | bytes 393224 | tf_op jit(solution)/shard_map/ppermute | solution.py:597
  49.7 4.8 %collective-permute-done.3.bot_ref = f32[4,2,16,256]{3,2,1,0:T(8,128)S(1)} collective-permute-done((f32[4,2,16,256]{3,2,1,0:T(8,128)S(1)}, f32[4,2,16,256]{3,2,1,0:T(8,128)S(1)}, u32[]{:S(2)}, u32[]{:S(2)}) %collective-permute-start.3) | collective-permute-done | bytes 131104 | tf_op jit(solution)/shard_map/ppermute | solution.py:598
  54.5 4.5 %all-to-all-start.2 = ((f32[4,32,16,256]{3,2,1,0:T(8,128)}), f32[4,32,16,256]{3,2,1,0:T(8,128)}, u32[]{:S(2)}, u32[]{:S(2)}) async-start(f32[4,32,16,256]{3,2,1,0:T(8,128)} %bitcast.30), calls=%async_computation.2 | async-start | bytes 4194304 | tf_op jit(solution)/shard_map/all_to_all | solution.py:588
  59.0 2.2 %copy-done.1 = f32[32,25,1024]{2,1,0:T(8,128)S(1)} copy-done((f32[32,25,1024]{2,1,0:T(8,128)S(1)}, f32[32,25,1024]{2,1,0:T(8,128)}, u32[]{:S(2)}) %copy-start.1) | copy-done | bytes 3276824
  61.2 6.4 %graph_v.1 = (f32[32,16,1024]{2,1,0:T(8,128)S(1)}, f32[16,128]{1,0:T(8,128)S(1)}) custom-call(f32[4,32,16,256]{3,2,1,0:T(8,128)S(1)} %all-to-all-done.v_ref.x_ref.rest_0_, f32[4,2,16,256]{3,2,1,0:T(8,128)S(1)} %collective-permute-done.2.top_ref, f32[4,2,16,256]{3,2,1,0:T(8,128)S(1)} %collective-permute-done.3.bot_ref, f32[32,25,1024]{2,1,0:T(8,128)S(1)} %copy-done.1, ...), custom_call_target="tpu_custom_call" | custom-call | flops 104857600 | bytes 9568256 | tf_op jit(solution)/shard_map/graph_v/pallas_call | solution.py:234
  70.3 2.1 collective-permute-done.5
  72.4 2.6 %collective-permute-start.6 = (f32[16,128]{1,0:T(8,128)S(1)}, f32[16,128]{1,0:T(8,128)S(1)}, u32[]{:S(2)}, u32[]{:S(2)}) collective-permute-start(f32[16,128]{1,0:T(8,128)S(1)} %add.59), channel_id=1, source_target_pairs={{0,16},{1,17},{2,18},{3,19},{4,20},{5,21},{6,22},{7,23},{8,24},{9,... | collective-permute-start | bytes 24584 | tf_op jit(solution)/shard_map/ppermute | solution.py:593
  75.0 2.0 collective-permute-done.6
  77.0 2.0 collective-permute-start.7
  79.0 3.6 %cosine_forward.3.fd_ref = f32[32,16,1024]{2,1,0:T(8,128)S(1)} custom-call(f32[4,32,16,256]{3,2,1,0:T(8,128)S(1)} %all-to-all-done.v_ref.x_ref.rest_0_, f32[32,1024]{1,0:T(8,128)S(1)} %get-tuple-element.32.deg_ref.rest_0_, bf16[1024,1024]{1,0:T(8,128)(2,1)S(1)} %copy-done.18, bf16[1024,1024]{1,0:T(8,128)(2,1)S(1)} %copy-done.19), custom_call_target="tpu_custom_call" | custom-call | flops 3221225472 | bytes 8388608 | tf_op jit(solution)/shard_map/cosine_forward/pallas_call | solution.py:281
  84.4 2.2 %collective-permute-start.8 = (f32[16,128]{1,0:T(8,128)S(1)}, f32[16,128]{1,0:T(8,128)S(1)}, u32[]{:S(2)}, u32[]{:S(2)}) collective-permute-start(f32[16,128]{1,0:T(8,128)S(1)} %add.61), channel_id=1, source_target_pairs={{0,2},{1,3},{2,0},{3,1},{4,6},{5,7},{6,4},{7,5},{8,10},{9,11},{10,... | collective-permute-start | bytes 24584 | tf_op jit(solution)/shard_map/ppermute | solution.py:593
  86.7 3.6 %cosine_forward.2.fg_ref = f32[32,16,1024]{2,1,0:T(8,128)S(1)} custom-call(f32[32,16,1024]{2,1,0:T(8,128)S(1)} %get-tuple-element.36.x_ref, bf16[1024,1024]{1,0:T(8,128)(2,1)S(1)} %copy-done.18, bf16[1024,1024]{1,0:T(8,128)(2,1)S(1)} %copy-done.19), custom_call_target="tpu_custom_call" | custom-call | flops 3221225472 | bytes 8388608 | tf_op jit(solution)/shard_map/cosine_forward/pallas_call | solution.py:281
  94.9 3.7 %row_solve.1 = (f32[32,16,1024]{2,1,0:T(8,128)S(1)}, f32[2,16,1024]{2,1,0:T(8,128)S(1)}) custom-call(f32[16,128]{1,0:T(8,128)S(1)} %add.62.gram_ref.first_ref, f32[32,16,1024]{2,1,0:T(8,128)S(1)} %copy-done.11, f32[32,16,1024]{2,1,0:T(8,128)S(1)} %copy-done.9, f32[32,1024]{1,0:T(8,128)S(1)} %copy-done.12, f32[1,1024]{1,0:T(1,128)S(1)} %copy-done.13), custom_call_target="tpu_custom_call" | custom-call | flops 104857600 | bytes 6291456 | tf_op jit(solution)/shard_map/row_solve/pallas_call | solution.py:331
  99.9 5.1 %collective-permute-done.9 = f32[2,16,1024]{2,1,0:T(8,128)S(1)} collective-permute-done((f32[2,16,1024]{2,1,0:T(8,128)S(1)}, f32[2,16,1024]{2,1,0:T(8,128)S(1)}, u32[]{:S(2)}, u32[]{:S(2)}) %collective-permute-start.9) | collective-permute-done | bytes 131104 | tf_op jit(solution)/shard_map/ppermute | solution.py:628
  105.4 1.7 fusion.8
  107.1 2.2 %collective-permute-start.14 = (f32[4,2,16,256]{3,2,1,0:T(8,128)}, f32[4,2,16,256]{3,2,1,0:T(8,128)S(1)}, u32[]{:S(2)}, u32[]{:S(2)}) collective-permute-start(f32[4,2,16,256]{3,2,1,0:T(8,128)} %get-tuple-element.52), channel_id=1, source_target_pairs={{0,1},{1,2},{2,3},{3,4},{4,5},{5,6},{6,7},{7,8},{8,9},{9,10},{10,1... | collective-permute-start | bytes 393224 | tf_op jit(solution)/shard_map/ppermute | solution.py:597
  111.5 1.9 collective-permute-start.11
  114.2 3.3 %collective-permute-done.15.bot_ref = f32[4,2,16,256]{3,2,1,0:T(8,128)S(1)} collective-permute-done((f32[4,2,16,256]{3,2,1,0:T(8,128)}, f32[4,2,16,256]{3,2,1,0:T(8,128)S(1)}, u32[]{:S(2)}, u32[]{:S(2)}) %collective-permute-start.15) | collective-permute-done | bytes 131104 | tf_op jit(solution)/shard_map/ppermute | solution.py:598
  117.6 2.2 %copy-done.2 = f32[32,25,1024]{2,1,0:T(8,128)S(1)} copy-done((f32[32,25,1024]{2,1,0:T(8,128)S(1)}, f32[32,25,1024]{2,1,0:T(8,128)}, u32[]{:S(2)}) %copy-start.2) | copy-done | bytes 3276824
  119.8 8.4 %graph_xv.1 = f32[32,128]{1,0:T(8,128)S(1)} custom-call(f32[4,32,16,256]{3,2,1,0:T(8,128)} %all-to-all-done.2.v_ref.rest_1_, f32[4,2,16,256]{3,2,1,0:T(8,128)S(1)} %collective-permute-done.14.top_ref, f32[4,2,16,256]{3,2,1,0:T(8,128)S(1)} %collective-permute-done.15.bot_ref, f32[32,25,1024]{2,1,0:T(8,128)S(1)} %copy-done.2, ...), custom_call_target="tpu_custom_call" | custom-call | flops 104857600 | bytes 9568256 | tf_op jit(solution)/shard_map/graph_xv/pallas_call | solution.py:234
  128.3 1.6 collective-permute-start.12
  130.0 3.4 %collective-permute-done.12 = f32[2,16,1024]{2,1,0:T(8,128)S(1)} collective-permute-done((f32[2,16,1024]{2,1,0:T(8,128)S(1)}, f32[2,16,1024]{2,1,0:T(8,128)S(1)}, u32[]{:S(2)}, u32[]{:S(2)}) %collective-permute-start.12) | collective-permute-done | bytes 131104 | tf_op jit(solution)/shard_map/ppermute | solution.py:628
  133.4 2.7 %collective-permute-start.13 = (f32[2,16,1024]{2,1,0:T(8,128)S(1)}, f32[2,16,1024]{2,1,0:T(8,128)S(1)}, u32[]{:S(2)}, u32[]{:S(2)}) collective-permute-start(f32[2,16,1024]{2,1,0:T(8,128)S(1)} %pad_maximum_fusion), channel_id=1, source_target_pairs={{0,16},{1,17},{2,18},{3,19},{4,20},{5,21},{6,22},{7,23},{8,24},{9,... | collective-permute-start | bytes 393224 | tf_op jit(solution)/shard_map/ppermute | solution.py:628
  136.1 4.7 %collective-permute-done.13 = f32[2,16,1024]{2,1,0:T(8,128)S(1)} collective-permute-done((f32[2,16,1024]{2,1,0:T(8,128)S(1)}, f32[2,16,1024]{2,1,0:T(8,128)S(1)}, u32[]{:S(2)}, u32[]{:S(2)}) %collective-permute-start.13) | collective-permute-done | bytes 131104 | tf_op jit(solution)/shard_map/ppermute | solution.py:628
  140.8 5.1 %row_inverse.1.v_ref = f32[4,32,16,256]{3,2,1,0:T(8,128)S(1)} custom-call(f32[16,1024]{1,0:T(8,128)S(1)} %get-tuple-element.80.refs_0_, f32[16,1024]{1,0:T(8,128)S(1)} %get-tuple-element.79.refs_1_, f32[16,1024]{1,0:T(8,128)S(1)} %get-tuple-element.78.refs_2_, f32[16,1024]{1,0:T(8,128)S(1)} %get-tuple-element.77.refs_3_, f32[16,1024]{1,0:T(8,128)S(1)} %fusion.4.refs_4_, ...), custom_call_target="tpu_custom_call" | custom-call | flops 3221225472 | bytes 8388608 | tf_op jit(solution)/shard_map/row_inverse/pallas_call | solution.py:396
  145.9 5.8 %collective-permute-start.16 = (f32[4,2,16,256]{3,2,1,0:T(8,128)S(1)}, f32[4,2,16,256]{3,2,1,0:T(8,128)S(1)}, u32[]{:S(2)}, u32[]{:S(2)}) collective-permute-start(f32[4,2,16,256]{3,2,1,0:T(8,128)S(1)} %get-tuple-element.50), channel_id=1, source_target_pairs={{0,1},{1,2},{2,3},{3,4},{4,5},{5,6},{6,7},{7,8},{8,9},{9,10},{10,1... | collective-permute-start | bytes 393224 | tf_op jit(solution)/shard_map/ppermute | solution.py:597
  153.0 2.1 collective-permute-done.16.top_ref
  155.1 3.5 %collective-permute-done.17.bot_ref = f32[4,2,16,256]{3,2,1,0:T(8,128)S(1)} collective-permute-done((f32[4,2,16,256]{3,2,1,0:T(8,128)S(1)}, f32[4,2,16,256]{3,2,1,0:T(8,128)S(1)}, u32[]{:S(2)}, u32[]{:S(2)}) %collective-permute-start.17) | collective-permute-done | bytes 131104 | tf_op jit(solution)/shard_map/ppermute | solution.py:598
  158.6 4.5 %all-to-all-start.3 = ((f32[4,32,16,256]{3,2,1,0:T(8,128)}), f32[4,32,16,256]{3,2,1,0:T(8,128)}, u32[]{:S(2)}, u32[]{:S(2)}) async-start(f32[4,32,16,256]{3,2,1,0:T(8,128)} %copy-done.4), calls=%async_computation.3 | async-start | bytes 4194304 | tf_op jit(solution)/shard_map/all_to_all | solution.py:640
  163.2 2.2 %copy-done.3 = f32[32,25,1024]{2,1,0:T(8,128)S(1)} copy-done((f32[32,25,1024]{2,1,0:T(8,128)S(1)}, f32[32,25,1024]{2,1,0:T(8,128)}, u32[]{:S(2)}) %copy-start.3) | copy-done | bytes 3276824
  166.9 8.7 %graph_xvp.1 = f32[48,128]{1,0:T(8,128)S(1)} custom-call(f32[4,32,16,256]{3,2,1,0:T(8,128)S(1)} %copy-done.5, f32[4,2,16,256]{3,2,1,0:T(8,128)S(1)} %collective-permute-done.16.top_ref, f32[4,2,16,256]{3,2,1,0:T(8,128)S(1)} %collective-permute-done.17.bot_ref, f32[32,25,1024]{2,1,0:T(8,128)S(1)} %copy-done.3, ...), custom_call_target="tpu_custom_call" | custom-call | flops 104857600 | bytes 9568256 | tf_op jit(solution)/shard_map/graph_xvp/pallas_call | solution.py:234
  176.9 3.8 %collective-permute-done.19 = f32[48,128]{1,0:T(8,128)S(1)} collective-permute-done((f32[48,128]{1,0:T(8,128)S(1)}, f32[48,128]{1,0:T(8,128)S(1)}, u32[]{:S(2)}, u32[]{:S(2)}) %collective-permute-start.19) | collective-permute-done | bytes 24608 | tf_op jit(solution)/shard_map/ppermute | solution.py:593
  182.0 3.4 %collective-permute-done.20 = f32[48,128]{1,0:T(8,128)S(1)} collective-permute-done((f32[48,128]{1,0:T(8,128)S(1)}, f32[48,128]{1,0:T(8,128)S(1)}, u32[]{:S(2)}, u32[]{:S(2)}) %collective-permute-start.20) | collective-permute-done | bytes 24608 | tf_op jit(solution)/shard_map/ppermute | solution.py:593
  185.5 2.0 collective-permute-start.21
  187.4 1.9 collective-permute-done.21
  189.3 2.0 collective-permute-start.22
  191.3 1.9 collective-permute-done.22
  193.1 9.9 %ritz.1 = (f32[16,128]{1,0:T(8,128)S(1)}, f32[48,16]{1,0:T(8,128)S(1)}) custom-call(f32[16,128]{1,0:T(8,128)S(1)} %add.62.gram_ref.first_ref, f32[48,128]{1,0:T(8,128)S(1)} %add.73.second_ref), custom_call_target="tpu_custom_call" | custom-call | flops 33554432 | bytes 65536 | tf_op jit(solution)/shard_map/ritz/pallas_call | solution.py:489
  203.7 1.6 copy-done.6
  206.9 5.8 %combine.1 = (f32[16,128,256]{2,1,0:T(8,128)}, f32[16,128,256]{2,1,0:T(8,128)}) custom-call(f32[48,16]{1,0:T(8,128)S(1)} %get-tuple-element.44.coeff_ref, f32[16,128,256]{2,1,0:T(8,128)S(1)} %copy-done.6, f32[128,16,256]{2,1,0:T(8,128)} %bitcast.16.h_ref, f32[16,128,256]{2,1,0:T(8,128)S(1)} %copy-done.7), custom_call_target="tpu_custom_call" | custom-call | flops 104857600 | bytes 10485760 | tf_op jit(solution)/shard_map/combine/pallas_call | solution.py:550
  (114 shorter events, 26.7 us)
Async XLA Ops:
  0.6 10.2 %all-to-all-start.1 = ((f32[4,32,256]{2,1,0:T(8,128)}), f32[4,32,256]{2,1,0:T(8,128)S(1)}, u32[]{:S(2)}, u32[]{:S(2)}) async-start(f32[4,32,256]{2,1,0:T(8,128)} %bitcast.35), calls=%async_computation.1 | async-start | bytes 262144 | tf_op jit(solution)/shard_map/all_to_all | solution.py:588
  10.8 33.0 %all-to-all-start = ((f32[4,32,16,256]{3,2,1,0:T(8,128)}), f32[4,32,16,256]{3,2,1,0:T(8,128)S(1)}, u32[]{:S(2)}, u32[]{:S(2)}) async-start(f32[4,32,16,256]{3,2,1,0:T(8,128)} %bitcast.31), calls=%async_computation | async-start | bytes 4194304 | tf_op jit(solution)/shard_map/all_to_all | solution.py:588
  14.5 24.2 %collective-permute-start.1 = (f32[2,1024]{1,0:T(2,128)S(1)}, f32[2,1024]{1,0:T(2,128)S(1)}, u32[]{:S(2)}, u32[]{:S(2)}) collective-permute-start(f32[2,1024]{1,0:T(2,128)S(1)} %bitcast.37), channel_id=1, source_target_pairs={{1,0},{2,1},{3,2},{4,3},{5,4},{6,5},{7,6},{8,7},{9,8},{10,9},{11,1... | collective-permute-start | bytes 24584 | tf_op jit(solution)/shard_map/ppermute | solution.py:608
  15.8 22.9 %collective-permute-start = (f32[2,1024]{1,0:T(2,128)S(1)}, f32[2,1024]{1,0:T(2,128)S(1)}, u32[]{:S(2)}, u32[]{:S(2)}) collective-permute-start(f32[2,1024]{1,0:T(2,128)S(1)} %bitcast.36), channel_id=1, source_target_pairs={{0,1},{1,2},{2,3},{3,4},{4,5},{5,6},{6,7},{7,8},{8,9},{9,10},{10,1... | collective-permute-start | bytes 24584 | tf_op jit(solution)/shard_map/ppermute | solution.py:608
  41.8 2.0 copy-start
  43.9 5.8 %collective-permute-start.2 = (f32[4,2,16,256]{3,2,1,0:T(8,128)S(1)}, f32[4,2,16,256]{3,2,1,0:T(8,128)S(1)}, u32[]{:S(2)}, u32[]{:S(2)}) collective-permute-start(f32[4,2,16,256]{3,2,1,0:T(8,128)S(1)} %get-tuple-element.54), channel_id=1, source_target_pairs={{0,1},{1,2},{2,3},{3,4},{4,5},{5,6},{6,7},{7,8},{8,9},{9,10},{10,1... | collective-permute-start | bytes 393224 | tf_op jit(solution)/shard_map/ppermute | solution.py:597
  47.2 7.3 %collective-permute-start.3 = (f32[4,2,16,256]{3,2,1,0:T(8,128)S(1)}, f32[4,2,16,256]{3,2,1,0:T(8,128)S(1)}, u32[]{:S(2)}, u32[]{:S(2)}) collective-permute-start(f32[4,2,16,256]{3,2,1,0:T(8,128)S(1)} %get-tuple-element.53), channel_id=1, source_target_pairs={{1,0},{2,1},{3,2},{4,3},{5,4},{6,5},{7,6},{8,7},{9,8},{10,9},{11,1... | collective-permute-start | bytes 393224 | tf_op jit(solution)/shard_map/ppermute | solution.py:598
  54.5 37.1 %all-to-all-start.2 = ((f32[4,32,16,256]{3,2,1,0:T(8,128)}), f32[4,32,16,256]{3,2,1,0:T(8,128)}, u32[]{:S(2)}, u32[]{:S(2)}) async-start(f32[4,32,16,256]{3,2,1,0:T(8,128)} %bitcast.30), calls=%async_computation.2 | async-start | bytes 4194304 | tf_op jit(solution)/shard_map/all_to_all | solution.py:588
  59.0 2.2 %copy-start.1 = (f32[32,25,1024]{2,1,0:T(8,128)S(1)}, f32[32,25,1024]{2,1,0:T(8,128)}, u32[]{:S(2)}) copy-start(f32[32,25,1024]{2,1,0:T(8,128)} %copy-done) | copy-start | bytes 9830404
  61.2 17.8 %copy-start.18 = (bf16[1024,1024]{1,0:T(8,128)(2,1)S(1)}, bf16[1024,1024]{1,0:T(8,128)(2,1)}, u32[]{:S(2)}) copy-start(bf16[1024,1024]{1,0:T(8,128)(2,1)} %constant.58.clone.rest_0_.rest_1_) | copy-start | bytes 6291460
  61.2 17.8 %copy-start.19 = (bf16[1024,1024]{1,0:T(8,128)(2,1)S(1)}, bf16[1024,1024]{1,0:T(8,128)(2,1)}, u32[]{:S(2)}) copy-start(bf16[1024,1024]{1,0:T(8,128)(2,1)} %constant.59.clone.rest_1_.rest_2_) | copy-start | bytes 6291460
  67.6 1.2 collective-permute-start.4
  68.8 3.7 %collective-permute-start.5 = (f32[16,128]{1,0:T(8,128)S(1)}, f32[16,128]{1,0:T(8,128)S(1)}, u32[]{:S(2)}, u32[]{:S(2)}) collective-permute-start(f32[16,128]{1,0:T(8,128)S(1)} %add.58), channel_id=1, source_target_pairs={{0,8},{1,9},{2,10},{3,11},{4,12},{5,13},{6,14},{7,15},{8,0},{9,1},... | collective-permute-start | bytes 24584 | tf_op jit(solution)/shard_map/ppermute | solution.py:593
  72.4 4.5 %collective-permute-start.6 = (f32[16,128]{1,0:T(8,128)S(1)}, f32[16,128]{1,0:T(8,128)S(1)}, u32[]{:S(2)}, u32[]{:S(2)}) collective-permute-start(f32[16,128]{1,0:T(8,128)S(1)} %add.59), channel_id=1, source_target_pairs={{0,16},{1,17},{2,18},{3,19},{4,20},{5,21},{6,22},{7,23},{8,24},{9,... | collective-permute-start | bytes 24584 | tf_op jit(solution)/shard_map/ppermute | solution.py:593
  77.0 7.5 %collective-permute-start.7 = (f32[16,128]{1,0:T(8,128)S(1)}, f32[16,128]{1,0:T(8,128)S(1)}, u32[]{:S(2)}, u32[]{:S(2)}) collective-permute-start(f32[16,128]{1,0:T(8,128)S(1)} %add.60), channel_id=1, source_target_pairs={{0,1},{1,0},{2,3},{3,2},{4,5},{5,4},{6,7},{7,6},{8,9},{9,8},{10,11... | collective-permute-start | bytes 24584 | tf_op jit(solution)/shard_map/ppermute | solution.py:593
  84.4 7.2 %collective-permute-start.8 = (f32[16,128]{1,0:T(8,128)S(1)}, f32[16,128]{1,0:T(8,128)S(1)}, u32[]{:S(2)}, u32[]{:S(2)}) collective-permute-start(f32[16,128]{1,0:T(8,128)S(1)} %add.61), channel_id=1, source_target_pairs={{0,2},{1,3},{2,0},{3,1},{4,6},{5,7},{6,4},{7,5},{8,10},{9,11},{10,... | collective-permute-start | bytes 24584 | tf_op jit(solution)/shard_map/ppermute | solution.py:593
  86.7 5.0 %copy-start.12 = (f32[32,1024]{1,0:T(8,128)S(1)}, f32[32,1024]{1,0:T(8,128)}, u32[]{:S(2)}) copy-start(f32[32,1024]{1,0:T(8,128)} %constant.50.clone.eps_ref.refs_8_) | copy-start | bytes 393220
  86.7 5.0 %copy-start.13 = (f32[1,1024]{1,0:T(1,128)S(1)}, f32[1,1024]{1,0:T(1,128)}, u32[]{:S(2)}) copy-start(f32[1,1024]{1,0:T(1,128)} %constant.51.clone.last_ref.refs_9_) | copy-start | bytes 12292
  94.9 10.1 %copy-start.22 = (f32[1024]{0:T(1024)S(1)}, f32[1024]{0:T(1024)}, u32[]{:S(2)}) copy-start(f32[1024]{0:T(1024)} %constant.61) | copy-start | bytes 12292
  94.9 10.1 %copy-start.27 = (f32[1024]{0:T(1024)S(1)}, f32[1024]{0:T(1024)}, u32[]{:S(2)}) copy-start(f32[1024]{0:T(1024)} %constant.63) | copy-start | bytes 12292
  99.8 10.9 %copy-start.23 = (f32[1024]{0:T(1024)S(1)}, f32[1024]{0:T(1024)}, u32[]{:S(2)}) copy-start(f32[1024]{0:T(1024)} %constant.65) | copy-start | bytes 12292
  99.8 10.9 %copy-start.26 = (f32[1024]{0:T(1024)S(1)}, f32[1024]{0:T(1024)}, u32[]{:S(2)}) copy-start(f32[1024]{0:T(1024)} %constant.67) | copy-start | bytes 12292
  99.8 5.1 %collective-permute-start.9 = (f32[2,16,1024]{2,1,0:T(8,128)S(1)}, f32[2,16,1024]{2,1,0:T(8,128)S(1)}, u32[]{:S(2)}, u32[]{:S(2)}) collective-permute-start(f32[2,16,1024]{2,1,0:T(8,128)S(1)} %get-tuple-element.37), channel_id=1, source_target_pairs={{0,1},{1,0},{2,3},{3,2},{4,5},{5,4},{6,7},{7,6},{8,9},{9,8},{10,11... | collective-permute-start | bytes 393224 | tf_op jit(solution)/shard_map/ppermute | solution.py:628
  105.0 5.7 %collective-permute-start.10 = (f32[2,16,1024]{2,1,0:T(8,128)S(1)}, f32[2,16,1024]{2,1,0:T(8,128)S(1)}, u32[]{:S(2)}, u32[]{:S(2)}) collective-permute-start(f32[2,16,1024]{2,1,0:T(8,128)S(1)} %pad_maximum_fusion.2), channel_id=1, source_target_pairs={{0,2},{1,3},{2,0},{3,1},{4,6},{5,7},{6,4},{7,5},{8,10},{9,11},{10,... | collective-permute-start | bytes 393224 | tf_op jit(solution)/shard_map/ppermute | solution.py:628
  107.1 7.1 %collective-permute-start.14 = (f32[4,2,16,256]{3,2,1,0:T(8,128)}, f32[4,2,16,256]{3,2,1,0:T(8,128)S(1)}, u32[]{:S(2)}, u32[]{:S(2)}) collective-permute-start(f32[4,2,16,256]{3,2,1,0:T(8,128)} %get-tuple-element.52), channel_id=1, source_target_pairs={{0,1},{1,2},{2,3},{3,4},{4,5},{5,6},{6,7},{7,8},{8,9},{9,10},{10,1... | collective-permute-start | bytes 393224 | tf_op jit(solution)/shard_map/ppermute | solution.py:597
  109.3 8.3 %collective-permute-start.15 = (f32[4,2,16,256]{3,2,1,0:T(8,128)}, f32[4,2,16,256]{3,2,1,0:T(8,128)S(1)}, u32[]{:S(2)}, u32[]{:S(2)}) collective-permute-start(f32[4,2,16,256]{3,2,1,0:T(8,128)} %get-tuple-element.51), channel_id=1, source_target_pairs={{1,0},{2,1},{3,2},{4,3},{5,4},{6,5},{7,6},{8,7},{9,8},{10,9},{11,1... | collective-permute-start | bytes 393224 | tf_op jit(solution)/shard_map/ppermute | solution.py:598
  111.5 16.7 %collective-permute-start.11 = (f32[2,16,1024]{2,1,0:T(8,128)}, f32[2,16,1024]{2,1,0:T(8,128)S(1)}, u32[]{:S(2)}, u32[]{:S(2)}) collective-permute-start(f32[2,16,1024]{2,1,0:T(8,128)} %pad_maximum_fusion.3), channel_id=1, source_target_pairs={{0,4},{1,5},{2,6},{3,7},{4,0},{5,1},{6,2},{7,3},{8,12},{9,13},{10,... | collective-permute-start | bytes 393224 | tf_op jit(solution)/shard_map/ppermute | solution.py:628
  113.4 14.9 %copy-start.20 = (f32[1024]{0:T(1024)S(1)}, f32[1024]{0:T(1024)}, u32[]{:S(2)}) copy-start(f32[1024]{0:T(1024)} %constant.69) | copy-start | bytes 12292
  113.4 14.9 %copy-start.25 = (f32[1024]{0:T(1024)S(1)}, f32[1024]{0:T(1024)}, u32[]{:S(2)}) copy-start(f32[1024]{0:T(1024)} %constant.71) | copy-start | bytes 12292
  117.6 2.2 %copy-start.2 = (f32[32,25,1024]{2,1,0:T(8,128)S(1)}, f32[32,25,1024]{2,1,0:T(8,128)}, u32[]{:S(2)}) copy-start(f32[32,25,1024]{2,1,0:T(8,128)} %copy-done) | copy-start | bytes 9830404
  119.7 21.1 %copy-start.16 = (bf16[1024,1024]{1,0:T(8,128)(2,1)S(1)}, bf16[1024,1024]{1,0:T(8,128)(2,1)}, u32[]{:S(2)}) copy-start(bf16[1024,1024]{1,0:T(8,128)(2,1)} %constant.56.clone.refs_10_) | copy-start | bytes 6291460
  119.8 21.1 %copy-start.17 = (bf16[1024,1024]{1,0:T(8,128)(2,1)S(1)}, bf16[1024,1024]{1,0:T(8,128)(2,1)}, u32[]{:S(2)}) copy-start(bf16[1024,1024]{1,0:T(8,128)(2,1)} %constant.57.clone.refs_11_) | copy-start | bytes 6291460
  128.2 5.2 %copy-start.21 = (f32[1024]{0:T(1024)S(1)}, f32[1024]{0:T(1024)}, u32[]{:S(2)}) copy-start(f32[1024]{0:T(1024)} %constant.73) | copy-start | bytes 12292
  128.2 5.2 %copy-start.24 = (f32[1024]{0:T(1024)S(1)}, f32[1024]{0:T(1024)}, u32[]{:S(2)}) copy-start(f32[1024]{0:T(1024)} %constant.75) | copy-start | bytes 12292
  128.2 12.6 %copy-start.28 = (f32[1024]{0:T(1024)S(1)}, f32[1024]{0:T(1024)}, u32[]{:S(2)}) copy-start(f32[1024]{0:T(1024)} %constant.77) | copy-start | bytes 12292
  128.2 12.6 %copy-start.15 = (f32[32,16,1024]{2,1,0:T(8,128)S(1)}, f32[32,16,1024]{2,1,0:T(8,128)}, u32[]{:S(2)}) copy-start(f32[32,16,1024]{2,1,0:T(8,128)} %copy-done.14) | copy-start | bytes 6291460
  128.3 5.0 %collective-permute-start.12 = (f32[2,16,1024]{2,1,0:T(8,128)S(1)}, f32[2,16,1024]{2,1,0:T(8,128)S(1)}, u32[]{:S(2)}, u32[]{:S(2)}) collective-permute-start(f32[2,16,1024]{2,1,0:T(8,128)S(1)} %pad_maximum_fusion.4), channel_id=1, source_target_pairs={{0,8},{1,9},{2,10},{3,11},{4,12},{5,13},{6,14},{7,15},{8,0},{9,1},... | collective-permute-start | bytes 393224 | tf_op jit(solution)/shard_map/ppermute | solution.py:628
  133.4 7.3 %collective-permute-start.13 = (f32[2,16,1024]{2,1,0:T(8,128)S(1)}, f32[2,16,1024]{2,1,0:T(8,128)S(1)}, u32[]{:S(2)}, u32[]{:S(2)}) collective-permute-start(f32[2,16,1024]{2,1,0:T(8,128)S(1)} %pad_maximum_fusion), channel_id=1, source_target_pairs={{0,16},{1,17},{2,18},{3,19},{4,20},{5,21},{6,22},{7,23},{8,24},{9,... | collective-permute-start | bytes 393224 | tf_op jit(solution)/shard_map/ppermute | solution.py:628
  145.9 9.2 %copy-start.4 = (f32[4,32,16,256]{3,2,1,0:T(8,128)}, f32[4,32,16,256]{3,2,1,0:T(8,128)S(1)}, u32[]{:S(2)}) copy-start(f32[4,32,16,256]{3,2,1,0:T(8,128)S(1)} %row_inverse.1.v_ref) | copy-start | bytes 6291460
  145.9 9.2 %collective-permute-start.16 = (f32[4,2,16,256]{3,2,1,0:T(8,128)S(1)}, f32[4,2,16,256]{3,2,1,0:T(8,128)S(1)}, u32[]{:S(2)}, u32[]{:S(2)}) collective-permute-start(f32[4,2,16,256]{3,2,1,0:T(8,128)S(1)} %get-tuple-element.50), channel_id=1, source_target_pairs={{0,1},{1,2},{2,3},{3,4},{4,5},{5,6},{6,7},{7,8},{8,9},{9,10},{10,1... | collective-permute-start | bytes 393224 | tf_op jit(solution)/shard_map/ppermute | solution.py:597
  151.7 6.9 %collective-permute-start.17 = (f32[4,2,16,256]{3,2,1,0:T(8,128)S(1)}, f32[4,2,16,256]{3,2,1,0:T(8,128)S(1)}, u32[]{:S(2)}, u32[]{:S(2)}) collective-permute-start(f32[4,2,16,256]{3,2,1,0:T(8,128)S(1)} %get-tuple-element.49), channel_id=1, source_target_pairs={{1,0},{2,1},{3,2},{4,3},{5,4},{6,5},{7,6},{8,7},{9,8},{10,9},{11,1... | collective-permute-start | bytes 393224 | tf_op jit(solution)/shard_map/ppermute | solution.py:598
  158.6 45.1 %all-to-all-start.3 = ((f32[4,32,16,256]{3,2,1,0:T(8,128)}), f32[4,32,16,256]{3,2,1,0:T(8,128)}, u32[]{:S(2)}, u32[]{:S(2)}) async-start(f32[4,32,16,256]{3,2,1,0:T(8,128)} %copy-done.4), calls=%async_computation.3 | async-start | bytes 4194304 | tf_op jit(solution)/shard_map/all_to_all | solution.py:640
  163.2 2.2 %copy-start.3 = (f32[32,25,1024]{2,1,0:T(8,128)S(1)}, f32[32,25,1024]{2,1,0:T(8,128)}, u32[]{:S(2)}) copy-start(f32[32,25,1024]{2,1,0:T(8,128)} %copy-done) | copy-start | bytes 9830404
  175.7 1.2 collective-permute-start.18
  176.9 3.8 %collective-permute-start.19 = (f32[48,128]{1,0:T(8,128)S(1)}, f32[48,128]{1,0:T(8,128)S(1)}, u32[]{:S(2)}, u32[]{:S(2)}) collective-permute-start(f32[48,128]{1,0:T(8,128)S(1)} %add.69), channel_id=1, source_target_pairs={{0,8},{1,9},{2,10},{3,11},{4,12},{5,13},{6,14},{7,15},{8,0},{9,1},... | collective-permute-start | bytes 73736 | tf_op jit(solution)/shard_map/ppermute | solution.py:593
  180.7 4.7 %collective-permute-start.20 = (f32[48,128]{1,0:T(8,128)S(1)}, f32[48,128]{1,0:T(8,128)S(1)}, u32[]{:S(2)}, u32[]{:S(2)}) collective-permute-start(f32[48,128]{1,0:T(8,128)S(1)} %add.70), channel_id=1, source_target_pairs={{0,16},{1,17},{2,18},{3,19},{4,20},{5,21},{6,22},{7,23},{8,24},{9,... | collective-permute-start | bytes 73736 | tf_op jit(solution)/shard_map/ppermute | solution.py:593
  185.5 3.8 %collective-permute-start.21 = (f32[48,128]{1,0:T(8,128)S(1)}, f32[48,128]{1,0:T(8,128)S(1)}, u32[]{:S(2)}, u32[]{:S(2)}) collective-permute-start(f32[48,128]{1,0:T(8,128)S(1)} %add.71), channel_id=1, source_target_pairs={{0,1},{1,0},{2,3},{3,2},{4,5},{5,4},{6,7},{7,6},{8,9},{9,8},{10,11... | collective-permute-start | bytes 73736 | tf_op jit(solution)/shard_map/ppermute | solution.py:593
  189.3 3.8 %collective-permute-start.22 = (f32[48,128]{1,0:T(8,128)S(1)}, f32[48,128]{1,0:T(8,128)S(1)}, u32[]{:S(2)}, u32[]{:S(2)}) collective-permute-start(f32[48,128]{1,0:T(8,128)S(1)} %add.72), channel_id=1, source_target_pairs={{0,2},{1,3},{2,0},{3,1},{4,6},{5,7},{6,4},{7,5},{8,10},{9,11},{10,... | collective-permute-start | bytes 73736 | tf_op jit(solution)/shard_map/ppermute | solution.py:593
  (8 other events, 11.9 us)

commit v3 on v2

--- a/solution.py
+++ b/solution.py
@@ -20,6 +20,8 @@
 BOTH = ("row", "col")
 LANES = 128
 UNROLL = 4
+VMEM = pl.BlockSpec(memory_space=pltpu.VMEM)
+SMEM = pl.BlockSpec(memory_space=pltpu.SMEM)
 OFFSETS = [(a, b) for a in range(-2, 3) for b in range(-2, 3)]
 
 
@@ -108,11 +110,149 @@
     return high, middle, (rest - middle.astype(f32)).astype(bf16)
 
 
-def weights_kernel(index_ref, image_ref, w_ref, deg_ref):
+def image_rows(count, fields):
+    return -(-count // fields)
+
+
+def spread(info_ref, chunk_refs, target):
+    width = chunk_refs[0].shape[-1]
+    count = target.shape[0]
+    for d, ref in enumerate(chunk_refs):
+        start = pl.multiple_of(info_ref[1 + d] * width, width)
+        if len(target.shape) == 3:
+            target[:, :, pl.ds(start, width)] = ref[0:count]
+        else:
+            below = ref[ref.shape[0] - image_rows(count, ref.shape[1]) :]
+            target[:, pl.ds(start, width)] = below.reshape(-1, width)[:count]
+
+
+def edges_kernel(x_top, x_bot, p_top, p_bot, i_top, i_bot, head_ref, tail_ref):
+    fields, _, _ = x_top.shape
+    for out_ref, rows, refs in (
+        (head_ref, slice(0, 2), (x_top, p_top, i_top)),
+        (tail_ref, slice(6, 8), (x_bot, p_bot, i_bot)),
+    ):
+        for f in range(fields):
+            out_ref[:, f, :] = refs[0][f, rows, :]
+            out_ref[:, fields + f, :] = refs[1][f, rows, :]
+        out_ref[:, 2 * fields, :] = refs[2][rows, :]
+
+
+def edges(x, p, image):
+    fields, height, width = x.shape
+    bottom = height // 8 - 1
+    top = pl.BlockSpec((fields, 8, width), lambda i: (0, 0, 0))
+    bot = pl.BlockSpec((fields, 8, width), lambda i: (0, bottom, 0))
+    image_top = pl.BlockSpec((8, width), lambda i: (0, 0))
+    image_bot = pl.BlockSpec((8, width), lambda i: (bottom, 0))
+    out = pl.BlockSpec((2, 2 * fields + 1, width), lambda i: (0, 0, 0))
+    return pl.pallas_call(
+        edges_kernel,
+        grid=(1,),
+        out_shape=(room(2, 2 * fields + 1, width),) * 2,
+        in_specs=[top, bot, top, bot, image_top, image_bot],
+        out_specs=(out, out),
+        compiler_params=pltpu.CompilerParams(vmem_limit_bytes=56 * 2**20),
+        cost_estimate=cost(0, 8 * 4 * fields * width * 4),
+        name="edges",
+    )(x, x, p, p, image, image)
+
+
+def pack_kernel(chunks, depth, with_image, info_ref, x_ref, *refs):
+    fields, height, width = x_ref.shape
+    if with_image:
+        image_ref, *pieces = refs
+    else:
+        pieces = refs
+    for d in range(chunks):
+        place = info_ref[1 + chunks + d]
+        start = pl.multiple_of(place * depth, depth)
+        before = pl.multiple_of(jnp.maximum(start - 8, 0), 8)
+        after = pl.multiple_of(jnp.minimum(start + depth, height - 8), 8)
+        piece = pieces[d]
+        for f in range(fields):
+            piece[2 : 2 + depth, f, :] = x_ref[f, pl.ds(start, depth), :]
+            piece[0:2, f, :] = x_ref[f, pl.ds(before, 8), :][6:8]
+            piece[2 + depth : 4 + depth, f, :] = x_ref[f, pl.ds(after, 8), :][0:2]
+        if with_image:
+            rows = jnp.concatenate(
+                [
+                    image_ref[pl.ds(before, 8), :][6:8],
+                    image_ref[pl.ds(start, depth), :],
+                    image_ref[pl.ds(after, 8), :][0:2],
+                ],
+                0,
+            )
+            count = depth + 4
+            for r in range(0, count, fields):
+                size = min(fields, count - r)
+                piece[depth + 4 + r // fields, 0:size, :] = rows[r : r + size]
+            rest = -count % fields
+            if rest:
+                piece[depth + 3 + image_rows(count, fields), fields - rest :, :] = jnp.zeros(
+                    (rest, width), f32
+                )
+
+
+def pack(info, x, image, chunks):
+    fields, height, width = x.shape
+    depth = height // chunks
+    count = depth + 4 + (image_rows(depth + 4, fields) if image is not None else 0)
+    args = (x,) if image is None else (x, image)
+    return pl.pallas_call(
+        functools.partial(pack_kernel, chunks, depth, image is not None),
+        out_shape=(room(count, fields, width),) * chunks,
+        in_specs=[SMEM] + [VMEM] * len(args),
+        out_specs=(VMEM,) * chunks,
+        compiler_params=params(*args, *(room(count, fields, width),) * chunks),
+        cost_estimate=cost(0, 8 * fields * height * width),
+        name="pack",
+    )(info, *args)
+
+
+def fill_kernel(chunks, depth, first, with_image, info_ref, above_ref, below_ref, *refs):
+    pieces = refs[chunks:]
+    fields = pieces[0].shape[1]
+    for d in range(chunks):
+        place = info_ref[1 + chunks + d]
+        piece = pieces[d]
+        for which, rows_ref, row in ((0, above_ref, 0), (chunks - 1, below_ref, depth + 2)):
+
+            @pl.when(place == which)
+            def _(piece=piece, rows_ref=rows_ref, row=row):
+                piece[row : row + 2] = rows_ref[:, first : first + fields, :]
+                if with_image:
+                    for i in range(2):
+                        line = depth + 4 + (row + i) // fields
+                        at = (row + i) % fields
+                        image = rows_ref[i, 2 * fields : 2 * fields + 1, :]
+                        piece[line, at : at + 1, :] = image
+
+
+def fill(info, above, below, pieces, first, with_image):
+    chunks = len(pieces)
+    count, fields, width = pieces[0].shape
+    depth = count - 4
+    if with_image:
+        depth = next(n for n in range(1, count) if n + 4 + image_rows(n + 4, fields) == count)
+    return pl.pallas_call(
+        functools.partial(fill_kernel, chunks, depth, first, with_image),
+        out_shape=(room(count, fields, width),) * chunks,
+        in_specs=[SMEM] + [VMEM] * (2 + chunks),
+        out_specs=(VMEM,) * chunks,
+        input_output_aliases={3 + d: d for d in range(chunks)},
+        compiler_params=params(*pieces),
+        cost_estimate=cost(0, 16 * fields * width),
+        name="fill",
+    )(info, above, below, *pieces)
+
+
+def weights_kernel(chunks, total_rows, info_ref, *rest):
+    chunk_refs, (w_ref, deg_ref, image_ref) = rest[:chunks], rest[chunks:]
     depth, cols = deg_ref.shape
-    total_rows = index_ref[1]
+    spread(info_ref, chunk_refs, image_ref)
     center = image_ref[2 : 2 + depth, :]
-    row = lax.broadcasted_iota(jnp.int32, (depth, cols), 0) + index_ref[0] * depth
+    row = lax.broadcasted_iota(jnp.int32, (depth, cols), 0) + info_ref[0] * depth
     col = lax.broadcasted_iota(jnp.int32, (depth, cols), 1)
     degree = jnp.zeros((depth, cols), f32)
     for b in range(-2, 3):
@@ -136,44 +276,44 @@
     deg_ref[...] = degree
 
 
-def make_weights(strip_index, image, depth, total_rows):
-    cols = image.shape[1]
-    index = jnp.stack([strip_index, jnp.int32(total_rows)]).astype(jnp.int32)
-    return pl.pallas_call(
-        weights_kernel,
-        out_shape=(
-            jax.ShapeDtypeStruct((depth, 25, cols), f32),
-            jax.ShapeDtypeStruct((depth, cols), f32),
-        ),
-        in_specs=[
-            pl.BlockSpec(memory_space=pltpu.SMEM),
-            pl.BlockSpec(memory_space=pltpu.VMEM),
-        ],
-        out_specs=(pl.BlockSpec(memory_space=pltpu.VMEM),) * 2,
-        compiler_params=params(image, room(depth, 25, cols), extra=16 * 2**20),
+def make_weights(info, pieces, depth, total_rows):
+    cols = pieces[0].shape[2] * len(pieces)
+    return pl.pallas_call(
+        functools.partial(weights_kernel, len(pieces), total_rows),
+        out_shape=(room(depth, 25, cols), room(depth, cols)),
+        in_specs=[SMEM] + [VMEM] * len(pieces),
+        out_specs=(VMEM,) * 2,
+        scratch_shapes=[pltpu.VMEM((depth + 4, cols), f32)],
+        compiler_params=params(*pieces, room(depth, 25, cols), extra=16 * 2**20),
         cost_estimate=cost(60 * depth * cols * 25, 25 * depth * cols * 4),
         name="weights",
-    )(index, image)
-
-
-def graph_kernel(order, keep, lane_shift, v_ref, top_ref, bot_ref, w_ref, deg_ref, *rest):
-    others, rest = rest[: len(order) - 1], rest[len(order) - 1 :]
-    if keep:
-        g_ref, gram_ref, pad_ref, acc_ref, sum_ref = rest
+    )(info, *pieces)
+
+
+def graph_kernel(order, keep, lane_shift, chunks, *refs):
+    if chunks:
+        info_ref, chunk_refs, refs = refs[0], refs[1 : 1 + chunks], refs[1 + chunks :]
     else:
-        gram_ref, pad_ref, acc_ref, sum_ref = rest
-    chunks, depth, fields, width = v_ref.shape
-    cols = chunks * width
-    for c in range(chunks):
-        lanes = slice(c * width, (c + 1) * width)
-        pad_ref[0:2, :, lanes] = top_ref[c]
-        pad_ref[2 : 2 + depth, :, lanes] = v_ref[c]
-        pad_ref[2 + depth : 4 + depth, :, lanes] = bot_ref[c]
+        v_ref, top_ref, bot_ref, *refs = refs
+    (w_ref, deg_ref), refs = refs[:2], refs[2:]
+    others, refs = refs[: len(order) - 1], list(refs[len(order) - 1 :])
+    g_ref = refs.pop(0) if keep else None
+    own_ref = refs.pop(0) if chunks else None
+    gram_ref, pad_ref, acc_ref, sum_ref = refs
+    depth, cols = deg_ref.shape
+    fields = pad_ref.shape[1]
+    if chunks:
+        spread(info_ref, chunk_refs, pad_ref)
+    else:
+        pad_ref[0:2] = top_ref[...]
+        pad_ref[2 : 2 + depth] = v_ref[...]
+        pad_ref[2 + depth : 4 + depth] = bot_ref[...]
     parts = len(order)
     groups = fields // 8
+    width = 256
 
     def one_row(r, acc):
-        for c in range(chunks):
+        for c in range(cols // width):
             lanes = slice(c * width, (c + 1) * width)
             values = [pad_ref[r + a, :, lanes].reshape(groups, 8, width) for a in range(5)]
             for b in range(-2, 3):
@@ -182,8 +322,7 @@
                     value = values[a + 2]
                     if a or b:
                         o = OFFSETS.index((a, b))
-                        weight = w_ref[r, o : o + 1, lanes]
-                        value = weight[None] * value
+                        value = w_ref[r, o : o + 1, lanes][None] * value
                     total = value if total is None else total + value
                 sum_ref[b + 2, :, lanes] = total.reshape(fields, width)
         result = sum_ref[2]
@@ -192,15 +331,16 @@
         if keep:
             g_ref[r] = result
         own = pad_ref[r + 2]
+        if chunks:
+            own_ref[r] = own
         weighted = deg_ref[pl.ds(r, 1), :] * own
         left, position = [], 0
         for which in order:
             if which == "v":
                 left.append(split(own))
             else:
-                ref = others[position]
+                left.append(split(others[position][r]))
                 position += 1
-                left.append(split(jnp.concatenate([ref[c, r] for c in range(chunks)], 1)))
         left = jnp.concatenate([p[0] for p in left] + [p[1] for p in left], 0)
         graph_pair, degree_pair = split(result), split(weighted)
         right = jnp.concatenate(
@@ -224,47 +364,45 @@
     gram_ref[...] = both
 
 
-def apply_graph(order, keep, lane_shift, v, top, bot, w, deg, *others):
-    chunks, depth, fields, width = v.shape
-    cols = chunks * width
+def apply_graph(order, keep, lane_shift, fields_in, w, deg, *others, info=None):
+    depth, cols = deg.shape
+    fields = fields_in[0].shape[1]
     parts = len(order)
-    out_shape = (jax.ShapeDtypeStruct((parts * fields, LANES), f32),)
-    if keep:
-        out_shape = (jax.ShapeDtypeStruct((depth, fields, cols), f32),) + out_shape
-    return pl.pallas_call(
-        functools.partial(graph_kernel, order, keep, lane_shift),
-        out_shape=out_shape,
-        in_specs=[pl.BlockSpec(memory_space=pltpu.VMEM)] * (5 + len(others)),
-        out_specs=(pl.BlockSpec(memory_space=pltpu.VMEM),) * len(out_shape),
+    chunks = len(fields_in) if info is not None else 0
+    out_shape = [room(depth, fields, cols)] * (int(keep) + int(chunks > 0))
+    out_shape += [room(parts * fields, LANES)]
+    args = ((info,) if chunks else ()) + tuple(fields_in) + (w, deg) + others
+    return pl.pallas_call(
+        functools.partial(graph_kernel, order, keep, lane_shift, chunks),
+        out_shape=tuple(out_shape),
+        in_specs=[SMEM] * int(chunks > 0) + [VMEM] * (len(args) - int(chunks > 0)),
+        out_specs=(VMEM,) * len(out_shape),
         scratch_shapes=[
             pltpu.VMEM((depth + 4, fields, cols), f32),
             pltpu.VMEM((parts * fields, LANES), f32),
             pltpu.VMEM((5, fields, cols), f32),
         ],
-        compiler_params=params(v, w, deg, *others, room(2 * depth + 10, fields, cols)),
+        compiler_params=params(w, deg, *fields_in, *others, *out_shape, room(depth + 9, fields, cols)),
         cost_estimate=cost(50 * fields * depth * cols * 4, 4 * cols * depth * (25 + 3 * fields)),
         name="graph_" + "".join(order),
-    )(v, top, bot, w, deg, *others)
+    )(*args)
 
 
 def forward_kernel(scaled, x_ref, *rest):
     if scaled:
         deg_ref, high_ref, low_ref, out_ref = rest
-        chunks, depth, fields, width = x_ref.shape
     else:
         high_ref, low_ref, out_ref = rest
-        depth, fields, _ = x_ref.shape
+    depth, fields, _ = x_ref.shape
     cols = high_ref.shape[0]
     block = math.gcd(depth, 16)
     contract = (((1,), (0,)), ((), ()))
 
     def one_block(i, _):
         start = i * block
+        value = x_ref[pl.ds(start, block)]
         if scaled:
-            value = jnp.concatenate([x_ref[c, pl.ds(start, block)] for c in range(chunks)], 2)
             value = value * deg_ref[pl.ds(start, block), :][:, None, :]
-        else:
-            value = x_ref[pl.ds(start, block)]
         high, low = split(value.reshape(block * fields, cols))
         result = lax.dot_general(high, high_ref[...], contract, preferred_element_type=f32)
         result += lax.dot_general(high, low_ref[...], contract, preferred_element_type=f32)
@@ -342,17 +480,45 @@
     )(gram, fg, fd, eps, last)
 
 
-def inverse_kernel(levels, *refs):
+def merge_kernel(level, last, info_ref, mine_ref, theirs_ref, gain_ref, cross_ref, g_ref, *ends_ref):
+    right = ((info_ref[0] >> level) & 1) == 1
+    mine, theirs = mine_ref[...], theirs_ref[...]
+    lower = jnp.where(right, theirs, mine)
+    upper = jnp.where(right, mine, theirs)
+    g = (lower[1] - upper[0]) * gain_ref[level : level + 1, :]
+    g_ref[...] = g
+    if not last:
+        moved = g * cross_ref[level : level + 1, :]
+        ends_ref[0][0] = lower[0] - moved
+        ends_ref[0][1] = upper[1] + moved
+
+
+def merge(level, last, info, mine, theirs, gain, cross):
+    _, fields, cols = mine.shape
+    out_shape = (room(fields, cols),) + (() if last else (room(2, fields, cols),))
+    return pl.pallas_call(
+        functools.partial(merge_kernel, level, last),
+        out_shape=out_shape,
+        in_specs=[SMEM] + [VMEM] * 4,
+        out_specs=(VMEM,) * len(out_shape),
+        compiler_params=params(),
+        cost_estimate=cost(10 * fields * cols, 28 * fields * cols),
+        name="merge",
+    )(info, mine, theirs, gain, cross)
+
+
+def inverse_kernel(levels, chunks, info_ref, *refs):
     g_refs = refs[:levels]
-    f_ref, top_ref, bot_ref, eps_ref, last_ref, high_ref, low_ref, out_ref, u_ref = refs[levels:]
+    f_ref, flux_ref, eps_ref, last_ref, high_ref, low_ref = refs[levels : levels + 6]
+    out_ref, head_ref, tail_ref, *piece_refs, u_ref = refs[levels + 6 :]
     depth, fields, cols = f_ref.shape
-    chunks, _, _, width = out_ref.shape
+    width = cols // chunks
     flux_top = jnp.zeros((fields, cols), f32)
     flux_bot = jnp.zeros((fields, cols), f32)
     for level in range(levels):
         g = g_refs[level][...]
-        flux_top = flux_top + g * top_ref[level : level + 1, :]
-        flux_bot = flux_bot - g * bot_ref[level : level + 1, :]
+        flux_top = flux_top + g * flux_ref[level : level + 1, :]
+        flux_bot = flux_bot - g * flux_ref[levels + level : levels + level + 1, :]
 
     u_ref[0] = f_ref[0] + flux_top
 
@@ -383,26 +549,31 @@
         result = jnp.dot(high, high_ref[...], preferred_element_type=f32)
         result += jnp.dot(high, low_ref[...], preferred_element_type=f32)
         result += jnp.dot(low, high_ref[...], preferred_element_type=f32)
-        result = result.reshape(block, fields, cols)
-        for c in range(chunks):
-            out_ref[c, pl.ds(start, block)] = result[:, :, c * width : (c + 1) * width]
+        out_ref[pl.ds(start, block)] = result.reshape(block, fields, cols)
+        for d in range(chunks):
+            lane = pl.multiple_of(info_ref[1 + d] * width, width)
+            piece_refs[d][pl.ds(start, block)] = out_ref[pl.ds(start, block), :, pl.ds(lane, width)]
         return 0
 
     lax.fori_loop(0, depth // block, one_block, 0)
-
-
-def row_inverse(gs, f, top, bot, eps, last, high, low, chunks):
+    head_ref[...] = out_ref[0:2]
+    tail_ref[...] = out_ref[depth - 2 : depth]
+
+
+def row_inverse(info, gs, f, flux, eps, last, high, low, chunks):
     depth, fields, cols = f.shape
-    return pl.pallas_call(
-        functools.partial(inverse_kernel, len(gs)),
-        out_shape=jax.ShapeDtypeStruct((chunks, depth, fields, cols // chunks), f32),
-        in_specs=[pl.BlockSpec(memory_space=pltpu.VMEM)] * (len(gs) + 7),
-        out_specs=pl.BlockSpec(memory_space=pltpu.VMEM),
+    out_shape = (room(depth, fields, cols),) + (room(2, fields, cols),) * 2
+    out_shape += (room(depth, fields, cols // chunks),) * chunks
+    return pl.pallas_call(
+        functools.partial(inverse_kernel, len(gs), chunks),
+        out_shape=out_shape,
+        in_specs=[SMEM] + [VMEM] * (len(gs) + 6),
+        out_specs=(VMEM,) * len(out_shape),
         scratch_shapes=[pltpu.VMEM((depth, fields, cols), f32)],
-        compiler_params=params(*gs, f, high, low, room(2 * depth, fields, cols), extra=12 * 2**20),
+        compiler_params=params(*gs, f, high, low, *out_shape, f, extra=12 * 2**20),
         cost_estimate=cost(6 * depth * fields * cols * cols, 4 * cols * (2 * depth * fields + cols)),
         name="row_inverse",
-    )(*gs, f, top, bot, eps, last, high, low)
+    )(info, *gs, f, flux, eps, last, high, low)
 
 
 def hdot(a, b, contract):
@@ -500,7 +671,8 @@
     )(first, second)
 
 
-def combine_kernel(tiles, coeff_ref, x_ref, h_ref, p_ref, block_ref, direction_ref, high_ref, low_ref):
+def combine_kernel(chunks, info_ref, coeff_ref, x_ref, p_ref, *refs):
+    pieces, (block_ref, direction_ref, h_ref, high_ref, low_ref) = refs[:chunks], refs[chunks:]
     fields = x_ref.shape[0]
     width = x_ref.shape[2]
     group = 8 * fields
@@ -526,8 +698,14 @@
             lanes = slice(part * group, (part + 1) * group)
             high_ref[:, lanes], low_ref[:, lanes] = split(wide)
 
+    for d in range(chunks):
+
+        @pl.when(pl.program_id(0) == d)
+        def _(d=d):
+            h_ref[...] = pieces[d][...]
+
     dot = functools.partial(jnp.dot, preferred_element_type=f32)
-    for t in range(tiles):
+    for t in range(x_ref.shape[1] // 8):
         rows = slice(8 * t, 8 * t + 8)
         x = split(x_ref[:, rows, :].reshape(group, width))
         h = split(h_ref[rows].reshape(group, width))
@@ -542,109 +720,117 @@
         direction_ref[:, rows, :] = direction.reshape(fields, 8, width)
 
 
-def combine(coeffs, x, h, p):
+def combine(info, coeffs, x, p, pieces):
     fields, rows, width = x.shape
-    tile = 32
-    spec = pl.BlockSpec((fields, tile, width), lambda i: (0, i, 0))
-    h_spec = pl.BlockSpec((tile, fields, width), lambda i: (i, 0, 0))
-    return pl.pallas_call(
-        functools.partial(combine_kernel, tile // 8),
-        grid=(rows // tile,),
-        out_shape=(jax.ShapeDtypeStruct((fields, rows, width), f32),) * 2,
-        in_specs=[pl.BlockSpec(coeffs.shape, lambda i: (0, 0)), spec, h_spec, spec],
-        out_specs=(spec, spec),
-        scratch_shapes=[pltpu.VMEM((8 * fields, 24 * fields), bf16)] * 2,
-        compiler_params=params(room(12 * tile, fields, width)),
+    chunks = len(pieces)
+    depth = rows // chunks
+    spec = pl.BlockSpec((fields, depth, width), lambda i, s: (0, s[1 + chunks + i], 0))
+    whole = pl.BlockSpec((depth, fields, width), lambda i, s: (0, 0, 0))
+    return pl.pallas_call(
+        functools.partial(combine_kernel, chunks),
+        out_shape=(room(fields, rows, width),) * 2,
+        grid_spec=pltpu.PrefetchScalarGridSpec(
+            num_scalar_prefetch=1,
+            grid=(chunks,),
+            in_specs=[pl.BlockSpec(coeffs.shape, lambda i, s: (0, 0)), spec, spec] + [whole] * chunks,
+            out_specs=(spec, spec),
+            scratch_shapes=[pltpu.VMEM((depth, fields, width), f32)]
+            + [pltpu.VMEM((8 * fields, 24 * fields), bf16)] * 2,
+        ),
+        compiler_params=params(room(16 * depth, fields, width)),
         cost_estimate=cost(200 * rows * fields * width, 20 * rows * fields * width),
         name="combine",
-    )(coeffs, x, h, p)
-
-
-def shifted(block, strips):
-    down = [(i, i + 1) for i in range(strips - 1)]
-    up = [(i + 1, i) for i in range(strips - 1)]
-    return down, up
+    )(info, coeffs, x, p, *pieces)
+
+
+def ring_order(count):
+    half = count // 2
+    return [*range(half), *reversed(range(half, count))] if count > 1 else [0]
+
+
+@functools.lru_cache(None)
+def device_table(strips, chunks):
+    order = ring_order(chunks)
+    place = [order.index(c) for c in range(chunks)]
+    table = []
+    for device in range(strips):
+        row, col = divmod(device, chunks)
+        others = [col ^ d for d in range(chunks)]
+        table.append([row * chunks + place[col], *others, *[place[c] for c in others]])
+    return np.asarray(table, np.int32)
 
 
 def local(intensity, start_block, old_direction):
     fields, height, width = start_block.shape
     chunks = lax.axis_size("col")
-    strips = lax.axis_size("row") * chunks
+    row_count = lax.axis_size("row")
+    strips = row_count * chunks
     depth = height // chunks
     rows, cols = strips * depth, chunks * width
-    strip = lax.axis_index("row") * chunks + lax.axis_index("col")
-    down, up = shifted(None, strips)
+    device = lax.axis_index("row") * chunks + lax.axis_index("col")
     levels = strips.bit_length() - 1
-
-    eps, last, gain, cross, top_all, bot_all = (
-        jnp.asarray(t) for t in row_tables(strips, depth, cols)
-    )
+    order = ring_order(chunks)
+    owner = [(s // chunks) * chunks + order[s % chunks] for s in range(strips)]
+
+    table = device_table(strips, chunks)
+    eps, last, gain, cross, top_all, bot_all = row_tables(strips, depth, cols)
+    by_device = np.concatenate([top_all[table[:, 0]], bot_all[table[:, 0]]], 1)
     high, low = (jnp.asarray(t) for t in cosine_tables(cols))
     high_t, low_t = (jnp.asarray(t.T.copy()) for t in cosine_tables(cols))
-    top_mine = lax.dynamic_index_in_dim(top_all, strip, 0, False)
-    bot_mine = lax.dynamic_index_in_dim(bot_all, strip, 0, False)
-
-    def to_strips(block):
-        return lax.all_to_all(block, "col", 0, 0)
-
-    def total(value):
+    eps, last, gain, cross = (jnp.asarray(t) for t in (eps, last, gain, cross))
+    info = lax.dynamic_index_in_dim(jnp.asarray(table), device, 0, False)
+    flux = lax.dynamic_index_in_dim(jnp.asarray(by_device), device, 0, False)
+
+    def total(value, tied=()):
         first = chunks.bit_length() - 1
         for level in [*range(first, levels), *range(first)]:
+            if level == 0:
+                value, tied = lax.optimization_barrier((value, tied))
             value = value + lax.ppermute(value, BOTH, [(i, i ^ (1 << level)) for i in range(strips)])
-        return value
-
-    def halo(block):
-        above = lax.ppermute(block[:, depth - 2 :], BOTH, down)
-        below = lax.ppermute(block[:, :2], BOTH, up)
-        return above, below
-
-    x_rows = jnp.transpose(start_block.reshape(fields, chunks, depth, width), (1, 2, 0, 3))
-    p_rows = jnp.transpose(old_direction.reshape(fields, chunks, depth, width), (1, 2, 0, 3))
-    image = to_strips(intensity.reshape(chunks, depth, width))
-    x_strip = to_strips(x_rows)
-
-    image = jnp.transpose(image, (1, 0, 2)).reshape(depth, cols)
-    image = jnp.concatenate(
-        [lax.ppermute(image[-2:], BOTH, down), image, lax.ppermute(image[:2], BOTH, up)], 0
-    )
-    w, deg = make_weights(strip, image, depth, rows)
-
-    x_strip, w, p_rows = lax.optimization_barrier((x_strip, w, p_rows))
-    x_halo = halo(x_strip)
-    p_rows, x_halo = lax.optimization_barrier((p_rows, x_halo))
-    p_strip = to_strips(p_rows)
-    graph_x, gram_x = apply_graph(("v",), True, 4 * fields, x_strip, *x_halo, w, deg)
-    gram_x = total(gram_x)
+        return value, tied
+
+    def exchange(pieces):
+        return [pieces[0]] + [
+            lax.ppermute(pieces[d], "col", [(c, c ^ d) for c in range(chunks)])
+            for d in range(1, chunks)
+        ]
+
+    head, tail = edges(start_block, old_direction, intensity)
+    above = lax.ppermute(tail, "row", [(i, i + 1) for i in range(row_count - 1)])
+    below = lax.ppermute(head, "row", [(i + 1, i) for i in range(row_count - 1)])
+    x_pieces = pack(info, start_block, intensity, chunks)
+    x_pieces = exchange(fill(info, above, below, x_pieces, 0, True))
+    p_pieces = pack(info, old_direction, None, chunks)
+    p_pieces = exchange(fill(info, above, below, p_pieces, fields, False))
+    x_pieces, flux = lax.optimization_barrier((x_pieces, flux))
+    w, deg = make_weights(info, x_pieces, depth, rows)
+    graph_x, x, gram_x = apply_graph(("v",), True, 4 * fields, x_pieces, w, deg, info=info)
+    gram_x, p_pieces = total(gram_x, p_pieces)
     spectrum_g = cosine_forward(graph_x, None, high_t, low_t, depth, fields)
-    spectrum_d = cosine_forward(x_strip, deg, high_t, low_t, depth, fields)
-    gram_x, p_strip = lax.optimization_barrier((gram_x, p_strip))
+    spectrum_d = cosine_forward(x, deg, high_t, low_t, depth, fields)
     f, ends = row_solve(gram_x, spectrum_g, spectrum_d, eps, last)
-    (gram_p,) = apply_graph(
-        ("x", "v"), False, 2 * fields, p_strip, *halo(p_strip), w, deg, x_strip
-    )
 
     gs = []
     for level in range(levels):
         theirs = lax.ppermute(ends, BOTH, [(i, i ^ (1 << level)) for i in range(strips)])
-        right = ((strip >> level) & 1) == 1
-        lower = jnp.where(right, theirs, ends)
-        upper = jnp.where(right, ends, theirs)
-        g = (lower[1] - upper[0]) * gain[level]
+        g, *ends = merge(level, level == levels - 1, info, ends, theirs, gain, cross)
+        ends = ends[0] if ends else None
         gs.append(g)
-        ends = jnp.stack([lower[0] - g * cross[level], upper[1] + g * cross[level]])
-
-    gs[-1], gram_p = lax.optimization_barrier((gs[-1], gram_p))
-    h_strip = row_inverse(gs, f, top_mine, bot_mine, eps, last, high, low, chunks)
-    h_halo = halo(h_strip)
-    h_send, h_halo = lax.optimization_barrier((h_strip, h_halo))
-    h_block = lax.all_to_all(h_send, "col", 0, 0).reshape(height, fields, width)
-    (gram_h,) = apply_graph(
-        ("x", "v", "p"), False, 0, h_strip, *h_halo, w, deg, x_strip, p_strip
+
+    h, head, tail, *h_pieces = row_inverse(info, gs, f, flux, eps, last, high, low, chunks)
+    h_above = lax.ppermute(tail, BOTH, [(owner[s], owner[s + 1]) for s in range(strips - 1)])
+    h_below = lax.ppermute(head, BOTH, [(owner[s + 1], owner[s]) for s in range(strips - 1)])
+    p_pieces, h = lax.optimization_barrier((p_pieces, h))
+    p, gram_p = apply_graph(("x", "v"), False, 2 * fields, p_pieces, w, deg, x, info=info)
+    h_pieces, h_above, h_below, gram_p = lax.optimization_barrier(
+        (h_pieces, h_above, h_below, gram_p)
     )
+    h_pieces = exchange(h_pieces)
+    (gram_h,) = apply_graph(("x", "v", "p"), False, 0, (h, h_above, h_below), w, deg, x, p)
     zero = jnp.zeros((fields, LANES), f32)
     gram = gram_h + jnp.concatenate([gram_p[:fields], zero, gram_p[fields:]], 0)
-    ritz, coeffs = ritz_step(gram_x, total(gram), fields, rows * cols)
-    new_block, new_direction = combine(coeffs, start_block, h_block, old_direction)
+    ritz, coeffs = ritz_step(gram_x, total(gram)[0], fields, rows * cols)
+    new_block, new_direction = combine(info, coeffs, start_block, old_direction, h_pieces)
     return new_block, new_direction, ritz[:, 0]
 
 

time: 214 us -> 176 us (0.82)
  local copies, waits for them, and re-layouts: 32.1 us -> 2.32 us
  starting transfers between devices: 59.2 us -> 47.4 us
  Pallas kernels: 58.3 us -> 65.9 us
    unnamed x60 -> x22, local copies, waits for them, and re-layouts: 28.8 us -> 0.06 us
    all_to_all x4 -> x0, starting transfers between devices: 17.7 us -> none  [the longest x3 13.3 us: to_strips(): return lax.all_to_all(block, 'col', 0, 0)]
    ppermute x8 -> x13, waiting for transfers between devices: 29 us -> 20.7 us  [the longest x9 19 us: exchange(): lax.ppermute(pieces[d], 'col', [(c, c ^ d) for c in range(chunks)])]
    pallas_call x6 -> x16, Pallas kernels: 37.4 us -> 45.1 us  [the longest x3 21.5 us: apply_graph(): pl.pallas_call(functools.partial(graph_kernel, order, keep, lane_shift, c...]
    ppermute x5, waiting for transfers between devices: 13.1 us -> 20.2 us  [local(): lax.ppermute(ends, BOTH, [(i, i ^ 1 << level) for i in range(strips)])]
    ppermute x5, starting transfers between devices: 6.57 us -> 9.56 us  [local(): lax.ppermute(ends, BOTH, [(i, i ^ 1 << level) for i in range(strips)])]
    ppermute x10, starting transfers between devices: 13.7 us -> 16 us  [total(): lax.ppermute(value, BOTH, [(i, i ^ 1 << level) for i in range(strips)])]
    ppermute x8 -> x13, starting transfers between devices: 21.2 us -> 21.8 us  [the longest x9 13.3 us: exchange(): lax.ppermute(pieces[d], 'col', [(c, c ^ d) for c in range(chunks)])]
  transfers between devices with their start and end apart: 27 -> 28, of which waited for: 19 -> 17; matrix products, arithmetic and copies ran while one was open for 6% -> 1% of each run, Pallas kernels for 21% -> 26%
where the time goes in v3:
time: 176 us
  Pallas kernels  65.9 us (37%)
  waiting for transfers between devices  59 us (34%)
  starting transfers between devices  47.4 us (27%)
  local copies, waits for them, and re-layouts  2.32 us (1%)
    pallas_call x3, Pallas kernels, apply_graph(): pl.pallas_call(functools.partial(graph_kernel, order, keep, lane_shift, c...  21.5 us
    ppermute x5, waiting for transfers between devices, local(): lax.ppermute(ends, BOTH, [(i, i ^ 1 << level) for i in range(strips)])  20.2 us
    ppermute x9, waiting for transfers between devices, exchange(): lax.ppermute(pieces[d], 'col', [(c, c ^ d) for c in range(chunks)])  19 us
    ppermute x10, waiting for transfers between devices, total(): lax.ppermute(value, BOTH, [(i, i ^ 1 << level) for i in range(strips)])  18 us
    ppermute x10, starting transfers between devices, total(): lax.ppermute(value, BOTH, [(i, i ^ 1 << level) for i in range(strips)])  16 us
    ppermute x9, starting transfers between devices, exchange(): lax.ppermute(pieces[d], 'col', [(c, c ^ d) for c in range(chunks)])  13.3 us
    pallas_call x1, Pallas kernels, ritz_step(): pl.pallas_call(functools.partial(ritz_kernel, fields, pixel_total), out_s...  9.91 us
    ppermute x5, starting transfers between devices, local(): lax.ppermute(ends, BOTH, [(i, i ^ 1 << level) for i in range(strips)])  9.56 us
  transfers between devices with their start and end apart: 28, of which 17 were waited for; matrix products, arithmetic and copies ran while one was open for 1% of the time, Pallas kernels for 26%

profile of v3, /device:TPU:0, one launch (start us, length us, event | category | flops | bytes accessed | tf_op | source)
XLA Modules:
  0.0 175.8 jit_solution(10549816533366116390)
XLA Ops:
  0.6 2.0 %edges.1 = (f32[2,33,256]{2,1,0:T(8,128)}, f32[2,33,256]{2,1,0:T(8,128)}) custom-call(f32[16,128,256]{2,1,0:T(8,128)} %x_ref.5, f32[16,128,256]{2,1,0:T(8,128)} %x_ref.5, f32[16,128,256]{2,1,0:T(8,128)} %p_ref.1, f32[16,128,256]{2,1,0:T(8,128)} %p_ref.1, f32[128,256]{1,0:T(8,128)} %refs_0_.1, f32[128,256]{1,0:T(8,128)} %refs_0_.1), custom_call_target="tpu_custom_call" | custom-call | bytes 524288 | tf_op jit(solution)/shard_map/edges/pallas_call | solution.py:149
  2.6 2.3 %collective-permute-start = (f32[2,33,256]{2,1,0:T(8,128)}, f32[2,33,256]{2,1,0:T(8,128)S(1)}, u32[]{:S(2)}, u32[]{:S(2)}) collective-permute-start(f32[2,33,256]{2,1,0:T(8,128)} %get-tuple-element.71), channel_id=1, source_target_pairs={{0,4},{4,8},{8,12},{12,16},{16,20},{20,24},{24,28},{1,5},{5,9},{9,... | collective-permute-start | bytes 202760 | tf_op jit(solution)/shard_map/ppermute | solution.py:799
  5.0 1.3 collective-permute-start.1
  7.0 1.8 %pack.2 = (f32[39,16,256]{2,1,0:T(8,128)S(1)}, f32[39,16,256]{2,1,0:T(8,128)S(1)}, f32[39,16,256]{2,1,0:T(8,128)S(1)}, f32[39,16,256]{2,1,0:T(8,128)S(1)}) custom-call(s32[9]{0:T(128)S(1)} %dynamic-slice_bitcast_fusion.1.info_ref.refs_0_, f32[16,128,256]{2,1,0:T(8,128)S(1)} %copy-done, f32[128,256]{1,0:T(8,128)S(1)} %copy-done.2), custom_call_target="tpu_custom_call" | custom-call | bytes 4194304 | tf_op jit(solution)/shard_map/pack/pallas_call | solution.py:202
  8.8 1.7 collective-permute-done.1.below_ref
  11.1 1.6 collective-permute-start.2
  12.7 1.5 collective-permute-start.3
  14.7 1.8 %pack.3 = (f32[36,16,256]{2,1,0:T(8,128)S(1)}, f32[36,16,256]{2,1,0:T(8,128)S(1)}, f32[36,16,256]{2,1,0:T(8,128)S(1)}, f32[36,16,256]{2,1,0:T(8,128)S(1)}) custom-call(s32[9]{0:T(128)S(1)} %dynamic-slice_bitcast_fusion.1.info_ref.refs_0_, f32[16,128,256]{2,1,0:T(8,128)S(1)} %copy-done.1), custom_call_target="tpu_custom_call" | custom-call | bytes 4194304 | tf_op jit(solution)/shard_map/pack/pallas_call | solution.py:202
  17.1 1.6 collective-permute-start.8
  18.7 1.5 collective-permute-start.9
  20.2 6.1 %collective-permute-done.2.rest_1_.refs_2_ = f32[39,16,256]{2,1,0:T(8,128)S(1)} collective-permute-done((f32[39,16,256]{2,1,0:T(8,128)S(1)}, f32[39,16,256]{2,1,0:T(8,128)S(1)}, u32[]{:S(2)}, u32[]{:S(2)}) %collective-permute-start.2) | collective-permute-done | bytes 639008 | tf_op jit(solution)/shard_map/ppermute | solution.py:794
  26.3 2.4 %collective-permute-start.10 = (f32[36,16,256]{2,1,0:T(8,128)S(1)}, f32[36,16,256]{2,1,0:T(8,128)S(1)}, u32[]{:S(2)}, u32[]{:S(2)}) collective-permute-start(f32[36,16,256]{2,1,0:T(8,128)S(1)} %get-tuple-element.95), channel_id=1, source_target_pairs={{0,3},{1,2},{2,1},{3,0},{4,7},{5,6},{6,5},{7,4},{8,11},{9,10},{10,... | collective-permute-start | bytes 1769480 | tf_op jit(solution)/shard_map/ppermute | solution.py:794
  29.6 11.5 %collective-permute-done.4.rest_3_.refs_4_ = f32[39,16,256]{2,1,0:T(8,128)S(1)} collective-permute-done((f32[39,16,256]{2,1,0:T(8,128)S(1)}, f32[39,16,256]{2,1,0:T(8,128)S(1)}, u32[]{:S(2)}, u32[]{:S(2)}) %collective-permute-start.4) | collective-permute-done | bytes 639008 | tf_op jit(solution)/shard_map/ppermute | solution.py:794
  41.0 3.1 %weights.1 = (f32[32,25,1024]{2,1,0:T(8,128)S(1)}, f32[32,1024]{1,0:T(8,128)S(1)}) custom-call(s32[9]{0:T(128)S(1)} %dynamic-slice_bitcast_fusion.1.info_ref.refs_0_, f32[39,16,256]{2,1,0:T(8,128)S(1)} %get-tuple-element.81.rest_0_.refs_1_, f32[39,16,256]{2,1,0:T(8,128)S(1)} %collective-permute-done.2.rest_1_.refs_2_, ...), custom_call_target="tpu_custom_call" | custom-call | flops 49152000 | bytes 3276800 | tf_op jit(solution)/shard_map/weights/pallas_call | solution.py:281
  44.1 7.1 %graph_v.1 = (f32[32,16,1024]{2,1,0:T(8,128)S(1)}, f32[32,16,1024]{2,1,0:T(8,128)S(1)}, f32[16,128]{1,0:T(8,128)S(1)}) custom-call(s32[9]{0:T(128)S(1)} %dynamic-slice_bitcast_fusion.1.info_ref.refs_0_, f32[39,16,256]{2,1,0:T(8,128)S(1)} %get-tuple-element.81.rest_0_.refs_1_, f32[39,16,256]{2,1,0:T(8,128)S(1)} %collective-permute-done.2.rest_1_.refs_2_, ...), custom_call_target="tpu_custom_call" | custom-call | flops 104857600 | bytes 9568256 | tf_op jit(solution)/shard_map/graph_v/pallas_call | solution.py:375
  51.2 4.6 %collective-permute-start.5 = (f32[16,128]{1,0:T(8,128)S(1)}, f32[16,128]{1,0:T(8,128)S(1)}, u32[]{:S(2)}, u32[]{:S(2)}) collective-permute-start(f32[16,128]{1,0:T(8,128)S(1)} %get-tuple-element.87), channel_id=1, source_target_pairs={{0,4},{1,5},{2,6},{3,7},{4,0},{5,1},{6,2},{7,3},{8,12},{9,13},{10,... | collective-permute-start | bytes 24584 | tf_op jit(solution)/shard_map/ppermute | solution.py:789
  56.7 1.5 collective-permute-start.6
  58.2 2.1 %collective-permute-done.6 = f32[16,128]{1,0:T(8,128)S(1)} collective-permute-done((f32[16,128]{1,0:T(8,128)S(1)}, f32[16,128]{1,0:T(8,128)S(1)}, u32[]{:S(2)}, u32[]{:S(2)}) %collective-permute-start.6) | collective-permute-done | bytes 8224 | tf_op jit(solution)/shard_map/ppermute | solution.py:789
  60.4 2.5 %collective-permute-start.7 = (f32[16,128]{1,0:T(8,128)S(1)}, f32[16,128]{1,0:T(8,128)S(1)}, u32[]{:S(2)}, u32[]{:S(2)}) collective-permute-start(f32[16,128]{1,0:T(8,128)S(1)} %add.45), channel_id=1, source_target_pairs={{0,16},{1,17},{2,18},{3,19},{4,20},{5,21},{6,22},{7,23},{8,24},{9,... | collective-permute-start | bytes 24584 | tf_op jit(solution)/shard_map/ppermute | solution.py:789
  62.9 2.0 %collective-permute-done.7 = f32[16,128]{1,0:T(8,128)S(1)} collective-permute-done((f32[16,128]{1,0:T(8,128)S(1)}, f32[16,128]{1,0:T(8,128)S(1)}, u32[]{:S(2)}, u32[]{:S(2)}) %collective-permute-start.7) | collective-permute-done | bytes 8224 | tf_op jit(solution)/shard_map/ppermute | solution.py:789
  64.9 1.4 collective-permute-done.10.refs_4_
  66.4 1.4 collective-permute-start.11
  67.8 3.6 %cosine_forward.2.fg_ref = f32[32,16,1024]{2,1,0:T(8,128)S(1)} custom-call(f32[32,16,1024]{2,1,0:T(8,128)S(1)} %get-tuple-element.101.x_ref, bf16[1024,1024]{1,0:T(8,128)(2,1)S(1)} %copy-done.9, bf16[1024,1024]{1,0:T(8,128)(2,1)S(1)} %copy-done.10), custom_call_target="tpu_custom_call" | custom-call | flops 3221225472 | bytes 8388608 | tf_op jit(solution)/shard_map/cosine_forward/pallas_call | solution.py:419
  72.1 3.6 %cosine_forward.3.fd_ref = f32[32,16,1024]{2,1,0:T(8,128)S(1)} custom-call(f32[32,16,1024]{2,1,0:T(8,128)S(1)} %get-tuple-element.102.x_ref.refs_7_.refs_5_, f32[32,1024]{1,0:T(8,128)S(1)} %get-tuple-element.86.refs_6_.rest_0_.refs_4_, bf16[1024,1024]{1,0:T(8,128)(2,1)S(1)} %copy-done.9, bf16[1024,1024]{1,0:T(8,128)(2,1)S(1)} %copy-done.10), custom_call_target="tpu_custom_call" | custom-call | flops 3221225472 | bytes 8388608 | tf_op jit(solution)/shard_map/cosine_forward/pallas_call | solution.py:419
  75.8 3.7 %row_solve.1 = (f32[32,16,1024]{2,1,0:T(8,128)S(1)}, f32[2,16,1024]{2,1,0:T(8,128)S(1)}) custom-call(f32[16,128]{1,0:T(8,128)S(1)} %add.48.gram_ref.first_ref, f32[32,16,1024]{2,1,0:T(8,128)S(1)} %cosine_forward.2.fg_ref, f32[32,16,1024]{2,1,0:T(8,128)S(1)} %cosine_forward.3.fd_ref, f32[32,1024]{1,0:T(8,128)S(1)} %copy-done.5, f32[1,1024]{1,0:T(1,128)S(1)} %copy-done.6), custom_call_target="tpu_custom_call" | custom-call | flops 104857600 | bytes 6291456 | tf_op jit(solution)/shard_map/row_solve/pallas_call | solution.py:469
  80.0 4.9 %collective-permute-done.13.theirs_ref = f32[2,16,1024]{2,1,0:T(8,128)S(1)} collective-permute-done((f32[2,16,1024]{2,1,0:T(8,128)S(1)}, f32[2,16,1024]{2,1,0:T(8,128)S(1)}, u32[]{:S(2)}, u32[]{:S(2)}) %collective-permute-start.13) | collective-permute-done | bytes 131104 | tf_op jit(solution)/shard_map/ppermute | solution.py:815
  85.5 2.1 %collective-permute-start.14 = (f32[2,16,1024]{2,1,0:T(8,128)S(1)}, f32[2,16,1024]{2,1,0:T(8,128)S(1)}, u32[]{:S(2)}, u32[]{:S(2)}) collective-permute-start(f32[2,16,1024]{2,1,0:T(8,128)S(1)} %get-tuple-element.105.mine_ref), channel_id=1, source_target_pairs={{0,2},{1,3},{2,0},{3,1},{4,6},{5,7},{6,4},{7,5},{8,10},{9,11},{10,... | collective-permute-start | bytes 393224 | tf_op jit(solution)/shard_map/ppermute | solution.py:815
  87.6 4.2 %collective-permute-done.14.theirs_ref = f32[2,16,1024]{2,1,0:T(8,128)S(1)} collective-permute-done((f32[2,16,1024]{2,1,0:T(8,128)S(1)}, f32[2,16,1024]{2,1,0:T(8,128)S(1)}, u32[]{:S(2)}, u32[]{:S(2)}) %collective-permute-start.14) | collective-permute-done | bytes 131104 | tf_op jit(solution)/shard_map/ppermute | solution.py:815
  92.4 1.3 collective-permute-done.15.theirs_ref
  94.3 4.1 %collective-permute-start.16 = (f32[2,16,1024]{2,1,0:T(8,128)S(1)}, f32[2,16,1024]{2,1,0:T(8,128)S(1)}, u32[]{:S(2)}, u32[]{:S(2)}) collective-permute-start(f32[2,16,1024]{2,1,0:T(8,128)S(1)} %get-tuple-element.109.mine_ref), channel_id=1, source_target_pairs={{0,8},{1,9},{2,10},{3,11},{4,12},{5,13},{6,14},{7,15},{8,0},{9,1},... | collective-permute-start | bytes 393224 | tf_op jit(solution)/shard_map/ppermute | solution.py:815
  98.4 3.8 %collective-permute-done.16.theirs_ref = f32[2,16,1024]{2,1,0:T(8,128)S(1)} collective-permute-done((f32[2,16,1024]{2,1,0:T(8,128)S(1)}, f32[2,16,1024]{2,1,0:T(8,128)S(1)}, u32[]{:S(2)}, u32[]{:S(2)}) %collective-permute-start.16) | collective-permute-done | bytes 131104 | tf_op jit(solution)/shard_map/ppermute | solution.py:815
  102.8 2.8 %collective-permute-start.17 = (f32[2,16,1024]{2,1,0:T(8,128)S(1)}, f32[2,16,1024]{2,1,0:T(8,128)S(1)}, u32[]{:S(2)}, u32[]{:S(2)}) collective-permute-start(f32[2,16,1024]{2,1,0:T(8,128)S(1)} %get-tuple-element.111.mine_ref), channel_id=1, source_target_pairs={{0,16},{1,17},{2,18},{3,19},{4,20},{5,21},{6,22},{7,23},{8,24},{9,... | collective-permute-start | bytes 393224 | tf_op jit(solution)/shard_map/ppermute | solution.py:815
  105.6 6.0 %collective-permute-done.17.theirs_ref = f32[2,16,1024]{2,1,0:T(8,128)S(1)} collective-permute-done((f32[2,16,1024]{2,1,0:T(8,128)S(1)}, f32[2,16,1024]{2,1,0:T(8,128)S(1)}, u32[]{:S(2)}, u32[]{:S(2)}) %collective-permute-start.17) | collective-permute-done | bytes 131104 | tf_op jit(solution)/shard_map/ppermute | solution.py:815
  112.2 5.8 %row_inverse.1 = (f32[32,16,1024]{2,1,0:T(8,128)S(1)}, f32[2,16,1024]{2,1,0:T(8,128)S(1)}, f32[2,16,1024]{2,1,0:T(8,128)S(1)}, f32[32,16,256]{2,1,0:T(8,128)S(1)...) custom-call(s32[9]{0:T(128)S(1)} %dynamic-slice_bitcast_fusion.1.info_ref.refs_0_, ...), custom_call_target="tpu_custom_call" | custom-call | flops 3221225472 | bytes 8388608 | tf_op jit(solution)/shard_map/row_inverse/pallas_call | solution.py:567
  118.0 3.4 %collective-permute-start.18 = (f32[2,16,1024]{2,1,0:T(8,128)S(1)}, f32[2,16,1024]{2,1,0:T(8,128)S(1)}, u32[]{:S(2)}, u32[]{:S(2)}) collective-permute-start(f32[2,16,1024]{2,1,0:T(8,128)S(1)} %get-tuple-element.120), channel_id=1, source_target_pairs={{0,1},{1,3},{3,2},{2,4},{4,5},{5,7},{7,6},{6,8},{8,9},{9,11},{11,1... | collective-permute-start | bytes 393224 | tf_op jit(solution)/shard_map/ppermute | solution.py:821
  121.4 1.5 collective-permute-start.19
  123.0 7.4 %graph_xv.1 = (f32[32,16,1024]{2,1,0:T(8,128)S(1)}, f32[32,128]{1,0:T(8,128)S(1)}) custom-call(s32[9]{0:T(128)S(1)} %dynamic-slice_bitcast_fusion.1.info_ref.refs_0_, f32[36,16,256]{2,1,0:T(8,128)S(1)} %get-tuple-element.122.refs_1_, f32[36,16,256]{2,1,0:T(8,128)S(1)} %collective-permute-done.8.refs_2_, f32[36,16,256]{2,1,0:T(8,128)S(1)} %collective-permute-done.9.refs_3_, ...), custom_call_target="tpu_custom_call" | custom-call | flops 104857600 | bytes 9568256 | tf_op jit(solution)/shard_map/graph_xv/pallas_call | solution.py:375
  130.4 2.7 %collective-permute-start.25 = (f32[32,16,256]{2,1,0:T(8,128)S(1)}, f32[32,16,256]{2,1,0:T(8,128)S(1)}, u32[]{:S(2)}, u32[]{:S(2)}) collective-permute-start(f32[32,16,256]{2,1,0:T(8,128)S(1)} %get-tuple-element.133), channel_id=1, source_target_pairs={{0,1},{1,0},{2,3},{3,2},{4,5},{5,4},{6,7},{7,6},{8,9},{9,8},{10,11... | collective-permute-start | bytes 1572872 | tf_op jit(solution)/shard_map/ppermute | solution.py:794
  134.6 7.0 %graph_xvp.1 = f32[48,128]{1,0:T(8,128)S(1)} custom-call(f32[32,16,1024]{2,1,0:T(8,128)S(1)} %get-tuple-element.115.refs_0_, f32[2,16,1024]{2,1,0:T(8,128)S(1)} %collective-permute-done.18.refs_1_, f32[2,16,1024]{2,1,0:T(8,128)S(1)} %collective-permute-done.19.refs_2_, f32[32,25,1024]{2,1,0:T(8,128)S(1)} %get-tuple-element.85.refs_5_.refs_3_, ...), custom_call_target="tpu_custom_call" | custom-call | flops 104857600 | bytes 9568256 | tf_op jit(solution)/shard_map/graph_xvp/pallas_call | solution.py:375
  141.7 1.2 collective-permute-done.20
  143.6 3.1 %collective-permute-done.21 = f32[48,128]{1,0:T(8,128)S(1)} collective-permute-done((f32[48,128]{1,0:T(8,128)S(1)}, f32[48,128]{1,0:T(8,128)S(1)}, u32[]{:S(2)}, u32[]{:S(2)}) %collective-permute-start.21) | collective-permute-done | bytes 24608 | tf_op jit(solution)/shard_map/ppermute | solution.py:789
  146.7 2.1 %collective-permute-start.22 = (f32[48,128]{1,0:T(8,128)S(1)}, f32[48,128]{1,0:T(8,128)S(1)}, u32[]{:S(2)}, u32[]{:S(2)}) collective-permute-start(f32[48,128]{1,0:T(8,128)S(1)} %add.51), channel_id=1, source_target_pairs={{0,16},{1,17},{2,18},{3,19},{4,20},{5,21},{6,22},{7,23},{8,24},{9,... | collective-permute-start | bytes 73736 | tf_op jit(solution)/shard_map/ppermute | solution.py:789
  148.8 2.6 %collective-permute-done.22 = f32[48,128]{1,0:T(8,128)S(1)} collective-permute-done((f32[48,128]{1,0:T(8,128)S(1)}, f32[48,128]{1,0:T(8,128)S(1)}, u32[]{:S(2)}, u32[]{:S(2)}) %collective-permute-start.22) | collective-permute-done | bytes 24608 | tf_op jit(solution)/shard_map/ppermute | solution.py:789
  151.5 1.9 %collective-permute-start.23 = (f32[48,128]{1,0:T(8,128)S(1)}, f32[48,128]{1,0:T(8,128)S(1)}, u32[]{:S(2)}, u32[]{:S(2)}) collective-permute-start(f32[48,128]{1,0:T(8,128)S(1)} %add.52), channel_id=1, source_target_pairs={{0,1},{1,0},{2,3},{3,2},{4,5},{5,4},{6,7},{7,6},{8,9},{9,8},{10,11... | collective-permute-start | bytes 73736 | tf_op jit(solution)/shard_map/ppermute | solution.py:789
  153.4 2.8 %collective-permute-done.23 = f32[48,128]{1,0:T(8,128)S(1)} collective-permute-done((f32[48,128]{1,0:T(8,128)S(1)}, f32[48,128]{1,0:T(8,128)S(1)}, u32[]{:S(2)}, u32[]{:S(2)}) %collective-permute-start.23) | collective-permute-done | bytes 24608 | tf_op jit(solution)/shard_map/ppermute | solution.py:789
  156.7 3.3 %collective-permute-done.24 = f32[48,128]{1,0:T(8,128)S(1)} collective-permute-done((f32[48,128]{1,0:T(8,128)S(1)}, f32[48,128]{1,0:T(8,128)S(1)}, u32[]{:S(2)}, u32[]{:S(2)}) %collective-permute-start.24) | collective-permute-done | bytes 24608 | tf_op jit(solution)/shard_map/ppermute | solution.py:789
  160.0 9.9 %ritz.1 = (f32[16,128]{1,0:T(8,128)S(1)}, f32[48,16]{1,0:T(8,128)S(1)}) custom-call(f32[16,128]{1,0:T(8,128)S(1)} %add.48.gram_ref.first_ref, f32[48,128]{1,0:T(8,128)S(1)} %add.54.second_ref), custom_call_target="tpu_custom_call" | custom-call | flops 33554432 | bytes 65536 | tf_op jit(solution)/shard_map/ritz/pallas_call | solution.py:660
  170.6 5.2 %combine.1 = (f32[16,128,256]{2,1,0:T(8,128)}, f32[16,128,256]{2,1,0:T(8,128)}) custom-call(s32[9]{0:T(128)S(1)} %dynamic-slice_bitcast_fusion.1.info_ref.refs_0_, f32[48,16]{1,0:T(8,128)S(1)} %get-tuple-element.131.coeff_ref, f32[16,128,256]{2,1,0:T(8,128)S(1)} %copy-done, f32[16,128,256]{2,1,0:T(8,128)S(1)} %copy-done.1, ...), custom_call_target="tpu_custom_call" | custom-call | flops 104857600 | bytes 10485760 | tf_op jit(solution)/shard_map/combine/pallas_call | solution.py:729
  (67 shorter events, 11.9 us)
Async XLA Ops:
  0.6 6.4 %copy-start = (f32[16,128,256]{2,1,0:T(8,128)S(1)}, f32[16,128,256]{2,1,0:T(8,128)}, u32[]{:S(2)}) copy-start(f32[16,128,256]{2,1,0:T(8,128)} %x_ref.5) | copy-start | bytes 6291460
  0.6 6.3 %copy-start.2 = (f32[128,256]{1,0:T(8,128)S(1)}, f32[128,256]{1,0:T(8,128)}, u32[]{:S(2)}) copy-start(f32[128,256]{1,0:T(8,128)} %refs_0_.1) | copy-start | bytes 393220
  2.6 6.2 %collective-permute-start = (f32[2,33,256]{2,1,0:T(8,128)}, f32[2,33,256]{2,1,0:T(8,128)S(1)}, u32[]{:S(2)}, u32[]{:S(2)}) collective-permute-start(f32[2,33,256]{2,1,0:T(8,128)} %get-tuple-element.71), channel_id=1, source_target_pairs={{0,4},{4,8},{8,12},{12,16},{16,20},{20,24},{24,28},{1,5},{5,9},{9,... | collective-permute-start | bytes 202760 | tf_op jit(solution)/shard_map/ppermute | solution.py:799
  5.0 5.6 %collective-permute-start.1 = (f32[2,33,256]{2,1,0:T(8,128)}, f32[2,33,256]{2,1,0:T(8,128)S(1)}, u32[]{:S(2)}, u32[]{:S(2)}) collective-permute-start(f32[2,33,256]{2,1,0:T(8,128)} %get-tuple-element.72), channel_id=1, source_target_pairs={{4,0},{8,4},{12,8},{16,12},{20,16},{24,20},{28,24},{5,1},{9,5},{13... | collective-permute-start | bytes 202760 | tf_op jit(solution)/shard_map/ppermute | solution.py:800
  7.0 7.7 %copy-start.1 = (f32[16,128,256]{2,1,0:T(8,128)S(1)}, f32[16,128,256]{2,1,0:T(8,128)}, u32[]{:S(2)}) copy-start(f32[16,128,256]{2,1,0:T(8,128)} %p_ref.1) | copy-start | bytes 6291460
  11.1 15.1 %collective-permute-start.2 = (f32[39,16,256]{2,1,0:T(8,128)S(1)}, f32[39,16,256]{2,1,0:T(8,128)S(1)}, u32[]{:S(2)}, u32[]{:S(2)}) collective-permute-start(f32[39,16,256]{2,1,0:T(8,128)S(1)} %get-tuple-element.78), channel_id=1, source_target_pairs={{0,1},{1,0},{2,3},{3,2},{4,5},{5,4},{6,7},{7,6},{8,9},{9,8},{10,11... | collective-permute-start | bytes 1916936 | tf_op jit(solution)/shard_map/ppermute | solution.py:794
  12.7 16.9 %collective-permute-start.3 = (f32[39,16,256]{2,1,0:T(8,128)S(1)}, f32[39,16,256]{2,1,0:T(8,128)S(1)}, u32[]{:S(2)}, u32[]{:S(2)}) collective-permute-start(f32[39,16,256]{2,1,0:T(8,128)S(1)} %get-tuple-element.79), channel_id=1, source_target_pairs={{0,2},{1,3},{2,0},{3,1},{4,6},{5,7},{6,4},{7,5},{8,10},{9,11},{10,... | collective-permute-start | bytes 1916936 | tf_op jit(solution)/shard_map/ppermute | solution.py:794
  14.2 26.8 %collective-permute-start.4 = (f32[39,16,256]{2,1,0:T(8,128)S(1)}, f32[39,16,256]{2,1,0:T(8,128)S(1)}, u32[]{:S(2)}, u32[]{:S(2)}) collective-permute-start(f32[39,16,256]{2,1,0:T(8,128)S(1)} %get-tuple-element.80), channel_id=1, source_target_pairs={{0,3},{1,2},{2,1},{3,0},{4,7},{5,6},{6,5},{7,4},{8,11},{9,10},{10,... | collective-permute-start | bytes 1916936 | tf_op jit(solution)/shard_map/ppermute | solution.py:794
  17.1 47.8 %collective-permute-start.8 = (f32[36,16,256]{2,1,0:T(8,128)S(1)}, f32[36,16,256]{2,1,0:T(8,128)S(1)}, u32[]{:S(2)}, u32[]{:S(2)}) collective-permute-start(f32[36,16,256]{2,1,0:T(8,128)S(1)} %get-tuple-element.93), channel_id=1, source_target_pairs={{0,1},{1,0},{2,3},{3,2},{4,5},{5,4},{6,7},{7,6},{8,9},{9,8},{10,11... | collective-permute-start | bytes 1769480 | tf_op jit(solution)/shard_map/ppermute | solution.py:794
  18.7 46.3 %collective-permute-start.9 = (f32[36,16,256]{2,1,0:T(8,128)S(1)}, f32[36,16,256]{2,1,0:T(8,128)S(1)}, u32[]{:S(2)}, u32[]{:S(2)}) collective-permute-start(f32[36,16,256]{2,1,0:T(8,128)S(1)} %get-tuple-element.94), channel_id=1, source_target_pairs={{0,2},{1,3},{2,0},{3,1},{4,6},{5,7},{6,4},{7,5},{8,10},{9,11},{10,... | collective-permute-start | bytes 1769480 | tf_op jit(solution)/shard_map/ppermute | solution.py:794
  26.3 40.1 %collective-permute-start.10 = (f32[36,16,256]{2,1,0:T(8,128)S(1)}, f32[36,16,256]{2,1,0:T(8,128)S(1)}, u32[]{:S(2)}, u32[]{:S(2)}) collective-permute-start(f32[36,16,256]{2,1,0:T(8,128)S(1)} %get-tuple-element.95), channel_id=1, source_target_pairs={{0,3},{1,2},{2,1},{3,0},{4,7},{5,6},{6,5},{7,4},{8,11},{9,10},{10,... | collective-permute-start | bytes 1769480 | tf_op jit(solution)/shard_map/ppermute | solution.py:794
  44.1 23.6 %copy-start.9 = (bf16[1024,1024]{1,0:T(8,128)(2,1)S(1)}, bf16[1024,1024]{1,0:T(8,128)(2,1)}, u32[]{:S(2)}) copy-start(bf16[1024,1024]{1,0:T(8,128)(2,1)} %constant.45.clone.rest_0_.rest_1_) | copy-start | bytes 6291460
  44.1 23.6 %copy-start.10 = (bf16[1024,1024]{1,0:T(8,128)(2,1)S(1)}, bf16[1024,1024]{1,0:T(8,128)(2,1)}, u32[]{:S(2)}) copy-start(bf16[1024,1024]{1,0:T(8,128)(2,1)} %constant.46.clone.rest_1_.rest_2_) | copy-start | bytes 6291460
  51.2 5.5 %collective-permute-start.5 = (f32[16,128]{1,0:T(8,128)S(1)}, f32[16,128]{1,0:T(8,128)S(1)}, u32[]{:S(2)}, u32[]{:S(2)}) collective-permute-start(f32[16,128]{1,0:T(8,128)S(1)} %get-tuple-element.87), channel_id=1, source_target_pairs={{0,4},{1,5},{2,6},{3,7},{4,0},{5,1},{6,2},{7,3},{8,12},{9,13},{10,... | collective-permute-start | bytes 24584 | tf_op jit(solution)/shard_map/ppermute | solution.py:789
  56.7 3.7 %collective-permute-start.6 = (f32[16,128]{1,0:T(8,128)S(1)}, f32[16,128]{1,0:T(8,128)S(1)}, u32[]{:S(2)}, u32[]{:S(2)}) collective-permute-start(f32[16,128]{1,0:T(8,128)S(1)} %add.44), channel_id=1, source_target_pairs={{0,8},{1,9},{2,10},{3,11},{4,12},{5,13},{6,14},{7,15},{8,0},{9,1},... | collective-permute-start | bytes 24584 | tf_op jit(solution)/shard_map/ppermute | solution.py:789
  60.4 4.5 %collective-permute-start.7 = (f32[16,128]{1,0:T(8,128)S(1)}, f32[16,128]{1,0:T(8,128)S(1)}, u32[]{:S(2)}, u32[]{:S(2)}) collective-permute-start(f32[16,128]{1,0:T(8,128)S(1)} %add.45), channel_id=1, source_target_pairs={{0,16},{1,17},{2,18},{3,19},{4,20},{5,21},{6,22},{7,23},{8,24},{9,... | collective-permute-start | bytes 24584 | tf_op jit(solution)/shard_map/ppermute | solution.py:789
  66.4 5.0 %collective-permute-start.11 = (f32[16,128]{1,0:T(8,128)S(1)}, f32[16,128]{1,0:T(8,128)S(1)}, u32[]{:S(2)}, u32[]{:S(2)}) collective-permute-start(f32[16,128]{1,0:T(8,128)S(1)} %add.46), channel_id=1, source_target_pairs={{0,1},{1,0},{2,3},{3,2},{4,5},{5,4},{6,7},{7,6},{8,9},{9,8},{10,11... | collective-permute-start | bytes 24584 | tf_op jit(solution)/shard_map/ppermute | solution.py:789
  71.4 4.3 %collective-permute-start.12 = (f32[16,128]{1,0:T(8,128)S(1)}, f32[16,128]{1,0:T(8,128)S(1)}, u32[]{:S(2)}, u32[]{:S(2)}) collective-permute-start(f32[16,128]{1,0:T(8,128)S(1)} %add.47), channel_id=1, source_target_pairs={{0,2},{1,3},{2,0},{3,1},{4,6},{5,7},{6,4},{7,5},{8,10},{9,11},{10,... | collective-permute-start | bytes 24584 | tf_op jit(solution)/shard_map/ppermute | solution.py:789
  72.1 3.7 %copy-start.5 = (f32[32,1024]{1,0:T(8,128)S(1)}, f32[32,1024]{1,0:T(8,128)}, u32[]{:S(2)}) copy-start(f32[32,1024]{1,0:T(8,128)} %constant.47.clone.eps_ref.refs_7_) | copy-start | bytes 393220
  72.1 3.7 %copy-start.6 = (f32[1,1024]{1,0:T(1,128)S(1)}, f32[1,1024]{1,0:T(1,128)}, u32[]{:S(2)}) copy-start(f32[1,1024]{1,0:T(1,128)} %constant.48.clone.last_ref.refs_8_) | copy-start | bytes 12292
  75.7 9.2 %copy-start.3 = (f32[5,1024]{1,0:T(8,128)S(1)}, f32[5,1024]{1,0:T(8,128)}, u32[]{:S(2)}) copy-start(f32[5,1024]{1,0:T(8,128)} %constant.49.clone.gain_ref) | copy-start | bytes 61444
  75.8 9.2 %copy-start.4 = (f32[5,1024]{1,0:T(8,128)S(1)}, f32[5,1024]{1,0:T(8,128)}, u32[]{:S(2)}) copy-start(f32[5,1024]{1,0:T(8,128)} %constant.50.clone.cross_ref) | copy-start | bytes 61444
  75.8 36.4 %copy-start.7 = (bf16[1024,1024]{1,0:T(8,128)(2,1)S(1)}, bf16[1024,1024]{1,0:T(8,128)(2,1)}, u32[]{:S(2)}) copy-start(bf16[1024,1024]{1,0:T(8,128)(2,1)} %constant.43.clone.refs_9_) | copy-start | bytes 6291460
  75.8 36.4 %copy-start.8 = (bf16[1024,1024]{1,0:T(8,128)(2,1)S(1)}, bf16[1024,1024]{1,0:T(8,128)(2,1)}, u32[]{:S(2)}) copy-start(bf16[1024,1024]{1,0:T(8,128)(2,1)} %constant.44.clone.refs_10_) | copy-start | bytes 6291460
  79.5 5.5 %collective-permute-start.13 = (f32[2,16,1024]{2,1,0:T(8,128)S(1)}, f32[2,16,1024]{2,1,0:T(8,128)S(1)}, u32[]{:S(2)}, u32[]{:S(2)}) collective-permute-start(f32[2,16,1024]{2,1,0:T(8,128)S(1)} %get-tuple-element.103.mine_ref), channel_id=1, source_target_pairs={{0,1},{1,0},{2,3},{3,2},{4,5},{5,4},{6,7},{7,6},{8,9},{9,8},{10,11... | collective-permute-start | bytes 393224 | tf_op jit(solution)/shard_map/ppermute | solution.py:815
  85.5 6.3 %collective-permute-start.14 = (f32[2,16,1024]{2,1,0:T(8,128)S(1)}, f32[2,16,1024]{2,1,0:T(8,128)S(1)}, u32[]{:S(2)}, u32[]{:S(2)}) collective-permute-start(f32[2,16,1024]{2,1,0:T(8,128)S(1)} %get-tuple-element.105.mine_ref), channel_id=1, source_target_pairs={{0,2},{1,3},{2,0},{3,1},{4,6},{5,7},{6,4},{7,5},{8,10},{9,11},{10,... | collective-permute-start | bytes 393224 | tf_op jit(solution)/shard_map/ppermute | solution.py:815
  92.4 1.4 collective-permute-start.15
  94.3 7.9 %collective-permute-start.16 = (f32[2,16,1024]{2,1,0:T(8,128)S(1)}, f32[2,16,1024]{2,1,0:T(8,128)S(1)}, u32[]{:S(2)}, u32[]{:S(2)}) collective-permute-start(f32[2,16,1024]{2,1,0:T(8,128)S(1)} %get-tuple-element.109.mine_ref), channel_id=1, source_target_pairs={{0,8},{1,9},{2,10},{3,11},{4,12},{5,13},{6,14},{7,15},{8,0},{9,1},... | collective-permute-start | bytes 393224 | tf_op jit(solution)/shard_map/ppermute | solution.py:815
  102.8 8.8 %collective-permute-start.17 = (f32[2,16,1024]{2,1,0:T(8,128)S(1)}, f32[2,16,1024]{2,1,0:T(8,128)S(1)}, u32[]{:S(2)}, u32[]{:S(2)}) collective-permute-start(f32[2,16,1024]{2,1,0:T(8,128)S(1)} %get-tuple-element.111.mine_ref), channel_id=1, source_target_pairs={{0,16},{1,17},{2,18},{3,19},{4,20},{5,21},{6,22},{7,23},{8,24},{9,... | collective-permute-start | bytes 393224 | tf_op jit(solution)/shard_map/ppermute | solution.py:815
  118.0 12.4 %collective-permute-start.18 = (f32[2,16,1024]{2,1,0:T(8,128)S(1)}, f32[2,16,1024]{2,1,0:T(8,128)S(1)}, u32[]{:S(2)}, u32[]{:S(2)}) collective-permute-start(f32[2,16,1024]{2,1,0:T(8,128)S(1)} %get-tuple-element.120), channel_id=1, source_target_pairs={{0,1},{1,3},{3,2},{2,4},{4,5},{5,7},{7,6},{6,8},{8,9},{9,11},{11,1... | collective-permute-start | bytes 393224 | tf_op jit(solution)/shard_map/ppermute | solution.py:821
  121.4 9.0 %collective-permute-start.19 = (f32[2,16,1024]{2,1,0:T(8,128)S(1)}, f32[2,16,1024]{2,1,0:T(8,128)S(1)}, u32[]{:S(2)}, u32[]{:S(2)}) collective-permute-start(f32[2,16,1024]{2,1,0:T(8,128)S(1)} %get-tuple-element.121), channel_id=1, source_target_pairs={{1,0},{3,1},{2,3},{4,2},{5,4},{7,5},{6,7},{8,6},{9,8},{11,9},{10,1... | collective-permute-start | bytes 393224 | tf_op jit(solution)/shard_map/ppermute | solution.py:822
  130.4 40.2 %collective-permute-start.25 = (f32[32,16,256]{2,1,0:T(8,128)S(1)}, f32[32,16,256]{2,1,0:T(8,128)S(1)}, u32[]{:S(2)}, u32[]{:S(2)}) collective-permute-start(f32[32,16,256]{2,1,0:T(8,128)S(1)} %get-tuple-element.133), channel_id=1, source_target_pairs={{0,1},{1,0},{2,3},{3,2},{4,5},{5,4},{6,7},{7,6},{8,9},{9,8},{10,11... | collective-permute-start | bytes 1572872 | tf_op jit(solution)/shard_map/ppermute | solution.py:794
  133.1 37.5 %collective-permute-start.26 = (f32[32,16,256]{2,1,0:T(8,128)S(1)}, f32[32,16,256]{2,1,0:T(8,128)S(1)}, u32[]{:S(2)}, u32[]{:S(2)}) collective-permute-start(f32[32,16,256]{2,1,0:T(8,128)S(1)} %get-tuple-element.134), channel_id=1, source_target_pairs={{0,2},{1,3},{2,0},{3,1},{4,6},{5,7},{6,4},{7,5},{8,10},{9,11},{10,... | collective-permute-start | bytes 1572872 | tf_op jit(solution)/shard_map/ppermute | solution.py:794
  133.6 37.0 %collective-permute-start.27 = (f32[32,16,256]{2,1,0:T(8,128)S(1)}, f32[32,16,256]{2,1,0:T(8,128)S(1)}, u32[]{:S(2)}, u32[]{:S(2)}) collective-permute-start(f32[32,16,256]{2,1,0:T(8,128)S(1)} %get-tuple-element.135), channel_id=1, source_target_pairs={{0,3},{1,2},{2,1},{3,0},{4,7},{5,6},{6,5},{7,4},{8,11},{9,10},{10,... | collective-permute-start | bytes 1572872 | tf_op jit(solution)/shard_map/ppermute | solution.py:794
  141.7 1.2 collective-permute-start.20
  142.9 3.8 %collective-permute-start.21 = (f32[48,128]{1,0:T(8,128)S(1)}, f32[48,128]{1,0:T(8,128)S(1)}, u32[]{:S(2)}, u32[]{:S(2)}) collective-permute-start(f32[48,128]{1,0:T(8,128)S(1)} %add.50), channel_id=1, source_target_pairs={{0,8},{1,9},{2,10},{3,11},{4,12},{5,13},{6,14},{7,15},{8,0},{9,1},... | collective-permute-start | bytes 73736 | tf_op jit(solution)/shard_map/ppermute | solution.py:789
  146.7 4.7 %collective-permute-start.22 = (f32[48,128]{1,0:T(8,128)S(1)}, f32[48,128]{1,0:T(8,128)S(1)}, u32[]{:S(2)}, u32[]{:S(2)}) collective-permute-start(f32[48,128]{1,0:T(8,128)S(1)} %add.51), channel_id=1, source_target_pairs={{0,16},{1,17},{2,18},{3,19},{4,20},{5,21},{6,22},{7,23},{8,24},{9,... | collective-permute-start | bytes 73736 | tf_op jit(solution)/shard_map/ppermute | solution.py:789
  151.5 4.7 %collective-permute-start.23 = (f32[48,128]{1,0:T(8,128)S(1)}, f32[48,128]{1,0:T(8,128)S(1)}, u32[]{:S(2)}, u32[]{:S(2)}) collective-permute-start(f32[48,128]{1,0:T(8,128)S(1)} %add.52), channel_id=1, source_target_pairs={{0,1},{1,0},{2,3},{3,2},{4,5},{5,4},{6,7},{7,6},{8,9},{9,8},{10,11... | collective-permute-start | bytes 73736 | tf_op jit(solution)/shard_map/ppermute | solution.py:789
  156.2 3.8 %collective-permute-start.24 = (f32[48,128]{1,0:T(8,128)S(1)}, f32[48,128]{1,0:T(8,128)S(1)}, u32[]{:S(2)}, u32[]{:S(2)}) collective-permute-start(f32[48,128]{1,0:T(8,128)S(1)} %add.53), channel_id=1, source_target_pairs={{0,2},{1,3},{2,0},{3,1},{4,6},{5,7},{6,4},{7,5},{8,10},{9,11},{10,... | collective-permute-start | bytes 73736 | tf_op jit(solution)/shard_map/ppermute | solution.py:789

commit v4 on v3

--- a/solution.py
+++ b/solution.py
@@ -480,31 +480,41 @@
     )(gram, fg, fd, eps, last)
 
 
-def merge_kernel(level, last, info_ref, mine_ref, theirs_ref, gain_ref, cross_ref, g_ref, *ends_ref):
-    right = ((info_ref[0] >> level) & 1) == 1
-    mine, theirs = mine_ref[...], theirs_ref[...]
-    lower = jnp.where(right, theirs, mine)
-    upper = jnp.where(right, mine, theirs)
-    g = (lower[1] - upper[0]) * gain_ref[level : level + 1, :]
-    g_ref[...] = g
+def merge_kernel(level, count, last, info_ref, gain_ref, cross_ref, *refs):
+    groups, outs = [ref[...] for ref in refs[:count]], refs[count:]
+    place = info_ref[0] >> level
+
+    def join(own, other, step, keep):
+        right = ((place >> step) & 1) == 1
+        lower, upper = jnp.where(right, other, own), jnp.where(right, own, other)
+        row = slice(level + step, level + step + 1)
+        g = (lower[1] - upper[0]) * gain_ref[row, :]
+        moved = g * cross_ref[row, :]
+        return g, jnp.stack([lower[0] - moved, upper[1] + moved]) if keep else None
+
+    g, ends = join(groups[0], groups[1], 0, count == 4 or not last)
+    outs[0][...] = g
+    if count == 4:
+        _, others = join(groups[2], groups[3], 0, True)
+        g, ends = join(ends, others, 1, not last)
+        outs[1][...] = g
     if not last:
-        moved = g * cross_ref[level : level + 1, :]
-        ends_ref[0][0] = lower[0] - moved
-        ends_ref[0][1] = upper[1] + moved
-
-
-def merge(level, last, info, mine, theirs, gain, cross):
-    _, fields, cols = mine.shape
-    out_shape = (room(fields, cols),) + (() if last else (room(2, fields, cols),))
-    return pl.pallas_call(
-        functools.partial(merge_kernel, level, last),
+        outs[-1][...] = ends
+
+
+def merge(level, last, info, groups, gain, cross):
+    _, fields, cols = groups[0].shape
+    count = len(groups)
+    out_shape = (room(fields, cols),) * (count // 2) + (() if last else (room(2, fields, cols),))
+    return pl.pallas_call(
+        functools.partial(merge_kernel, level, count, last),
         out_shape=out_shape,
-        in_specs=[SMEM] + [VMEM] * 4,
+        in_specs=[SMEM] + [VMEM] * (2 + count),
         out_specs=(VMEM,) * len(out_shape),
-        compiler_params=params(),
+        compiler_params=params(*groups, *out_shape),
         cost_estimate=cost(10 * fields * cols, 28 * fields * cols),
         name="merge",
-    )(info, mine, theirs, gain, cross)
+    )(info, gain, cross, *groups)
 
 
 def inverse_kernel(levels, chunks, info_ref, *refs):
@@ -649,10 +659,9 @@
     basis = cholesky_apply(hdot(images, images, ((1,), (1,))), images)
     images = hdot(basis, power, ((1,), (0,)))
     basis = cholesky_apply(hdot(images, images, ((1,), (1,))), images)
-    basis = cholesky_apply(hdot(basis, basis, ((1,), (1,))), basis)
     images = hdot(basis, reduced, ((1,), (0,)))
-    ritz = jnp.sum(basis * images, 1, keepdims=True) - ritz_offset
-    ritz_ref[...] = jnp.broadcast_to(ritz, ritz_ref.shape)
+    ones = jnp.ones((8, size), f32)
+    ritz_ref[...] = hdot(ones, basis * images, ((1,), (1,)))[0:1] - ritz_offset
     coeff_ref[...] = math.sqrt(pixel_total) * scale_col * hdot(inverse, basis, ((0,), (1,)))
 
 
@@ -660,8 +669,8 @@
     return pl.pallas_call(
         functools.partial(ritz_kernel, fields, pixel_total),
         out_shape=(
-            jax.ShapeDtypeStruct((fields, LANES), f32),
-            jax.ShapeDtypeStruct((3 * fields, fields), f32),
+            room(1, fields),
+            room(3 * fields, fields),
         ),
         in_specs=[pl.BlockSpec(memory_space=pltpu.VMEM)] * 2,
         out_specs=(pl.BlockSpec(memory_space=pltpu.VMEM),) * 2,
@@ -781,19 +790,25 @@
     info = lax.dynamic_index_in_dim(jnp.asarray(table), device, 0, False)
     flux = lax.dynamic_index_in_dim(jnp.asarray(by_device), device, 0, False)
 
-    def total(value, tied=()):
-        first = chunks.bit_length() - 1
-        for level in [*range(first, levels), *range(first)]:
-            if level == 0:
-                value, tied = lax.optimization_barrier((value, tied))
-            value = value + lax.ppermute(value, BOTH, [(i, i ^ (1 << level)) for i in range(strips)])
-        return value, tied
+    first = chunks.bit_length() - 1
+    row_groups = [[first]] + [[*range(b, min(b + 2, levels))] for b in range(first + 1, levels, 2)]
+    col_groups = [[*range(b, min(b + 2, first))] for b in range(0, first, 2)]
+
+    def add_up(value, groups, late=None):
+        for group in groups:
+            away = [1 << b for b in group]
+            away += [sum(away)] if len(away) == 2 else []
+            got = [lax.ppermute(value, BOTH, [(i, i ^ m) for i in range(strips)]) for m in away]
+            if late is not None and group is groups[-1]:
+                late, got = lax.optimization_barrier((late, got))
+            value = value + got[0] + (got[1] + got[2]) if len(got) == 3 else value + got[0]
+        return value, late
+
+    def away(piece, d):
+        return lax.ppermute(piece, "col", [(c, c ^ d) for c in range(chunks)])
 
     def exchange(pieces):
-        return [pieces[0]] + [
-            lax.ppermute(pieces[d], "col", [(c, c ^ d) for c in range(chunks)])
-            for d in range(1, chunks)
-        ]
+        return [pieces[0]] + [away(pieces[d], d) for d in range(1, chunks)]
 
     head, tail = edges(start_block, old_direction, intensity)
     above = lax.ppermute(tail, "row", [(i, i + 1) for i in range(row_count - 1)])
@@ -805,33 +820,48 @@
     x_pieces, flux = lax.optimization_barrier((x_pieces, flux))
     w, deg = make_weights(info, x_pieces, depth, rows)
     graph_x, x, gram_x = apply_graph(("v",), True, 4 * fields, x_pieces, w, deg, info=info)
-    gram_x, p_pieces = total(gram_x, p_pieces)
+    gram_x, _ = add_up(gram_x, row_groups)
+    gram_x, p_pieces = lax.optimization_barrier((gram_x, p_pieces))
+    gram_x, _ = add_up(gram_x, col_groups)
     spectrum_g = cosine_forward(graph_x, None, high_t, low_t, depth, fields)
     spectrum_d = cosine_forward(x, deg, high_t, low_t, depth, fields)
     f, ends = row_solve(gram_x, spectrum_g, spectrum_d, eps, last)
 
     gs = []
-    for level in range(levels):
-        theirs = lax.ppermute(ends, BOTH, [(i, i ^ (1 << level)) for i in range(strips)])
-        g, *ends = merge(level, level == levels - 1, info, ends, theirs, gain, cross)
-        ends = ends[0] if ends else None
-        gs.append(g)
+    groups = col_groups + row_groups
+    for group in groups:
+        level = group[0]
+        found = {0: ends}
+        for d in range(1, 1 << len(group)):
+            place = (int(table[d << level, 0]) ^ int(table[0, 0])) >> level
+            pairs = [(i, i ^ (d << level)) for i in range(strips)]
+            found[place & (1 << len(group)) - 1] = lax.ppermute(ends, BOTH, pairs)
+        is_last = group is groups[-1]
+        *new, ends = merge(level, is_last, info, [found[e] for e in sorted(found)], gain, cross) + (
+            (None,) if is_last else ()
+        )
+        gs += new
+        if group is groups[-2]:
+            p_pieces, ends = lax.optimization_barrier((p_pieces, ends))
+    p, gram_p = apply_graph(("x", "v"), False, 2 * fields, p_pieces, w, deg, x, info=info)
+    gs[-1], gram_p = lax.optimization_barrier((gs[-1], gram_p))
 
     h, head, tail, *h_pieces = row_inverse(info, gs, f, flux, eps, last, high, low, chunks)
     h_above = lax.ppermute(tail, BOTH, [(owner[s], owner[s + 1]) for s in range(strips - 1)])
     h_below = lax.ppermute(head, BOTH, [(owner[s + 1], owner[s]) for s in range(strips - 1)])
-    p_pieces, h = lax.optimization_barrier((p_pieces, h))
-    p, gram_p = apply_graph(("x", "v"), False, 2 * fields, p_pieces, w, deg, x, info=info)
-    h_pieces, h_above, h_below, gram_p = lax.optimization_barrier(
-        (h_pieces, h_above, h_below, gram_p)
-    )
-    h_pieces = exchange(h_pieces)
+    h_own, *h_early, h_late = h_pieces
+    h_early, h_above, h_below = lax.optimization_barrier((h_early, h_above, h_below))
+    h_early = [away(piece, d) for d, piece in enumerate(h_early, 1)]
     (gram_h,) = apply_graph(("x", "v", "p"), False, 0, (h, h_above, h_below), w, deg, x, p)
     zero = jnp.zeros((fields, LANES), f32)
     gram = gram_h + jnp.concatenate([gram_p[:fields], zero, gram_p[fields:]], 0)
-    ritz, coeffs = ritz_step(gram_x, total(gram)[0], fields, rows * cols)
+    gram, _ = add_up(gram, row_groups)
+    gram, h_early = lax.optimization_barrier((gram, h_early))
+    gram, h_late = add_up(gram, col_groups, h_late)
+    h_pieces = [h_own, *h_early, away(h_late, chunks - 1)]
+    ritz, coeffs = ritz_step(gram_x, gram, fields, rows * cols)
     new_block, new_direction = combine(info, coeffs, start_block, old_direction, h_pieces)
-    return new_block, new_direction, ritz[:, 0]
+    return new_block, new_direction, ritz.reshape(fields)
 
 
 def solution(mesh):

time: 176 us -> 167 us (0.949)
  waiting for transfers between devices: 59 us -> 46.9 us
  starting transfers between devices: 47.4 us -> 53.4 us
  Pallas kernels: 65.9 us -> 63.9 us
    ppermute x24 -> x30, waiting for transfers between devices: 57.2 us -> 39.5 us  [the longest x9 18 us: away(): return lax.ppermute(piece, 'col', [(c, c ^ d) for c in range(chunks)])]
    ppermute x24 -> x30, starting transfers between devices: 38.9 us -> 45.8 us  [the longest x14 22.7 us: add_up(): lax.ppermute(value, BOTH, [(i, i ^ m) for i in range(strips)])]
    ppermute x1, waiting for transfers between devices: 0.01 us -> 4.7 us  [local(): lax.ppermute(head, BOTH, [(owner[s + 1], owner[s]) for s in range(strips...]
  transfers between devices with their start and end apart: 28 -> 34, of which waited for: 17 -> 19; matrix products, arithmetic and copies ran while one was open for 1% -> 1% of each run, Pallas kernels for 26% -> 27%
where the time goes in v4:
time: 167 us
  Pallas kernels  63.9 us (38%)
  starting transfers between devices  53.4 us (32%)
  waiting for transfers between devices  46.9 us (28%)
  local copies, waits for them, and re-layouts  1.68 us (1%)
    ppermute x14, starting transfers between devices, add_up(): lax.ppermute(value, BOTH, [(i, i ^ m) for i in range(strips)])  22.7 us
    pallas_call x3, Pallas kernels, apply_graph(): pl.pallas_call(functools.partial(graph_kernel, order, keep, lane_shift, c...  21.5 us
    ppermute x9, waiting for transfers between devices, away(): return lax.ppermute(piece, 'col', [(c, c ^ d) for c in range(chunks)])  18 us
    ppermute x9, starting transfers between devices, away(): return lax.ppermute(piece, 'col', [(c, c ^ d) for c in range(chunks)])  13.7 us
    ppermute x7, waiting for transfers between devices, local(): found[place & (1 << len(group)) - 1] = lax.ppermute(ends, BOTH, pairs)  12.9 us
    ppermute x7, starting transfers between devices, local(): found[place & (1 << len(group)) - 1] = lax.ppermute(ends, BOTH, pairs)  9.42 us
    pallas_call x1, Pallas kernels, ritz_step(): pl.pallas_call(functools.partial(ritz_kernel, fields, pixel_total), out_s...  9.04 us
    ppermute x14, waiting for transfers between devices, add_up(): lax.ppermute(value, BOTH, [(i, i ^ m) for i in range(strips)])  8.69 us
  transfers between devices with their start and end apart: 34, of which 19 were waited for; matrix products, arithmetic and copies ran while one was open for 1% of the time, Pallas kernels for 27%

profile of v4, /device:TPU:0, one launch (start us, length us, event | category | flops | bytes accessed | tf_op | source)
XLA Modules:
  0.0 167.0 jit_solution(12010848670792909790)
XLA Ops:
  0.6 2.0 %edges.1 = (f32[2,33,256]{2,1,0:T(8,128)}, f32[2,33,256]{2,1,0:T(8,128)}) custom-call(f32[16,128,256]{2,1,0:T(8,128)} %x_ref.5, f32[16,128,256]{2,1,0:T(8,128)} %x_ref.5, f32[16,128,256]{2,1,0:T(8,128)} %p_ref.1, f32[16,128,256]{2,1,0:T(8,128)} %p_ref.1, f32[128,256]{1,0:T(8,128)} %refs_0_.1, f32[128,256]{1,0:T(8,128)} %refs_0_.1), custom_call_target="tpu_custom_call" | custom-call | bytes 524288 | tf_op jit(solution)/shard_map/edges/pallas_call | solution.py:149
  2.6 2.3 %collective-permute-start = (f32[2,33,256]{2,1,0:T(8,128)}, f32[2,33,256]{2,1,0:T(8,128)S(1)}, u32[]{:S(2)}, u32[]{:S(2)}) collective-permute-start(f32[2,33,256]{2,1,0:T(8,128)} %get-tuple-element.76), channel_id=1, source_target_pairs={{0,4},{4,8},{8,12},{12,16},{16,20},{20,24},{24,28},{1,5},{5,9},{9,... | collective-permute-start | bytes 202760 | tf_op jit(solution)/shard_map/ppermute | solution.py:814
  5.0 1.3 collective-permute-start.1
  7.0 1.8 %pack.2 = (f32[39,16,256]{2,1,0:T(8,128)S(1)}, f32[39,16,256]{2,1,0:T(8,128)S(1)}, f32[39,16,256]{2,1,0:T(8,128)S(1)}, f32[39,16,256]{2,1,0:T(8,128)S(1)}) custom-call(s32[9]{0:T(128)S(1)} %dynamic-slice_bitcast_fusion.1.info_ref.refs_0_, f32[16,128,256]{2,1,0:T(8,128)S(1)} %copy-done, f32[128,256]{1,0:T(8,128)S(1)} %copy-done.2), custom_call_target="tpu_custom_call" | custom-call | bytes 4194304 | tf_op jit(solution)/shard_map/pack/pallas_call | solution.py:202
  8.8 1.7 %collective-permute-done.1.below_ref = f32[2,33,256]{2,1,0:T(8,128)S(1)} collective-permute-done((f32[2,33,256]{2,1,0:T(8,128)}, f32[2,33,256]{2,1,0:T(8,128)S(1)}, u32[]{:S(2)}, u32[]{:S(2)}) %collective-permute-start.1) | collective-permute-done | bytes 67616 | tf_op jit(solution)/shard_map/ppermute | solution.py:815
  11.1 1.6 collective-permute-start.2
  12.7 1.5 collective-permute-start.3
  14.7 1.8 %pack.3 = (f32[36,16,256]{2,1,0:T(8,128)S(1)}, f32[36,16,256]{2,1,0:T(8,128)S(1)}, f32[36,16,256]{2,1,0:T(8,128)S(1)}, f32[36,16,256]{2,1,0:T(8,128)S(1)}) custom-call(s32[9]{0:T(128)S(1)} %dynamic-slice_bitcast_fusion.1.info_ref.refs_0_, f32[16,128,256]{2,1,0:T(8,128)S(1)} %copy-done.1), custom_call_target="tpu_custom_call" | custom-call | bytes 4194304 | tf_op jit(solution)/shard_map/pack/pallas_call | solution.py:202
  17.1 1.6 collective-permute-start.9
  18.7 1.5 collective-permute-start.10
  20.2 6.1 %collective-permute-done.2.rest_1_.refs_2_ = f32[39,16,256]{2,1,0:T(8,128)S(1)} collective-permute-done((f32[39,16,256]{2,1,0:T(8,128)S(1)}, f32[39,16,256]{2,1,0:T(8,128)S(1)}, u32[]{:S(2)}, u32[]{:S(2)}) %collective-permute-start.2) | collective-permute-done | bytes 639008 | tf_op jit(solution)/shard_map/ppermute | solution.py:808
  26.3 2.4 %collective-permute-start.11 = (f32[36,16,256]{2,1,0:T(8,128)S(1)}, f32[36,16,256]{2,1,0:T(8,128)S(1)}, u32[]{:S(2)}, u32[]{:S(2)}) collective-permute-start(f32[36,16,256]{2,1,0:T(8,128)S(1)} %get-tuple-element.100), channel_id=1, source_target_pairs={{0,3},{1,2},{2,1},{3,0},{4,7},{5,6},{6,5},{7,4},{8,11},{9,10},{10,... | collective-permute-start | bytes 1769480 | tf_op jit(solution)/shard_map/ppermute | solution.py:808
  29.6 11.5 %collective-permute-done.4.rest_3_.refs_4_ = f32[39,16,256]{2,1,0:T(8,128)S(1)} collective-permute-done((f32[39,16,256]{2,1,0:T(8,128)S(1)}, f32[39,16,256]{2,1,0:T(8,128)S(1)}, u32[]{:S(2)}, u32[]{:S(2)}) %collective-permute-start.4) | collective-permute-done | bytes 639008 | tf_op jit(solution)/shard_map/ppermute | solution.py:808
  41.0 3.1 %weights.1 = (f32[32,25,1024]{2,1,0:T(8,128)S(1)}, f32[32,1024]{1,0:T(8,128)S(1)}) custom-call(s32[9]{0:T(128)S(1)} %dynamic-slice_bitcast_fusion.1.info_ref.refs_0_, f32[39,16,256]{2,1,0:T(8,128)S(1)} %get-tuple-element.86.rest_0_.refs_1_, f32[39,16,256]{2,1,0:T(8,128)S(1)} %collective-permute-done.2.rest_1_.refs_2_, ...), custom_call_target="tpu_custom_call" | custom-call | flops 49152000 | bytes 3276800 | tf_op jit(solution)/shard_map/weights/pallas_call | solution.py:281
  44.1 7.1 %graph_v.1 = (f32[32,16,1024]{2,1,0:T(8,128)S(1)}, f32[32,16,1024]{2,1,0:T(8,128)S(1)}, f32[16,128]{1,0:T(8,128)S(1)}) custom-call(s32[9]{0:T(128)S(1)} %dynamic-slice_bitcast_fusion.1.info_ref.refs_0_, f32[39,16,256]{2,1,0:T(8,128)S(1)} %get-tuple-element.86.rest_0_.refs_1_, f32[39,16,256]{2,1,0:T(8,128)S(1)} %collective-permute-done.2.rest_1_.refs_2_, ...), custom_call_target="tpu_custom_call" | custom-call | flops 104857600 | bytes 9568256 | tf_op jit(solution)/shard_map/graph_v/pallas_call | solution.py:375
  51.2 4.6 %collective-permute-start.5 = (f32[16,128]{1,0:T(8,128)S(1)}, f32[16,128]{1,0:T(8,128)S(1)}, u32[]{:S(2)}, u32[]{:S(2)}) collective-permute-start(f32[16,128]{1,0:T(8,128)S(1)} %get-tuple-element.92), channel_id=1, source_target_pairs={{0,4},{1,5},{2,6},{3,7},{4,0},{5,1},{6,2},{7,3},{8,12},{9,13},{10,... | collective-permute-start | bytes 24584 | tf_op jit(solution)/shard_map/ppermute | solution.py:801
  56.7 2.5 %collective-permute-start.7 = (f32[16,128]{1,0:T(8,128)S(1)}, f32[16,128]{1,0:T(8,128)S(1)}, u32[]{:S(2)}, u32[]{:S(2)}) collective-permute-start(f32[16,128]{1,0:T(8,128)S(1)} %add.56), channel_id=1, source_target_pairs={{0,16},{1,17},{2,18},{3,19},{4,20},{5,21},{6,22},{7,23},{8,24},{9,... | collective-permute-start | bytes 24584 | tf_op jit(solution)/shard_map/ppermute | solution.py:801
  59.2 1.3 collective-permute-start.8
  61.3 1.5 collective-permute-start.6
  62.8 3.6 %cosine_forward.2.fg_ref = f32[32,16,1024]{2,1,0:T(8,128)S(1)} custom-call(f32[32,16,1024]{2,1,0:T(8,128)S(1)} %get-tuple-element.102.x_ref, bf16[1024,1024]{1,0:T(8,128)(2,1)S(1)} %copy-done.9, bf16[1024,1024]{1,0:T(8,128)(2,1)S(1)} %copy-done.10), custom_call_target="tpu_custom_call" | custom-call | flops 3221225472 | bytes 8388608 | tf_op jit(solution)/shard_map/cosine_forward/pallas_call | solution.py:419
  66.5 1.6 collective-permute-start.13
  68.0 1.2 collective-permute-start.14
  70.0 3.6 %cosine_forward.3.fd_ref = f32[32,16,1024]{2,1,0:T(8,128)S(1)} custom-call(f32[32,16,1024]{2,1,0:T(8,128)S(1)} %get-tuple-element.103.x_ref.refs_7_.refs_5_, f32[32,1024]{1,0:T(8,128)S(1)} %get-tuple-element.91.refs_6_.rest_0_.refs_4_, bf16[1024,1024]{1,0:T(8,128)(2,1)S(1)} %copy-done.9, bf16[1024,1024]{1,0:T(8,128)(2,1)S(1)} %copy-done.10), custom_call_target="tpu_custom_call" | custom-call | flops 3221225472 | bytes 8388608 | tf_op jit(solution)/shard_map/cosine_forward/pallas_call | solution.py:419
  73.7 3.7 %row_solve.1 = (f32[32,16,1024]{2,1,0:T(8,128)S(1)}, f32[2,16,1024]{2,1,0:T(8,128)S(1)}) custom-call(f32[16,128]{1,0:T(8,128)S(1)} %add_add_fusion.2.gram_ref.first_ref, f32[32,16,1024]{2,1,0:T(8,128)S(1)} %cosine_forward.2.fg_ref, f32[32,16,1024]{2,1,0:T(8,128)S(1)} %cosine_forward.3.fd_ref, f32[32,1024]{1,0:T(8,128)S(1)} %copy-done.5, f32[1,1024]{1,0:T(1,128)S(1)} %copy-done.6), custom_call_target="tpu_custom_call" | custom-call | flops 104857600 | bytes 6291456 | tf_op jit(solution)/shard_map/row_solve/pallas_call | solution.py:469
  77.4 1.3 collective-permute-start.15
  78.7 1.8 %collective-permute-start.16 = (f32[2,16,1024]{2,1,0:T(8,128)S(1)}, f32[2,16,1024]{2,1,0:T(8,128)S(1)}, u32[]{:S(2)}, u32[]{:S(2)}) collective-permute-start(f32[2,16,1024]{2,1,0:T(8,128)S(1)} %get-tuple-element.104.refs_0_), channel_id=1, source_target_pairs={{0,3},{1,2},{2,1},{3,0},{4,7},{5,6},{6,5},{7,4},{8,11},{9,10},{10,... | collective-permute-start | bytes 393224 | tf_op jit(solution)/shard_map/ppermute | solution.py:838
  80.9 2.5 %collective-permute-done.15.refs_1_ = f32[2,16,1024]{2,1,0:T(8,128)S(1)} collective-permute-done((f32[2,16,1024]{2,1,0:T(8,128)S(1)}, f32[2,16,1024]{2,1,0:T(8,128)S(1)}, u32[]{:S(2)}, u32[]{:S(2)}) %collective-permute-start.15) | collective-permute-done | bytes 131104 | tf_op jit(solution)/shard_map/ppermute | solution.py:838
  83.5 3.9 %collective-permute-done.16.refs_2_ = f32[2,16,1024]{2,1,0:T(8,128)S(1)} collective-permute-done((f32[2,16,1024]{2,1,0:T(8,128)S(1)}, f32[2,16,1024]{2,1,0:T(8,128)S(1)}, u32[]{:S(2)}, u32[]{:S(2)}) %collective-permute-start.16) | collective-permute-done | bytes 131104 | tf_op jit(solution)/shard_map/ppermute | solution.py:838
  87.3 2.1 %collective-permute-done.17.refs_3_ = f32[2,16,1024]{2,1,0:T(8,128)S(1)} collective-permute-done((f32[2,16,1024]{2,1,0:T(8,128)S(1)}, f32[2,16,1024]{2,1,0:T(8,128)S(1)}, u32[]{:S(2)}, u32[]{:S(2)}) %collective-permute-start.17) | collective-permute-done | bytes 131104 | tf_op jit(solution)/shard_map/ppermute | solution.py:838
  90.2 1.3 collective-permute-done.18.refs_1_
  92.1 3.3 %collective-permute-start.19 = (f32[2,16,1024]{2,1,0:T(8,128)S(1)}, f32[2,16,1024]{2,1,0:T(8,128)S(1)}, u32[]{:S(2)}, u32[]{:S(2)}) collective-permute-start(f32[2,16,1024]{2,1,0:T(8,128)S(1)} %get-tuple-element.114.refs_0_), channel_id=1, source_target_pairs={{0,8},{1,9},{2,10},{3,11},{4,12},{5,13},{6,14},{7,15},{8,0},{9,1},... | collective-permute-start | bytes 393224 | tf_op jit(solution)/shard_map/ppermute | solution.py:838
  96.5 1.4 collective-permute-start.21
  97.9 7.4 %graph_xv.1 = (f32[32,16,1024]{2,1,0:T(8,128)S(1)}, f32[32,128]{1,0:T(8,128)S(1)}) custom-call(s32[9]{0:T(128)S(1)} %dynamic-slice_bitcast_fusion.1.info_ref.refs_0_, f32[36,16,256]{2,1,0:T(8,128)S(1)} %get-tuple-element.117.refs_1_, f32[36,16,256]{2,1,0:T(8,128)S(1)} %collective-permute-done.9.refs_2_, f32[36,16,256]{2,1,0:T(8,128)S(1)} %collective-permute-done.10.refs_3_, ...), custom_call_target="tpu_custom_call" | custom-call | flops 104857600 | bytes 9568256 | tf_op jit(solution)/shard_map/graph_xv/pallas_call | solution.py:375
  105.3 3.0 %collective-permute-done.20.refs_2_ = f32[2,16,1024]{2,1,0:T(8,128)S(1)} collective-permute-done((f32[2,16,1024]{2,1,0:T(8,128)S(1)}, f32[2,16,1024]{2,1,0:T(8,128)S(1)}, u32[]{:S(2)}, u32[]{:S(2)}) %collective-permute-start.20) | collective-permute-done | bytes 131104 | tf_op jit(solution)/shard_map/ppermute | solution.py:838
  109.0 5.8 %row_inverse.1 = (f32[32,16,1024]{2,1,0:T(8,128)S(1)}, f32[2,16,1024]{2,1,0:T(8,128)S(1)}, f32[2,16,1024]{2,1,0:T(8,128)S(1)}, f32[32,16,256]{2,1,0:T(8,128)S(1)...) custom-call(s32[9]{0:T(128)S(1)} %dynamic-slice_bitcast_fusion.1.info_ref.refs_0_, ...), custom_call_target="tpu_custom_call" | custom-call | flops 3221225472 | bytes 8388608 | tf_op jit(solution)/shard_map/row_inverse/pallas_call | solution.py:577
  114.7 2.4 %collective-permute-start.22 = (f32[2,16,1024]{2,1,0:T(8,128)S(1)}, f32[2,16,1024]{2,1,0:T(8,128)S(1)}, u32[]{:S(2)}, u32[]{:S(2)}) collective-permute-start(f32[2,16,1024]{2,1,0:T(8,128)S(1)} %get-tuple-element.128), channel_id=1, source_target_pairs={{0,1},{1,3},{3,2},{2,4},{4,5},{5,7},{7,6},{6,8},{8,9},{9,11},{11,1... | collective-permute-start | bytes 393224 | tf_op jit(solution)/shard_map/ppermute | solution.py:850
  117.2 1.5 collective-permute-start.23
  119.7 4.7 %collective-permute-done.23.refs_2_ = f32[2,16,1024]{2,1,0:T(8,128)S(1)} collective-permute-done((f32[2,16,1024]{2,1,0:T(8,128)S(1)}, f32[2,16,1024]{2,1,0:T(8,128)S(1)}, u32[]{:S(2)}, u32[]{:S(2)}) %collective-permute-start.23) | collective-permute-done | bytes 131104 | tf_op jit(solution)/shard_map/ppermute | solution.py:851
  125.0 1.8 %collective-permute-start.29 = (f32[32,16,256]{2,1,0:T(8,128)S(1)}, f32[32,16,256]{2,1,0:T(8,128)S(1)}, u32[]{:S(2)}, u32[]{:S(2)}) collective-permute-start(f32[32,16,256]{2,1,0:T(8,128)S(1)} %get-tuple-element.135), channel_id=1, source_target_pairs={{0,2},{1,3},{2,0},{3,1},{4,6},{5,7},{6,4},{7,5},{8,10},{9,11},{10,... | collective-permute-start | bytes 1572872 | tf_op jit(solution)/shard_map/ppermute | solution.py:808
  126.8 7.0 %graph_xvp.1 = f32[48,128]{1,0:T(8,128)S(1)} custom-call(f32[32,16,1024]{2,1,0:T(8,128)S(1)} %get-tuple-element.125.refs_0_, f32[2,16,1024]{2,1,0:T(8,128)S(1)} %collective-permute-done.22.refs_1_, f32[2,16,1024]{2,1,0:T(8,128)S(1)} %collective-permute-done.23.refs_2_, f32[32,25,1024]{2,1,0:T(8,128)S(1)} %get-tuple-element.90.refs_5_.refs_3_, ...), custom_call_target="tpu_custom_call" | custom-call | flops 104857600 | bytes 9568256 | tf_op jit(solution)/shard_map/graph_xvp/pallas_call | solution.py:375
  135.3 2.2 %collective-permute-start.26 = (f32[48,128]{1,0:T(8,128)S(1)}, f32[48,128]{1,0:T(8,128)S(1)}, u32[]{:S(2)}, u32[]{:S(2)}) collective-permute-start(f32[48,128]{1,0:T(8,128)S(1)} %add.64), channel_id=1, source_target_pairs={{0,16},{1,17},{2,18},{3,19},{4,20},{5,21},{6,22},{7,23},{8,24},{9,... | collective-permute-start | bytes 73736 | tf_op jit(solution)/shard_map/ppermute | solution.py:801
  137.6 2.7 %collective-permute-start.27 = (f32[48,128]{1,0:T(8,128)S(1)}, f32[48,128]{1,0:T(8,128)S(1)}, u32[]{:S(2)}, u32[]{:S(2)}) collective-permute-start(f32[48,128]{1,0:T(8,128)S(1)} %add.64), channel_id=1, source_target_pairs={{0,24},{1,25},{2,26},{3,27},{4,28},{5,29},{6,30},{7,31},{8,16},{9,... | collective-permute-start | bytes 73736 | tf_op jit(solution)/shard_map/ppermute | solution.py:801
  140.3 2.9 %collective-permute-done.27 = f32[48,128]{1,0:T(8,128)S(1)} collective-permute-done((f32[48,128]{1,0:T(8,128)S(1)}, f32[48,128]{1,0:T(8,128)S(1)}, u32[]{:S(2)}, u32[]{:S(2)}) %collective-permute-start.27) | collective-permute-done | bytes 24608 | tf_op jit(solution)/shard_map/ppermute | solution.py:801
  145.5 2.2 %collective-permute-start.32 = (f32[48,128]{1,0:T(8,128)S(1)}, f32[48,128]{1,0:T(8,128)S(1)}, u32[]{:S(2)}, u32[]{:S(2)}) collective-permute-start(f32[48,128]{1,0:T(8,128)S(1)} %add_add_fusion.1), channel_id=1, source_target_pairs={{0,3},{1,2},{2,1},{3,0},{4,7},{5,6},{6,5},{7,4},{8,11},{9,10},{10,... | collective-permute-start | bytes 73736 | tf_op jit(solution)/shard_map/ppermute | solution.py:801
  148.7 1.4 collective-permute-done.32
  150.2 2.2 %collective-permute-start.33 = (f32[32,16,256]{2,1,0:T(8,128)S(1)}, f32[32,16,256]{2,1,0:T(8,128)S(1)}, u32[]{:S(2)}, u32[]{:S(2)}) collective-permute-start(f32[32,16,256]{2,1,0:T(8,128)S(1)} %get-tuple-element.145), channel_id=1, source_target_pairs={{0,3},{1,2},{2,1},{3,0},{4,7},{5,6},{6,5},{7,4},{8,11},{9,10},{10,... | collective-permute-start | bytes 1572872 | tf_op jit(solution)/shard_map/ppermute | solution.py:808
  152.4 9.0 %ritz.1 = (f32[1,16]{1,0:T(1,128)}, f32[48,16]{1,0:T(8,128)S(1)}) custom-call(f32[16,128]{1,0:T(8,128)S(1)} %add_add_fusion.2.gram_ref.first_ref, f32[48,128]{1,0:T(8,128)S(1)} %add_add_fusion.second_ref), custom_call_target="tpu_custom_call" | custom-call | flops 33554432 | bytes 65536 | tf_op jit(solution)/shard_map/ritz/pallas_call | solution.py:669
  161.8 5.2 %combine.1 = (f32[16,128,256]{2,1,0:T(8,128)}, f32[16,128,256]{2,1,0:T(8,128)}) custom-call(s32[9]{0:T(128)S(1)} %dynamic-slice_bitcast_fusion.1.info_ref.refs_0_, f32[48,16]{1,0:T(8,128)S(1)} %get-tuple-element.141.coeff_ref, f32[16,128,256]{2,1,0:T(8,128)S(1)} %copy-done, f32[16,128,256]{2,1,0:T(8,128)S(1)} %copy-done.1, ...), custom_call_target="tpu_custom_call" | custom-call | flops 104857600 | bytes 10485760 | tf_op jit(solution)/shard_map/combine/pallas_call | solution.py:738
  (72 shorter events, 16.0 us)
Async XLA Ops:
  0.6 6.4 %copy-start = (f32[16,128,256]{2,1,0:T(8,128)S(1)}, f32[16,128,256]{2,1,0:T(8,128)}, u32[]{:S(2)}) copy-start(f32[16,128,256]{2,1,0:T(8,128)} %x_ref.5) | copy-start | bytes 6291460
  0.6 6.3 %copy-start.2 = (f32[128,256]{1,0:T(8,128)S(1)}, f32[128,256]{1,0:T(8,128)}, u32[]{:S(2)}) copy-start(f32[128,256]{1,0:T(8,128)} %refs_0_.1) | copy-start | bytes 393220
  2.6 6.2 %collective-permute-start = (f32[2,33,256]{2,1,0:T(8,128)}, f32[2,33,256]{2,1,0:T(8,128)S(1)}, u32[]{:S(2)}, u32[]{:S(2)}) collective-permute-start(f32[2,33,256]{2,1,0:T(8,128)} %get-tuple-element.76), channel_id=1, source_target_pairs={{0,4},{4,8},{8,12},{12,16},{16,20},{20,24},{24,28},{1,5},{5,9},{9,... | collective-permute-start | bytes 202760 | tf_op jit(solution)/shard_map/ppermute | solution.py:814
  5.0 5.6 %collective-permute-start.1 = (f32[2,33,256]{2,1,0:T(8,128)}, f32[2,33,256]{2,1,0:T(8,128)S(1)}, u32[]{:S(2)}, u32[]{:S(2)}) collective-permute-start(f32[2,33,256]{2,1,0:T(8,128)} %get-tuple-element.77), channel_id=1, source_target_pairs={{4,0},{8,4},{12,8},{16,12},{20,16},{24,20},{28,24},{5,1},{9,5},{13... | collective-permute-start | bytes 202760 | tf_op jit(solution)/shard_map/ppermute | solution.py:815
  7.0 7.7 %copy-start.1 = (f32[16,128,256]{2,1,0:T(8,128)S(1)}, f32[16,128,256]{2,1,0:T(8,128)}, u32[]{:S(2)}) copy-start(f32[16,128,256]{2,1,0:T(8,128)} %p_ref.1) | copy-start | bytes 6291460
  11.1 15.1 %collective-permute-start.2 = (f32[39,16,256]{2,1,0:T(8,128)S(1)}, f32[39,16,256]{2,1,0:T(8,128)S(1)}, u32[]{:S(2)}, u32[]{:S(2)}) collective-permute-start(f32[39,16,256]{2,1,0:T(8,128)S(1)} %get-tuple-element.83), channel_id=1, source_target_pairs={{0,1},{1,0},{2,3},{3,2},{4,5},{5,4},{6,7},{7,6},{8,9},{9,8},{10,11... | collective-permute-start | bytes 1916936 | tf_op jit(solution)/shard_map/ppermute | solution.py:808
  12.7 16.9 %collective-permute-start.3 = (f32[39,16,256]{2,1,0:T(8,128)S(1)}, f32[39,16,256]{2,1,0:T(8,128)S(1)}, u32[]{:S(2)}, u32[]{:S(2)}) collective-permute-start(f32[39,16,256]{2,1,0:T(8,128)S(1)} %get-tuple-element.84), channel_id=1, source_target_pairs={{0,2},{1,3},{2,0},{3,1},{4,6},{5,7},{6,4},{7,5},{8,10},{9,11},{10,... | collective-permute-start | bytes 1916936 | tf_op jit(solution)/shard_map/ppermute | solution.py:808
  14.2 26.8 %collective-permute-start.4 = (f32[39,16,256]{2,1,0:T(8,128)S(1)}, f32[39,16,256]{2,1,0:T(8,128)S(1)}, u32[]{:S(2)}, u32[]{:S(2)}) collective-permute-start(f32[39,16,256]{2,1,0:T(8,128)S(1)} %get-tuple-element.85), channel_id=1, source_target_pairs={{0,3},{1,2},{2,1},{3,0},{4,7},{5,6},{6,5},{7,4},{8,11},{9,10},{10,... | collective-permute-start | bytes 1916936 | tf_op jit(solution)/shard_map/ppermute | solution.py:808
  17.1 49.3 %collective-permute-start.9 = (f32[36,16,256]{2,1,0:T(8,128)S(1)}, f32[36,16,256]{2,1,0:T(8,128)S(1)}, u32[]{:S(2)}, u32[]{:S(2)}) collective-permute-start(f32[36,16,256]{2,1,0:T(8,128)S(1)} %get-tuple-element.98), channel_id=1, source_target_pairs={{0,1},{1,0},{2,3},{3,2},{4,5},{5,4},{6,7},{7,6},{8,9},{9,8},{10,11... | collective-permute-start | bytes 1769480 | tf_op jit(solution)/shard_map/ppermute | solution.py:808
  18.7 47.8 %collective-permute-start.10 = (f32[36,16,256]{2,1,0:T(8,128)S(1)}, f32[36,16,256]{2,1,0:T(8,128)S(1)}, u32[]{:S(2)}, u32[]{:S(2)}) collective-permute-start(f32[36,16,256]{2,1,0:T(8,128)S(1)} %get-tuple-element.99), channel_id=1, source_target_pairs={{0,2},{1,3},{2,0},{3,1},{4,6},{5,7},{6,4},{7,5},{8,10},{9,11},{10,... | collective-permute-start | bytes 1769480 | tf_op jit(solution)/shard_map/ppermute | solution.py:808
  26.3 40.2 %collective-permute-start.11 = (f32[36,16,256]{2,1,0:T(8,128)S(1)}, f32[36,16,256]{2,1,0:T(8,128)S(1)}, u32[]{:S(2)}, u32[]{:S(2)}) collective-permute-start(f32[36,16,256]{2,1,0:T(8,128)S(1)} %get-tuple-element.100), channel_id=1, source_target_pairs={{0,3},{1,2},{2,1},{3,0},{4,7},{5,6},{6,5},{7,4},{8,11},{9,10},{10,... | collective-permute-start | bytes 1769480 | tf_op jit(solution)/shard_map/ppermute | solution.py:808
  44.1 18.7 %copy-start.9 = (bf16[1024,1024]{1,0:T(8,128)(2,1)S(1)}, bf16[1024,1024]{1,0:T(8,128)(2,1)}, u32[]{:S(2)}) copy-start(bf16[1024,1024]{1,0:T(8,128)(2,1)} %constant.45.clone.rest_0_.rest_1_) | copy-start | bytes 6291460
  44.1 18.7 %copy-start.10 = (bf16[1024,1024]{1,0:T(8,128)(2,1)S(1)}, bf16[1024,1024]{1,0:T(8,128)(2,1)}, u32[]{:S(2)}) copy-start(bf16[1024,1024]{1,0:T(8,128)(2,1)} %constant.46.clone.rest_1_.rest_2_) | copy-start | bytes 6291460
  51.2 5.5 %collective-permute-start.5 = (f32[16,128]{1,0:T(8,128)S(1)}, f32[16,128]{1,0:T(8,128)S(1)}, u32[]{:S(2)}, u32[]{:S(2)}) collective-permute-start(f32[16,128]{1,0:T(8,128)S(1)} %get-tuple-element.92), channel_id=1, source_target_pairs={{0,4},{1,5},{2,6},{3,7},{4,0},{5,1},{6,2},{7,3},{8,12},{9,13},{10,... | collective-permute-start | bytes 24584 | tf_op jit(solution)/shard_map/ppermute | solution.py:801
  56.7 4.5 %collective-permute-start.7 = (f32[16,128]{1,0:T(8,128)S(1)}, f32[16,128]{1,0:T(8,128)S(1)}, u32[]{:S(2)}, u32[]{:S(2)}) collective-permute-start(f32[16,128]{1,0:T(8,128)S(1)} %add.56), channel_id=1, source_target_pairs={{0,16},{1,17},{2,18},{3,19},{4,20},{5,21},{6,22},{7,23},{8,24},{9,... | collective-permute-start | bytes 24584 | tf_op jit(solution)/shard_map/ppermute | solution.py:801
  59.2 7.1 %collective-permute-start.8 = (f32[16,128]{1,0:T(8,128)S(1)}, f32[16,128]{1,0:T(8,128)S(1)}, u32[]{:S(2)}, u32[]{:S(2)}) collective-permute-start(f32[16,128]{1,0:T(8,128)S(1)} %add.56), channel_id=1, source_target_pairs={{0,24},{1,25},{2,26},{3,27},{4,28},{5,29},{6,30},{7,31},{8,16},{9,... | collective-permute-start | bytes 24584 | tf_op jit(solution)/shard_map/ppermute | solution.py:801
  61.3 5.1 %collective-permute-start.6 = (f32[16,128]{1,0:T(8,128)S(1)}, f32[16,128]{1,0:T(8,128)S(1)}, u32[]{:S(2)}, u32[]{:S(2)}) collective-permute-start(f32[16,128]{1,0:T(8,128)S(1)} %add.56), channel_id=1, source_target_pairs={{0,8},{1,9},{2,10},{3,11},{4,12},{5,13},{6,14},{7,15},{8,0},{9,1},... | collective-permute-start | bytes 24584 | tf_op jit(solution)/shard_map/ppermute | solution.py:801
  66.5 7.2 %collective-permute-start.13 = (f32[16,128]{1,0:T(8,128)S(1)}, f32[16,128]{1,0:T(8,128)S(1)}, u32[]{:S(2)}, u32[]{:S(2)}) collective-permute-start(f32[16,128]{1,0:T(8,128)S(1)} %add_add_fusion.3), channel_id=1, source_target_pairs={{0,2},{1,3},{2,0},{3,1},{4,6},{5,7},{6,4},{7,5},{8,10},{9,11},{10,... | collective-permute-start | bytes 24584 | tf_op jit(solution)/shard_map/ppermute | solution.py:801
  68.0 5.6 %collective-permute-start.14 = (f32[16,128]{1,0:T(8,128)S(1)}, f32[16,128]{1,0:T(8,128)S(1)}, u32[]{:S(2)}, u32[]{:S(2)}) collective-permute-start(f32[16,128]{1,0:T(8,128)S(1)} %add_add_fusion.3), channel_id=1, source_target_pairs={{0,3},{1,2},{2,1},{3,0},{4,7},{5,6},{6,5},{7,4},{8,11},{9,10},{10,... | collective-permute-start | bytes 24584 | tf_op jit(solution)/shard_map/ppermute | solution.py:801
  69.2 4.4 %collective-permute-start.12 = (f32[16,128]{1,0:T(8,128)S(1)}, f32[16,128]{1,0:T(8,128)S(1)}, u32[]{:S(2)}, u32[]{:S(2)}) collective-permute-start(f32[16,128]{1,0:T(8,128)S(1)} %add_add_fusion.3), channel_id=1, source_target_pairs={{0,1},{1,0},{2,3},{3,2},{4,5},{5,4},{6,7},{7,6},{8,9},{9,8},{10,11... | collective-permute-start | bytes 24584 | tf_op jit(solution)/shard_map/ppermute | solution.py:801
  70.0 3.7 %copy-start.5 = (f32[32,1024]{1,0:T(8,128)S(1)}, f32[32,1024]{1,0:T(8,128)}, u32[]{:S(2)}) copy-start(f32[32,1024]{1,0:T(8,128)} %constant.47.clone.eps_ref.refs_7_) | copy-start | bytes 393220
  70.0 3.7 %copy-start.6 = (f32[1,1024]{1,0:T(1,128)S(1)}, f32[1,1024]{1,0:T(1,128)}, u32[]{:S(2)}) copy-start(f32[1,1024]{1,0:T(1,128)} %constant.48.clone.last_ref.refs_8_) | copy-start | bytes 12292
  73.7 15.8 %copy-start.3 = (f32[5,1024]{1,0:T(8,128)S(1)}, f32[5,1024]{1,0:T(8,128)}, u32[]{:S(2)}) copy-start(f32[5,1024]{1,0:T(8,128)} %constant.49.clone.gain_ref) | copy-start | bytes 61444
  73.7 15.8 %copy-start.4 = (f32[5,1024]{1,0:T(8,128)S(1)}, f32[5,1024]{1,0:T(8,128)}, u32[]{:S(2)}) copy-start(f32[5,1024]{1,0:T(8,128)} %constant.50.clone.cross_ref) | copy-start | bytes 61444
  77.4 6.1 %collective-permute-start.15 = (f32[2,16,1024]{2,1,0:T(8,128)S(1)}, f32[2,16,1024]{2,1,0:T(8,128)S(1)}, u32[]{:S(2)}, u32[]{:S(2)}) collective-permute-start(f32[2,16,1024]{2,1,0:T(8,128)S(1)} %get-tuple-element.104.refs_0_), channel_id=1, source_target_pairs={{0,1},{1,0},{2,3},{3,2},{4,5},{5,4},{6,7},{7,6},{8,9},{9,8},{10,11... | collective-permute-start | bytes 393224 | tf_op jit(solution)/shard_map/ppermute | solution.py:838
  78.7 8.7 %collective-permute-start.16 = (f32[2,16,1024]{2,1,0:T(8,128)S(1)}, f32[2,16,1024]{2,1,0:T(8,128)S(1)}, u32[]{:S(2)}, u32[]{:S(2)}) collective-permute-start(f32[2,16,1024]{2,1,0:T(8,128)S(1)} %get-tuple-element.104.refs_0_), channel_id=1, source_target_pairs={{0,3},{1,2},{2,1},{3,0},{4,7},{5,6},{6,5},{7,4},{8,11},{9,10},{10,... | collective-permute-start | bytes 393224 | tf_op jit(solution)/shard_map/ppermute | solution.py:838
  80.4 9.0 %collective-permute-start.17 = (f32[2,16,1024]{2,1,0:T(8,128)S(1)}, f32[2,16,1024]{2,1,0:T(8,128)S(1)}, u32[]{:S(2)}, u32[]{:S(2)}) collective-permute-start(f32[2,16,1024]{2,1,0:T(8,128)S(1)} %get-tuple-element.104.refs_0_), channel_id=1, source_target_pairs={{0,2},{1,3},{2,0},{3,1},{4,6},{5,7},{6,4},{7,5},{8,10},{9,11},{10,... | collective-permute-start | bytes 393224 | tf_op jit(solution)/shard_map/ppermute | solution.py:838
  90.1 1.4 collective-permute-start.18
  92.1 16.9 %copy-start.7 = (bf16[1024,1024]{1,0:T(8,128)(2,1)S(1)}, bf16[1024,1024]{1,0:T(8,128)(2,1)}, u32[]{:S(2)}) copy-start(bf16[1024,1024]{1,0:T(8,128)(2,1)} %constant.43.clone.refs_9_) | copy-start | bytes 6291460
  92.1 16.9 %copy-start.8 = (bf16[1024,1024]{1,0:T(8,128)(2,1)S(1)}, bf16[1024,1024]{1,0:T(8,128)(2,1)}, u32[]{:S(2)}) copy-start(bf16[1024,1024]{1,0:T(8,128)(2,1)} %constant.44.clone.refs_10_) | copy-start | bytes 6291460
  92.1 13.2 %collective-permute-start.19 = (f32[2,16,1024]{2,1,0:T(8,128)S(1)}, f32[2,16,1024]{2,1,0:T(8,128)S(1)}, u32[]{:S(2)}, u32[]{:S(2)}) collective-permute-start(f32[2,16,1024]{2,1,0:T(8,128)S(1)} %get-tuple-element.114.refs_0_), channel_id=1, source_target_pairs={{0,8},{1,9},{2,10},{3,11},{4,12},{5,13},{6,14},{7,15},{8,0},{9,1},... | collective-permute-start | bytes 393224 | tf_op jit(solution)/shard_map/ppermute | solution.py:838
  95.4 12.9 %collective-permute-start.20 = (f32[2,16,1024]{2,1,0:T(8,128)S(1)}, f32[2,16,1024]{2,1,0:T(8,128)S(1)}, u32[]{:S(2)}, u32[]{:S(2)}) collective-permute-start(f32[2,16,1024]{2,1,0:T(8,128)S(1)} %get-tuple-element.114.refs_0_), channel_id=1, source_target_pairs={{0,16},{1,17},{2,18},{3,19},{4,20},{5,21},{6,22},{7,23},{8,24},{9,... | collective-permute-start | bytes 393224 | tf_op jit(solution)/shard_map/ppermute | solution.py:838
  96.5 11.8 %collective-permute-start.21 = (f32[2,16,1024]{2,1,0:T(8,128)S(1)}, f32[2,16,1024]{2,1,0:T(8,128)S(1)}, u32[]{:S(2)}, u32[]{:S(2)}) collective-permute-start(f32[2,16,1024]{2,1,0:T(8,128)S(1)} %get-tuple-element.114.refs_0_), channel_id=1, source_target_pairs={{0,24},{1,25},{2,26},{3,27},{4,28},{5,29},{6,30},{7,31},{8,16},{9,... | collective-permute-start | bytes 393224 | tf_op jit(solution)/shard_map/ppermute | solution.py:838
  114.7 4.9 %collective-permute-start.22 = (f32[2,16,1024]{2,1,0:T(8,128)S(1)}, f32[2,16,1024]{2,1,0:T(8,128)S(1)}, u32[]{:S(2)}, u32[]{:S(2)}) collective-permute-start(f32[2,16,1024]{2,1,0:T(8,128)S(1)} %get-tuple-element.128), channel_id=1, source_target_pairs={{0,1},{1,3},{3,2},{2,4},{4,5},{5,7},{7,6},{6,8},{8,9},{9,11},{11,1... | collective-permute-start | bytes 393224 | tf_op jit(solution)/shard_map/ppermute | solution.py:850
  117.2 7.2 %collective-permute-start.23 = (f32[2,16,1024]{2,1,0:T(8,128)S(1)}, f32[2,16,1024]{2,1,0:T(8,128)S(1)}, u32[]{:S(2)}, u32[]{:S(2)}) collective-permute-start(f32[2,16,1024]{2,1,0:T(8,128)S(1)} %get-tuple-element.129), channel_id=1, source_target_pairs={{1,0},{3,1},{2,3},{4,2},{5,4},{7,5},{6,7},{8,6},{9,8},{11,9},{10,1... | collective-permute-start | bytes 393224 | tf_op jit(solution)/shard_map/ppermute | solution.py:851
  124.4 19.7 %collective-permute-start.28 = (f32[32,16,256]{2,1,0:T(8,128)S(1)}, f32[32,16,256]{2,1,0:T(8,128)S(1)}, u32[]{:S(2)}, u32[]{:S(2)}) collective-permute-start(f32[32,16,256]{2,1,0:T(8,128)S(1)} %get-tuple-element.134), channel_id=1, source_target_pairs={{0,1},{1,0},{2,3},{3,2},{4,5},{5,4},{6,7},{7,6},{8,9},{9,8},{10,11... | collective-permute-start | bytes 1572872 | tf_op jit(solution)/shard_map/ppermute | solution.py:808
  125.0 19.1 %collective-permute-start.29 = (f32[32,16,256]{2,1,0:T(8,128)S(1)}, f32[32,16,256]{2,1,0:T(8,128)S(1)}, u32[]{:S(2)}, u32[]{:S(2)}) collective-permute-start(f32[32,16,256]{2,1,0:T(8,128)S(1)} %get-tuple-element.135), channel_id=1, source_target_pairs={{0,2},{1,3},{2,0},{3,1},{4,6},{5,7},{6,4},{7,5},{8,10},{9,11},{10,... | collective-permute-start | bytes 1572872 | tf_op jit(solution)/shard_map/ppermute | solution.py:808
  133.9 1.5 collective-permute-start.24
  135.3 4.9 %collective-permute-start.26 = (f32[48,128]{1,0:T(8,128)S(1)}, f32[48,128]{1,0:T(8,128)S(1)}, u32[]{:S(2)}, u32[]{:S(2)}) collective-permute-start(f32[48,128]{1,0:T(8,128)S(1)} %add.64), channel_id=1, source_target_pairs={{0,16},{1,17},{2,18},{3,19},{4,20},{5,21},{6,22},{7,23},{8,24},{9,... | collective-permute-start | bytes 73736 | tf_op jit(solution)/shard_map/ppermute | solution.py:801
  137.6 5.6 %collective-permute-start.27 = (f32[48,128]{1,0:T(8,128)S(1)}, f32[48,128]{1,0:T(8,128)S(1)}, u32[]{:S(2)}, u32[]{:S(2)}) collective-permute-start(f32[48,128]{1,0:T(8,128)S(1)} %add.64), channel_id=1, source_target_pairs={{0,24},{1,25},{2,26},{3,27},{4,28},{5,29},{6,30},{7,31},{8,16},{9,... | collective-permute-start | bytes 73736 | tf_op jit(solution)/shard_map/ppermute | solution.py:801
  140.3 3.8 %collective-permute-start.25 = (f32[48,128]{1,0:T(8,128)S(1)}, f32[48,128]{1,0:T(8,128)S(1)}, u32[]{:S(2)}, u32[]{:S(2)}) collective-permute-start(f32[48,128]{1,0:T(8,128)S(1)} %add.64), channel_id=1, source_target_pairs={{0,8},{1,9},{2,10},{3,11},{4,12},{5,13},{6,14},{7,15},{8,0},{9,1},... | collective-permute-start | bytes 73736 | tf_op jit(solution)/shard_map/ppermute | solution.py:801
  144.1 3.9 %collective-permute-start.30 = (f32[48,128]{1,0:T(8,128)S(1)}, f32[48,128]{1,0:T(8,128)S(1)}, u32[]{:S(2)}, u32[]{:S(2)}) collective-permute-start(f32[48,128]{1,0:T(8,128)S(1)} %add_add_fusion.1), channel_id=1, source_target_pairs={{0,1},{1,0},{2,3},{3,2},{4,5},{5,4},{6,7},{7,6},{8,9},{9,8},{10,11... | collective-permute-start | bytes 73736 | tf_op jit(solution)/shard_map/ppermute | solution.py:801
  144.9 3.8 %collective-permute-start.31 = (f32[48,128]{1,0:T(8,128)S(1)}, f32[48,128]{1,0:T(8,128)S(1)}, u32[]{:S(2)}, u32[]{:S(2)}) collective-permute-start(f32[48,128]{1,0:T(8,128)S(1)} %add_add_fusion.1), channel_id=1, source_target_pairs={{0,2},{1,3},{2,0},{3,1},{4,6},{5,7},{6,4},{7,5},{8,10},{9,11},{10,... | collective-permute-start | bytes 73736 | tf_op jit(solution)/shard_map/ppermute | solution.py:801
  145.5 4.7 %collective-permute-start.32 = (f32[48,128]{1,0:T(8,128)S(1)}, f32[48,128]{1,0:T(8,128)S(1)}, u32[]{:S(2)}, u32[]{:S(2)}) collective-permute-start(f32[48,128]{1,0:T(8,128)S(1)} %add_add_fusion.1), channel_id=1, source_target_pairs={{0,3},{1,2},{2,1},{3,0},{4,7},{5,6},{6,5},{7,4},{8,11},{9,10},{10,... | collective-permute-start | bytes 73736 | tf_op jit(solution)/shard_map/ppermute | solution.py:801
  150.2 11.7 %collective-permute-start.33 = (f32[32,16,256]{2,1,0:T(8,128)S(1)}, f32[32,16,256]{2,1,0:T(8,128)S(1)}, u32[]{:S(2)}, u32[]{:S(2)}) collective-permute-start(f32[32,16,256]{2,1,0:T(8,128)S(1)} %get-tuple-element.145), channel_id=1, source_target_pairs={{0,3},{1,2},{2,1},{3,0},{4,7},{5,6},{6,5},{7,4},{8,11},{9,10},{10,... | collective-permute-start | bytes 1572872 | tf_op jit(solution)/shard_map/ppermute | solution.py:808

commit v5 on v4

--- a/solution.py
+++ b/solution.py
@@ -290,9 +290,11 @@
     )(info, *pieces)
 
 
-def graph_kernel(order, keep, lane_shift, chunks, *refs):
+def graph_kernel(order, keep, lane_shift, chunks, part, *refs):
     if chunks:
         info_ref, chunk_refs, refs = refs[0], refs[1 : 1 + chunks], refs[1 + chunks :]
+    elif part == "inner":
+        v_ref, *refs = refs
     else:
         v_ref, top_ref, bot_ref, *refs = refs
     (w_ref, deg_ref), refs = refs[:2], refs[2:]
@@ -301,21 +303,25 @@
     own_ref = refs.pop(0) if chunks else None
     gram_ref, pad_ref, acc_ref, sum_ref = refs
     depth, cols = deg_ref.shape
-    fields = pad_ref.shape[1]
+    fields = sum_ref.shape[1]
     if chunks:
         spread(info_ref, chunk_refs, pad_ref)
-    else:
+    elif part == "outer":
         pad_ref[0:2] = top_ref[...]
-        pad_ref[2 : 2 + depth] = v_ref[...]
+        pad_ref[2:6] = v_ref[0:4]
+        pad_ref[depth - 2 : depth + 2] = v_ref[depth - 4 : depth]
         pad_ref[2 + depth : 4 + depth] = bot_ref[...]
     parts = len(order)
     groups = fields // 8
     width = 256
+    source_ref, shift = (v_ref, 2) if part == "inner" else (pad_ref, 0)
 
     def one_row(r, acc):
         for c in range(cols // width):
             lanes = slice(c * width, (c + 1) * width)
-            values = [pad_ref[r + a, :, lanes].reshape(groups, 8, width) for a in range(5)]
+            values = [
+                source_ref[r + a - shift, :, lanes].reshape(groups, 8, width) for a in range(5)
+            ]
             for b in range(-2, 3):
                 total = None
                 for a in range(-2, 3):
@@ -330,7 +336,7 @@
             result = result + pltpu.roll(sum_ref[b + 2], (-b) % cols, 1)
         if keep:
             g_ref[r] = result
-        own = pad_ref[r + 2]
+        own = source_ref[r + 2 - shift]
         if chunks:
             own_ref[r] = own
         weighted = deg_ref[pl.ds(r, 1), :] * own
@@ -351,7 +357,13 @@
         )
 
     start = jnp.zeros((2 * parts * fields, 4 * fields), f32)
-    acc = lax.fori_loop(0, depth, one_row, start, unroll=UNROLL)
+    if part == "outer":
+        acc = start
+        for r in (0, 1, depth - 2, depth - 1):
+            acc = one_row(r, acc)
+    else:
+        skip = 2 if part == "inner" else 0
+        acc = lax.fori_loop(skip, depth - skip, one_row, start, unroll=UNROLL)
     half = parts * fields
     acc_ref[...] = jnp.zeros(acc_ref.shape, f32)
     acc_ref[:, 0 : 4 * fields] = acc[:half] + acc[half:]
@@ -364,7 +376,7 @@
     gram_ref[...] = both
 
 
-def apply_graph(order, keep, lane_shift, fields_in, w, deg, *others, info=None):
+def apply_graph(order, keep, lane_shift, fields_in, w, deg, *others, info=None, part="all"):
     depth, cols = deg.shape
     fields = fields_in[0].shape[1]
     parts = len(order)
@@ -373,65 +385,23 @@
     out_shape += [room(parts * fields, LANES)]
     args = ((info,) if chunks else ()) + tuple(fields_in) + (w, deg) + others
     return pl.pallas_call(
-        functools.partial(graph_kernel, order, keep, lane_shift, chunks),
+        functools.partial(graph_kernel, order, keep, lane_shift, chunks, part),
         out_shape=tuple(out_shape),
         in_specs=[SMEM] * int(chunks > 0) + [VMEM] * (len(args) - int(chunks > 0)),
         out_specs=(VMEM,) * len(out_shape),
         scratch_shapes=[
-            pltpu.VMEM((depth + 4, fields, cols), f32),
+            pltpu.VMEM((8 if part == "inner" else depth + 4, fields, cols), f32),
             pltpu.VMEM((parts * fields, LANES), f32),
             pltpu.VMEM((5, fields, cols), f32),
         ],
         compiler_params=params(w, deg, *fields_in, *others, *out_shape, room(depth + 9, fields, cols)),
         cost_estimate=cost(50 * fields * depth * cols * 4, 4 * cols * depth * (25 + 3 * fields)),
-        name="graph_" + "".join(order),
+        name="graph_" + "".join(order) + "_" + part,
     )(*args)
 
 
-def forward_kernel(scaled, x_ref, *rest):
-    if scaled:
-        deg_ref, high_ref, low_ref, out_ref = rest
-    else:
-        high_ref, low_ref, out_ref = rest
-    depth, fields, _ = x_ref.shape
-    cols = high_ref.shape[0]
-    block = math.gcd(depth, 16)
-    contract = (((1,), (0,)), ((), ()))
-
-    def one_block(i, _):
-        start = i * block
-        value = x_ref[pl.ds(start, block)]
-        if scaled:
-            value = value * deg_ref[pl.ds(start, block), :][:, None, :]
-        high, low = split(value.reshape(block * fields, cols))
-        result = lax.dot_general(high, high_ref[...], contract, preferred_element_type=f32)
-        result += lax.dot_general(high, low_ref[...], contract, preferred_element_type=f32)
-        result += lax.dot_general(low, high_ref[...], contract, preferred_element_type=f32)
-        out_ref[pl.ds(start, block)] = result.reshape(block, fields, cols)
-        return 0
-
-    lax.fori_loop(0, depth // block, one_block, 0)
-
-
-def cosine_forward(x, deg, high, low, depth, fields):
-    cols = high.shape[0]
-    args = (x,) + ((deg,) if deg is not None else ()) + (high, low)
-    return pl.pallas_call(
-        functools.partial(forward_kernel, deg is not None),
-        out_shape=jax.ShapeDtypeStruct((depth, fields, cols), f32),
-        in_specs=[pl.BlockSpec(memory_space=pltpu.VMEM)] * len(args),
-        out_specs=pl.BlockSpec(memory_space=pltpu.VMEM),
-        compiler_params=params(*args, room(depth, fields, cols), extra=12 * 2**20),
-        cost_estimate=cost(6 * depth * fields * cols * cols, 4 * cols * (2 * depth * fields + cols)),
-        name="cosine_forward",
-    )(*args)
-
-
-def solve_kernel(gram_ref, fg_ref, fd_ref, eps_ref, last_ref, f_ref, ends_ref):
-    depth, fields, cols = fg_ref.shape
-    gram = gram_ref[...]
-    affinity = pltpu.roll(gram, LANES - 4 * fields, 1)[:, :fields]
-    mass = pltpu.roll(gram, LANES - 5 * fields, 1)[:, :fields]
+def solve_rayleigh(affinity, mass):
+    fields = mass.shape[0]
     row = lax.broadcasted_iota(jnp.int32, (fields, fields), 0)
     for k in range(fields):
         inverse = 1.0 / mass[k : k + 1, k : k + 1]
@@ -440,44 +410,57 @@
         affinity_row = affinity[k : k + 1, :] * inverse
         affinity = jnp.where(row == k, affinity_row, affinity - column * affinity_row)
         mass = jnp.where(row == k, mass_row, mass - column * mass_row)
-    ray = split3(affinity.T)
+    return affinity
+
+
+def residual_kernel(gram_ref, g_ref, x_ref, deg_ref, eps_ref, last_ref, high_ref, low_ref, f_ref, ends_ref):
+    depth, fields, cols = x_ref.shape
+    gram = gram_ref[...]
+    affinity = pltpu.roll(gram, LANES - 4 * fields, 1)[:, :fields]
+    mass = pltpu.roll(gram, LANES - 5 * fields, 1)[:, :fields]
+    ray = split3(solve_rayleigh(affinity, mass).T)
     left = jnp.concatenate([ray[i] for i in (0, 0, 0, 1, 1, 2)], 1)
-
-    def one_row(r, carry):
-        piece = split3(fd_ref[r])
-        right = jnp.concatenate([piece[i] for i in (0, 1, 2, 0, 1, 0)], 0)
-        value = fg_ref[r] - jnp.dot(left, right, preferred_element_type=f32)
-        f_ref[r] = value
-        keep = eps_ref[pl.ds(jnp.maximum(r - 1, 0), 1), :]
-        return value + (carry - keep * carry)
-
-    down = lax.fori_loop(0, depth, one_row, jnp.zeros((fields, cols), f32), unroll=UNROLL)
-
-    def back_row(i, carry):
-        r = depth - 1 - i
+    block = math.gcd(depth, 16)
+    dot = functools.partial(jnp.dot, preferred_element_type=f32)
+
+    def one_block(i, _):
+        start = pl.multiple_of(i * block, block)
+        rows = []
+        for r in range(block):
+            piece = split3(x_ref[start + r] * deg_ref[pl.ds(start + r, 1), :])
+            right = jnp.concatenate([piece[i] for i in (0, 1, 2, 0, 1, 0)], 0)
+            rows.append(g_ref[start + r] - dot(left, right))
+        high, low = split(jnp.concatenate(rows, 0))
+        result = dot(high, high_ref[...]) + dot(high, low_ref[...]) + dot(low, high_ref[...])
+        f_ref[pl.ds(start, block)] = result.reshape(block, fields, cols)
+        return 0
+
+    lax.fori_loop(0, depth // block, one_block, 0)
+
+    def sweep(i, carry):
+        up, down = carry
         keep = eps_ref[pl.ds(jnp.maximum(i - 1, 0), 1), :]
-        return f_ref[r] + (carry - keep * carry)
-
-    up = lax.fori_loop(0, depth, back_row, jnp.zeros((fields, cols), f32), unroll=UNROLL)
+        return f_ref[depth - 1 - i] + (up - keep * up), f_ref[i] + (down - keep * down)
+
+    zero = jnp.zeros((fields, cols), f32)
+    up, down = lax.fori_loop(0, depth, sweep, (zero, zero), unroll=UNROLL)
     last = last_ref[...]
     ends_ref[0] = up * last
     ends_ref[1] = down * last
 
 
-def row_solve(gram, fg, fd, eps, last):
-    depth, fields, cols = fg.shape
-    return pl.pallas_call(
-        solve_kernel,
-        out_shape=(
-            jax.ShapeDtypeStruct((depth, fields, cols), f32),
-            jax.ShapeDtypeStruct((2, fields, cols), f32),
-        ),
-        in_specs=[pl.BlockSpec(memory_space=pltpu.VMEM)] * 5,
-        out_specs=(pl.BlockSpec(memory_space=pltpu.VMEM),) * 2,
-        compiler_params=params(fg, fd, eps, room(depth, fields, cols)),
-        cost_estimate=cost(200 * depth * fields * cols, 4 * 3 * depth * fields * cols),
-        name="row_solve",
-    )(gram, fg, fd, eps, last)
+def residual_spectrum(gram, g, x, deg, eps, last, high, low):
+    depth, fields, cols = x.shape
+    out_shape = (room(depth, fields, cols), room(2, fields, cols))
+    return pl.pallas_call(
+        residual_kernel,
+        out_shape=out_shape,
+        in_specs=[VMEM] * 8,
+        out_specs=(VMEM,) * 2,
+        compiler_params=params(g, x, deg, high, low, *out_shape, extra=12 * 2**20),
+        cost_estimate=cost(6 * depth * fields * cols * cols, 12 * depth * fields * cols),
+        name="residual_spectrum",
+    )(gram, g, x, deg, eps, last, high, low)
 
 
 def merge_kernel(level, count, last, info_ref, gain_ref, cross_ref, *refs):
@@ -530,28 +513,18 @@
         flux_top = flux_top + g * flux_ref[level : level + 1, :]
         flux_bot = flux_bot - g * flux_ref[levels + level : levels + level + 1, :]
 
-    u_ref[0] = f_ref[0] + flux_top
-
-    def down_row(r, carry):
-        keep = eps_ref[pl.ds(r - 1, 1), :]
-        value = f_ref[r] + (carry - keep * carry)
+    value = f_ref[0] + flux_top
+    u_ref[0] = value
+    for r in range(1, depth):
+        value = f_ref[r] + (value - eps_ref[r - 1 : r, :] * value)
         u_ref[r] = value
-        return value
-
-    value = lax.fori_loop(1, depth, down_row, u_ref[0])
     value = (value + flux_bot) * last_ref[...]
     u_ref[depth - 1] = value
-
-    def up_row(i, carry):
-        r = depth - 2 - i
-        keep = eps_ref[pl.ds(r, 1), :]
-        total = u_ref[r] + carry
-        total = total - keep * total
-        u_ref[r] = total
-        return total
-
-    lax.fori_loop(0, depth - 1, up_row, value)
-    block = 8
+    for r in range(depth - 2, -1, -1):
+        value = u_ref[r] + value
+        value = value - eps_ref[r : r + 1, :] * value
+        u_ref[r] = value
+    block = math.gcd(depth, 16)
 
     def one_block(i, _):
         start = i * block
@@ -680,13 +653,17 @@
     )(first, second)
 
 
-def combine_kernel(chunks, info_ref, coeff_ref, x_ref, p_ref, *refs):
-    pieces, (block_ref, direction_ref, h_ref, high_ref, low_ref) = refs[:chunks], refs[chunks:]
+def combine_kernel(count, begun, info_ref, coeff_ref, x_ref, p_ref, *refs):
+    pieces, refs = refs[:count], refs[count:]
+    if begun:
+        _, _, high_ref, low_ref, block_ref, direction_ref, h_ref = refs
+    else:
+        block_ref, direction_ref, high_ref, low_ref, h_ref = refs
     fields = x_ref.shape[0]
     width = x_ref.shape[2]
     group = 8 * fields
 
-    @pl.when(pl.program_id(0) == 0)
+    @pl.when((pl.program_id(0) == 0) & (not begun))
     def _():
         r = lax.broadcasted_iota(jnp.int32, (group, fields), 0)
         c = lax.broadcasted_iota(jnp.int32, (group, fields), 1)
@@ -707,7 +684,7 @@
             lanes = slice(part * group, (part + 1) * group)
             high_ref[:, lanes], low_ref[:, lanes] = split(wide)
 
-    for d in range(chunks):
+    for d in range(count):
 
         @pl.when(pl.program_id(0) == d)
         def _(d=d):
@@ -729,27 +706,33 @@
         direction_ref[:, rows, :] = direction.reshape(fields, 8, width)
 
 
-def combine(info, coeffs, x, p, pieces):
+def combine(info, coeffs, x, p, pieces, chunks, first=0, begun=()):
     fields, rows, width = x.shape
-    chunks = len(pieces)
+    count = len(pieces)
     depth = rows // chunks
-    spec = pl.BlockSpec((fields, depth, width), lambda i, s: (0, s[1 + chunks + i], 0))
+    spec = pl.BlockSpec((fields, depth, width), lambda i, s: (0, s[1 + chunks + first + i], 0))
     whole = pl.BlockSpec((depth, fields, width), lambda i, s: (0, 0, 0))
-    return pl.pallas_call(
-        functools.partial(combine_kernel, chunks),
-        out_shape=(room(fields, rows, width),) * 2,
+    left = pl.BlockSpec(memory_space=pl.ANY)
+    wide = (8 * fields, 24 * fields)
+    same = pl.BlockSpec(wide, lambda i, s: (0, 0))
+    again = (jax.ShapeDtypeStruct(wide, bf16),) * 2
+    return pl.pallas_call(
+        functools.partial(combine_kernel, count, bool(begun)),
+        out_shape=(room(fields, rows, width),) * 2 + (() if begun else again),
         grid_spec=pltpu.PrefetchScalarGridSpec(
             num_scalar_prefetch=1,
-            grid=(chunks,),
-            in_specs=[pl.BlockSpec(coeffs.shape, lambda i, s: (0, 0)), spec, spec] + [whole] * chunks,
-            out_specs=(spec, spec),
-            scratch_shapes=[pltpu.VMEM((depth, fields, width), f32)]
-            + [pltpu.VMEM((8 * fields, 24 * fields), bf16)] * 2,
+            grid=(count,),
+            in_specs=[pl.BlockSpec(coeffs.shape, lambda i, s: (0, 0)), spec, spec]
+            + [whole] * count
+            + ([left, left, same, same] if begun else []),
+            out_specs=(spec, spec) + (() if begun else (same, same)),
+            scratch_shapes=[pltpu.VMEM((depth, fields, width), f32)],
         ),
+        input_output_aliases={4 + count + i: i for i in range(2)} if begun else {},
         compiler_params=params(room(16 * depth, fields, width)),
-        cost_estimate=cost(200 * rows * fields * width, 20 * rows * fields * width),
+        cost_estimate=cost(50 * count * depth * fields * width, 20 * count * depth * fields * width),
         name="combine",
-    )(info, coeffs, x, p, *pieces)
+    )(info, coeffs, x, p, *pieces, *begun)
 
 
 def ring_order(count):
@@ -816,16 +799,17 @@
     x_pieces = pack(info, start_block, intensity, chunks)
     x_pieces = exchange(fill(info, above, below, x_pieces, 0, True))
     p_pieces = pack(info, old_direction, None, chunks)
-    p_pieces = exchange(fill(info, above, below, p_pieces, fields, False))
+    p_own, *p_early, p_late = fill(info, above, below, p_pieces, fields, False)
+    p_early = [away(piece, d) for d, piece in enumerate(p_early, 1)]
+    p_late, x_pieces[1] = lax.optimization_barrier((p_late, x_pieces[1]))
+    p_pieces = [p_own, *p_early, away(p_late, chunks - 1)]
     x_pieces, flux = lax.optimization_barrier((x_pieces, flux))
     w, deg = make_weights(info, x_pieces, depth, rows)
     graph_x, x, gram_x = apply_graph(("v",), True, 4 * fields, x_pieces, w, deg, info=info)
     gram_x, _ = add_up(gram_x, row_groups)
     gram_x, p_pieces = lax.optimization_barrier((gram_x, p_pieces))
     gram_x, _ = add_up(gram_x, col_groups)
-    spectrum_g = cosine_forward(graph_x, None, high_t, low_t, depth, fields)
-    spectrum_d = cosine_forward(x, deg, high_t, low_t, depth, fields)
-    f, ends = row_solve(gram_x, spectrum_g, spectrum_d, eps, last)
+    f, ends = residual_spectrum(gram_x, graph_x, x, deg, eps, last, high_t, low_t)
 
     gs = []
     groups = col_groups + row_groups
@@ -850,17 +834,24 @@
     h_above = lax.ppermute(tail, BOTH, [(owner[s], owner[s + 1]) for s in range(strips - 1)])
     h_below = lax.ppermute(head, BOTH, [(owner[s + 1], owner[s]) for s in range(strips - 1)])
     h_own, *h_early, h_late = h_pieces
-    h_early, h_above, h_below = lax.optimization_barrier((h_early, h_above, h_below))
+    (gram_inner,) = apply_graph(("x", "v", "p"), False, 0, (h,), w, deg, x, p, part="inner")
+    h_early, h_above, h_below, gram_inner = lax.optimization_barrier(
+        (h_early, h_above, h_below, gram_inner)
+    )
     h_early = [away(piece, d) for d, piece in enumerate(h_early, 1)]
-    (gram_h,) = apply_graph(("x", "v", "p"), False, 0, (h, h_above, h_below), w, deg, x, p)
+    (gram_outer,) = apply_graph(
+        ("x", "v", "p"), False, 0, (h, h_above, h_below), w, deg, x, p, part="outer"
+    )
     zero = jnp.zeros((fields, LANES), f32)
-    gram = gram_h + jnp.concatenate([gram_p[:fields], zero, gram_p[fields:]], 0)
+    gram = gram_inner + gram_outer + jnp.concatenate([gram_p[:fields], zero, gram_p[fields:]], 0)
     gram, _ = add_up(gram, row_groups)
     gram, h_early = lax.optimization_barrier((gram, h_early))
     gram, h_late = add_up(gram, col_groups, h_late)
-    h_pieces = [h_own, *h_early, away(h_late, chunks - 1)]
+    h_late = away(h_late, chunks - 1)
     ritz, coeffs = ritz_step(gram_x, gram, fields, rows * cols)
-    new_block, new_direction = combine(info, coeffs, start_block, old_direction, h_pieces)
+    given = info, coeffs, start_block, old_direction
+    begun = combine(*given, [h_own, *h_early], chunks)
+    new_block, new_direction = combine(*given, [h_late], chunks, chunks - 1, begun)
     return new_block, new_direction, ritz.reshape(fields)
 
 

time: 167 us -> 165 us (0.988)
  Pallas kernels: 63.9 us -> 60.1 us
    ppermute x14, waiting for transfers between devices: 8.69 us -> 16.4 us  [add_up(): lax.ppermute(value, BOTH, [(i, i ^ m) for i in range(strips)])]
    ppermute x1, waiting for transfers between devices: 4.7 us -> 0.01 us  [local(): lax.ppermute(head, BOTH, [(owner[s + 1], owner[s]) for s in range(strips...]
    pallas_call x4 -> x3, Pallas kernels: 16 us -> 13.2 us  [the longest x1 6.6 us: residual_spectrum(): pl.pallas_call(residual_kernel, out_shape=out_shape, in_specs=[VMEM] * 8,...]
    pallas_call x3 -> x4, Pallas kernels: 21.5 us -> 21.4 us  [apply_graph(): pl.pallas_call(functools.partial(graph_kernel, order, keep, lane_shift, c...]
  transfers between devices with their start and end apart: 34 -> 34, of which waited for: 19 -> 20; matrix products, arithmetic and copies ran while one was open for 1% -> 1% of each run, Pallas kernels for 27% -> 26%
where the time goes in v5:
time: 165 us
  Pallas kernels  60.1 us (36%)
  starting transfers between devices  54.6 us (33%)
  waiting for transfers between devices  47.5 us (29%)
  local copies, waits for them, and re-layouts  1.69 us (1%)
    ppermute x14, starting transfers between devices, add_up(): lax.ppermute(value, BOTH, [(i, i ^ m) for i in range(strips)])  23.7 us
    pallas_call x4, Pallas kernels, apply_graph(): pl.pallas_call(functools.partial(graph_kernel, order, keep, lane_shift, c...  21.4 us
    ppermute x9, waiting for transfers between devices, away(): return lax.ppermute(piece, 'col', [(c, c ^ d) for c in range(chunks)])  18 us
    ppermute x14, waiting for transfers between devices, add_up(): lax.ppermute(value, BOTH, [(i, i ^ m) for i in range(strips)])  16.4 us
    ppermute x9, starting transfers between devices, away(): return lax.ppermute(piece, 'col', [(c, c ^ d) for c in range(chunks)])  13.4 us
    ppermute x7, waiting for transfers between devices, local(): found[place & (1 << len(group)) - 1] = lax.ppermute(ends, BOTH, pairs)  11.5 us
    ppermute x7, starting transfers between devices, local(): found[place & (1 << len(group)) - 1] = lax.ppermute(ends, BOTH, pairs)  9.59 us
    pallas_call x1, Pallas kernels, ritz_step(): pl.pallas_call(functools.partial(ritz_kernel, fields, pixel_total), out_s...  9.04 us
  transfers between devices with their start and end apart: 34, of which 20 were waited for; matrix products, arithmetic and copies ran while one was open for 1% of the time, Pallas kernels for 26%

profile of v5, /device:TPU:0, one launch (start us, length us, event | category | flops | bytes accessed | tf_op | source)
XLA Modules:
  0.0 165.0 jit_solution(1971484138664646662)
XLA Ops:
  0.6 2.0 %edges.1 = (f32[2,33,256]{2,1,0:T(8,128)}, f32[2,33,256]{2,1,0:T(8,128)}) custom-call(f32[16,128,256]{2,1,0:T(8,128)} %x_ref.7, f32[16,128,256]{2,1,0:T(8,128)} %x_ref.7, f32[16,128,256]{2,1,0:T(8,128)} %p_ref.3, f32[16,128,256]{2,1,0:T(8,128)} %p_ref.3, f32[128,256]{1,0:T(8,128)} %refs_0_.1, f32[128,256]{1,0:T(8,128)} %refs_0_.1), custom_call_target="tpu_custom_call" | custom-call | bytes 524288 | tf_op jit(solution)/shard_map/edges/pallas_call | solution.py:149
  2.6 2.3 %collective-permute-start = (f32[2,33,256]{2,1,0:T(8,128)}, f32[2,33,256]{2,1,0:T(8,128)S(1)}, u32[]{:S(2)}, u32[]{:S(2)}) collective-permute-start(f32[2,33,256]{2,1,0:T(8,128)} %get-tuple-element.83), channel_id=1, source_target_pairs={{0,4},{4,8},{8,12},{12,16},{16,20},{20,24},{24,28},{1,5},{5,9},{9,... | collective-permute-start | bytes 202760 | tf_op jit(solution)/shard_map/ppermute | solution.py:797
  7.0 1.8 %pack.2 = (f32[39,16,256]{2,1,0:T(8,128)S(1)}, f32[39,16,256]{2,1,0:T(8,128)S(1)}, f32[39,16,256]{2,1,0:T(8,128)S(1)}, f32[39,16,256]{2,1,0:T(8,128)S(1)}) custom-call(s32[9]{0:T(128)S(1)} %dynamic-slice_bitcast_fusion.1.info_ref.refs_0_, f32[16,128,256]{2,1,0:T(8,128)S(1)} %copy-done, f32[128,256]{1,0:T(8,128)S(1)} %copy-done.2), custom_call_target="tpu_custom_call" | custom-call | bytes 4194304 | tf_op jit(solution)/shard_map/pack/pallas_call | solution.py:202
  8.8 1.7 %collective-permute-done.1.below_ref = f32[2,33,256]{2,1,0:T(8,128)S(1)} collective-permute-done((f32[2,33,256]{2,1,0:T(8,128)}, f32[2,33,256]{2,1,0:T(8,128)S(1)}, u32[]{:S(2)}, u32[]{:S(2)}) %collective-permute-start.1) | collective-permute-done | bytes 67616 | tf_op jit(solution)/shard_map/ppermute | solution.py:798
  11.1 1.6 collective-permute-start.2
  12.7 1.5 collective-permute-start.3
  14.7 1.8 %pack.3 = (f32[36,16,256]{2,1,0:T(8,128)S(1)}, f32[36,16,256]{2,1,0:T(8,128)S(1)}, f32[36,16,256]{2,1,0:T(8,128)S(1)}, f32[36,16,256]{2,1,0:T(8,128)S(1)}) custom-call(s32[9]{0:T(128)S(1)} %dynamic-slice_bitcast_fusion.1.info_ref.refs_0_, f32[16,128,256]{2,1,0:T(8,128)S(1)} %copy-done.1), custom_call_target="tpu_custom_call" | custom-call | bytes 4194304 | tf_op jit(solution)/shard_map/pack/pallas_call | solution.py:202
  17.1 1.6 collective-permute-start.10
  18.7 1.5 collective-permute-start.9
  20.2 6.1 %collective-permute-done.2.rest_1_.refs_2_ = f32[39,16,256]{2,1,0:T(8,128)S(1)} collective-permute-done((f32[39,16,256]{2,1,0:T(8,128)S(1)}, f32[39,16,256]{2,1,0:T(8,128)S(1)}, u32[]{:S(2)}, u32[]{:S(2)}) %collective-permute-start.2) | collective-permute-done | bytes 639008 | tf_op jit(solution)/shard_map/ppermute | solution.py:791
  26.3 2.4 %collective-permute-start.11 = (f32[36,16,256]{2,1,0:T(8,128)S(1)}, f32[36,16,256]{2,1,0:T(8,128)S(1)}, u32[]{:S(2)}, u32[]{:S(2)}) collective-permute-start(f32[36,16,256]{2,1,0:T(8,128)S(1)} %get-tuple-element.109), channel_id=1, source_target_pairs={{0,3},{1,2},{2,1},{3,0},{4,7},{5,6},{6,5},{7,4},{8,11},{9,10},{10,... | collective-permute-start | bytes 1769480 | tf_op jit(solution)/shard_map/ppermute | solution.py:791
  29.6 11.5 %collective-permute-done.4.rest_3_.refs_4_ = f32[39,16,256]{2,1,0:T(8,128)S(1)} collective-permute-done((f32[39,16,256]{2,1,0:T(8,128)S(1)}, f32[39,16,256]{2,1,0:T(8,128)S(1)}, u32[]{:S(2)}, u32[]{:S(2)}) %collective-permute-start.4) | collective-permute-done | bytes 639008 | tf_op jit(solution)/shard_map/ppermute | solution.py:791
  41.0 3.1 %weights.1 = (f32[32,25,1024]{2,1,0:T(8,128)S(1)}, f32[32,1024]{1,0:T(8,128)S(1)}) custom-call(s32[9]{0:T(128)S(1)} %dynamic-slice_bitcast_fusion.1.info_ref.refs_0_, f32[39,16,256]{2,1,0:T(8,128)S(1)} %get-tuple-element.99.rest_0_.refs_1_, f32[39,16,256]{2,1,0:T(8,128)S(1)} %collective-permute-done.2.rest_1_.refs_2_, ...), custom_call_target="tpu_custom_call" | custom-call | flops 49152000 | bytes 3276800 | tf_op jit(solution)/shard_map/weights/pallas_call | solution.py:281
  44.2 7.1 %graph_v_all.1 = (f32[32,16,1024]{2,1,0:T(8,128)S(1)}, f32[32,16,1024]{2,1,0:T(8,128)S(1)}, f32[16,128]{1,0:T(8,128)S(1)}) custom-call(s32[9]{0:T(128)S(1)} %dynamic-slice_bitcast_fusion.1.info_ref.refs_0_, f32[39,16,256]{2,1,0:T(8,128)S(1)} %get-tuple-element.99.rest_0_.refs_1_, f32[39,16,256]{2,1,0:T(8,128)S(1)} %collective-permute-done.2.rest_1_.refs_2_, ...), custom_call_target="tpu_custom_call" | custom-call | flops 104857600 | bytes 9568256 | tf_op jit(solution)/shard_map/graph_v_all/pallas_call | solution.py:387
  51.3 4.6 %collective-permute-start.5 = (f32[16,128]{1,0:T(8,128)S(1)}, f32[16,128]{1,0:T(8,128)S(1)}, u32[]{:S(2)}, u32[]{:S(2)}) collective-permute-start(f32[16,128]{1,0:T(8,128)S(1)} %get-tuple-element.105), channel_id=1, source_target_pairs={{0,4},{1,5},{2,6},{3,7},{4,0},{5,1},{6,2},{7,3},{8,12},{9,13},{10,... | collective-permute-start | bytes 24584 | tf_op jit(solution)/shard_map/ppermute | solution.py:784
  56.7 1.5 collective-permute-start.6
  58.3 2.7 %collective-permute-start.7 = (f32[16,128]{1,0:T(8,128)S(1)}, f32[16,128]{1,0:T(8,128)S(1)}, u32[]{:S(2)}, u32[]{:S(2)}) collective-permute-start(f32[16,128]{1,0:T(8,128)S(1)} %add.59), channel_id=1, source_target_pairs={{0,16},{1,17},{2,18},{3,19},{4,20},{5,21},{6,22},{7,23},{8,24},{9,... | collective-permute-start | bytes 24584 | tf_op jit(solution)/shard_map/ppermute | solution.py:784
  60.9 3.1 %collective-permute-start.8 = (f32[16,128]{1,0:T(8,128)S(1)}, f32[16,128]{1,0:T(8,128)S(1)}, u32[]{:S(2)}, u32[]{:S(2)}) collective-permute-start(f32[16,128]{1,0:T(8,128)S(1)} %add.59), channel_id=1, source_target_pairs={{0,24},{1,25},{2,26},{3,27},{4,28},{5,29},{6,30},{7,31},{8,16},{9,... | collective-permute-start | bytes 24584 | tf_op jit(solution)/shard_map/ppermute | solution.py:784
  64.0 2.4 %collective-permute-done.8 = f32[16,128]{1,0:T(8,128)S(1)} collective-permute-done((f32[16,128]{1,0:T(8,128)S(1)}, f32[16,128]{1,0:T(8,128)S(1)}, u32[]{:S(2)}, u32[]{:S(2)}) %collective-permute-start.8) | collective-permute-done | bytes 8224 | tf_op jit(solution)/shard_map/ppermute | solution.py:784
  68.6 1.4 collective-permute-start.14
  71.4 1.7 %collective-permute-done.14 = f32[16,128]{1,0:T(8,128)S(1)} collective-permute-done((f32[16,128]{1,0:T(8,128)S(1)}, f32[16,128]{1,0:T(8,128)S(1)}, u32[]{:S(2)}, u32[]{:S(2)}) %collective-permute-start.14) | collective-permute-done | bytes 8224 | tf_op jit(solution)/shard_map/ppermute | solution.py:784
  73.2 6.6 %residual_spectrum.1 = (f32[32,16,1024]{2,1,0:T(8,128)S(1)}, f32[2,16,1024]{2,1,0:T(8,128)S(1)}) custom-call(f32[16,128]{1,0:T(8,128)S(1)} %add_add_fusion.2.gram_ref.first_ref, f32[32,16,1024]{2,1,0:T(8,128)S(1)} %get-tuple-element.111.g_ref, f32[32,16,1024]{2,1,0:T(8,128)S(1)} %get-tuple-element.112.x_ref.refs_7_.refs_3_.refs_5_, ...), custom_call_target="tpu_custom_call" | custom-call | flops 3221225472 | bytes 6291456 | tf_op jit(solution)/shard_map/residual_spectrum/pallas_call | solution.py:455
  79.8 1.6 collective-permute-start.15
  83.3 2.8 %collective-permute-done.15.refs_1_ = f32[2,16,1024]{2,1,0:T(8,128)S(1)} collective-permute-done((f32[2,16,1024]{2,1,0:T(8,128)S(1)}, f32[2,16,1024]{2,1,0:T(8,128)S(1)}, u32[]{:S(2)}, u32[]{:S(2)}) %collective-permute-start.15) | collective-permute-done | bytes 131104 | tf_op jit(solution)/shard_map/ppermute | solution.py:822
  86.1 3.0 %collective-permute-done.16.refs_2_ = f32[2,16,1024]{2,1,0:T(8,128)S(1)} collective-permute-done((f32[2,16,1024]{2,1,0:T(8,128)S(1)}, f32[2,16,1024]{2,1,0:T(8,128)S(1)}, u32[]{:S(2)}, u32[]{:S(2)}) %collective-permute-start.16) | collective-permute-done | bytes 131104 | tf_op jit(solution)/shard_map/ppermute | solution.py:822
  89.1 1.4 collective-permute-done.17.refs_3_
  91.2 1.3 collective-permute-done.18.refs_1_
  93.1 3.5 %collective-permute-start.19 = (f32[2,16,1024]{2,1,0:T(8,128)S(1)}, f32[2,16,1024]{2,1,0:T(8,128)S(1)}, u32[]{:S(2)}, u32[]{:S(2)}) collective-permute-start(f32[2,16,1024]{2,1,0:T(8,128)S(1)} %get-tuple-element.123.refs_0_), channel_id=1, source_target_pairs={{0,8},{1,9},{2,10},{3,11},{4,12},{5,13},{6,14},{7,15},{8,0},{9,1},... | collective-permute-start | bytes 393224 | tf_op jit(solution)/shard_map/ppermute | solution.py:822
  97.7 1.4 collective-permute-start.21
  99.1 7.4 %graph_xv_all.1 = (f32[32,16,1024]{2,1,0:T(8,128)S(1)}, f32[32,128]{1,0:T(8,128)S(1)}) custom-call(s32[9]{0:T(128)S(1)} %dynamic-slice_bitcast_fusion.1.info_ref.refs_0_, f32[36,16,256]{2,1,0:T(8,128)S(1)} %get-tuple-element.126.refs_1_, f32[36,16,256]{2,1,0:T(8,128)S(1)} %collective-permute-done.9.refs_2_, ...), custom_call_target="tpu_custom_call" | custom-call | flops 104857600 | bytes 9568256 | tf_op jit(solution)/shard_map/graph_xv_all/pallas_call | solution.py:387
  106.5 3.0 %collective-permute-done.20.refs_2_ = f32[2,16,1024]{2,1,0:T(8,128)S(1)} collective-permute-done((f32[2,16,1024]{2,1,0:T(8,128)S(1)}, f32[2,16,1024]{2,1,0:T(8,128)S(1)}, u32[]{:S(2)}, u32[]{:S(2)}) %collective-permute-start.20) | collective-permute-done | bytes 131104 | tf_op jit(solution)/shard_map/ppermute | solution.py:822
  110.1 4.9 %row_inverse.1 = (f32[32,16,1024]{2,1,0:T(8,128)S(1)}, f32[2,16,1024]{2,1,0:T(8,128)S(1)}, f32[2,16,1024]{2,1,0:T(8,128)S(1)}, f32[32,16,256]{2,1,0:T(8,128)S(1)...) custom-call(s32[9]{0:T(128)S(1)} %dynamic-slice_bitcast_fusion.1.info_ref.refs_0_, ...), custom_call_target="tpu_custom_call" | custom-call | flops 3221225472 | bytes 8388608 | tf_op jit(solution)/shard_map/row_inverse/pallas_call | solution.py:550
  115.0 2.8 %collective-permute-start.22 = (f32[2,16,1024]{2,1,0:T(8,128)S(1)}, f32[2,16,1024]{2,1,0:T(8,128)S(1)}, u32[]{:S(2)}, u32[]{:S(2)}) collective-permute-start(f32[2,16,1024]{2,1,0:T(8,128)S(1)} %get-tuple-element.136), channel_id=1, source_target_pairs={{0,1},{1,3},{3,2},{2,4},{4,5},{5,7},{7,6},{6,8},{8,9},{9,11},{11,1... | collective-permute-start | bytes 393224 | tf_op jit(solution)/shard_map/ppermute | solution.py:834
  117.8 1.5 collective-permute-start.23
  119.4 5.9 %graph_xvp_inner.1 = f32[48,128]{1,0:T(8,128)S(1)} custom-call(f32[32,16,1024]{2,1,0:T(8,128)S(1)} %get-tuple-element.138.refs_0_, f32[32,25,1024]{2,1,0:T(8,128)S(1)} %get-tuple-element.103.refs_5_.refs_1_.refs_3_, f32[32,1024]{1,0:T(8,128)S(1)} %get-tuple-element.104.refs_6_.deg_ref.refs_2_.refs_4_, ...), custom_call_target="tpu_custom_call" | custom-call | flops 104857600 | bytes 9568256 | tf_op jit(solution)/shard_map/graph_xvp_inner/pallas_call | solution.py:387
  125.3 2.7 %collective-permute-start.28 = (f32[32,16,256]{2,1,0:T(8,128)S(1)}, f32[32,16,256]{2,1,0:T(8,128)S(1)}, u32[]{:S(2)}, u32[]{:S(2)}) collective-permute-start(f32[32,16,256]{2,1,0:T(8,128)S(1)} %get-tuple-element.144), channel_id=1, source_target_pairs={{0,1},{1,0},{2,3},{3,2},{4,5},{5,4},{6,7},{7,6},{8,9},{9,8},{10,11... | collective-permute-start | bytes 1572872 | tf_op jit(solution)/shard_map/ppermute | solution.py:791
  128.0 1.5 collective-permute-start.29
  131.8 2.3 %collective-permute-start.25 = (f32[48,128]{1,0:T(8,128)S(1)}, f32[48,128]{1,0:T(8,128)S(1)}, u32[]{:S(2)}, u32[]{:S(2)}) collective-permute-start(f32[48,128]{1,0:T(8,128)S(1)} %add.68), channel_id=1, source_target_pairs={{0,8},{1,9},{2,10},{3,11},{4,12},{5,13},{6,14},{7,15},{8,0},{9,1},... | collective-permute-start | bytes 73736 | tf_op jit(solution)/shard_map/ppermute | solution.py:784
  135.1 1.4 collective-permute-start.27
  136.5 2.4 %collective-permute-done.26 = f32[48,128]{1,0:T(8,128)S(1)} collective-permute-done((f32[48,128]{1,0:T(8,128)S(1)}, f32[48,128]{1,0:T(8,128)S(1)}, u32[]{:S(2)}, u32[]{:S(2)}) %collective-permute-start.26) | collective-permute-done | bytes 24608 | tf_op jit(solution)/shard_map/ppermute | solution.py:784
  138.9 1.8 %collective-permute-done.27 = f32[48,128]{1,0:T(8,128)S(1)} collective-permute-done((f32[48,128]{1,0:T(8,128)S(1)}, f32[48,128]{1,0:T(8,128)S(1)}, u32[]{:S(2)}, u32[]{:S(2)}) %collective-permute-start.27) | collective-permute-done | bytes 24608 | tf_op jit(solution)/shard_map/ppermute | solution.py:784
  141.1 1.7 %collective-permute-start.30 = (f32[48,128]{1,0:T(8,128)S(1)}, f32[48,128]{1,0:T(8,128)S(1)}, u32[]{:S(2)}, u32[]{:S(2)}) collective-permute-start(f32[48,128]{1,0:T(8,128)S(1)} %add_add_fusion.1), channel_id=1, source_target_pairs={{0,1},{1,0},{2,3},{3,2},{4,5},{5,4},{6,7},{7,6},{8,9},{9,8},{10,11... | collective-permute-start | bytes 73736 | tf_op jit(solution)/shard_map/ppermute | solution.py:784
  142.8 1.7 %collective-permute-start.31 = (f32[48,128]{1,0:T(8,128)S(1)}, f32[48,128]{1,0:T(8,128)S(1)}, u32[]{:S(2)}, u32[]{:S(2)}) collective-permute-start(f32[48,128]{1,0:T(8,128)S(1)} %add_add_fusion.1), channel_id=1, source_target_pairs={{0,2},{1,3},{2,0},{3,1},{4,6},{5,7},{6,4},{7,5},{8,10},{9,11},{10,... | collective-permute-start | bytes 73736 | tf_op jit(solution)/shard_map/ppermute | solution.py:784
  145.0 1.7 %collective-permute-done.31 = f32[48,128]{1,0:T(8,128)S(1)} collective-permute-done((f32[48,128]{1,0:T(8,128)S(1)}, f32[48,128]{1,0:T(8,128)S(1)}, u32[]{:S(2)}, u32[]{:S(2)}) %collective-permute-start.31) | collective-permute-done | bytes 24608 | tf_op jit(solution)/shard_map/ppermute | solution.py:784
  146.6 2.6 %collective-permute-done.32 = f32[48,128]{1,0:T(8,128)S(1)} collective-permute-done((f32[48,128]{1,0:T(8,128)S(1)}, f32[48,128]{1,0:T(8,128)S(1)}, u32[]{:S(2)}, u32[]{:S(2)}) %collective-permute-start.32) | collective-permute-done | bytes 24608 | tf_op jit(solution)/shard_map/ppermute | solution.py:784
  149.4 9.0 %ritz.1 = (f32[1,16]{1,0:T(1,128)}, f32[48,16]{1,0:T(8,128)S(1)}) custom-call(f32[16,128]{1,0:T(8,128)S(1)} %add_add_fusion.2.gram_ref.first_ref, f32[48,128]{1,0:T(8,128)S(1)} %add_add_fusion.second_ref), custom_call_target="tpu_custom_call" | custom-call | flops 33554432 | bytes 65536 | tf_op jit(solution)/shard_map/ritz/pallas_call | solution.py:642
  158.4 4.5 %combine.2 = (f32[16,128,256]{2,1,0:T(8,128)}, f32[16,128,256]{2,1,0:T(8,128)}, bf16[128,384]{1,0:T(8,128)(2,1)S(1)}, bf16[128,384]{1,0:T(8,128)(2,1)S(1)}) custom-call(s32[9]{0:T(128)S(1)} %dynamic-slice_bitcast_fusion.1.info_ref.refs_0_, f32[48,16]{1,0:T(8,128)S(1)} %get-tuple-element.151.coeff_ref, f32[16,128,256]{2,1,0:T(8,128)S(1)} %copy-done, ...), custom_call_target="tpu_custom_call" | custom-call | flops 19660800 | bytes 7864320 | tf_op jit(solution)/shard_map/combine/pallas_call | solution.py:719
  162.9 2.0 %combine.3 = (f32[16,128,256]{2,1,0:T(8,128)}, f32[16,128,256]{2,1,0:T(8,128)}) custom-call(s32[9]{0:T(128)S(1)} %dynamic-slice_bitcast_fusion.1.info_ref.refs_0_, f32[48,16]{1,0:T(8,128)S(1)} %get-tuple-element.151.coeff_ref, f32[16,128,256]{2,1,0:T(8,128)S(1)} %copy-done, ...), custom_call_target="tpu_custom_call", output_to_operand_aliasing={{0}: (5, {}), {1}: (6, {})} | custom-call | flops 6553600 | bytes 2621440 | tf_op jit(solution)/shard_map/combine/pallas_call | solution.py:719
  (72 shorter events, 18.2 us)
Async XLA Ops:
  0.6 6.4 %copy-start.2 = (f32[128,256]{1,0:T(8,128)S(1)}, f32[128,256]{1,0:T(8,128)}, u32[]{:S(2)}) copy-start(f32[128,256]{1,0:T(8,128)} %refs_0_.1) | copy-start | bytes 393220
  0.6 6.3 %copy-start = (f32[16,128,256]{2,1,0:T(8,128)S(1)}, f32[16,128,256]{2,1,0:T(8,128)}, u32[]{:S(2)}) copy-start(f32[16,128,256]{2,1,0:T(8,128)} %x_ref.7) | copy-start | bytes 6291460
  2.6 6.2 %collective-permute-start = (f32[2,33,256]{2,1,0:T(8,128)}, f32[2,33,256]{2,1,0:T(8,128)S(1)}, u32[]{:S(2)}, u32[]{:S(2)}) collective-permute-start(f32[2,33,256]{2,1,0:T(8,128)} %get-tuple-element.83), channel_id=1, source_target_pairs={{0,4},{4,8},{8,12},{12,16},{16,20},{20,24},{24,28},{1,5},{5,9},{9,... | collective-permute-start | bytes 202760 | tf_op jit(solution)/shard_map/ppermute | solution.py:797
  5.0 5.6 %collective-permute-start.1 = (f32[2,33,256]{2,1,0:T(8,128)}, f32[2,33,256]{2,1,0:T(8,128)S(1)}, u32[]{:S(2)}, u32[]{:S(2)}) collective-permute-start(f32[2,33,256]{2,1,0:T(8,128)} %get-tuple-element.84), channel_id=1, source_target_pairs={{4,0},{8,4},{12,8},{16,12},{20,16},{24,20},{28,24},{5,1},{9,5},{13... | collective-permute-start | bytes 202760 | tf_op jit(solution)/shard_map/ppermute | solution.py:798
  7.0 7.7 %copy-start.1 = (f32[16,128,256]{2,1,0:T(8,128)S(1)}, f32[16,128,256]{2,1,0:T(8,128)}, u32[]{:S(2)}) copy-start(f32[16,128,256]{2,1,0:T(8,128)} %p_ref.3) | copy-start | bytes 6291460
  11.1 15.1 %collective-permute-start.2 = (f32[39,16,256]{2,1,0:T(8,128)S(1)}, f32[39,16,256]{2,1,0:T(8,128)S(1)}, u32[]{:S(2)}, u32[]{:S(2)}) collective-permute-start(f32[39,16,256]{2,1,0:T(8,128)S(1)} %get-tuple-element.95), channel_id=1, source_target_pairs={{0,1},{1,0},{2,3},{3,2},{4,5},{5,4},{6,7},{7,6},{8,9},{9,8},{10,11... | collective-permute-start | bytes 1916936 | tf_op jit(solution)/shard_map/ppermute | solution.py:791
  12.7 16.9 %collective-permute-start.3 = (f32[39,16,256]{2,1,0:T(8,128)S(1)}, f32[39,16,256]{2,1,0:T(8,128)S(1)}, u32[]{:S(2)}, u32[]{:S(2)}) collective-permute-start(f32[39,16,256]{2,1,0:T(8,128)S(1)} %get-tuple-element.97), channel_id=1, source_target_pairs={{0,2},{1,3},{2,0},{3,1},{4,6},{5,7},{6,4},{7,5},{8,10},{9,11},{10,... | collective-permute-start | bytes 1916936 | tf_op jit(solution)/shard_map/ppermute | solution.py:791
  14.2 26.8 %collective-permute-start.4 = (f32[39,16,256]{2,1,0:T(8,128)S(1)}, f32[39,16,256]{2,1,0:T(8,128)S(1)}, u32[]{:S(2)}, u32[]{:S(2)}) collective-permute-start(f32[39,16,256]{2,1,0:T(8,128)S(1)} %get-tuple-element.98), channel_id=1, source_target_pairs={{0,3},{1,2},{2,1},{3,0},{4,7},{5,6},{6,5},{7,4},{8,11},{9,10},{10,... | collective-permute-start | bytes 1916936 | tf_op jit(solution)/shard_map/ppermute | solution.py:791
  17.1 49.3 %collective-permute-start.10 = (f32[36,16,256]{2,1,0:T(8,128)S(1)}, f32[36,16,256]{2,1,0:T(8,128)S(1)}, u32[]{:S(2)}, u32[]{:S(2)}) collective-permute-start(f32[36,16,256]{2,1,0:T(8,128)S(1)} %get-tuple-element.108), channel_id=1, source_target_pairs={{0,2},{1,3},{2,0},{3,1},{4,6},{5,7},{6,4},{7,5},{8,10},{9,11},{10,... | collective-permute-start | bytes 1769480 | tf_op jit(solution)/shard_map/ppermute | solution.py:791
  18.7 47.7 %collective-permute-start.9 = (f32[36,16,256]{2,1,0:T(8,128)S(1)}, f32[36,16,256]{2,1,0:T(8,128)S(1)}, u32[]{:S(2)}, u32[]{:S(2)}) collective-permute-start(f32[36,16,256]{2,1,0:T(8,128)S(1)} %get-tuple-element.107), channel_id=1, source_target_pairs={{0,1},{1,0},{2,3},{3,2},{4,5},{5,4},{6,7},{7,6},{8,9},{9,8},{10,11... | collective-permute-start | bytes 1769480 | tf_op jit(solution)/shard_map/ppermute | solution.py:791
  26.3 40.1 %collective-permute-start.11 = (f32[36,16,256]{2,1,0:T(8,128)S(1)}, f32[36,16,256]{2,1,0:T(8,128)S(1)}, u32[]{:S(2)}, u32[]{:S(2)}) collective-permute-start(f32[36,16,256]{2,1,0:T(8,128)S(1)} %get-tuple-element.109), channel_id=1, source_target_pairs={{0,3},{1,2},{2,1},{3,0},{4,7},{5,6},{6,5},{7,4},{8,11},{9,10},{10,... | collective-permute-start | bytes 1769480 | tf_op jit(solution)/shard_map/ppermute | solution.py:791
  44.1 29.0 %copy-start.7 = (bf16[1024,1024]{1,0:T(8,128)(2,1)S(1)}, bf16[1024,1024]{1,0:T(8,128)(2,1)}, u32[]{:S(2)}) copy-start(bf16[1024,1024]{1,0:T(8,128)(2,1)} %constant.45.clone.high_ref) | copy-start | bytes 6291460
  44.1 29.0 %copy-start.8 = (bf16[1024,1024]{1,0:T(8,128)(2,1)S(1)}, bf16[1024,1024]{1,0:T(8,128)(2,1)}, u32[]{:S(2)}) copy-start(bf16[1024,1024]{1,0:T(8,128)(2,1)} %constant.46.clone.low_ref) | copy-start | bytes 6291460
  44.1 29.0 %copy-start.9 = (f32[32,1024]{1,0:T(8,128)S(1)}, f32[32,1024]{1,0:T(8,128)}, u32[]{:S(2)}) copy-start(f32[32,1024]{1,0:T(8,128)} %constant.47.clone.eps_ref.refs_7_) | copy-start | bytes 393220
  44.1 29.0 %copy-start.10 = (f32[1,1024]{1,0:T(1,128)S(1)}, f32[1,1024]{1,0:T(1,128)}, u32[]{:S(2)}) copy-start(f32[1,1024]{1,0:T(1,128)} %constant.48.clone.last_ref.refs_8_) | copy-start | bytes 12292
  51.3 5.5 %collective-permute-start.5 = (f32[16,128]{1,0:T(8,128)S(1)}, f32[16,128]{1,0:T(8,128)S(1)}, u32[]{:S(2)}, u32[]{:S(2)}) collective-permute-start(f32[16,128]{1,0:T(8,128)S(1)} %get-tuple-element.105), channel_id=1, source_target_pairs={{0,4},{1,5},{2,6},{3,7},{4,0},{5,1},{6,2},{7,3},{8,12},{9,13},{10,... | collective-permute-start | bytes 24584 | tf_op jit(solution)/shard_map/ppermute | solution.py:784
  56.7 4.2 %collective-permute-start.6 = (f32[16,128]{1,0:T(8,128)S(1)}, f32[16,128]{1,0:T(8,128)S(1)}, u32[]{:S(2)}, u32[]{:S(2)}) collective-permute-start(f32[16,128]{1,0:T(8,128)S(1)} %add.59), channel_id=1, source_target_pairs={{0,8},{1,9},{2,10},{3,11},{4,12},{5,13},{6,14},{7,15},{8,0},{9,1},... | collective-permute-start | bytes 24584 | tf_op jit(solution)/shard_map/ppermute | solution.py:784
  58.3 5.8 %collective-permute-start.7 = (f32[16,128]{1,0:T(8,128)S(1)}, f32[16,128]{1,0:T(8,128)S(1)}, u32[]{:S(2)}, u32[]{:S(2)}) collective-permute-start(f32[16,128]{1,0:T(8,128)S(1)} %add.59), channel_id=1, source_target_pairs={{0,16},{1,17},{2,18},{3,19},{4,20},{5,21},{6,22},{7,23},{8,24},{9,... | collective-permute-start | bytes 24584 | tf_op jit(solution)/shard_map/ppermute | solution.py:784
  60.9 5.4 %collective-permute-start.8 = (f32[16,128]{1,0:T(8,128)S(1)}, f32[16,128]{1,0:T(8,128)S(1)}, u32[]{:S(2)}, u32[]{:S(2)}) collective-permute-start(f32[16,128]{1,0:T(8,128)S(1)} %add.59), channel_id=1, source_target_pairs={{0,24},{1,25},{2,26},{3,27},{4,28},{5,29},{6,30},{7,31},{8,16},{9,... | collective-permute-start | bytes 24584 | tf_op jit(solution)/shard_map/ppermute | solution.py:784
  66.4 3.7 %collective-permute-start.12 = (f32[16,128]{1,0:T(8,128)S(1)}, f32[16,128]{1,0:T(8,128)S(1)}, u32[]{:S(2)}, u32[]{:S(2)}) collective-permute-start(f32[16,128]{1,0:T(8,128)S(1)} %add_add_fusion.3), channel_id=1, source_target_pairs={{0,1},{1,0},{2,3},{3,2},{4,5},{5,4},{6,7},{7,6},{8,9},{9,8},{10,11... | collective-permute-start | bytes 24584 | tf_op jit(solution)/shard_map/ppermute | solution.py:784
  67.7 3.7 %collective-permute-start.13 = (f32[16,128]{1,0:T(8,128)S(1)}, f32[16,128]{1,0:T(8,128)S(1)}, u32[]{:S(2)}, u32[]{:S(2)}) collective-permute-start(f32[16,128]{1,0:T(8,128)S(1)} %add_add_fusion.3), channel_id=1, source_target_pairs={{0,2},{1,3},{2,0},{3,1},{4,6},{5,7},{6,4},{7,5},{8,10},{9,11},{10,... | collective-permute-start | bytes 24584 | tf_op jit(solution)/shard_map/ppermute | solution.py:784
  68.6 4.5 %collective-permute-start.14 = (f32[16,128]{1,0:T(8,128)S(1)}, f32[16,128]{1,0:T(8,128)S(1)}, u32[]{:S(2)}, u32[]{:S(2)}) collective-permute-start(f32[16,128]{1,0:T(8,128)S(1)} %add_add_fusion.3), channel_id=1, source_target_pairs={{0,3},{1,2},{2,1},{3,0},{4,7},{5,6},{6,5},{7,4},{8,11},{9,10},{10,... | collective-permute-start | bytes 24584 | tf_op jit(solution)/shard_map/ppermute | solution.py:784
  73.1 17.3 %copy-start.3 = (f32[5,1024]{1,0:T(8,128)S(1)}, f32[5,1024]{1,0:T(8,128)}, u32[]{:S(2)}) copy-start(f32[5,1024]{1,0:T(8,128)} %constant.49.clone.gain_ref) | copy-start | bytes 61444
  73.1 17.3 %copy-start.4 = (f32[5,1024]{1,0:T(8,128)S(1)}, f32[5,1024]{1,0:T(8,128)}, u32[]{:S(2)}) copy-start(f32[5,1024]{1,0:T(8,128)} %constant.50.clone.cross_ref) | copy-start | bytes 61444
  79.8 6.4 %collective-permute-start.15 = (f32[2,16,1024]{2,1,0:T(8,128)S(1)}, f32[2,16,1024]{2,1,0:T(8,128)S(1)}, u32[]{:S(2)}, u32[]{:S(2)}) collective-permute-start(f32[2,16,1024]{2,1,0:T(8,128)S(1)} %get-tuple-element.113.refs_0_), channel_id=1, source_target_pairs={{0,1},{1,0},{2,3},{3,2},{4,5},{5,4},{6,7},{7,6},{8,9},{9,8},{10,11... | collective-permute-start | bytes 393224 | tf_op jit(solution)/shard_map/ppermute | solution.py:822
  81.3 7.8 %collective-permute-start.16 = (f32[2,16,1024]{2,1,0:T(8,128)S(1)}, f32[2,16,1024]{2,1,0:T(8,128)S(1)}, u32[]{:S(2)}, u32[]{:S(2)}) collective-permute-start(f32[2,16,1024]{2,1,0:T(8,128)S(1)} %get-tuple-element.113.refs_0_), channel_id=1, source_target_pairs={{0,3},{1,2},{2,1},{3,0},{4,7},{5,6},{6,5},{7,4},{8,11},{9,10},{10,... | collective-permute-start | bytes 393224 | tf_op jit(solution)/shard_map/ppermute | solution.py:822
  82.5 7.9 %collective-permute-start.17 = (f32[2,16,1024]{2,1,0:T(8,128)S(1)}, f32[2,16,1024]{2,1,0:T(8,128)S(1)}, u32[]{:S(2)}, u32[]{:S(2)}) collective-permute-start(f32[2,16,1024]{2,1,0:T(8,128)S(1)} %get-tuple-element.113.refs_0_), channel_id=1, source_target_pairs={{0,2},{1,3},{2,0},{3,1},{4,6},{5,7},{6,4},{7,5},{8,10},{9,11},{10,... | collective-permute-start | bytes 393224 | tf_op jit(solution)/shard_map/ppermute | solution.py:822
  91.1 1.4 collective-permute-start.18
  93.1 17.0 %copy-start.5 = (bf16[1024,1024]{1,0:T(8,128)(2,1)S(1)}, bf16[1024,1024]{1,0:T(8,128)(2,1)}, u32[]{:S(2)}) copy-start(bf16[1024,1024]{1,0:T(8,128)(2,1)} %constant.43.clone.refs_9_) | copy-start | bytes 6291460
  93.1 17.0 %copy-start.6 = (bf16[1024,1024]{1,0:T(8,128)(2,1)S(1)}, bf16[1024,1024]{1,0:T(8,128)(2,1)}, u32[]{:S(2)}) copy-start(bf16[1024,1024]{1,0:T(8,128)(2,1)} %constant.44.clone.refs_10_) | copy-start | bytes 6291460
  93.1 13.4 %collective-permute-start.19 = (f32[2,16,1024]{2,1,0:T(8,128)S(1)}, f32[2,16,1024]{2,1,0:T(8,128)S(1)}, u32[]{:S(2)}, u32[]{:S(2)}) collective-permute-start(f32[2,16,1024]{2,1,0:T(8,128)S(1)} %get-tuple-element.123.refs_0_), channel_id=1, source_target_pairs={{0,8},{1,9},{2,10},{3,11},{4,12},{5,13},{6,14},{7,15},{8,0},{9,1},... | collective-permute-start | bytes 393224 | tf_op jit(solution)/shard_map/ppermute | solution.py:822
  96.6 12.9 %collective-permute-start.20 = (f32[2,16,1024]{2,1,0:T(8,128)S(1)}, f32[2,16,1024]{2,1,0:T(8,128)S(1)}, u32[]{:S(2)}, u32[]{:S(2)}) collective-permute-start(f32[2,16,1024]{2,1,0:T(8,128)S(1)} %get-tuple-element.123.refs_0_), channel_id=1, source_target_pairs={{0,16},{1,17},{2,18},{3,19},{4,20},{5,21},{6,22},{7,23},{8,24},{9,... | collective-permute-start | bytes 393224 | tf_op jit(solution)/shard_map/ppermute | solution.py:822
  97.7 11.8 %collective-permute-start.21 = (f32[2,16,1024]{2,1,0:T(8,128)S(1)}, f32[2,16,1024]{2,1,0:T(8,128)S(1)}, u32[]{:S(2)}, u32[]{:S(2)}) collective-permute-start(f32[2,16,1024]{2,1,0:T(8,128)S(1)} %get-tuple-element.123.refs_0_), channel_id=1, source_target_pairs={{0,24},{1,25},{2,26},{3,27},{4,28},{5,29},{6,30},{7,31},{8,16},{9,... | collective-permute-start | bytes 393224 | tf_op jit(solution)/shard_map/ppermute | solution.py:822
  115.0 10.2 %collective-permute-start.22 = (f32[2,16,1024]{2,1,0:T(8,128)S(1)}, f32[2,16,1024]{2,1,0:T(8,128)S(1)}, u32[]{:S(2)}, u32[]{:S(2)}) collective-permute-start(f32[2,16,1024]{2,1,0:T(8,128)S(1)} %get-tuple-element.136), channel_id=1, source_target_pairs={{0,1},{1,3},{3,2},{2,4},{4,5},{5,7},{7,6},{6,8},{8,9},{9,11},{11,1... | collective-permute-start | bytes 393224 | tf_op jit(solution)/shard_map/ppermute | solution.py:834
  117.8 7.4 %collective-permute-start.23 = (f32[2,16,1024]{2,1,0:T(8,128)S(1)}, f32[2,16,1024]{2,1,0:T(8,128)S(1)}, u32[]{:S(2)}, u32[]{:S(2)}) collective-permute-start(f32[2,16,1024]{2,1,0:T(8,128)S(1)} %get-tuple-element.137), channel_id=1, source_target_pairs={{1,0},{3,1},{2,3},{4,2},{5,4},{7,5},{6,7},{8,6},{9,8},{11,9},{10,1... | collective-permute-start | bytes 393224 | tf_op jit(solution)/shard_map/ppermute | solution.py:835
  125.3 15.5 %collective-permute-start.28 = (f32[32,16,256]{2,1,0:T(8,128)S(1)}, f32[32,16,256]{2,1,0:T(8,128)S(1)}, u32[]{:S(2)}, u32[]{:S(2)}) collective-permute-start(f32[32,16,256]{2,1,0:T(8,128)S(1)} %get-tuple-element.144), channel_id=1, source_target_pairs={{0,1},{1,0},{2,3},{3,2},{4,5},{5,4},{6,7},{7,6},{8,9},{9,8},{10,11... | collective-permute-start | bytes 1572872 | tf_op jit(solution)/shard_map/ppermute | solution.py:791
  128.0 13.2 %collective-permute-start.29 = (f32[32,16,256]{2,1,0:T(8,128)S(1)}, f32[32,16,256]{2,1,0:T(8,128)S(1)}, u32[]{:S(2)}, u32[]{:S(2)}) collective-permute-start(f32[32,16,256]{2,1,0:T(8,128)S(1)} %get-tuple-element.145), channel_id=1, source_target_pairs={{0,2},{1,3},{2,0},{3,1},{4,6},{5,7},{6,4},{7,5},{8,10},{9,11},{10,... | collective-permute-start | bytes 1572872 | tf_op jit(solution)/shard_map/ppermute | solution.py:791
  130.5 1.2 collective-permute-start.24
  131.8 4.7 %collective-permute-start.25 = (f32[48,128]{1,0:T(8,128)S(1)}, f32[48,128]{1,0:T(8,128)S(1)}, u32[]{:S(2)}, u32[]{:S(2)}) collective-permute-start(f32[48,128]{1,0:T(8,128)S(1)} %add.68), channel_id=1, source_target_pairs={{0,8},{1,9},{2,10},{3,11},{4,12},{5,13},{6,14},{7,15},{8,0},{9,1},... | collective-permute-start | bytes 73736 | tf_op jit(solution)/shard_map/ppermute | solution.py:784
  134.1 4.9 %collective-permute-start.26 = (f32[48,128]{1,0:T(8,128)S(1)}, f32[48,128]{1,0:T(8,128)S(1)}, u32[]{:S(2)}, u32[]{:S(2)}) collective-permute-start(f32[48,128]{1,0:T(8,128)S(1)} %add.68), channel_id=1, source_target_pairs={{0,16},{1,17},{2,18},{3,19},{4,20},{5,21},{6,22},{7,23},{8,24},{9,... | collective-permute-start | bytes 73736 | tf_op jit(solution)/shard_map/ppermute | solution.py:784
  135.1 5.6 %collective-permute-start.27 = (f32[48,128]{1,0:T(8,128)S(1)}, f32[48,128]{1,0:T(8,128)S(1)}, u32[]{:S(2)}, u32[]{:S(2)}) collective-permute-start(f32[48,128]{1,0:T(8,128)S(1)} %add.68), channel_id=1, source_target_pairs={{0,24},{1,25},{2,26},{3,27},{4,28},{5,29},{6,30},{7,31},{8,16},{9,... | collective-permute-start | bytes 73736 | tf_op jit(solution)/shard_map/ppermute | solution.py:784
  141.1 3.8 %collective-permute-start.30 = (f32[48,128]{1,0:T(8,128)S(1)}, f32[48,128]{1,0:T(8,128)S(1)}, u32[]{:S(2)}, u32[]{:S(2)}) collective-permute-start(f32[48,128]{1,0:T(8,128)S(1)} %add_add_fusion.1), channel_id=1, source_target_pairs={{0,1},{1,0},{2,3},{3,2},{4,5},{5,4},{6,7},{7,6},{8,9},{9,8},{10,11... | collective-permute-start | bytes 73736 | tf_op jit(solution)/shard_map/ppermute | solution.py:784
  142.8 3.8 %collective-permute-start.31 = (f32[48,128]{1,0:T(8,128)S(1)}, f32[48,128]{1,0:T(8,128)S(1)}, u32[]{:S(2)}, u32[]{:S(2)}) collective-permute-start(f32[48,128]{1,0:T(8,128)S(1)} %add_add_fusion.1), channel_id=1, source_target_pairs={{0,2},{1,3},{2,0},{3,1},{4,6},{5,7},{6,4},{7,5},{8,10},{9,11},{10,... | collective-permute-start | bytes 73736 | tf_op jit(solution)/shard_map/ppermute | solution.py:784
  144.5 4.7 %collective-permute-start.32 = (f32[48,128]{1,0:T(8,128)S(1)}, f32[48,128]{1,0:T(8,128)S(1)}, u32[]{:S(2)}, u32[]{:S(2)}) collective-permute-start(f32[48,128]{1,0:T(8,128)S(1)} %add_add_fusion.1), channel_id=1, source_target_pairs={{0,3},{1,2},{2,1},{3,0},{4,7},{5,6},{6,5},{7,4},{8,11},{9,10},{10,... | collective-permute-start | bytes 73736 | tf_op jit(solution)/shard_map/ppermute | solution.py:784
  149.3 13.6 %collective-permute-start.33 = (f32[32,16,256]{2,1,0:T(8,128)S(1)}, f32[32,16,256]{2,1,0:T(8,128)S(1)}, u32[]{:S(2)}, u32[]{:S(2)}) collective-permute-start(f32[32,16,256]{2,1,0:T(8,128)S(1)} %get-tuple-element.152), channel_id=1, source_target_pairs={{0,3},{1,2},{2,1},{3,0},{4,7},{5,6},{6,5},{7,4},{8,11},{9,10},{10,... | collective-permute-start | bytes 1572872 | tf_op jit(solution)/shard_map/ppermute | solution.py:791

commit v6 on v5

--- a/solution.py
+++ b/solution.py
@@ -14,6 +14,7 @@
 spatial_rate = 0.25
 shift_numerator = 16.0
 ritz_offset = 1.5
+far = 1e4
 highest = lax.Precision.HIGHEST
 f32 = jnp.float32
 bf16 = jnp.bfloat16
@@ -251,25 +252,25 @@
     chunk_refs, (w_ref, deg_ref, image_ref) = rest[:chunks], rest[chunks:]
     depth, cols = deg_ref.shape
     spread(info_ref, chunk_refs, image_ref)
+    row = lax.broadcasted_iota(jnp.int32, (2, cols), 0) + info_ref[0] * depth
+    image_ref[0:2, :] = jnp.where(row - 2 >= 0, image_ref[0:2, :], far)
+    inside = row + depth < total_rows
+    image_ref[2 + depth :, :] = jnp.where(inside, image_ref[2 + depth :, :], far)
     center = image_ref[2 : 2 + depth, :]
-    row = lax.broadcasted_iota(jnp.int32, (depth, cols), 0) + info_ref[0] * depth
     col = lax.broadcasted_iota(jnp.int32, (depth, cols), 1)
     degree = jnp.zeros((depth, cols), f32)
     for b in range(-2, 3):
-        moved = pltpu.roll(center, b % cols, 1) if b else center
-        col_ok = (col - b >= 0) & (col - b < cols)
+        moved = center
+        if b:
+            col_ok = (col - b >= 0) & (col - b < cols)
+            moved = jnp.where(col_ok, pltpu.roll(center, b % cols, 1), -far)
         total = None
         for a in range(-2, 3):
             if a == 0 and b == 0:
                 weight = jnp.ones((depth, cols), f32)
             else:
                 contrast = moved - image_ref[2 + a : 2 + a + depth, :]
-                ok = col_ok & (row + a >= 0) & (row + a < total_rows)
-                weight = jnp.where(
-                    ok,
-                    jnp.exp(-beta_value * contrast * contrast - spatial_rate * (a * a + b * b)),
-                    0.0,
-                )
+                weight = jnp.exp(-beta_value * contrast * contrast - spatial_rate * (a * a + b * b))
             w_ref[:, OFFSETS.index((a, b)), :] = weight
             total = weight if total is None else total + weight
         degree = degree + (pltpu.roll(total, (-b) % cols, 1) if b else total)

time: 165 us -> 165 us (level)
  transfers between devices with their start and end apart: 34 -> 34, of which waited for: 20 -> 21; matrix products, arithmetic and copies ran while one was open for 1% -> 1% of each run, Pallas kernels for 26% -> 25%
where the time goes in v6:
time: 165 us
  Pallas kernels  59.7 us (36%)
  starting transfers between devices  54.5 us (33%)
  waiting for transfers between devices  48 us (29%)
  local copies, waits for them, and re-layouts  1.69 us (1%)
    ppermute x14, starting transfers between devices, add_up(): lax.ppermute(value, BOTH, [(i, i ^ m) for i in range(strips)])  23.7 us
    pallas_call x4, Pallas kernels, apply_graph(): pl.pallas_call(functools.partial(graph_kernel, order, keep, lane_shift, c...  21.4 us
    ppermute x9, waiting for transfers between devices, away(): return lax.ppermute(piece, 'col', [(c, c ^ d) for c in range(chunks)])  18.2 us
    ppermute x14, waiting for transfers between devices, add_up(): lax.ppermute(value, BOTH, [(i, i ^ m) for i in range(strips)])  16.3 us
    ppermute x9, starting transfers between devices, away(): return lax.ppermute(piece, 'col', [(c, c ^ d) for c in range(chunks)])  13.4 us
    ppermute x7, waiting for transfers between devices, local(): found[place & (1 << len(group)) - 1] = lax.ppermute(ends, BOTH, pairs)  11.7 us
    ppermute x7, starting transfers between devices, local(): found[place & (1 << len(group)) - 1] = lax.ppermute(ends, BOTH, pairs)  9.59 us
    pallas_call x1, Pallas kernels, ritz_step(): pl.pallas_call(functools.partial(ritz_kernel, fields, pixel_total), out_s...  9.04 us
  transfers between devices with their start and end apart: 34, of which 21 were waited for; matrix products, arithmetic and copies ran while one was open for 1% of the time, Pallas kernels for 25%

profile of v6, /device:TPU:0, one launch (start us, length us, event | category | flops | bytes accessed | tf_op | source)
XLA Modules:
  0.0 165.0 jit_solution(6019007495448915310)
XLA Ops:
  0.6 2.0 %edges.1 = (f32[2,33,256]{2,1,0:T(8,128)}, f32[2,33,256]{2,1,0:T(8,128)}) custom-call(f32[16,128,256]{2,1,0:T(8,128)} %x_ref.7, f32[16,128,256]{2,1,0:T(8,128)} %x_ref.7, f32[16,128,256]{2,1,0:T(8,128)} %p_ref.3, f32[16,128,256]{2,1,0:T(8,128)} %p_ref.3, f32[128,256]{1,0:T(8,128)} %refs_0_.1, f32[128,256]{1,0:T(8,128)} %refs_0_.1), custom_call_target="tpu_custom_call" | custom-call | bytes 524288 | tf_op jit(solution)/shard_map/edges/pallas_call | solution.py:150
  2.6 2.3 %collective-permute-start = (f32[2,33,256]{2,1,0:T(8,128)}, f32[2,33,256]{2,1,0:T(8,128)S(1)}, u32[]{:S(2)}, u32[]{:S(2)}) collective-permute-start(f32[2,33,256]{2,1,0:T(8,128)} %get-tuple-element.83), channel_id=1, source_target_pairs={{0,4},{4,8},{8,12},{12,16},{16,20},{20,24},{24,28},{1,5},{5,9},{9,... | collective-permute-start | bytes 202760 | tf_op jit(solution)/shard_map/ppermute | solution.py:798
  7.0 1.8 %pack.2 = (f32[39,16,256]{2,1,0:T(8,128)S(1)}, f32[39,16,256]{2,1,0:T(8,128)S(1)}, f32[39,16,256]{2,1,0:T(8,128)S(1)}, f32[39,16,256]{2,1,0:T(8,128)S(1)}) custom-call(s32[9]{0:T(128)S(1)} %dynamic-slice_bitcast_fusion.1.info_ref.refs_0_, f32[16,128,256]{2,1,0:T(8,128)S(1)} %copy-done, f32[128,256]{1,0:T(8,128)S(1)} %copy-done.2), custom_call_target="tpu_custom_call" | custom-call | bytes 4194304 | tf_op jit(solution)/shard_map/pack/pallas_call | solution.py:203
  8.8 1.7 %collective-permute-done.1.below_ref = f32[2,33,256]{2,1,0:T(8,128)S(1)} collective-permute-done((f32[2,33,256]{2,1,0:T(8,128)}, f32[2,33,256]{2,1,0:T(8,128)S(1)}, u32[]{:S(2)}, u32[]{:S(2)}) %collective-permute-start.1) | collective-permute-done | bytes 67616 | tf_op jit(solution)/shard_map/ppermute | solution.py:799
  11.1 1.6 collective-permute-start.2
  12.7 1.5 collective-permute-start.3
  14.7 1.8 %pack.3 = (f32[36,16,256]{2,1,0:T(8,128)S(1)}, f32[36,16,256]{2,1,0:T(8,128)S(1)}, f32[36,16,256]{2,1,0:T(8,128)S(1)}, f32[36,16,256]{2,1,0:T(8,128)S(1)}) custom-call(s32[9]{0:T(128)S(1)} %dynamic-slice_bitcast_fusion.1.info_ref.refs_0_, f32[16,128,256]{2,1,0:T(8,128)S(1)} %copy-done.1), custom_call_target="tpu_custom_call" | custom-call | bytes 4194304 | tf_op jit(solution)/shard_map/pack/pallas_call | solution.py:203
  17.1 1.6 collective-permute-start.10
  18.7 1.5 collective-permute-start.9
  20.2 6.1 %collective-permute-done.2.rest_1_.refs_2_ = f32[39,16,256]{2,1,0:T(8,128)S(1)} collective-permute-done((f32[39,16,256]{2,1,0:T(8,128)S(1)}, f32[39,16,256]{2,1,0:T(8,128)S(1)}, u32[]{:S(2)}, u32[]{:S(2)}) %collective-permute-start.2) | collective-permute-done | bytes 639008 | tf_op jit(solution)/shard_map/ppermute | solution.py:792
  26.3 2.4 %collective-permute-start.11 = (f32[36,16,256]{2,1,0:T(8,128)S(1)}, f32[36,16,256]{2,1,0:T(8,128)S(1)}, u32[]{:S(2)}, u32[]{:S(2)}) collective-permute-start(f32[36,16,256]{2,1,0:T(8,128)S(1)} %get-tuple-element.109), channel_id=1, source_target_pairs={{0,3},{1,2},{2,1},{3,0},{4,7},{5,6},{6,5},{7,4},{8,11},{9,10},{10,... | collective-permute-start | bytes 1769480 | tf_op jit(solution)/shard_map/ppermute | solution.py:792
  29.6 11.5 %collective-permute-done.4.rest_3_.refs_4_ = f32[39,16,256]{2,1,0:T(8,128)S(1)} collective-permute-done((f32[39,16,256]{2,1,0:T(8,128)S(1)}, f32[39,16,256]{2,1,0:T(8,128)S(1)}, u32[]{:S(2)}, u32[]{:S(2)}) %collective-permute-start.4) | collective-permute-done | bytes 639008 | tf_op jit(solution)/shard_map/ppermute | solution.py:792
  41.0 2.7 %weights.1 = (f32[32,25,1024]{2,1,0:T(8,128)S(1)}, f32[32,1024]{1,0:T(8,128)S(1)}) custom-call(s32[9]{0:T(128)S(1)} %dynamic-slice_bitcast_fusion.1.info_ref.refs_0_, f32[39,16,256]{2,1,0:T(8,128)S(1)} %get-tuple-element.99.rest_0_.refs_1_, f32[39,16,256]{2,1,0:T(8,128)S(1)} %collective-permute-done.2.rest_1_.refs_2_, ...), custom_call_target="tpu_custom_call" | custom-call | flops 49152000 | bytes 3276800 | tf_op jit(solution)/shard_map/weights/pallas_call | solution.py:282
  43.8 7.1 %graph_v_all.1 = (f32[32,16,1024]{2,1,0:T(8,128)S(1)}, f32[32,16,1024]{2,1,0:T(8,128)S(1)}, f32[16,128]{1,0:T(8,128)S(1)}) custom-call(s32[9]{0:T(128)S(1)} %dynamic-slice_bitcast_fusion.1.info_ref.refs_0_, f32[39,16,256]{2,1,0:T(8,128)S(1)} %get-tuple-element.99.rest_0_.refs_1_, f32[39,16,256]{2,1,0:T(8,128)S(1)} %collective-permute-done.2.rest_1_.refs_2_, ...), custom_call_target="tpu_custom_call" | custom-call | flops 104857600 | bytes 9568256 | tf_op jit(solution)/shard_map/graph_v_all/pallas_call | solution.py:388
  50.9 4.6 %collective-permute-start.5 = (f32[16,128]{1,0:T(8,128)S(1)}, f32[16,128]{1,0:T(8,128)S(1)}, u32[]{:S(2)}, u32[]{:S(2)}) collective-permute-start(f32[16,128]{1,0:T(8,128)S(1)} %get-tuple-element.105), channel_id=1, source_target_pairs={{0,4},{1,5},{2,6},{3,7},{4,0},{5,1},{6,2},{7,3},{8,12},{9,13},{10,... | collective-permute-start | bytes 24584 | tf_op jit(solution)/shard_map/ppermute | solution.py:785
  56.4 1.5 collective-permute-start.6
  57.9 2.7 %collective-permute-start.7 = (f32[16,128]{1,0:T(8,128)S(1)}, f32[16,128]{1,0:T(8,128)S(1)}, u32[]{:S(2)}, u32[]{:S(2)}) collective-permute-start(f32[16,128]{1,0:T(8,128)S(1)} %add.59), channel_id=1, source_target_pairs={{0,16},{1,17},{2,18},{3,19},{4,20},{5,21},{6,22},{7,23},{8,24},{9,... | collective-permute-start | bytes 24584 | tf_op jit(solution)/shard_map/ppermute | solution.py:785
  60.6 3.1 %collective-permute-start.8 = (f32[16,128]{1,0:T(8,128)S(1)}, f32[16,128]{1,0:T(8,128)S(1)}, u32[]{:S(2)}, u32[]{:S(2)}) collective-permute-start(f32[16,128]{1,0:T(8,128)S(1)} %add.59), channel_id=1, source_target_pairs={{0,24},{1,25},{2,26},{3,27},{4,28},{5,29},{6,30},{7,31},{8,16},{9,... | collective-permute-start | bytes 24584 | tf_op jit(solution)/shard_map/ppermute | solution.py:785
  63.7 2.4 %collective-permute-done.8 = f32[16,128]{1,0:T(8,128)S(1)} collective-permute-done((f32[16,128]{1,0:T(8,128)S(1)}, f32[16,128]{1,0:T(8,128)S(1)}, u32[]{:S(2)}, u32[]{:S(2)}) %collective-permute-start.8) | collective-permute-done | bytes 8224 | tf_op jit(solution)/shard_map/ppermute | solution.py:785
  66.4 1.4 collective-permute-start.12
  68.4 1.5 collective-permute-start.14
  70.0 1.4 collective-permute-done.13
  71.4 1.5 collective-permute-done.14
  73.0 6.6 %residual_spectrum.1 = (f32[32,16,1024]{2,1,0:T(8,128)S(1)}, f32[2,16,1024]{2,1,0:T(8,128)S(1)}) custom-call(f32[16,128]{1,0:T(8,128)S(1)} %add_add_fusion.2.gram_ref.first_ref, f32[32,16,1024]{2,1,0:T(8,128)S(1)} %get-tuple-element.111.g_ref, f32[32,16,1024]{2,1,0:T(8,128)S(1)} %get-tuple-element.112.x_ref.refs_7_.refs_3_.refs_5_, ...), custom_call_target="tpu_custom_call" | custom-call | flops 3221225472 | bytes 6291456 | tf_op jit(solution)/shard_map/residual_spectrum/pallas_call | solution.py:456
  79.6 1.4 collective-permute-start.15
  81.0 1.5 collective-permute-start.16
  83.1 2.9 %collective-permute-done.15.refs_1_ = f32[2,16,1024]{2,1,0:T(8,128)S(1)} collective-permute-done((f32[2,16,1024]{2,1,0:T(8,128)S(1)}, f32[2,16,1024]{2,1,0:T(8,128)S(1)}, u32[]{:S(2)}, u32[]{:S(2)}) %collective-permute-start.15) | collective-permute-done | bytes 131104 | tf_op jit(solution)/shard_map/ppermute | solution.py:823
  86.0 3.1 %collective-permute-done.16.refs_2_ = f32[2,16,1024]{2,1,0:T(8,128)S(1)} collective-permute-done((f32[2,16,1024]{2,1,0:T(8,128)S(1)}, f32[2,16,1024]{2,1,0:T(8,128)S(1)}, u32[]{:S(2)}, u32[]{:S(2)}) %collective-permute-start.16) | collective-permute-done | bytes 131104 | tf_op jit(solution)/shard_map/ppermute | solution.py:823
  93.1 3.5 %collective-permute-start.19 = (f32[2,16,1024]{2,1,0:T(8,128)S(1)}, f32[2,16,1024]{2,1,0:T(8,128)S(1)}, u32[]{:S(2)}, u32[]{:S(2)}) collective-permute-start(f32[2,16,1024]{2,1,0:T(8,128)S(1)} %get-tuple-element.123.refs_0_), channel_id=1, source_target_pairs={{0,8},{1,9},{2,10},{3,11},{4,12},{5,13},{6,14},{7,15},{8,0},{9,1},... | collective-permute-start | bytes 393224 | tf_op jit(solution)/shard_map/ppermute | solution.py:823
  99.1 7.4 %graph_xv_all.1 = (f32[32,16,1024]{2,1,0:T(8,128)S(1)}, f32[32,128]{1,0:T(8,128)S(1)}) custom-call(s32[9]{0:T(128)S(1)} %dynamic-slice_bitcast_fusion.1.info_ref.refs_0_, f32[36,16,256]{2,1,0:T(8,128)S(1)} %get-tuple-element.126.refs_1_, f32[36,16,256]{2,1,0:T(8,128)S(1)} %collective-permute-done.9.refs_2_, ...), custom_call_target="tpu_custom_call" | custom-call | flops 104857600 | bytes 9568256 | tf_op jit(solution)/shard_map/graph_xv_all/pallas_call | solution.py:388
  106.5 3.0 %collective-permute-done.20.refs_2_ = f32[2,16,1024]{2,1,0:T(8,128)S(1)} collective-permute-done((f32[2,16,1024]{2,1,0:T(8,128)S(1)}, f32[2,16,1024]{2,1,0:T(8,128)S(1)}, u32[]{:S(2)}, u32[]{:S(2)}) %collective-permute-start.20) | collective-permute-done | bytes 131104 | tf_op jit(solution)/shard_map/ppermute | solution.py:823
  110.1 4.9 %row_inverse.1 = (f32[32,16,1024]{2,1,0:T(8,128)S(1)}, f32[2,16,1024]{2,1,0:T(8,128)S(1)}, f32[2,16,1024]{2,1,0:T(8,128)S(1)}, f32[32,16,256]{2,1,0:T(8,128)S(1)...) custom-call(s32[9]{0:T(128)S(1)} %dynamic-slice_bitcast_fusion.1.info_ref.refs_0_, ...), custom_call_target="tpu_custom_call" | custom-call | flops 3221225472 | bytes 8388608 | tf_op jit(solution)/shard_map/row_inverse/pallas_call | solution.py:551
  115.0 2.8 %collective-permute-start.22 = (f32[2,16,1024]{2,1,0:T(8,128)S(1)}, f32[2,16,1024]{2,1,0:T(8,128)S(1)}, u32[]{:S(2)}, u32[]{:S(2)}) collective-permute-start(f32[2,16,1024]{2,1,0:T(8,128)S(1)} %get-tuple-element.136), channel_id=1, source_target_pairs={{0,1},{1,3},{3,2},{2,4},{4,5},{5,7},{7,6},{6,8},{8,9},{9,11},{11,1... | collective-permute-start | bytes 393224 | tf_op jit(solution)/shard_map/ppermute | solution.py:835
  117.8 1.5 collective-permute-start.23
  119.4 5.9 %graph_xvp_inner.1 = f32[48,128]{1,0:T(8,128)S(1)} custom-call(f32[32,16,1024]{2,1,0:T(8,128)S(1)} %get-tuple-element.138.refs_0_, f32[32,25,1024]{2,1,0:T(8,128)S(1)} %get-tuple-element.103.refs_5_.refs_1_.refs_3_, f32[32,1024]{1,0:T(8,128)S(1)} %get-tuple-element.104.refs_6_.deg_ref.refs_2_.refs_4_, ...), custom_call_target="tpu_custom_call" | custom-call | flops 104857600 | bytes 9568256 | tf_op jit(solution)/shard_map/graph_xvp_inner/pallas_call | solution.py:388
  125.3 2.7 %collective-permute-start.28 = (f32[32,16,256]{2,1,0:T(8,128)S(1)}, f32[32,16,256]{2,1,0:T(8,128)S(1)}, u32[]{:S(2)}, u32[]{:S(2)}) collective-permute-start(f32[32,16,256]{2,1,0:T(8,128)S(1)} %get-tuple-element.144), channel_id=1, source_target_pairs={{0,1},{1,0},{2,3},{3,2},{4,5},{5,4},{6,7},{7,6},{8,9},{9,8},{10,11... | collective-permute-start | bytes 1572872 | tf_op jit(solution)/shard_map/ppermute | solution.py:792
  128.0 1.5 collective-permute-start.29
  131.8 2.3 %collective-permute-start.25 = (f32[48,128]{1,0:T(8,128)S(1)}, f32[48,128]{1,0:T(8,128)S(1)}, u32[]{:S(2)}, u32[]{:S(2)}) collective-permute-start(f32[48,128]{1,0:T(8,128)S(1)} %add.68), channel_id=1, source_target_pairs={{0,8},{1,9},{2,10},{3,11},{4,12},{5,13},{6,14},{7,15},{8,0},{9,1},... | collective-permute-start | bytes 73736 | tf_op jit(solution)/shard_map/ppermute | solution.py:785
  135.1 1.4 collective-permute-start.27
  136.5 2.4 %collective-permute-done.26 = f32[48,128]{1,0:T(8,128)S(1)} collective-permute-done((f32[48,128]{1,0:T(8,128)S(1)}, f32[48,128]{1,0:T(8,128)S(1)}, u32[]{:S(2)}, u32[]{:S(2)}) %collective-permute-start.26) | collective-permute-done | bytes 24608 | tf_op jit(solution)/shard_map/ppermute | solution.py:785
  138.9 1.8 %collective-permute-done.27 = f32[48,128]{1,0:T(8,128)S(1)} collective-permute-done((f32[48,128]{1,0:T(8,128)S(1)}, f32[48,128]{1,0:T(8,128)S(1)}, u32[]{:S(2)}, u32[]{:S(2)}) %collective-permute-start.27) | collective-permute-done | bytes 24608 | tf_op jit(solution)/shard_map/ppermute | solution.py:785
  141.1 1.7 %collective-permute-start.30 = (f32[48,128]{1,0:T(8,128)S(1)}, f32[48,128]{1,0:T(8,128)S(1)}, u32[]{:S(2)}, u32[]{:S(2)}) collective-permute-start(f32[48,128]{1,0:T(8,128)S(1)} %add_add_fusion.1), channel_id=1, source_target_pairs={{0,1},{1,0},{2,3},{3,2},{4,5},{5,4},{6,7},{7,6},{8,9},{9,8},{10,11... | collective-permute-start | bytes 73736 | tf_op jit(solution)/shard_map/ppermute | solution.py:785
  142.8 1.7 %collective-permute-start.31 = (f32[48,128]{1,0:T(8,128)S(1)}, f32[48,128]{1,0:T(8,128)S(1)}, u32[]{:S(2)}, u32[]{:S(2)}) collective-permute-start(f32[48,128]{1,0:T(8,128)S(1)} %add_add_fusion.1), channel_id=1, source_target_pairs={{0,2},{1,3},{2,0},{3,1},{4,6},{5,7},{6,4},{7,5},{8,10},{9,11},{10,... | collective-permute-start | bytes 73736 | tf_op jit(solution)/shard_map/ppermute | solution.py:785
  145.0 1.7 %collective-permute-done.31 = f32[48,128]{1,0:T(8,128)S(1)} collective-permute-done((f32[48,128]{1,0:T(8,128)S(1)}, f32[48,128]{1,0:T(8,128)S(1)}, u32[]{:S(2)}, u32[]{:S(2)}) %collective-permute-start.31) | collective-permute-done | bytes 24608 | tf_op jit(solution)/shard_map/ppermute | solution.py:785
  146.6 2.6 %collective-permute-done.32 = f32[48,128]{1,0:T(8,128)S(1)} collective-permute-done((f32[48,128]{1,0:T(8,128)S(1)}, f32[48,128]{1,0:T(8,128)S(1)}, u32[]{:S(2)}, u32[]{:S(2)}) %collective-permute-start.32) | collective-permute-done | bytes 24608 | tf_op jit(solution)/shard_map/ppermute | solution.py:785
  149.4 9.0 %ritz.1 = (f32[1,16]{1,0:T(1,128)}, f32[48,16]{1,0:T(8,128)S(1)}) custom-call(f32[16,128]{1,0:T(8,128)S(1)} %add_add_fusion.2.gram_ref.first_ref, f32[48,128]{1,0:T(8,128)S(1)} %add_add_fusion.second_ref), custom_call_target="tpu_custom_call" | custom-call | flops 33554432 | bytes 65536 | tf_op jit(solution)/shard_map/ritz/pallas_call | solution.py:643
  158.4 4.5 %combine.2 = (f32[16,128,256]{2,1,0:T(8,128)}, f32[16,128,256]{2,1,0:T(8,128)}, bf16[128,384]{1,0:T(8,128)(2,1)S(1)}, bf16[128,384]{1,0:T(8,128)(2,1)S(1)}) custom-call(s32[9]{0:T(128)S(1)} %dynamic-slice_bitcast_fusion.1.info_ref.refs_0_, f32[48,16]{1,0:T(8,128)S(1)} %get-tuple-element.151.coeff_ref, f32[16,128,256]{2,1,0:T(8,128)S(1)} %copy-done, ...), custom_call_target="tpu_custom_call" | custom-call | flops 19660800 | bytes 7864320 | tf_op jit(solution)/shard_map/combine/pallas_call | solution.py:720
  162.9 2.0 %combine.3 = (f32[16,128,256]{2,1,0:T(8,128)}, f32[16,128,256]{2,1,0:T(8,128)}) custom-call(s32[9]{0:T(128)S(1)} %dynamic-slice_bitcast_fusion.1.info_ref.refs_0_, f32[48,16]{1,0:T(8,128)S(1)} %get-tuple-element.151.coeff_ref, f32[16,128,256]{2,1,0:T(8,128)S(1)} %copy-done, ...), custom_call_target="tpu_custom_call", output_to_operand_aliasing={{0}: (5, {}), {1}: (6, {})} | custom-call | flops 6553600 | bytes 2621440 | tf_op jit(solution)/shard_map/combine/pallas_call | solution.py:720
  (72 shorter events, 18.4 us)
Async XLA Ops:
  0.6 6.4 %copy-start.2 = (f32[128,256]{1,0:T(8,128)S(1)}, f32[128,256]{1,0:T(8,128)}, u32[]{:S(2)}) copy-start(f32[128,256]{1,0:T(8,128)} %refs_0_.1) | copy-start | bytes 393220
  0.6 6.3 %copy-start = (f32[16,128,256]{2,1,0:T(8,128)S(1)}, f32[16,128,256]{2,1,0:T(8,128)}, u32[]{:S(2)}) copy-start(f32[16,128,256]{2,1,0:T(8,128)} %x_ref.7) | copy-start | bytes 6291460
  2.6 6.2 %collective-permute-start = (f32[2,33,256]{2,1,0:T(8,128)}, f32[2,33,256]{2,1,0:T(8,128)S(1)}, u32[]{:S(2)}, u32[]{:S(2)}) collective-permute-start(f32[2,33,256]{2,1,0:T(8,128)} %get-tuple-element.83), channel_id=1, source_target_pairs={{0,4},{4,8},{8,12},{12,16},{16,20},{20,24},{24,28},{1,5},{5,9},{9,... | collective-permute-start | bytes 202760 | tf_op jit(solution)/shard_map/ppermute | solution.py:798
  5.0 5.6 %collective-permute-start.1 = (f32[2,33,256]{2,1,0:T(8,128)}, f32[2,33,256]{2,1,0:T(8,128)S(1)}, u32[]{:S(2)}, u32[]{:S(2)}) collective-permute-start(f32[2,33,256]{2,1,0:T(8,128)} %get-tuple-element.84), channel_id=1, source_target_pairs={{4,0},{8,4},{12,8},{16,12},{20,16},{24,20},{28,24},{5,1},{9,5},{13... | collective-permute-start | bytes 202760 | tf_op jit(solution)/shard_map/ppermute | solution.py:799
  7.0 7.7 %copy-start.1 = (f32[16,128,256]{2,1,0:T(8,128)S(1)}, f32[16,128,256]{2,1,0:T(8,128)}, u32[]{:S(2)}) copy-start(f32[16,128,256]{2,1,0:T(8,128)} %p_ref.3) | copy-start | bytes 6291460
  11.1 15.1 %collective-permute-start.2 = (f32[39,16,256]{2,1,0:T(8,128)S(1)}, f32[39,16,256]{2,1,0:T(8,128)S(1)}, u32[]{:S(2)}, u32[]{:S(2)}) collective-permute-start(f32[39,16,256]{2,1,0:T(8,128)S(1)} %get-tuple-element.95), channel_id=1, source_target_pairs={{0,1},{1,0},{2,3},{3,2},{4,5},{5,4},{6,7},{7,6},{8,9},{9,8},{10,11... | collective-permute-start | bytes 1916936 | tf_op jit(solution)/shard_map/ppermute | solution.py:792
  12.7 16.9 %collective-permute-start.3 = (f32[39,16,256]{2,1,0:T(8,128)S(1)}, f32[39,16,256]{2,1,0:T(8,128)S(1)}, u32[]{:S(2)}, u32[]{:S(2)}) collective-permute-start(f32[39,16,256]{2,1,0:T(8,128)S(1)} %get-tuple-element.97), channel_id=1, source_target_pairs={{0,2},{1,3},{2,0},{3,1},{4,6},{5,7},{6,4},{7,5},{8,10},{9,11},{10,... | collective-permute-start | bytes 1916936 | tf_op jit(solution)/shard_map/ppermute | solution.py:792
  14.2 26.8 %collective-permute-start.4 = (f32[39,16,256]{2,1,0:T(8,128)S(1)}, f32[39,16,256]{2,1,0:T(8,128)S(1)}, u32[]{:S(2)}, u32[]{:S(2)}) collective-permute-start(f32[39,16,256]{2,1,0:T(8,128)S(1)} %get-tuple-element.98), channel_id=1, source_target_pairs={{0,3},{1,2},{2,1},{3,0},{4,7},{5,6},{6,5},{7,4},{8,11},{9,10},{10,... | collective-permute-start | bytes 1916936 | tf_op jit(solution)/shard_map/ppermute | solution.py:792
  17.1 49.0 %collective-permute-start.10 = (f32[36,16,256]{2,1,0:T(8,128)S(1)}, f32[36,16,256]{2,1,0:T(8,128)S(1)}, u32[]{:S(2)}, u32[]{:S(2)}) collective-permute-start(f32[36,16,256]{2,1,0:T(8,128)S(1)} %get-tuple-element.108), channel_id=1, source_target_pairs={{0,2},{1,3},{2,0},{3,1},{4,6},{5,7},{6,4},{7,5},{8,10},{9,11},{10,... | collective-permute-start | bytes 1769480 | tf_op jit(solution)/shard_map/ppermute | solution.py:792
  18.7 47.4 %collective-permute-start.9 = (f32[36,16,256]{2,1,0:T(8,128)S(1)}, f32[36,16,256]{2,1,0:T(8,128)S(1)}, u32[]{:S(2)}, u32[]{:S(2)}) collective-permute-start(f32[36,16,256]{2,1,0:T(8,128)S(1)} %get-tuple-element.107), channel_id=1, source_target_pairs={{0,1},{1,0},{2,3},{3,2},{4,5},{5,4},{6,7},{7,6},{8,9},{9,8},{10,11... | collective-permute-start | bytes 1769480 | tf_op jit(solution)/shard_map/ppermute | solution.py:792
  26.3 40.1 %collective-permute-start.11 = (f32[36,16,256]{2,1,0:T(8,128)S(1)}, f32[36,16,256]{2,1,0:T(8,128)S(1)}, u32[]{:S(2)}, u32[]{:S(2)}) collective-permute-start(f32[36,16,256]{2,1,0:T(8,128)S(1)} %get-tuple-element.109), channel_id=1, source_target_pairs={{0,3},{1,2},{2,1},{3,0},{4,7},{5,6},{6,5},{7,4},{8,11},{9,10},{10,... | collective-permute-start | bytes 1769480 | tf_op jit(solution)/shard_map/ppermute | solution.py:792
  43.8 29.1 %copy-start.7 = (bf16[1024,1024]{1,0:T(8,128)(2,1)S(1)}, bf16[1024,1024]{1,0:T(8,128)(2,1)}, u32[]{:S(2)}) copy-start(bf16[1024,1024]{1,0:T(8,128)(2,1)} %constant.45.clone.high_ref) | copy-start | bytes 6291460
  43.8 29.1 %copy-start.8 = (bf16[1024,1024]{1,0:T(8,128)(2,1)S(1)}, bf16[1024,1024]{1,0:T(8,128)(2,1)}, u32[]{:S(2)}) copy-start(bf16[1024,1024]{1,0:T(8,128)(2,1)} %constant.46.clone.low_ref) | copy-start | bytes 6291460
  43.8 29.1 %copy-start.9 = (f32[32,1024]{1,0:T(8,128)S(1)}, f32[32,1024]{1,0:T(8,128)}, u32[]{:S(2)}) copy-start(f32[32,1024]{1,0:T(8,128)} %constant.47.clone.eps_ref.refs_7_) | copy-start | bytes 393220
  43.8 29.1 %copy-start.10 = (f32[1,1024]{1,0:T(1,128)S(1)}, f32[1,1024]{1,0:T(1,128)}, u32[]{:S(2)}) copy-start(f32[1,1024]{1,0:T(1,128)} %constant.48.clone.last_ref.refs_8_) | copy-start | bytes 12292
  50.9 5.5 %collective-permute-start.5 = (f32[16,128]{1,0:T(8,128)S(1)}, f32[16,128]{1,0:T(8,128)S(1)}, u32[]{:S(2)}, u32[]{:S(2)}) collective-permute-start(f32[16,128]{1,0:T(8,128)S(1)} %get-tuple-element.105), channel_id=1, source_target_pairs={{0,4},{1,5},{2,6},{3,7},{4,0},{5,1},{6,2},{7,3},{8,12},{9,13},{10,... | collective-permute-start | bytes 24584 | tf_op jit(solution)/shard_map/ppermute | solution.py:785
  56.4 4.2 %collective-permute-start.6 = (f32[16,128]{1,0:T(8,128)S(1)}, f32[16,128]{1,0:T(8,128)S(1)}, u32[]{:S(2)}, u32[]{:S(2)}) collective-permute-start(f32[16,128]{1,0:T(8,128)S(1)} %add.59), channel_id=1, source_target_pairs={{0,8},{1,9},{2,10},{3,11},{4,12},{5,13},{6,14},{7,15},{8,0},{9,1},... | collective-permute-start | bytes 24584 | tf_op jit(solution)/shard_map/ppermute | solution.py:785
  57.9 5.8 %collective-permute-start.7 = (f32[16,128]{1,0:T(8,128)S(1)}, f32[16,128]{1,0:T(8,128)S(1)}, u32[]{:S(2)}, u32[]{:S(2)}) collective-permute-start(f32[16,128]{1,0:T(8,128)S(1)} %add.59), channel_id=1, source_target_pairs={{0,16},{1,17},{2,18},{3,19},{4,20},{5,21},{6,22},{7,23},{8,24},{9,... | collective-permute-start | bytes 24584 | tf_op jit(solution)/shard_map/ppermute | solution.py:785
  60.6 5.4 %collective-permute-start.8 = (f32[16,128]{1,0:T(8,128)S(1)}, f32[16,128]{1,0:T(8,128)S(1)}, u32[]{:S(2)}, u32[]{:S(2)}) collective-permute-start(f32[16,128]{1,0:T(8,128)S(1)} %add.59), channel_id=1, source_target_pairs={{0,24},{1,25},{2,26},{3,27},{4,28},{5,29},{6,30},{7,31},{8,16},{9,... | collective-permute-start | bytes 24584 | tf_op jit(solution)/shard_map/ppermute | solution.py:785
  66.4 3.7 %collective-permute-start.12 = (f32[16,128]{1,0:T(8,128)S(1)}, f32[16,128]{1,0:T(8,128)S(1)}, u32[]{:S(2)}, u32[]{:S(2)}) collective-permute-start(f32[16,128]{1,0:T(8,128)S(1)} %add_add_fusion.3), channel_id=1, source_target_pairs={{0,1},{1,0},{2,3},{3,2},{4,5},{5,4},{6,7},{7,6},{8,9},{9,8},{10,11... | collective-permute-start | bytes 24584 | tf_op jit(solution)/shard_map/ppermute | solution.py:785
  67.7 3.7 %collective-permute-start.13 = (f32[16,128]{1,0:T(8,128)S(1)}, f32[16,128]{1,0:T(8,128)S(1)}, u32[]{:S(2)}, u32[]{:S(2)}) collective-permute-start(f32[16,128]{1,0:T(8,128)S(1)} %add_add_fusion.3), channel_id=1, source_target_pairs={{0,2},{1,3},{2,0},{3,1},{4,6},{5,7},{6,4},{7,5},{8,10},{9,11},{10,... | collective-permute-start | bytes 24584 | tf_op jit(solution)/shard_map/ppermute | solution.py:785
  68.4 4.5 %collective-permute-start.14 = (f32[16,128]{1,0:T(8,128)S(1)}, f32[16,128]{1,0:T(8,128)S(1)}, u32[]{:S(2)}, u32[]{:S(2)}) collective-permute-start(f32[16,128]{1,0:T(8,128)S(1)} %add_add_fusion.3), channel_id=1, source_target_pairs={{0,3},{1,2},{2,1},{3,0},{4,7},{5,6},{6,5},{7,4},{8,11},{9,10},{10,... | collective-permute-start | bytes 24584 | tf_op jit(solution)/shard_map/ppermute | solution.py:785
  72.9 17.5 %copy-start.3 = (f32[5,1024]{1,0:T(8,128)S(1)}, f32[5,1024]{1,0:T(8,128)}, u32[]{:S(2)}) copy-start(f32[5,1024]{1,0:T(8,128)} %constant.49.clone.gain_ref) | copy-start | bytes 61444
  73.0 17.5 %copy-start.4 = (f32[5,1024]{1,0:T(8,128)S(1)}, f32[5,1024]{1,0:T(8,128)}, u32[]{:S(2)}) copy-start(f32[5,1024]{1,0:T(8,128)} %constant.50.clone.cross_ref) | copy-start | bytes 61444
  79.6 6.4 %collective-permute-start.15 = (f32[2,16,1024]{2,1,0:T(8,128)S(1)}, f32[2,16,1024]{2,1,0:T(8,128)S(1)}, u32[]{:S(2)}, u32[]{:S(2)}) collective-permute-start(f32[2,16,1024]{2,1,0:T(8,128)S(1)} %get-tuple-element.113.refs_0_), channel_id=1, source_target_pairs={{0,1},{1,0},{2,3},{3,2},{4,5},{5,4},{6,7},{7,6},{8,9},{9,8},{10,11... | collective-permute-start | bytes 393224 | tf_op jit(solution)/shard_map/ppermute | solution.py:823
  81.0 8.1 %collective-permute-start.16 = (f32[2,16,1024]{2,1,0:T(8,128)S(1)}, f32[2,16,1024]{2,1,0:T(8,128)S(1)}, u32[]{:S(2)}, u32[]{:S(2)}) collective-permute-start(f32[2,16,1024]{2,1,0:T(8,128)S(1)} %get-tuple-element.113.refs_0_), channel_id=1, source_target_pairs={{0,3},{1,2},{2,1},{3,0},{4,7},{5,6},{6,5},{7,4},{8,11},{9,10},{10,... | collective-permute-start | bytes 393224 | tf_op jit(solution)/shard_map/ppermute | solution.py:823
  82.5 7.9 %collective-permute-start.17 = (f32[2,16,1024]{2,1,0:T(8,128)S(1)}, f32[2,16,1024]{2,1,0:T(8,128)S(1)}, u32[]{:S(2)}, u32[]{:S(2)}) collective-permute-start(f32[2,16,1024]{2,1,0:T(8,128)S(1)} %get-tuple-element.113.refs_0_), channel_id=1, source_target_pairs={{0,2},{1,3},{2,0},{3,1},{4,6},{5,7},{6,4},{7,5},{8,10},{9,11},{10,... | collective-permute-start | bytes 393224 | tf_op jit(solution)/shard_map/ppermute | solution.py:823
  91.1 1.4 collective-permute-start.18
  93.1 17.0 %copy-start.5 = (bf16[1024,1024]{1,0:T(8,128)(2,1)S(1)}, bf16[1024,1024]{1,0:T(8,128)(2,1)}, u32[]{:S(2)}) copy-start(bf16[1024,1024]{1,0:T(8,128)(2,1)} %constant.43.clone.refs_9_) | copy-start | bytes 6291460
  93.1 17.0 %copy-start.6 = (bf16[1024,1024]{1,0:T(8,128)(2,1)S(1)}, bf16[1024,1024]{1,0:T(8,128)(2,1)}, u32[]{:S(2)}) copy-start(bf16[1024,1024]{1,0:T(8,128)(2,1)} %constant.44.clone.refs_10_) | copy-start | bytes 6291460
  93.1 13.4 %collective-permute-start.19 = (f32[2,16,1024]{2,1,0:T(8,128)S(1)}, f32[2,16,1024]{2,1,0:T(8,128)S(1)}, u32[]{:S(2)}, u32[]{:S(2)}) collective-permute-start(f32[2,16,1024]{2,1,0:T(8,128)S(1)} %get-tuple-element.123.refs_0_), channel_id=1, source_target_pairs={{0,8},{1,9},{2,10},{3,11},{4,12},{5,13},{6,14},{7,15},{8,0},{9,1},... | collective-permute-start | bytes 393224 | tf_op jit(solution)/shard_map/ppermute | solution.py:823
  96.6 12.9 %collective-permute-start.20 = (f32[2,16,1024]{2,1,0:T(8,128)S(1)}, f32[2,16,1024]{2,1,0:T(8,128)S(1)}, u32[]{:S(2)}, u32[]{:S(2)}) collective-permute-start(f32[2,16,1024]{2,1,0:T(8,128)S(1)} %get-tuple-element.123.refs_0_), channel_id=1, source_target_pairs={{0,16},{1,17},{2,18},{3,19},{4,20},{5,21},{6,22},{7,23},{8,24},{9,... | collective-permute-start | bytes 393224 | tf_op jit(solution)/shard_map/ppermute | solution.py:823
  97.7 11.8 %collective-permute-start.21 = (f32[2,16,1024]{2,1,0:T(8,128)S(1)}, f32[2,16,1024]{2,1,0:T(8,128)S(1)}, u32[]{:S(2)}, u32[]{:S(2)}) collective-permute-start(f32[2,16,1024]{2,1,0:T(8,128)S(1)} %get-tuple-element.123.refs_0_), channel_id=1, source_target_pairs={{0,24},{1,25},{2,26},{3,27},{4,28},{5,29},{6,30},{7,31},{8,16},{9,... | collective-permute-start | bytes 393224 | tf_op jit(solution)/shard_map/ppermute | solution.py:823
  115.0 10.2 %collective-permute-start.22 = (f32[2,16,1024]{2,1,0:T(8,128)S(1)}, f32[2,16,1024]{2,1,0:T(8,128)S(1)}, u32[]{:S(2)}, u32[]{:S(2)}) collective-permute-start(f32[2,16,1024]{2,1,0:T(8,128)S(1)} %get-tuple-element.136), channel_id=1, source_target_pairs={{0,1},{1,3},{3,2},{2,4},{4,5},{5,7},{7,6},{6,8},{8,9},{9,11},{11,1... | collective-permute-start | bytes 393224 | tf_op jit(solution)/shard_map/ppermute | solution.py:835
  117.8 7.4 %collective-permute-start.23 = (f32[2,16,1024]{2,1,0:T(8,128)S(1)}, f32[2,16,1024]{2,1,0:T(8,128)S(1)}, u32[]{:S(2)}, u32[]{:S(2)}) collective-permute-start(f32[2,16,1024]{2,1,0:T(8,128)S(1)} %get-tuple-element.137), channel_id=1, source_target_pairs={{1,0},{3,1},{2,3},{4,2},{5,4},{7,5},{6,7},{8,6},{9,8},{11,9},{10,1... | collective-permute-start | bytes 393224 | tf_op jit(solution)/shard_map/ppermute | solution.py:836
  125.3 15.5 %collective-permute-start.28 = (f32[32,16,256]{2,1,0:T(8,128)S(1)}, f32[32,16,256]{2,1,0:T(8,128)S(1)}, u32[]{:S(2)}, u32[]{:S(2)}) collective-permute-start(f32[32,16,256]{2,1,0:T(8,128)S(1)} %get-tuple-element.144), channel_id=1, source_target_pairs={{0,1},{1,0},{2,3},{3,2},{4,5},{5,4},{6,7},{7,6},{8,9},{9,8},{10,11... | collective-permute-start | bytes 1572872 | tf_op jit(solution)/shard_map/ppermute | solution.py:792
  128.0 13.2 %collective-permute-start.29 = (f32[32,16,256]{2,1,0:T(8,128)S(1)}, f32[32,16,256]{2,1,0:T(8,128)S(1)}, u32[]{:S(2)}, u32[]{:S(2)}) collective-permute-start(f32[32,16,256]{2,1,0:T(8,128)S(1)} %get-tuple-element.145), channel_id=1, source_target_pairs={{0,2},{1,3},{2,0},{3,1},{4,6},{5,7},{6,4},{7,5},{8,10},{9,11},{10,... | collective-permute-start | bytes 1572872 | tf_op jit(solution)/shard_map/ppermute | solution.py:792
  130.5 1.2 collective-permute-start.24
  131.8 4.7 %collective-permute-start.25 = (f32[48,128]{1,0:T(8,128)S(1)}, f32[48,128]{1,0:T(8,128)S(1)}, u32[]{:S(2)}, u32[]{:S(2)}) collective-permute-start(f32[48,128]{1,0:T(8,128)S(1)} %add.68), channel_id=1, source_target_pairs={{0,8},{1,9},{2,10},{3,11},{4,12},{5,13},{6,14},{7,15},{8,0},{9,1},... | collective-permute-start | bytes 73736 | tf_op jit(solution)/shard_map/ppermute | solution.py:785
  134.1 4.9 %collective-permute-start.26 = (f32[48,128]{1,0:T(8,128)S(1)}, f32[48,128]{1,0:T(8,128)S(1)}, u32[]{:S(2)}, u32[]{:S(2)}) collective-permute-start(f32[48,128]{1,0:T(8,128)S(1)} %add.68), channel_id=1, source_target_pairs={{0,16},{1,17},{2,18},{3,19},{4,20},{5,21},{6,22},{7,23},{8,24},{9,... | collective-permute-start | bytes 73736 | tf_op jit(solution)/shard_map/ppermute | solution.py:785
  135.1 5.6 %collective-permute-start.27 = (f32[48,128]{1,0:T(8,128)S(1)}, f32[48,128]{1,0:T(8,128)S(1)}, u32[]{:S(2)}, u32[]{:S(2)}) collective-permute-start(f32[48,128]{1,0:T(8,128)S(1)} %add.68), channel_id=1, source_target_pairs={{0,24},{1,25},{2,26},{3,27},{4,28},{5,29},{6,30},{7,31},{8,16},{9,... | collective-permute-start | bytes 73736 | tf_op jit(solution)/shard_map/ppermute | solution.py:785
  141.1 3.8 %collective-permute-start.30 = (f32[48,128]{1,0:T(8,128)S(1)}, f32[48,128]{1,0:T(8,128)S(1)}, u32[]{:S(2)}, u32[]{:S(2)}) collective-permute-start(f32[48,128]{1,0:T(8,128)S(1)} %add_add_fusion.1), channel_id=1, source_target_pairs={{0,1},{1,0},{2,3},{3,2},{4,5},{5,4},{6,7},{7,6},{8,9},{9,8},{10,11... | collective-permute-start | bytes 73736 | tf_op jit(solution)/shard_map/ppermute | solution.py:785
  142.8 3.8 %collective-permute-start.31 = (f32[48,128]{1,0:T(8,128)S(1)}, f32[48,128]{1,0:T(8,128)S(1)}, u32[]{:S(2)}, u32[]{:S(2)}) collective-permute-start(f32[48,128]{1,0:T(8,128)S(1)} %add_add_fusion.1), channel_id=1, source_target_pairs={{0,2},{1,3},{2,0},{3,1},{4,6},{5,7},{6,4},{7,5},{8,10},{9,11},{10,... | collective-permute-start | bytes 73736 | tf_op jit(solution)/shard_map/ppermute | solution.py:785
  144.5 4.7 %collective-permute-start.32 = (f32[48,128]{1,0:T(8,128)S(1)}, f32[48,128]{1,0:T(8,128)S(1)}, u32[]{:S(2)}, u32[]{:S(2)}) collective-permute-start(f32[48,128]{1,0:T(8,128)S(1)} %add_add_fusion.1), channel_id=1, source_target_pairs={{0,3},{1,2},{2,1},{3,0},{4,7},{5,6},{6,5},{7,4},{8,11},{9,10},{10,... | collective-permute-start | bytes 73736 | tf_op jit(solution)/shard_map/ppermute | solution.py:785
  149.3 13.6 %collective-permute-start.33 = (f32[32,16,256]{2,1,0:T(8,128)S(1)}, f32[32,16,256]{2,1,0:T(8,128)S(1)}, u32[]{:S(2)}, u32[]{:S(2)}) collective-permute-start(f32[32,16,256]{2,1,0:T(8,128)S(1)} %get-tuple-element.152), channel_id=1, source_target_pairs={{0,3},{1,2},{2,1},{3,0},{4,7},{5,6},{6,5},{7,4},{8,11},{9,10},{10,... | collective-permute-start | bytes 1572872 | tf_op jit(solution)/shard_map/ppermute | solution.py:792

commit v7 on v6

--- a/solution.py
+++ b/solution.py
@@ -364,7 +364,8 @@
             acc = one_row(r, acc)
     else:
         skip = 2 if part == "inner" else 0
-        acc = lax.fori_loop(skip, depth - skip, one_row, start, unroll=UNROLL)
+        turns = math.gcd(depth - 2 * skip, 2 * UNROLL)
+        acc = lax.fori_loop(skip, depth - skip, one_row, start, unroll=turns)
     half = parts * fields
     acc_ref[...] = jnp.zeros(acc_ref.shape, f32)
     acc_ref[:, 0 : 4 * fields] = acc[:half] + acc[half:]

time: 165 us -> 165 us (level)
  no operation moved by 1% of the time
where the time goes in v7:
time: 165 us
  Pallas kernels  59.3 us (36%)
  starting transfers between devices  54.5 us (33%)
  waiting for transfers between devices  48.4 us (29%)
  local copies, waits for them, and re-layouts  1.69 us (1%)
    ppermute x14, starting transfers between devices, add_up(): lax.ppermute(value, BOTH, [(i, i ^ m) for i in range(strips)])  23.7 us
    pallas_call x4, Pallas kernels, apply_graph(): pl.pallas_call(functools.partial(graph_kernel, order, keep, lane_shift, c...  20.9 us
    ppermute x9, waiting for transfers between devices, away(): return lax.ppermute(piece, 'col', [(c, c ^ d) for c in range(chunks)])  18.5 us
    ppermute x14, waiting for transfers between devices, add_up(): lax.ppermute(value, BOTH, [(i, i ^ m) for i in range(strips)])  16.3 us
    ppermute x9, starting transfers between devices, away(): return lax.ppermute(piece, 'col', [(c, c ^ d) for c in range(chunks)])  13.4 us
    ppermute x7, waiting for transfers between devices, local(): found[place & (1 << len(group)) - 1] = lax.ppermute(ends, BOTH, pairs)  11.9 us
    ppermute x7, starting transfers between devices, local(): found[place & (1 << len(group)) - 1] = lax.ppermute(ends, BOTH, pairs)  9.59 us
    pallas_call x1, Pallas kernels, ritz_step(): pl.pallas_call(functools.partial(ritz_kernel, fields, pixel_total), out_s...  9.04 us
  transfers between devices with their start and end apart: 34, of which 21 were waited for; matrix products, arithmetic and copies ran while one was open for 1% of the time, Pallas kernels for 25%

profile of v7, /device:TPU:0, one launch (start us, length us, event | category | flops | bytes accessed | tf_op | source)
XLA Modules:
  0.0 165.0 jit_solution(18334984283966573388)
XLA Ops:
  0.6 2.0 %edges.1 = (f32[2,33,256]{2,1,0:T(8,128)}, f32[2,33,256]{2,1,0:T(8,128)}) custom-call(f32[16,128,256]{2,1,0:T(8,128)} %x_ref.7, f32[16,128,256]{2,1,0:T(8,128)} %x_ref.7, f32[16,128,256]{2,1,0:T(8,128)} %p_ref.3, f32[16,128,256]{2,1,0:T(8,128)} %p_ref.3, f32[128,256]{1,0:T(8,128)} %refs_0_.1, f32[128,256]{1,0:T(8,128)} %refs_0_.1), custom_call_target="tpu_custom_call" | custom-call | bytes 524288 | tf_op jit(solution)/shard_map/edges/pallas_call | solution.py:150
  2.6 2.3 %collective-permute-start = (f32[2,33,256]{2,1,0:T(8,128)}, f32[2,33,256]{2,1,0:T(8,128)S(1)}, u32[]{:S(2)}, u32[]{:S(2)}) collective-permute-start(f32[2,33,256]{2,1,0:T(8,128)} %get-tuple-element.83), channel_id=1, source_target_pairs={{0,4},{4,8},{8,12},{12,16},{16,20},{20,24},{24,28},{1,5},{5,9},{9,... | collective-permute-start | bytes 202760 | tf_op jit(solution)/shard_map/ppermute | solution.py:799
  7.0 1.8 %pack.2 = (f32[39,16,256]{2,1,0:T(8,128)S(1)}, f32[39,16,256]{2,1,0:T(8,128)S(1)}, f32[39,16,256]{2,1,0:T(8,128)S(1)}, f32[39,16,256]{2,1,0:T(8,128)S(1)}) custom-call(s32[9]{0:T(128)S(1)} %dynamic-slice_bitcast_fusion.1.info_ref.refs_0_, f32[16,128,256]{2,1,0:T(8,128)S(1)} %copy-done, f32[128,256]{1,0:T(8,128)S(1)} %copy-done.2), custom_call_target="tpu_custom_call" | custom-call | bytes 4194304 | tf_op jit(solution)/shard_map/pack/pallas_call | solution.py:203
  8.8 1.7 %collective-permute-done.1.below_ref = f32[2,33,256]{2,1,0:T(8,128)S(1)} collective-permute-done((f32[2,33,256]{2,1,0:T(8,128)}, f32[2,33,256]{2,1,0:T(8,128)S(1)}, u32[]{:S(2)}, u32[]{:S(2)}) %collective-permute-start.1) | collective-permute-done | bytes 67616 | tf_op jit(solution)/shard_map/ppermute | solution.py:800
  11.1 1.6 collective-permute-start.2
  12.7 1.5 collective-permute-start.3
  14.7 1.8 %pack.3 = (f32[36,16,256]{2,1,0:T(8,128)S(1)}, f32[36,16,256]{2,1,0:T(8,128)S(1)}, f32[36,16,256]{2,1,0:T(8,128)S(1)}, f32[36,16,256]{2,1,0:T(8,128)S(1)}) custom-call(s32[9]{0:T(128)S(1)} %dynamic-slice_bitcast_fusion.1.info_ref.refs_0_, f32[16,128,256]{2,1,0:T(8,128)S(1)} %copy-done.1), custom_call_target="tpu_custom_call" | custom-call | bytes 4194304 | tf_op jit(solution)/shard_map/pack/pallas_call | solution.py:203
  17.1 1.6 collective-permute-start.10
  18.7 1.5 collective-permute-start.9
  20.2 6.1 %collective-permute-done.2.rest_1_.refs_2_ = f32[39,16,256]{2,1,0:T(8,128)S(1)} collective-permute-done((f32[39,16,256]{2,1,0:T(8,128)S(1)}, f32[39,16,256]{2,1,0:T(8,128)S(1)}, u32[]{:S(2)}, u32[]{:S(2)}) %collective-permute-start.2) | collective-permute-done | bytes 639008 | tf_op jit(solution)/shard_map/ppermute | solution.py:793
  26.3 2.4 %collective-permute-start.11 = (f32[36,16,256]{2,1,0:T(8,128)S(1)}, f32[36,16,256]{2,1,0:T(8,128)S(1)}, u32[]{:S(2)}, u32[]{:S(2)}) collective-permute-start(f32[36,16,256]{2,1,0:T(8,128)S(1)} %get-tuple-element.109), channel_id=1, source_target_pairs={{0,3},{1,2},{2,1},{3,0},{4,7},{5,6},{6,5},{7,4},{8,11},{9,10},{10,... | collective-permute-start | bytes 1769480 | tf_op jit(solution)/shard_map/ppermute | solution.py:793
  29.6 11.5 %collective-permute-done.4.rest_3_.refs_4_ = f32[39,16,256]{2,1,0:T(8,128)S(1)} collective-permute-done((f32[39,16,256]{2,1,0:T(8,128)S(1)}, f32[39,16,256]{2,1,0:T(8,128)S(1)}, u32[]{:S(2)}, u32[]{:S(2)}) %collective-permute-start.4) | collective-permute-done | bytes 639008 | tf_op jit(solution)/shard_map/ppermute | solution.py:793
  41.0 2.7 %weights.1 = (f32[32,25,1024]{2,1,0:T(8,128)S(1)}, f32[32,1024]{1,0:T(8,128)S(1)}) custom-call(s32[9]{0:T(128)S(1)} %dynamic-slice_bitcast_fusion.1.info_ref.refs_0_, f32[39,16,256]{2,1,0:T(8,128)S(1)} %get-tuple-element.99.rest_0_.refs_1_, f32[39,16,256]{2,1,0:T(8,128)S(1)} %collective-permute-done.2.rest_1_.refs_2_, ...), custom_call_target="tpu_custom_call" | custom-call | flops 49152000 | bytes 3276800 | tf_op jit(solution)/shard_map/weights/pallas_call | solution.py:282
  43.8 6.9 %graph_v_all.1 = (f32[32,16,1024]{2,1,0:T(8,128)S(1)}, f32[32,16,1024]{2,1,0:T(8,128)S(1)}, f32[16,128]{1,0:T(8,128)S(1)}) custom-call(s32[9]{0:T(128)S(1)} %dynamic-slice_bitcast_fusion.1.info_ref.refs_0_, f32[39,16,256]{2,1,0:T(8,128)S(1)} %get-tuple-element.99.rest_0_.refs_1_, f32[39,16,256]{2,1,0:T(8,128)S(1)} %collective-permute-done.2.rest_1_.refs_2_, ...), custom_call_target="tpu_custom_call" | custom-call | flops 104857600 | bytes 9568256 | tf_op jit(solution)/shard_map/graph_v_all/pallas_call | solution.py:389
  50.7 4.6 %collective-permute-start.5 = (f32[16,128]{1,0:T(8,128)S(1)}, f32[16,128]{1,0:T(8,128)S(1)}, u32[]{:S(2)}, u32[]{:S(2)}) collective-permute-start(f32[16,128]{1,0:T(8,128)S(1)} %get-tuple-element.105), channel_id=1, source_target_pairs={{0,4},{1,5},{2,6},{3,7},{4,0},{5,1},{6,2},{7,3},{8,12},{9,13},{10,... | collective-permute-start | bytes 24584 | tf_op jit(solution)/shard_map/ppermute | solution.py:786
  56.2 1.5 collective-permute-start.6
  57.7 2.7 %collective-permute-start.7 = (f32[16,128]{1,0:T(8,128)S(1)}, f32[16,128]{1,0:T(8,128)S(1)}, u32[]{:S(2)}, u32[]{:S(2)}) collective-permute-start(f32[16,128]{1,0:T(8,128)S(1)} %add.59), channel_id=1, source_target_pairs={{0,16},{1,17},{2,18},{3,19},{4,20},{5,21},{6,22},{7,23},{8,24},{9,... | collective-permute-start | bytes 24584 | tf_op jit(solution)/shard_map/ppermute | solution.py:786
  60.4 3.1 %collective-permute-start.8 = (f32[16,128]{1,0:T(8,128)S(1)}, f32[16,128]{1,0:T(8,128)S(1)}, u32[]{:S(2)}, u32[]{:S(2)}) collective-permute-start(f32[16,128]{1,0:T(8,128)S(1)} %add.59), channel_id=1, source_target_pairs={{0,24},{1,25},{2,26},{3,27},{4,28},{5,29},{6,30},{7,31},{8,16},{9,... | collective-permute-start | bytes 24584 | tf_op jit(solution)/shard_map/ppermute | solution.py:786
  63.4 2.4 %collective-permute-done.8 = f32[16,128]{1,0:T(8,128)S(1)} collective-permute-done((f32[16,128]{1,0:T(8,128)S(1)}, f32[16,128]{1,0:T(8,128)S(1)}, u32[]{:S(2)}, u32[]{:S(2)}) %collective-permute-start.8) | collective-permute-done | bytes 8224 | tf_op jit(solution)/shard_map/ppermute | solution.py:786
  66.4 1.4 collective-permute-start.12
  68.4 1.5 collective-permute-start.14
  70.0 1.4 collective-permute-done.13
  71.4 1.5 collective-permute-done.14
  73.0 6.6 %residual_spectrum.1 = (f32[32,16,1024]{2,1,0:T(8,128)S(1)}, f32[2,16,1024]{2,1,0:T(8,128)S(1)}) custom-call(f32[16,128]{1,0:T(8,128)S(1)} %add_add_fusion.2.gram_ref.first_ref, f32[32,16,1024]{2,1,0:T(8,128)S(1)} %get-tuple-element.111.g_ref, f32[32,16,1024]{2,1,0:T(8,128)S(1)} %get-tuple-element.112.x_ref.refs_7_.refs_3_.refs_5_, ...), custom_call_target="tpu_custom_call" | custom-call | flops 3221225472 | bytes 6291456 | tf_op jit(solution)/shard_map/residual_spectrum/pallas_call | solution.py:457
  80.7 1.8 %collective-permute-start.16 = (f32[2,16,1024]{2,1,0:T(8,128)S(1)}, f32[2,16,1024]{2,1,0:T(8,128)S(1)}, u32[]{:S(2)}, u32[]{:S(2)}) collective-permute-start(f32[2,16,1024]{2,1,0:T(8,128)S(1)} %get-tuple-element.113.refs_0_), channel_id=1, source_target_pairs={{0,3},{1,2},{2,1},{3,0},{4,7},{5,6},{6,5},{7,4},{8,11},{9,10},{10,... | collective-permute-start | bytes 393224 | tf_op jit(solution)/shard_map/ppermute | solution.py:824
  83.1 2.9 %collective-permute-done.15.refs_1_ = f32[2,16,1024]{2,1,0:T(8,128)S(1)} collective-permute-done((f32[2,16,1024]{2,1,0:T(8,128)S(1)}, f32[2,16,1024]{2,1,0:T(8,128)S(1)}, u32[]{:S(2)}, u32[]{:S(2)}) %collective-permute-start.15) | collective-permute-done | bytes 131104 | tf_op jit(solution)/shard_map/ppermute | solution.py:824
  86.0 3.1 %collective-permute-done.16.refs_2_ = f32[2,16,1024]{2,1,0:T(8,128)S(1)} collective-permute-done((f32[2,16,1024]{2,1,0:T(8,128)S(1)}, f32[2,16,1024]{2,1,0:T(8,128)S(1)}, u32[]{:S(2)}, u32[]{:S(2)}) %collective-permute-start.16) | collective-permute-done | bytes 131104 | tf_op jit(solution)/shard_map/ppermute | solution.py:824
  93.1 3.5 %collective-permute-start.19 = (f32[2,16,1024]{2,1,0:T(8,128)S(1)}, f32[2,16,1024]{2,1,0:T(8,128)S(1)}, u32[]{:S(2)}, u32[]{:S(2)}) collective-permute-start(f32[2,16,1024]{2,1,0:T(8,128)S(1)} %get-tuple-element.123.refs_0_), channel_id=1, source_target_pairs={{0,8},{1,9},{2,10},{3,11},{4,12},{5,13},{6,14},{7,15},{8,0},{9,1},... | collective-permute-start | bytes 393224 | tf_op jit(solution)/shard_map/ppermute | solution.py:824
  97.7 1.4 collective-permute-start.21
  99.1 7.2 %graph_xv_all.1 = (f32[32,16,1024]{2,1,0:T(8,128)S(1)}, f32[32,128]{1,0:T(8,128)S(1)}) custom-call(s32[9]{0:T(128)S(1)} %dynamic-slice_bitcast_fusion.1.info_ref.refs_0_, f32[36,16,256]{2,1,0:T(8,128)S(1)} %get-tuple-element.126.refs_1_, f32[36,16,256]{2,1,0:T(8,128)S(1)} %collective-permute-done.9.refs_2_, ...), custom_call_target="tpu_custom_call" | custom-call | flops 104857600 | bytes 9568256 | tf_op jit(solution)/shard_map/graph_xv_all/pallas_call | solution.py:389
  106.3 3.2 %collective-permute-done.20.refs_2_ = f32[2,16,1024]{2,1,0:T(8,128)S(1)} collective-permute-done((f32[2,16,1024]{2,1,0:T(8,128)S(1)}, f32[2,16,1024]{2,1,0:T(8,128)S(1)}, u32[]{:S(2)}, u32[]{:S(2)}) %collective-permute-start.20) | collective-permute-done | bytes 131104 | tf_op jit(solution)/shard_map/ppermute | solution.py:824
  110.1 4.9 %row_inverse.1 = (f32[32,16,1024]{2,1,0:T(8,128)S(1)}, f32[2,16,1024]{2,1,0:T(8,128)S(1)}, f32[2,16,1024]{2,1,0:T(8,128)S(1)}, f32[32,16,256]{2,1,0:T(8,128)S(1)...) custom-call(s32[9]{0:T(128)S(1)} %dynamic-slice_bitcast_fusion.1.info_ref.refs_0_, ...), custom_call_target="tpu_custom_call" | custom-call | flops 3221225472 | bytes 8388608 | tf_op jit(solution)/shard_map/row_inverse/pallas_call | solution.py:552
  115.0 2.8 %collective-permute-start.22 = (f32[2,16,1024]{2,1,0:T(8,128)S(1)}, f32[2,16,1024]{2,1,0:T(8,128)S(1)}, u32[]{:S(2)}, u32[]{:S(2)}) collective-permute-start(f32[2,16,1024]{2,1,0:T(8,128)S(1)} %get-tuple-element.136), channel_id=1, source_target_pairs={{0,1},{1,3},{3,2},{2,4},{4,5},{5,7},{7,6},{6,8},{8,9},{9,11},{11,1... | collective-permute-start | bytes 393224 | tf_op jit(solution)/shard_map/ppermute | solution.py:836
  117.8 1.5 collective-permute-start.23
  119.4 5.9 %graph_xvp_inner.1 = f32[48,128]{1,0:T(8,128)S(1)} custom-call(f32[32,16,1024]{2,1,0:T(8,128)S(1)} %get-tuple-element.138.refs_0_, f32[32,25,1024]{2,1,0:T(8,128)S(1)} %get-tuple-element.103.refs_5_.refs_1_.refs_3_, f32[32,1024]{1,0:T(8,128)S(1)} %get-tuple-element.104.refs_6_.deg_ref.refs_2_.refs_4_, ...), custom_call_target="tpu_custom_call" | custom-call | flops 104857600 | bytes 9568256 | tf_op jit(solution)/shard_map/graph_xvp_inner/pallas_call | solution.py:389
  125.3 2.7 %collective-permute-start.28 = (f32[32,16,256]{2,1,0:T(8,128)S(1)}, f32[32,16,256]{2,1,0:T(8,128)S(1)}, u32[]{:S(2)}, u32[]{:S(2)}) collective-permute-start(f32[32,16,256]{2,1,0:T(8,128)S(1)} %get-tuple-element.144), channel_id=1, source_target_pairs={{0,1},{1,0},{2,3},{3,2},{4,5},{5,4},{6,7},{7,6},{8,9},{9,8},{10,11... | collective-permute-start | bytes 1572872 | tf_op jit(solution)/shard_map/ppermute | solution.py:793
  128.0 1.5 collective-permute-start.29
  131.8 2.3 %collective-permute-start.25 = (f32[48,128]{1,0:T(8,128)S(1)}, f32[48,128]{1,0:T(8,128)S(1)}, u32[]{:S(2)}, u32[]{:S(2)}) collective-permute-start(f32[48,128]{1,0:T(8,128)S(1)} %add.68), channel_id=1, source_target_pairs={{0,8},{1,9},{2,10},{3,11},{4,12},{5,13},{6,14},{7,15},{8,0},{9,1},... | collective-permute-start | bytes 73736 | tf_op jit(solution)/shard_map/ppermute | solution.py:786
  135.1 1.4 collective-permute-start.27
  136.5 2.4 %collective-permute-done.26 = f32[48,128]{1,0:T(8,128)S(1)} collective-permute-done((f32[48,128]{1,0:T(8,128)S(1)}, f32[48,128]{1,0:T(8,128)S(1)}, u32[]{:S(2)}, u32[]{:S(2)}) %collective-permute-start.26) | collective-permute-done | bytes 24608 | tf_op jit(solution)/shard_map/ppermute | solution.py:786
  138.9 1.8 %collective-permute-done.27 = f32[48,128]{1,0:T(8,128)S(1)} collective-permute-done((f32[48,128]{1,0:T(8,128)S(1)}, f32[48,128]{1,0:T(8,128)S(1)}, u32[]{:S(2)}, u32[]{:S(2)}) %collective-permute-start.27) | collective-permute-done | bytes 24608 | tf_op jit(solution)/shard_map/ppermute | solution.py:786
  141.1 1.7 %collective-permute-start.30 = (f32[48,128]{1,0:T(8,128)S(1)}, f32[48,128]{1,0:T(8,128)S(1)}, u32[]{:S(2)}, u32[]{:S(2)}) collective-permute-start(f32[48,128]{1,0:T(8,128)S(1)} %add_add_fusion.1), channel_id=1, source_target_pairs={{0,1},{1,0},{2,3},{3,2},{4,5},{5,4},{6,7},{7,6},{8,9},{9,8},{10,11... | collective-permute-start | bytes 73736 | tf_op jit(solution)/shard_map/ppermute | solution.py:786
  142.8 1.7 %collective-permute-start.31 = (f32[48,128]{1,0:T(8,128)S(1)}, f32[48,128]{1,0:T(8,128)S(1)}, u32[]{:S(2)}, u32[]{:S(2)}) collective-permute-start(f32[48,128]{1,0:T(8,128)S(1)} %add_add_fusion.1), channel_id=1, source_target_pairs={{0,2},{1,3},{2,0},{3,1},{4,6},{5,7},{6,4},{7,5},{8,10},{9,11},{10,... | collective-permute-start | bytes 73736 | tf_op jit(solution)/shard_map/ppermute | solution.py:786
  145.0 1.7 %collective-permute-done.31 = f32[48,128]{1,0:T(8,128)S(1)} collective-permute-done((f32[48,128]{1,0:T(8,128)S(1)}, f32[48,128]{1,0:T(8,128)S(1)}, u32[]{:S(2)}, u32[]{:S(2)}) %collective-permute-start.31) | collective-permute-done | bytes 24608 | tf_op jit(solution)/shard_map/ppermute | solution.py:786
  146.6 2.6 %collective-permute-done.32 = f32[48,128]{1,0:T(8,128)S(1)} collective-permute-done((f32[48,128]{1,0:T(8,128)S(1)}, f32[48,128]{1,0:T(8,128)S(1)}, u32[]{:S(2)}, u32[]{:S(2)}) %collective-permute-start.32) | collective-permute-done | bytes 24608 | tf_op jit(solution)/shard_map/ppermute | solution.py:786
  149.4 9.0 %ritz.1 = (f32[1,16]{1,0:T(1,128)}, f32[48,16]{1,0:T(8,128)S(1)}) custom-call(f32[16,128]{1,0:T(8,128)S(1)} %add_add_fusion.2.gram_ref.first_ref, f32[48,128]{1,0:T(8,128)S(1)} %add_add_fusion.second_ref), custom_call_target="tpu_custom_call" | custom-call | flops 33554432 | bytes 65536 | tf_op jit(solution)/shard_map/ritz/pallas_call | solution.py:644
  158.4 4.5 %combine.2 = (f32[16,128,256]{2,1,0:T(8,128)}, f32[16,128,256]{2,1,0:T(8,128)}, bf16[128,384]{1,0:T(8,128)(2,1)S(1)}, bf16[128,384]{1,0:T(8,128)(2,1)S(1)}) custom-call(s32[9]{0:T(128)S(1)} %dynamic-slice_bitcast_fusion.1.info_ref.refs_0_, f32[48,16]{1,0:T(8,128)S(1)} %get-tuple-element.151.coeff_ref, f32[16,128,256]{2,1,0:T(8,128)S(1)} %copy-done, ...), custom_call_target="tpu_custom_call" | custom-call | flops 19660800 | bytes 7864320 | tf_op jit(solution)/shard_map/combine/pallas_call | solution.py:721
  162.9 2.0 %combine.3 = (f32[16,128,256]{2,1,0:T(8,128)}, f32[16,128,256]{2,1,0:T(8,128)}) custom-call(s32[9]{0:T(128)S(1)} %dynamic-slice_bitcast_fusion.1.info_ref.refs_0_, f32[48,16]{1,0:T(8,128)S(1)} %get-tuple-element.151.coeff_ref, f32[16,128,256]{2,1,0:T(8,128)S(1)} %copy-done, ...), custom_call_target="tpu_custom_call", output_to_operand_aliasing={{0}: (5, {}), {1}: (6, {})} | custom-call | flops 6553600 | bytes 2621440 | tf_op jit(solution)/shard_map/combine/pallas_call | solution.py:721
  (72 shorter events, 18.4 us)
Async XLA Ops:
  0.6 6.4 %copy-start.2 = (f32[128,256]{1,0:T(8,128)S(1)}, f32[128,256]{1,0:T(8,128)}, u32[]{:S(2)}) copy-start(f32[128,256]{1,0:T(8,128)} %refs_0_.1) | copy-start | bytes 393220
  0.6 6.3 %copy-start = (f32[16,128,256]{2,1,0:T(8,128)S(1)}, f32[16,128,256]{2,1,0:T(8,128)}, u32[]{:S(2)}) copy-start(f32[16,128,256]{2,1,0:T(8,128)} %x_ref.7) | copy-start | bytes 6291460
  2.6 6.2 %collective-permute-start = (f32[2,33,256]{2,1,0:T(8,128)}, f32[2,33,256]{2,1,0:T(8,128)S(1)}, u32[]{:S(2)}, u32[]{:S(2)}) collective-permute-start(f32[2,33,256]{2,1,0:T(8,128)} %get-tuple-element.83), channel_id=1, source_target_pairs={{0,4},{4,8},{8,12},{12,16},{16,20},{20,24},{24,28},{1,5},{5,9},{9,... | collective-permute-start | bytes 202760 | tf_op jit(solution)/shard_map/ppermute | solution.py:799
  5.0 5.6 %collective-permute-start.1 = (f32[2,33,256]{2,1,0:T(8,128)}, f32[2,33,256]{2,1,0:T(8,128)S(1)}, u32[]{:S(2)}, u32[]{:S(2)}) collective-permute-start(f32[2,33,256]{2,1,0:T(8,128)} %get-tuple-element.84), channel_id=1, source_target_pairs={{4,0},{8,4},{12,8},{16,12},{20,16},{24,20},{28,24},{5,1},{9,5},{13... | collective-permute-start | bytes 202760 | tf_op jit(solution)/shard_map/ppermute | solution.py:800
  7.0 7.7 %copy-start.1 = (f32[16,128,256]{2,1,0:T(8,128)S(1)}, f32[16,128,256]{2,1,0:T(8,128)}, u32[]{:S(2)}) copy-start(f32[16,128,256]{2,1,0:T(8,128)} %p_ref.3) | copy-start | bytes 6291460
  11.1 15.1 %collective-permute-start.2 = (f32[39,16,256]{2,1,0:T(8,128)S(1)}, f32[39,16,256]{2,1,0:T(8,128)S(1)}, u32[]{:S(2)}, u32[]{:S(2)}) collective-permute-start(f32[39,16,256]{2,1,0:T(8,128)S(1)} %get-tuple-element.95), channel_id=1, source_target_pairs={{0,1},{1,0},{2,3},{3,2},{4,5},{5,4},{6,7},{7,6},{8,9},{9,8},{10,11... | collective-permute-start | bytes 1916936 | tf_op jit(solution)/shard_map/ppermute | solution.py:793
  12.7 16.9 %collective-permute-start.3 = (f32[39,16,256]{2,1,0:T(8,128)S(1)}, f32[39,16,256]{2,1,0:T(8,128)S(1)}, u32[]{:S(2)}, u32[]{:S(2)}) collective-permute-start(f32[39,16,256]{2,1,0:T(8,128)S(1)} %get-tuple-element.97), channel_id=1, source_target_pairs={{0,2},{1,3},{2,0},{3,1},{4,6},{5,7},{6,4},{7,5},{8,10},{9,11},{10,... | collective-permute-start | bytes 1916936 | tf_op jit(solution)/shard_map/ppermute | solution.py:793
  14.2 26.8 %collective-permute-start.4 = (f32[39,16,256]{2,1,0:T(8,128)S(1)}, f32[39,16,256]{2,1,0:T(8,128)S(1)}, u32[]{:S(2)}, u32[]{:S(2)}) collective-permute-start(f32[39,16,256]{2,1,0:T(8,128)S(1)} %get-tuple-element.98), channel_id=1, source_target_pairs={{0,3},{1,2},{2,1},{3,0},{4,7},{5,6},{6,5},{7,4},{8,11},{9,10},{10,... | collective-permute-start | bytes 1916936 | tf_op jit(solution)/shard_map/ppermute | solution.py:793
  17.1 48.7 %collective-permute-start.10 = (f32[36,16,256]{2,1,0:T(8,128)S(1)}, f32[36,16,256]{2,1,0:T(8,128)S(1)}, u32[]{:S(2)}, u32[]{:S(2)}) collective-permute-start(f32[36,16,256]{2,1,0:T(8,128)S(1)} %get-tuple-element.108), channel_id=1, source_target_pairs={{0,2},{1,3},{2,0},{3,1},{4,6},{5,7},{6,4},{7,5},{8,10},{9,11},{10,... | collective-permute-start | bytes 1769480 | tf_op jit(solution)/shard_map/ppermute | solution.py:793
  18.7 47.1 %collective-permute-start.9 = (f32[36,16,256]{2,1,0:T(8,128)S(1)}, f32[36,16,256]{2,1,0:T(8,128)S(1)}, u32[]{:S(2)}, u32[]{:S(2)}) collective-permute-start(f32[36,16,256]{2,1,0:T(8,128)S(1)} %get-tuple-element.107), channel_id=1, source_target_pairs={{0,1},{1,0},{2,3},{3,2},{4,5},{5,4},{6,7},{7,6},{8,9},{9,8},{10,11... | collective-permute-start | bytes 1769480 | tf_op jit(solution)/shard_map/ppermute | solution.py:793
  26.3 40.1 %collective-permute-start.11 = (f32[36,16,256]{2,1,0:T(8,128)S(1)}, f32[36,16,256]{2,1,0:T(8,128)S(1)}, u32[]{:S(2)}, u32[]{:S(2)}) collective-permute-start(f32[36,16,256]{2,1,0:T(8,128)S(1)} %get-tuple-element.109), channel_id=1, source_target_pairs={{0,3},{1,2},{2,1},{3,0},{4,7},{5,6},{6,5},{7,4},{8,11},{9,10},{10,... | collective-permute-start | bytes 1769480 | tf_op jit(solution)/shard_map/ppermute | solution.py:793
  43.8 29.1 %copy-start.7 = (bf16[1024,1024]{1,0:T(8,128)(2,1)S(1)}, bf16[1024,1024]{1,0:T(8,128)(2,1)}, u32[]{:S(2)}) copy-start(bf16[1024,1024]{1,0:T(8,128)(2,1)} %constant.45.clone.high_ref) | copy-start | bytes 6291460
  43.8 29.1 %copy-start.8 = (bf16[1024,1024]{1,0:T(8,128)(2,1)S(1)}, bf16[1024,1024]{1,0:T(8,128)(2,1)}, u32[]{:S(2)}) copy-start(bf16[1024,1024]{1,0:T(8,128)(2,1)} %constant.46.clone.low_ref) | copy-start | bytes 6291460
  43.8 29.1 %copy-start.9 = (f32[32,1024]{1,0:T(8,128)S(1)}, f32[32,1024]{1,0:T(8,128)}, u32[]{:S(2)}) copy-start(f32[32,1024]{1,0:T(8,128)} %constant.47.clone.eps_ref.refs_7_) | copy-start | bytes 393220
  43.8 29.1 %copy-start.10 = (f32[1,1024]{1,0:T(1,128)S(1)}, f32[1,1024]{1,0:T(1,128)}, u32[]{:S(2)}) copy-start(f32[1,1024]{1,0:T(1,128)} %constant.48.clone.last_ref.refs_8_) | copy-start | bytes 12292
  50.7 5.5 %collective-permute-start.5 = (f32[16,128]{1,0:T(8,128)S(1)}, f32[16,128]{1,0:T(8,128)S(1)}, u32[]{:S(2)}, u32[]{:S(2)}) collective-permute-start(f32[16,128]{1,0:T(8,128)S(1)} %get-tuple-element.105), channel_id=1, source_target_pairs={{0,4},{1,5},{2,6},{3,7},{4,0},{5,1},{6,2},{7,3},{8,12},{9,13},{10,... | collective-permute-start | bytes 24584 | tf_op jit(solution)/shard_map/ppermute | solution.py:786
  56.2 4.2 %collective-permute-start.6 = (f32[16,128]{1,0:T(8,128)S(1)}, f32[16,128]{1,0:T(8,128)S(1)}, u32[]{:S(2)}, u32[]{:S(2)}) collective-permute-start(f32[16,128]{1,0:T(8,128)S(1)} %add.59), channel_id=1, source_target_pairs={{0,8},{1,9},{2,10},{3,11},{4,12},{5,13},{6,14},{7,15},{8,0},{9,1},... | collective-permute-start | bytes 24584 | tf_op jit(solution)/shard_map/ppermute | solution.py:786
  57.7 5.8 %collective-permute-start.7 = (f32[16,128]{1,0:T(8,128)S(1)}, f32[16,128]{1,0:T(8,128)S(1)}, u32[]{:S(2)}, u32[]{:S(2)}) collective-permute-start(f32[16,128]{1,0:T(8,128)S(1)} %add.59), channel_id=1, source_target_pairs={{0,16},{1,17},{2,18},{3,19},{4,20},{5,21},{6,22},{7,23},{8,24},{9,... | collective-permute-start | bytes 24584 | tf_op jit(solution)/shard_map/ppermute | solution.py:786
  60.4 5.4 %collective-permute-start.8 = (f32[16,128]{1,0:T(8,128)S(1)}, f32[16,128]{1,0:T(8,128)S(1)}, u32[]{:S(2)}, u32[]{:S(2)}) collective-permute-start(f32[16,128]{1,0:T(8,128)S(1)} %add.59), channel_id=1, source_target_pairs={{0,24},{1,25},{2,26},{3,27},{4,28},{5,29},{6,30},{7,31},{8,16},{9,... | collective-permute-start | bytes 24584 | tf_op jit(solution)/shard_map/ppermute | solution.py:786
  66.4 3.7 %collective-permute-start.12 = (f32[16,128]{1,0:T(8,128)S(1)}, f32[16,128]{1,0:T(8,128)S(1)}, u32[]{:S(2)}, u32[]{:S(2)}) collective-permute-start(f32[16,128]{1,0:T(8,128)S(1)} %add_add_fusion.3), channel_id=1, source_target_pairs={{0,1},{1,0},{2,3},{3,2},{4,5},{5,4},{6,7},{7,6},{8,9},{9,8},{10,11... | collective-permute-start | bytes 24584 | tf_op jit(solution)/shard_map/ppermute | solution.py:786
  67.7 3.7 %collective-permute-start.13 = (f32[16,128]{1,0:T(8,128)S(1)}, f32[16,128]{1,0:T(8,128)S(1)}, u32[]{:S(2)}, u32[]{:S(2)}) collective-permute-start(f32[16,128]{1,0:T(8,128)S(1)} %add_add_fusion.3), channel_id=1, source_target_pairs={{0,2},{1,3},{2,0},{3,1},{4,6},{5,7},{6,4},{7,5},{8,10},{9,11},{10,... | collective-permute-start | bytes 24584 | tf_op jit(solution)/shard_map/ppermute | solution.py:786
  68.4 4.5 %collective-permute-start.14 = (f32[16,128]{1,0:T(8,128)S(1)}, f32[16,128]{1,0:T(8,128)S(1)}, u32[]{:S(2)}, u32[]{:S(2)}) collective-permute-start(f32[16,128]{1,0:T(8,128)S(1)} %add_add_fusion.3), channel_id=1, source_target_pairs={{0,3},{1,2},{2,1},{3,0},{4,7},{5,6},{6,5},{7,4},{8,11},{9,10},{10,... | collective-permute-start | bytes 24584 | tf_op jit(solution)/shard_map/ppermute | solution.py:786
  72.9 17.5 %copy-start.3 = (f32[5,1024]{1,0:T(8,128)S(1)}, f32[5,1024]{1,0:T(8,128)}, u32[]{:S(2)}) copy-start(f32[5,1024]{1,0:T(8,128)} %constant.49.clone.gain_ref) | copy-start | bytes 61444
  73.0 17.5 %copy-start.4 = (f32[5,1024]{1,0:T(8,128)S(1)}, f32[5,1024]{1,0:T(8,128)}, u32[]{:S(2)}) copy-start(f32[5,1024]{1,0:T(8,128)} %constant.50.clone.cross_ref) | copy-start | bytes 61444
  79.6 6.4 %collective-permute-start.15 = (f32[2,16,1024]{2,1,0:T(8,128)S(1)}, f32[2,16,1024]{2,1,0:T(8,128)S(1)}, u32[]{:S(2)}, u32[]{:S(2)}) collective-permute-start(f32[2,16,1024]{2,1,0:T(8,128)S(1)} %get-tuple-element.113.refs_0_), channel_id=1, source_target_pairs={{0,1},{1,0},{2,3},{3,2},{4,5},{5,4},{6,7},{7,6},{8,9},{9,8},{10,11... | collective-permute-start | bytes 393224 | tf_op jit(solution)/shard_map/ppermute | solution.py:824
  80.7 8.4 %collective-permute-start.16 = (f32[2,16,1024]{2,1,0:T(8,128)S(1)}, f32[2,16,1024]{2,1,0:T(8,128)S(1)}, u32[]{:S(2)}, u32[]{:S(2)}) collective-permute-start(f32[2,16,1024]{2,1,0:T(8,128)S(1)} %get-tuple-element.113.refs_0_), channel_id=1, source_target_pairs={{0,3},{1,2},{2,1},{3,0},{4,7},{5,6},{6,5},{7,4},{8,11},{9,10},{10,... | collective-permute-start | bytes 393224 | tf_op jit(solution)/shard_map/ppermute | solution.py:824
  82.5 7.9 %collective-permute-start.17 = (f32[2,16,1024]{2,1,0:T(8,128)S(1)}, f32[2,16,1024]{2,1,0:T(8,128)S(1)}, u32[]{:S(2)}, u32[]{:S(2)}) collective-permute-start(f32[2,16,1024]{2,1,0:T(8,128)S(1)} %get-tuple-element.113.refs_0_), channel_id=1, source_target_pairs={{0,2},{1,3},{2,0},{3,1},{4,6},{5,7},{6,4},{7,5},{8,10},{9,11},{10,... | collective-permute-start | bytes 393224 | tf_op jit(solution)/shard_map/ppermute | solution.py:824
  91.1 1.4 collective-permute-start.18
  93.1 17.0 %copy-start.5 = (bf16[1024,1024]{1,0:T(8,128)(2,1)S(1)}, bf16[1024,1024]{1,0:T(8,128)(2,1)}, u32[]{:S(2)}) copy-start(bf16[1024,1024]{1,0:T(8,128)(2,1)} %constant.43.clone.refs_9_) | copy-start | bytes 6291460
  93.1 17.0 %copy-start.6 = (bf16[1024,1024]{1,0:T(8,128)(2,1)S(1)}, bf16[1024,1024]{1,0:T(8,128)(2,1)}, u32[]{:S(2)}) copy-start(bf16[1024,1024]{1,0:T(8,128)(2,1)} %constant.44.clone.refs_10_) | copy-start | bytes 6291460
  93.1 13.2 %collective-permute-start.19 = (f32[2,16,1024]{2,1,0:T(8,128)S(1)}, f32[2,16,1024]{2,1,0:T(8,128)S(1)}, u32[]{:S(2)}, u32[]{:S(2)}) collective-permute-start(f32[2,16,1024]{2,1,0:T(8,128)S(1)} %get-tuple-element.123.refs_0_), channel_id=1, source_target_pairs={{0,8},{1,9},{2,10},{3,11},{4,12},{5,13},{6,14},{7,15},{8,0},{9,1},... | collective-permute-start | bytes 393224 | tf_op jit(solution)/shard_map/ppermute | solution.py:824
  96.6 12.9 %collective-permute-start.20 = (f32[2,16,1024]{2,1,0:T(8,128)S(1)}, f32[2,16,1024]{2,1,0:T(8,128)S(1)}, u32[]{:S(2)}, u32[]{:S(2)}) collective-permute-start(f32[2,16,1024]{2,1,0:T(8,128)S(1)} %get-tuple-element.123.refs_0_), channel_id=1, source_target_pairs={{0,16},{1,17},{2,18},{3,19},{4,20},{5,21},{6,22},{7,23},{8,24},{9,... | collective-permute-start | bytes 393224 | tf_op jit(solution)/shard_map/ppermute | solution.py:824
  97.7 11.8 %collective-permute-start.21 = (f32[2,16,1024]{2,1,0:T(8,128)S(1)}, f32[2,16,1024]{2,1,0:T(8,128)S(1)}, u32[]{:S(2)}, u32[]{:S(2)}) collective-permute-start(f32[2,16,1024]{2,1,0:T(8,128)S(1)} %get-tuple-element.123.refs_0_), channel_id=1, source_target_pairs={{0,24},{1,25},{2,26},{3,27},{4,28},{5,29},{6,30},{7,31},{8,16},{9,... | collective-permute-start | bytes 393224 | tf_op jit(solution)/shard_map/ppermute | solution.py:824
  115.0 10.2 %collective-permute-start.22 = (f32[2,16,1024]{2,1,0:T(8,128)S(1)}, f32[2,16,1024]{2,1,0:T(8,128)S(1)}, u32[]{:S(2)}, u32[]{:S(2)}) collective-permute-start(f32[2,16,1024]{2,1,0:T(8,128)S(1)} %get-tuple-element.136), channel_id=1, source_target_pairs={{0,1},{1,3},{3,2},{2,4},{4,5},{5,7},{7,6},{6,8},{8,9},{9,11},{11,1... | collective-permute-start | bytes 393224 | tf_op jit(solution)/shard_map/ppermute | solution.py:836
  117.8 7.4 %collective-permute-start.23 = (f32[2,16,1024]{2,1,0:T(8,128)S(1)}, f32[2,16,1024]{2,1,0:T(8,128)S(1)}, u32[]{:S(2)}, u32[]{:S(2)}) collective-permute-start(f32[2,16,1024]{2,1,0:T(8,128)S(1)} %get-tuple-element.137), channel_id=1, source_target_pairs={{1,0},{3,1},{2,3},{4,2},{5,4},{7,5},{6,7},{8,6},{9,8},{11,9},{10,1... | collective-permute-start | bytes 393224 | tf_op jit(solution)/shard_map/ppermute | solution.py:837
  125.3 15.5 %collective-permute-start.28 = (f32[32,16,256]{2,1,0:T(8,128)S(1)}, f32[32,16,256]{2,1,0:T(8,128)S(1)}, u32[]{:S(2)}, u32[]{:S(2)}) collective-permute-start(f32[32,16,256]{2,1,0:T(8,128)S(1)} %get-tuple-element.144), channel_id=1, source_target_pairs={{0,1},{1,0},{2,3},{3,2},{4,5},{5,4},{6,7},{7,6},{8,9},{9,8},{10,11... | collective-permute-start | bytes 1572872 | tf_op jit(solution)/shard_map/ppermute | solution.py:793
  128.0 13.2 %collective-permute-start.29 = (f32[32,16,256]{2,1,0:T(8,128)S(1)}, f32[32,16,256]{2,1,0:T(8,128)S(1)}, u32[]{:S(2)}, u32[]{:S(2)}) collective-permute-start(f32[32,16,256]{2,1,0:T(8,128)S(1)} %get-tuple-element.145), channel_id=1, source_target_pairs={{0,2},{1,3},{2,0},{3,1},{4,6},{5,7},{6,4},{7,5},{8,10},{9,11},{10,... | collective-permute-start | bytes 1572872 | tf_op jit(solution)/shard_map/ppermute | solution.py:793
  130.5 1.2 collective-permute-start.24
  131.8 4.7 %collective-permute-start.25 = (f32[48,128]{1,0:T(8,128)S(1)}, f32[48,128]{1,0:T(8,128)S(1)}, u32[]{:S(2)}, u32[]{:S(2)}) collective-permute-start(f32[48,128]{1,0:T(8,128)S(1)} %add.68), channel_id=1, source_target_pairs={{0,8},{1,9},{2,10},{3,11},{4,12},{5,13},{6,14},{7,15},{8,0},{9,1},... | collective-permute-start | bytes 73736 | tf_op jit(solution)/shard_map/ppermute | solution.py:786
  134.1 4.9 %collective-permute-start.26 = (f32[48,128]{1,0:T(8,128)S(1)}, f32[48,128]{1,0:T(8,128)S(1)}, u32[]{:S(2)}, u32[]{:S(2)}) collective-permute-start(f32[48,128]{1,0:T(8,128)S(1)} %add.68), channel_id=1, source_target_pairs={{0,16},{1,17},{2,18},{3,19},{4,20},{5,21},{6,22},{7,23},{8,24},{9,... | collective-permute-start | bytes 73736 | tf_op jit(solution)/shard_map/ppermute | solution.py:786
  135.1 5.6 %collective-permute-start.27 = (f32[48,128]{1,0:T(8,128)S(1)}, f32[48,128]{1,0:T(8,128)S(1)}, u32[]{:S(2)}, u32[]{:S(2)}) collective-permute-start(f32[48,128]{1,0:T(8,128)S(1)} %add.68), channel_id=1, source_target_pairs={{0,24},{1,25},{2,26},{3,27},{4,28},{5,29},{6,30},{7,31},{8,16},{9,... | collective-permute-start | bytes 73736 | tf_op jit(solution)/shard_map/ppermute | solution.py:786
  141.1 3.8 %collective-permute-start.30 = (f32[48,128]{1,0:T(8,128)S(1)}, f32[48,128]{1,0:T(8,128)S(1)}, u32[]{:S(2)}, u32[]{:S(2)}) collective-permute-start(f32[48,128]{1,0:T(8,128)S(1)} %add_add_fusion.1), channel_id=1, source_target_pairs={{0,1},{1,0},{2,3},{3,2},{4,5},{5,4},{6,7},{7,6},{8,9},{9,8},{10,11... | collective-permute-start | bytes 73736 | tf_op jit(solution)/shard_map/ppermute | solution.py:786
  142.8 3.8 %collective-permute-start.31 = (f32[48,128]{1,0:T(8,128)S(1)}, f32[48,128]{1,0:T(8,128)S(1)}, u32[]{:S(2)}, u32[]{:S(2)}) collective-permute-start(f32[48,128]{1,0:T(8,128)S(1)} %add_add_fusion.1), channel_id=1, source_target_pairs={{0,2},{1,3},{2,0},{3,1},{4,6},{5,7},{6,4},{7,5},{8,10},{9,11},{10,... | collective-permute-start | bytes 73736 | tf_op jit(solution)/shard_map/ppermute | solution.py:786
  144.5 4.7 %collective-permute-start.32 = (f32[48,128]{1,0:T(8,128)S(1)}, f32[48,128]{1,0:T(8,128)S(1)}, u32[]{:S(2)}, u32[]{:S(2)}) collective-permute-start(f32[48,128]{1,0:T(8,128)S(1)} %add_add_fusion.1), channel_id=1, source_target_pairs={{0,3},{1,2},{2,1},{3,0},{4,7},{5,6},{6,5},{7,4},{8,11},{9,10},{10,... | collective-permute-start | bytes 73736 | tf_op jit(solution)/shard_map/ppermute | solution.py:786
  149.3 13.6 %collective-permute-start.33 = (f32[32,16,256]{2,1,0:T(8,128)S(1)}, f32[32,16,256]{2,1,0:T(8,128)S(1)}, u32[]{:S(2)}, u32[]{:S(2)}) collective-permute-start(f32[32,16,256]{2,1,0:T(8,128)S(1)} %get-tuple-element.152), channel_id=1, source_target_pairs={{0,3},{1,2},{2,1},{3,0},{4,7},{5,6},{6,5},{7,4},{8,11},{9,10},{10,... | collective-permute-start | bytes 1572872 | tf_op jit(solution)/shard_map/ppermute | solution.py:793
